TPU v7x, 32 devices: a whole 2x2x4 slice. The times are simulated.
32 devices in a mesh: proto: 8 (over z, x), design: 4 (over y, core).
Axes of the slice: x: 2, y: 2, z: 4, core: 2. Of those that a mesh axis runs over, the one named last changes fastest.
Arguments:
- designs: bfloat16 [32768, 1024], P(('proto', 'design')), may hold values from -32 to 32
- prototypes: float32 [16384, 1024], P('proto'), may hold values from -6 to 6
- candidates: int32 [32, 24], P(('proto', 'design')), may hold values from 0 to 127, as said below
- positives: int32 [32768], P(('proto', 'design')), may hold values from 0 to 16383, as said below
Outputs:
- losses: float32 [32768], P(('proto', 'design'))
- design_grad: bfloat16 [32768, 1024], P(('proto', 'design'))
- proto_grad: float32 [16384, 1024], P(('proto', 'design'))
Inputs may be any that keep to these rules, and one draw needn't show every extreme that they name: `candidates`: row g lists 24 distinct blocks for the designs of device g along proto+design. Block b lies in proto shard b // 16; at most 4 blocks of a row lie in one proto shard, and in every draw one shard holds exactly 4 blocks of every row. `positives`: the positive row of design i lies in one of the blocks of row i // 1024 of candidates.
All inputs are finite; a program needn't handle non-finite values.
Results may differ from a plain program's by a relative error of at most 0.0062.
Values may be sent and summed in bfloat16 or wider, within the bound.
No kernel may reach another device: no remote copies, remote signals or barrier semaphores. Data moves between devices by JAX's collectives and lax.ppermute only.
A program may use at most 128 MiB of HBM per device.

v0:
```python
import functools

import jax
import jax.numpy as jnp
from jax import lax
from jax.experimental import pallas as pl
from jax.experimental.pallas import tpu as pltpu
from jax.sharding import PartitionSpec as P


D = 1024
TILE = 128
BF = jnp.bfloat16
F32 = jnp.float32
NEG = -1e30
PARTS = 2


def xor_proto(x, shift):
    count = lax.axis_size("proto")
    return lax.ppermute(x, "proto", [(i, i ^ shift) for i in range(count)])


def xor_design(x, shift):
    count = lax.axis_size("design")
    return lax.ppermute(x, "design", [(i, i ^ shift) for i in range(count)])


def request_table(block_list, blocks_dev, capacity, proto_count):
    owners = block_list // blocks_dev
    local_ids = block_list % blocks_dev
    ids = jnp.arange(block_list.shape[0], dtype=jnp.int32)
    earlier = (owners[:, None] == owners[None, :]) & (ids[None, :] < ids[:, None])
    rank_of = jnp.sum(earlier.astype(jnp.int32), axis=1)
    slot_of = owners * capacity + rank_of
    slots = jnp.arange(proto_count * capacity, dtype=jnp.int32)
    hit = slot_of[None, :] == slots[:, None]
    return jnp.sum(jnp.where(hit, local_ids[None, :] + 1, 0), axis=1) - 1


HBM = pl.BlockSpec(memory_space=pl.ANY)
VM = pl.BlockSpec(memory_space=pltpu.VMEM)
SM = pl.BlockSpec(memory_space=pltpu.SMEM)
WIDE = pltpu.CompilerParams(vmem_limit_bytes=40 << 20)
PARAMS = pltpu.CompilerParams(vmem_limit_bytes=16 << 20)


def gather_round_kernel(parts, table, src, *refs):
    outs, buf, sems = refs[:parts], refs[parts], refs[parts + 1]
    cap, _, step = outs[0].shape
    copies = []
    for k in range(cap):
        row = jnp.maximum(table[k], 0)
        copies.append(pltpu.make_async_copy(src.at[row], buf.at[k], sems.at[k]))
    for copy in copies:
        copy.start()
    for k, copy in enumerate(copies):
        copy.wait()
        for i in range(parts):
            outs[i][k] = buf[k, :, i * step : (i + 1) * step].astype(BF)


def gather_round(table, shard, parts):
    cap = table.shape[0]
    _, tile, width = shard.shape
    return pl.pallas_call(
        functools.partial(gather_round_kernel, parts),
        out_shape=[jax.ShapeDtypeStruct((cap, tile, width // parts), BF)] * parts,
        in_specs=[SM, HBM],
        out_specs=[VM] * parts,
        scratch_shapes=[
            pltpu.VMEM((cap, tile, width), F32),
            pltpu.SemaphoreType.DMA((cap,)),
        ],
        compiler_params=PARAMS,
        name="gather_round",
    )(table, shard)


def gather_held_kernel(n_src, n_out, quarter, lanes, me, *refs):
    tables, srcs = refs[:n_out], refs[n_out : n_out + n_src]
    outs, sems = refs[n_out + n_src : -1], refs[-1]
    cap = outs[0].shape[0]
    y, c = me[0] // 2, me[0] % 2
    for i in range(n_out * cap):
        row = jnp.maximum(tables[i // cap][i % cap], 0)
        owner, inside = row // quarter, row % quarter
        which = ((owner % 2) ^ c) * lanes + ((owner // 2) ^ y)
        for a in range(n_src):

            @pl.when(which == a)
            def _():
                pltpu.make_async_copy(
                    srcs[a].at[inside], outs[i // cap].at[i % cap], sems.at[i]
                ).start()

    for i in range(n_out * cap):
        pltpu.make_async_copy(srcs[0].at[0], outs[i // cap].at[i % cap], sems.at[i]).wait()


def gather_held(me, tables, srcs, lanes):
    n = len(tables)
    cap = tables[0].shape[0]
    quarter = srcs[0].shape[0]
    shape = (cap,) + srcs[0].shape[1:]
    return pl.pallas_call(
        functools.partial(gather_held_kernel, len(srcs), n, quarter, lanes),
        out_shape=[jax.ShapeDtypeStruct(shape, BF)] * n,
        in_specs=[SM] * (n + 1) + [HBM] * len(srcs),
        out_specs=[VM] * n,
        scratch_shapes=[pltpu.SemaphoreType.DMA((n * cap,))],
        compiler_params=PARAMS,
        name="gather_held",
    )(me, *tables, *srcs)


def contract(rows, x, lanes):
    step = rows[0].shape[1]
    total = None
    for i, part in enumerate(rows):
        got = lax.dot_general(
            part[...],
            x[lanes, i * step : (i + 1) * step],
            (((1,), (1,)), ((), ())),
            preferred_element_type=F32,
        )
        total = got if total is None else total + got
    return total


EXP_SCALE = (D ** (-0.5)) * 1.4426950408889634


def fold(tile, op):
    return op(tile.reshape(tile.shape[0] // 8, 8, tile.shape[1]), axis=0)


def slot_stats(base, rel, slots):
    top = None
    hit = None
    for n, ref in slots:
        piece = ref[...]
        target = rel == base[n]
        found = fold(jnp.where(target, piece, 0.0), jnp.sum)
        piece = piece + jnp.where(base[n] < 0, NEG, 0.0)
        high = fold(piece, jnp.max)
        top = high if top is None else jnp.maximum(top, high)
        hit = found if hit is None else hit + found
    return jnp.max(top, axis=0, keepdims=True), jnp.sum(hit, axis=0, keepdims=True)


def slot_power(base, n, ref, top):
    piece = ref[...] + jnp.where(base[n] < 0, NEG, 0.0)
    return jnp.exp2((piece - top) * EXP_SCALE)


def relative(pos, lanes):
    line = lax.broadcasted_iota(jnp.int32, (TILE, lanes), 0)
    return pos - line


def own_kernel(group, cap, lanes, parts, base, x, pos, *refs):
    rows = [refs[s * parts : (s + 1) * parts] for s in range(group)]
    logits = refs[group * parts : group * (parts + 1)]
    top_out, sum_out, hit_out = refs[group * (parts + 1) :]
    count = x.shape[0]
    for j in range(0, count, lanes):
        at = pl.ds(j, lanes)
        for s in range(group):
            logits[s][:, at] = contract(rows[s], x, slice(j, j + lanes))
        slots = [
            (s * cap + k, logits[s].at[pl.ds(k * TILE, TILE), at])
            for s in range(group)
            for k in range(cap)
        ]
        top, hit = slot_stats(base, relative(pos[:, at], lanes), slots)
        total = None
        for n, ref in slots:
            part = fold(slot_power(base, n, ref, top), jnp.sum)
            total = part if total is None else total + part
        top_out[:, at] = top
        hit_out[:, at] = hit
        sum_out[:, at] = jnp.sum(total, axis=0, keepdims=True)


def own_logits(base, x, pos, rows, cap, lanes=256):
    group, parts = len(rows), len(rows[0])
    rows = [r for row in rows for r in row]
    count = x.shape[0]
    line = (1, count)
    shape = (rows[0].shape[0], count)
    return pl.pallas_call(
        functools.partial(own_kernel, group, cap, lanes, parts),
        out_shape=[jax.ShapeDtypeStruct(shape, F32)] * group
        + [jax.ShapeDtypeStruct(line, F32)] * 3,
        in_specs=[SM] + [VM] * (2 + len(rows)),
        out_specs=[VM] * (group + 3),
        compiler_params=PARAMS,
        name="own_logits",
    )(base, x, pos, *rows)


def far_kernel(group, cap, lanes, parts, base, x, pos, top_own, sum_own, hit_own, *refs):
    rows = [refs[s * parts : (s + 1) * parts] for s in range(group)]
    refs = refs[group * parts :]
    losses, top_out, inv_out = refs[:3]
    grads = refs[3 : group + 3]
    tiles = refs[group + 3 : -1]
    logits = refs[-1]
    count, width = x.shape
    scale = D ** (-0.5)
    for j in range(0, count, lanes):
        turn = (j // lanes) % 2
        at = pl.ds(j, lanes)
        for s in range(group):
            logits[turn, s * cap * TILE : (s + 1) * cap * TILE, :] = contract(
                rows[s], x, slice(j, j + lanes)
            )
        slots = [
            (n, logits.at[turn, pl.ds(n * TILE, TILE), :]) for n in range(group * cap)
        ]
        rel = relative(pos[:, at], lanes)
        top, hit = slot_stats(base, rel, slots)
        mine = top_own[:, at]
        both = jnp.maximum(top, mine)
        total = None
        for n, ref in slots:
            power = slot_power(base, n, ref, both)
            ref[...] = power
            part = fold(power, jnp.sum)
            total = part if total is None else total + part
        total = jnp.sum(total, axis=0, keepdims=True)
        total = total + sum_own[:, at] * jnp.exp2((mine - both) * EXP_SCALE)
        losses[:, at] = both * scale + jnp.log(total) - (hit + hit_own[:, at]) * scale
        inv = 1.0 / total
        top_out[:, at] = both
        inv_out[:, at] = inv
        for n, ref in slots:
            s, k = n // cap, n % cap
            target = jnp.where(rel == base[n], 1.0, 0.0)
            grads[s][k * TILE : (k + 1) * TILE, at] = (ref[...] * inv - target).astype(BF)
    step = width // parts
    for i in range(parts):
        for s in range(group):
            tiles[i * group + s][...] = jnp.dot(
                grads[s][...], x[:, i * step : (i + 1) * step], preferred_element_type=F32
            ).astype(BF)


def far_grads(base, x, pos, stats, rows, cap, parts, lanes=256):
    group = len(rows)
    rows = [r for row in rows for r in row]
    count, width = x.shape
    size = rows[0].shape[0]
    outs = [((1, count), F32)] * 3 + [((size, count), BF)] * group
    outs += [((size, width // parts), BF)] * (group * parts)
    got = pl.pallas_call(
        functools.partial(far_kernel, group, cap, lanes, parts),
        out_shape=[jax.ShapeDtypeStruct(*o) for o in outs],
        in_specs=[SM] + [VM] * (5 + len(rows)),
        out_specs=[VM] * len(outs),
        scratch_shapes=[pltpu.VMEM((2, group * size, lanes), F32)],
        compiler_params=PARAMS,
        name="far_grads",
    )(base, x, pos, *stats, *rows)
    tiles = got[3 + group :]
    return got[:3], got[3 : 3 + group], [tiles[i * group : (i + 1) * group] for i in range(parts)]


def own_grad_kernel(cap, parts, base, x, pos, top, inv, logits, grad, *tiles):
    count, width = x.shape
    rel = relative(pos[...], count)
    for k in range(cap):
        ref = logits.at[pl.ds(k * TILE, TILE), :]
        power = slot_power(base, k, ref, top[...])
        target = jnp.where(rel == base[k], 1.0, 0.0)
        grad[k * TILE : (k + 1) * TILE, :] = (power * inv[...] - target).astype(BF)
    step = width // parts
    for i in range(parts):
        tiles[i][...] = jnp.dot(
            grad[...], x[:, i * step : (i + 1) * step], preferred_element_type=F32
        ).astype(BF)


def own_grad(base, x, pos, top, inv, logits, cap, parts):
    count, width = x.shape
    size = logits.shape[0]
    outs = [((size, count), BF)] + [((size, width // parts), BF)] * parts
    got = pl.pallas_call(
        functools.partial(own_grad_kernel, cap, parts),
        out_shape=[jax.ShapeDtypeStruct(*o) for o in outs],
        in_specs=[SM] + [VM] * 5,
        out_specs=[VM] * len(outs),
        compiler_params=PARAMS,
        name="own_grad",
    )(base, x, pos, top, inv, logits)
    return got[0], got[1:]


def design_grad_kernel(n, *refs):
    grads, rows, out = refs[:n], refs[n : 2 * n], refs[2 * n]
    acc = None
    for g, r in zip(grads, rows):
        part = lax.dot_general(
            g[...], r[...], (((0,), (0,)), ((), ())), preferred_element_type=F32
        )
        acc = part if acc is None else acc + part
    out[...] = acc.astype(BF)


def design_grad(grads, rows, chunk=256):
    n = len(grads)
    cols, count = grads[0].shape
    width = rows[0].shape[1]
    return pl.pallas_call(
        functools.partial(design_grad_kernel, n),
        out_shape=jax.ShapeDtypeStruct((count, width), BF),
        grid=(count // chunk,),
        in_specs=[pl.BlockSpec((cols, chunk), lambda i: (0, i))] * n
        + [pl.BlockSpec((cols, width), lambda i: (0, 0))] * n,
        out_specs=pl.BlockSpec((chunk, width), lambda i: (i, 0)),
        compiler_params=WIDE,
        name="design_grad",
    )(*grads, *rows)


def collect_kernel(n, cap, spot, *refs):
    parts = refs[:n]
    keep, give, acc = refs[n:]
    kept = keep.shape[0]
    acc[...] = jnp.zeros_like(acc)
    for i in range(n * cap):

        @pl.when(spot[i] >= 0)
        def _():
            s, k = i // cap, i % cap
            acc[spot[i]] += parts[s][k * TILE : (k + 1) * TILE, :].astype(F32)

    keep[...] = acc[:kept]
    give[...] = acc[kept:].astype(BF)


def collect(spot, parts, cap, kept):
    n = len(parts)
    width = parts[0].shape[1]
    shape = (kept, TILE, width)
    return pl.pallas_call(
        functools.partial(collect_kernel, n, cap),
        out_shape=[jax.ShapeDtypeStruct(shape, F32), jax.ShapeDtypeStruct(shape, BF)],
        in_specs=[SM] + [VM] * n,
        out_specs=[VM] * 2,
        scratch_shapes=[pltpu.VMEM((2 * kept, TILE, width), F32)],
        compiler_params=PARAMS,
        name="collect",
    )(spot, *parts)


def body(designs, prototypes, candidates, positives):
    proto_count = lax.axis_size("proto")
    design_axis = lax.axis_size("design")
    half = proto_count // 2
    lanes = design_axis // 2
    cand_count = candidates.shape[1]
    width = designs.shape[1]
    count = designs.shape[0]
    blocks_dev = prototypes.shape[0] // TILE
    quarter = blocks_dev // design_axis
    cap = max(2, (4 * cand_count + 3 * proto_count - 1) // (3 * proto_count))
    parts = PARTS
    step = width // parts
    p = lax.axis_index("proto").astype(jnp.int32)
    d = lax.axis_index("design").astype(jnp.int32)
    q = p % half
    h = p // half
    y = d // 2
    c = d % 2
    me = d.reshape(1)
    shifts = list(range(half - 1, 0, -1))
    evens = list(range(2, half, 2))
    columns = [slice(i * step, (i + 1) * step) for i in range(parts)]

    wanted = request_table(candidates[0], blocks_dev, cap, proto_count)
    wanted = wanted.reshape(2, half, cap)
    near = [wanted[h, q ^ s] for s in range(half)]
    other = [wanted[1 - h, q ^ s] for s in range(half)]
    asking = {0: other[0]}
    for s in shifts:
        if s == 1:
            note = jnp.stack([other[1]] + [near[u ^ 1] for u in [0] + evens])
            note = xor_proto(note, 1)
            asking[1] = note[0]
            beside = {u: note[1 + n] for n, u in enumerate([0] + evens)}
        else:
            asking[s] = xor_proto(other[s], s)

    shard = prototypes.reshape(blocks_dev, TILE, width)
    mine = lax.dynamic_slice_in_dim(shard, d * quarter, quarter, axis=0).astype(BF)
    sent = {}
    for i in range(parts):
        piece = mine[:, :, columns[i]]
        for u in evens:
            sent[u, i] = xor_proto(piece, u)
        sent["far", i] = xor_proto(piece, half)

    def share(piece):
        held = [piece]
        for ys in range(1, lanes):
            held.append(xor_design(piece, 2 * ys))
        return held + [xor_design(held[ys], 1) for ys in range(lanes)]

    def flat(piece):
        return piece.reshape(cap * TILE, step)

    own_rows = [[None] * parts for _ in range(half)]
    far_rows = [[None] * parts for _ in range(half)]
    out = gather_round(beside[0], shard, parts)
    for i in range(parts):
        own_rows[1][i] = flat(xor_proto(out[i], 1))
    out = gather_round(near[0], shard, parts)
    for i in range(parts):
        own_rows[0][i] = flat(out[i])
    for i in range(parts):
        for u in evens:
            held = share(sent[u, i])
            (out,) = gather_held(me, [beside[u]], held, lanes)
            own_rows[u ^ 1][i] = flat(xor_proto(out, 1))
            (out,) = gather_held(me, [near[u]], held, lanes)
            own_rows[u][i] = flat(out)
        held = share(sent["far", i])
        outs = gather_held(me, [asking[s] for s in shifts], held, lanes)
        for s, out in zip(shifts, outs):
            far_rows[s][i] = flat(xor_proto(out, s))
        (out,) = gather_held(me, [asking[0]], held, lanes)
        far_rows[0][i] = flat(out)

    def bases(lists, which_half):
        out = []
        for s in range(half):
            first = (which_half * half + (q ^ s)) * blocks_dev
            out.append(jnp.where(lists[s] >= 0, (first + lists[s]) * TILE, -(2**30)))
        return jnp.concatenate(out)

    pos = positives.reshape(1, count)
    own_base = bases(near, h)
    *logits, top, total, hit = own_logits(own_base, designs, pos, own_rows, cap)
    stats, far_g, far_tiles = far_grads(
        bases(other, 1 - h), designs, pos, (top, total, hit), far_rows, cap, parts
    )
    losses, top, inv = stats
    own_base = own_base.reshape(half, cap)
    own_g, own_tiles = [], []
    for s in range(half):
        g, t = own_grad(own_base[s], designs, pos, top, inv, logits[s], cap, parts)
        own_g.append(g)
        own_tiles.append(t)

    kept = lanes * quarter

    def spots(tables):
        table = jnp.concatenate(tables)
        owner = table // quarter
        at = ((owner // 2) ^ y) * quarter + table % quarter
        at = at + jnp.where(owner % 2 == c, 0, kept)
        return jnp.where(table >= 0, at, -1)

    def reduce_shard(tables, tiles):
        keep, give = collect(spots(tables), tiles, cap, kept)
        keep = keep + xor_design(give, 1).astype(F32)
        keep = keep.reshape(lanes, quarter, TILE, step)
        total = keep[0]
        for ys in range(1, lanes):
            back = xor_design(keep[ys].astype(BF), 2 * ys)
            total = total + back.astype(F32)
        return total

    result = []
    dgrad = []
    far_tables = [asking[s] for s in range(half)]
    for i in range(parts):
        tiles = [far_tiles[i][0]]
        tiles += [xor_proto(far_tiles[i][s], s) for s in range(1, half)]
        total = reduce_shard(far_tables, tiles)
        landed = [xor_proto(total.astype(BF), half)]
        for u in evens:
            tile = xor_proto(own_tiles[u ^ 1][i], 1)
            total = reduce_shard([near[u], beside[u]], [own_tiles[u][i], tile])
            landed.append(xor_proto(total.astype(BF), u))
        tile = xor_proto(own_tiles[1][i], 1)
        total = reduce_shard([near[0], beside[0]], [own_tiles[0][i], tile])
        for piece in landed:
            total = total + piece.astype(F32)
        result.append(total)
        dgrad.append(
            design_grad(own_g + list(far_g), [r[i] for r in own_rows + far_rows])
        )
    result = jnp.concatenate(result, axis=-1).reshape(quarter * TILE, width)
    return (losses.reshape(count), jnp.concatenate(dgrad, axis=-1), result)


def solution(mesh):
    return jax.shard_map(
        body,
        mesh=mesh,
        in_specs=(
            P(("proto", "design"), None),
            P("proto", None),
            P(("proto", "design"), None),
            P(("proto", "design")),
        ),
        out_specs=(
            P(("proto", "design")),
            P(("proto", "design"), None),
            P(("proto", "design"), None),
        ),
        check_vma=False,
    )
```

profile of v0, /device:TPU:0, one launch (start us, length us, event | category | flops | bytes accessed | tf_op | source)
XLA Modules:
  0.0 428.7 jit_solution(5205429978398622270)
XLA Ops:
  0.6 1.7 dynamic-slice_convert_fusion
  3.3 4.1 collective-permute-start.17
  7.3 1.6 collective-permute-start.7
  9.8 2.9 collective-permute-start.21
  12.8 41.7 %collective-permute-done.21.refs_0_ = s32[4]{0:T(128)S(1)} collective-permute-done((s32[4]{0:T(128)S(1)}, s32[4]{0:T(128)S(1)}, u32[]{:S(2)}, u32[]{:S(2)}) %collective-permute-start.21) | collective-permute-done | bytes 48 | tf_op jit(solution)/shard_map/ppermute | solution.py:21
  56.0 2.1 collective-permute-done.22.refs_1_
  58.5 3.1 collective-permute-done
  65.8 10.6 %collective-permute-done.18.refs_2_.refs_4_ = bf16[4,128,512]{2,1,0:T(8,128)(2,1)S(1)} collective-permute-done((bf16[4,128,512]{2,1,0:T(8,128)(2,1)S(1)}, bf16[4,128,512]{2,1,0:T(8,128)(2,1)S(1)}, u32[]{:S(2)}, u32[]{:S(2)}) %collective-permute-start.18) | collective-permute-done | bytes 524320 | tf_op jit(solution)/shard_map/ppermute | solution.py:26
  76.9 10.7 %collective-permute-done.8.refs_2_ = bf16[4,128,512]{2,1,0:T(8,128)(2,1)S(1)} collective-permute-done((bf16[4,128,512]{2,1,0:T(8,128)(2,1)S(1)}, bf16[4,128,512]{2,1,0:T(8,128)(2,1)S(1)}, u32[]{:S(2)}, u32[]{:S(2)}) %collective-permute-start.8) | collective-permute-done | bytes 524320 | tf_op jit(solution)/shard_map/ppermute | solution.py:26
  87.7 11.2 %collective-permute-done.14.refs_2_.refs_4_ = bf16[4,128,512]{2,1,0:T(8,128)(2,1)S(1)} collective-permute-done((bf16[4,128,512]{2,1,0:T(8,128)(2,1)S(1)}, bf16[4,128,512]{2,1,0:T(8,128)(2,1)S(1)}, u32[]{:S(2)}, u32[]{:S(2)}) %collective-permute-start.14) | collective-permute-done | bytes 524320 | tf_op jit(solution)/shard_map/ppermute | solution.py:26
  98.9 7.5 %collective-permute-done.4.refs_2_ = bf16[4,128,512]{2,1,0:T(8,128)(2,1)S(1)} collective-permute-done((bf16[4,128,512]{2,1,0:T(8,128)(2,1)S(1)}, bf16[4,128,512]{2,1,0:T(8,128)(2,1)S(1)}, u32[]{:S(2)}, u32[]{:S(2)}) %collective-permute-start.4) | collective-permute-done | bytes 524320 | tf_op jit(solution)/shard_map/ppermute | solution.py:26
  107.0 3.4 copy-done.1
  111.2 3.1 gather_held.15
  118.4 1.6 collective-permute-start.12
  122.0 3.1 gather_held.14
  125.1 4.1 collective-permute-done.1
  129.9 10.5 %collective-permute-done.2 = bf16[4,128,512]{2,1,0:T(8,128)(2,1)S(1)} collective-permute-done((bf16[4,128,512]{2,1,0:T(8,128)(2,1)S(1)}, bf16[4,128,512]{2,1,0:T(8,128)(2,1)S(1)}, u32[]{:S(2)}, u32[]{:S(2)}) %collective-permute-start.2) | collective-permute-done | bytes 524320 | tf_op jit(solution)/shard_map/ppermute | solution.py:21
  141.1 21.8 %collective-permute-done.24 = bf16[4,128,512]{2,1,0:T(8,128)(2,1)S(1)} collective-permute-done((bf16[4,128,512]{2,1,0:T(8,128)(2,1)S(1)}, bf16[4,128,512]{2,1,0:T(8,128)(2,1)S(1)}, u32[]{:S(2)}, u32[]{:S(2)}) %collective-permute-start.24) | collective-permute-done | bytes 524320 | tf_op jit(solution)/shard_map/ppermute | solution.py:21
  163.4 10.7 %collective-permute-done.12 = bf16[4,128,512]{2,1,0:T(8,128)(2,1)S(1)} collective-permute-done((bf16[4,128,512]{2,1,0:T(8,128)(2,1)S(1)}, bf16[4,128,512]{2,1,0:T(8,128)(2,1)S(1)}, u32[]{:S(2)}, u32[]{:S(2)}) %collective-permute-start.12) | collective-permute-done | bytes 524320 | tf_op jit(solution)/shard_map/ppermute | solution.py:21
  174.9 10.5 %collective-permute-done.11 = bf16[4,128,512]{2,1,0:T(8,128)(2,1)S(1)} collective-permute-done((bf16[4,128,512]{2,1,0:T(8,128)(2,1)S(1)}, bf16[4,128,512]{2,1,0:T(8,128)(2,1)S(1)}, u32[]{:S(2)}, u32[]{:S(2)}) %collective-permute-start.11) | collective-permute-done | bytes 524320 | tf_op jit(solution)/shard_map/ppermute | solution.py:21
  191.4 1.9 gather_held.8
  193.4 6.6 %own_logits.1 = (f32[512,1024]{1,0:T(8,128)S(1)}, f32[512,1024]{1,0:T(8,128)S(1)}, f32[512,1024]{1,0:T(8,128)S(1)}, f32[512,1024]{1,0:T(8,128)S(1)}, f32[1,1024]...) custom-call(s32[16]{0:T(128)S(1)} %pad_add_fusion.2.base, bf16[1024,1024]{1,0:T(8,128)(2,1)S(1)} %copy-done, ...), custom_call_target="tpu_custom_call" | custom-call | tf_op jit(solution)/shard_map/own_logits/pallas_call | solution.py:192
  205.2 1.6 collective-permute-done.23
  206.9 13.7 %far_grads.1 = (f32[1,1024]{1,0:T(1,128)}, f32[1,1024]{1,0:T(1,128)S(1)}, f32[1,1024]{1,0:T(1,128)S(1)}, bf16[512,1024]{1,0:T(8,128)(2,1)S(1)}, bf16[512,1024]{1...) custom-call(s32[16]{0:T(128)S(1)} %pad_add_fusion.1.base, ...), custom_call_target="tpu_custom_call" | custom-call | tf_op jit(solution)/shard_map/far_grads/pallas_call | solution.py:257
  227.5 2.2 collective-permute-start.34
  231.0 19.5 %collective-permute-done.32.refs_1_ = bf16[512,512]{1,0:T(8,128)(2,1)S(1)} collective-permute-done((bf16[512,512]{1,0:T(8,128)(2,1)S(1)}, bf16[512,512]{1,0:T(8,128)(2,1)S(1)}, u32[]{:S(2)}, u32[]{:S(2)}) %collective-permute-start.32) | collective-permute-done | bytes 524320 | tf_op jit(solution)/shard_map/ppermute | solution.py:21
  252.1 1.6 copy-done.25
  253.7 1.9 own_grad.5
  255.6 1.6 collective-permute-start.42
  257.3 2.3 collect.7
  259.7 15.1 %collective-permute-done.45.refs_1_ = bf16[512,512]{1,0:T(8,128)(2,1)} collective-permute-done((bf16[512,512]{1,0:T(8,128)(2,1)}, bf16[512,512]{1,0:T(8,128)(2,1)}, u32[]{:S(2)}, u32[]{:S(2)}) %collective-permute-start.45) | collective-permute-done | bytes 524320 | tf_op jit(solution)/shard_map/ppermute | solution.py:21
  275.4 2.3 collect.10
  277.9 1.9 own_grad.7
  281.3 4.7 %collective-permute-done.42.refs_1_ = bf16[512,512]{1,0:T(8,128)(2,1)S(1)} collective-permute-done((bf16[512,512]{1,0:T(8,128)(2,1)S(1)}, bf16[512,512]{1,0:T(8,128)(2,1)S(1)}, u32[]{:S(2)}, u32[]{:S(2)}) %collective-permute-start.42) | collective-permute-done | bytes 524320 | tf_op jit(solution)/shard_map/ppermute | solution.py:21
  286.7 1.9 own_grad.4
  289.9 7.3 %collective-permute-done.29.refs_1_ = bf16[512,512]{1,0:T(8,128)(2,1)S(1)} collective-permute-done((bf16[512,512]{1,0:T(8,128)(2,1)S(1)}, bf16[512,512]{1,0:T(8,128)(2,1)S(1)}, u32[]{:S(2)}, u32[]{:S(2)}) %collective-permute-start.29) | collective-permute-done | bytes 524320 | tf_op jit(solution)/shard_map/ppermute | solution.py:21
  297.4 1.9 own_grad.6
  300.6 7.9 %collective-permute-done.51.refs_1_ = bf16[512,512]{1,0:T(8,128)(2,1)S(1)} collective-permute-done((bf16[512,512]{1,0:T(8,128)(2,1)S(1)}, bf16[512,512]{1,0:T(8,128)(2,1)S(1)}, u32[]{:S(2)}, u32[]{:S(2)}) %collective-permute-start.51) | collective-permute-done | bytes 524320 | tf_op jit(solution)/shard_map/ppermute | solution.py:21
  310.0 7.9 %collective-permute-done.38.refs_1_ = bf16[512,512]{1,0:T(8,128)(2,1)S(1)} collective-permute-done((bf16[512,512]{1,0:T(8,128)(2,1)S(1)}, bf16[512,512]{1,0:T(8,128)(2,1)S(1)}, u32[]{:S(2)}, u32[]{:S(2)}) %collective-permute-start.38) | collective-permute-done | bytes 524320 | tf_op jit(solution)/shard_map/ppermute | solution.py:21
  320.2 1.6 collective-permute-start.36
  323.3 1.6 collective-permute-start.44
  329.2 17.1 %collective-permute-done.49 = bf16[4,128,512]{2,1,0:T(8,128)(2,1)S(1)} collective-permute-done((bf16[4,128,512]{2,1,0:T(8,128)(2,1)S(1)}, bf16[4,128,512]{2,1,0:T(8,128)(2,1)S(1)}, u32[]{:S(2)}, u32[]{:S(2)}) %collective-permute-start.49) | collective-permute-done | bytes 524320 | tf_op jit(solution)/shard_map/ppermute | solution.py:26
  348.0 32.0 %collective-permute-done.53 = bf16[4,128,512]{2,1,0:T(8,128)(2,1)S(1)} collective-permute-done((bf16[4,128,512]{2,1,0:T(8,128)(2,1)S(1)}, bf16[4,128,512]{2,1,0:T(8,128)(2,1)S(1)}, u32[]{:S(2)}, u32[]{:S(2)}) %collective-permute-start.53) | collective-permute-done | bytes 524320 | tf_op jit(solution)/shard_map/ppermute | solution.py:26
  382.5 7.9 %collective-permute-done.40 = bf16[4,128,512]{2,1,0:T(8,128)(2,1)S(1)} collective-permute-done((bf16[4,128,512]{2,1,0:T(8,128)(2,1)S(1)}, bf16[4,128,512]{2,1,0:T(8,128)(2,1)S(1)}, u32[]{:S(2)}, u32[]{:S(2)}) %collective-permute-start.40) | collective-permute-done | bytes 524320 | tf_op jit(solution)/shard_map/ppermute | solution.py:26
  392.7 6.3 %design_grad.3 = bf16[1024,512]{1,0:T(8,128)(2,1)S(1)} custom-call(bf16[512,1024]{1,0:T(8,128)(2,1)S(1)} %get-tuple-element.76.refs_0_, bf16[512,1024]{1,0:T(8,128)(2,1)S(1)} %get-tuple-element.78.refs_1_, bf16[512,1024]{1,0:T(8,128)(2,1)S(1)} %get-tuple-element.80.refs_2_, bf16[512,1024]{1,0:T(8,128)(2,1)S(1)} %get-tuple-element.82.refs_3_, ...), custom_call_target="tpu_custom_call" | custom-call | tf_op jit(solution)/shard_map/design_grad/pallas_call | solution.py:315
  399.1 6.3 %design_grad.2 = bf16[1024,512]{1,0:T(8,128)(2,1)S(1)} custom-call(bf16[512,1024]{1,0:T(8,128)(2,1)S(1)} %get-tuple-element.76.refs_0_, bf16[512,1024]{1,0:T(8,128)(2,1)S(1)} %get-tuple-element.78.refs_1_, bf16[512,1024]{1,0:T(8,128)(2,1)S(1)} %get-tuple-element.80.refs_2_, bf16[512,1024]{1,0:T(8,128)(2,1)S(1)} %get-tuple-element.82.refs_3_, ...), custom_call_target="tpu_custom_call" | custom-call | tf_op jit(solution)/shard_map/design_grad/pallas_call | solution.py:315
  405.5 1.6 pad_maximum_fusion
  408.2 18.6 %collective-permute-done.37 = bf16[4,128,512]{2,1,0:T(8,128)(2,1)S(1)} collective-permute-done((bf16[4,128,512]{2,1,0:T(8,128)(2,1)S(1)}, bf16[4,128,512]{2,1,0:T(8,128)(2,1)S(1)}, u32[]{:S(2)}, u32[]{:S(2)}) %collective-permute-start.37) | collective-permute-done | bytes 524320 | tf_op jit(solution)/shard_map/ppermute | solution.py:21
  (253 shorter events, 63.5 us)
Async XLA Ops:
  3.3 52.7 %collective-permute-start.17 = (bf16[4,128,512]{2,1,0:T(8,128)(2,1)}, bf16[4,128,512]{2,1,0:T(8,128)(2,1)S(1)}, u32[]{:S(2)}, u32[]{:S(2)}) collective-permute-start(bf16[4,128,512]{2,1,0:T(8,128)(2,1)} %get-tuple-element.125), channel_id=1, source_target_pairs={{0,16},{4,20},{8,24},{12,28},{16,0},{20,4},{24,8},{28,12},{1,17},{... | collective-permute-start | bytes 1572872 | tf_op jit(solution)/shard_map/ppermute | solution.py:21
  7.3 55.8 %collective-permute-start.7 = (bf16[4,128,512]{2,1,0:T(8,128)(2,1)}, bf16[4,128,512]{2,1,0:T(8,128)(2,1)S(1)}, u32[]{:S(2)}, u32[]{:S(2)}) collective-permute-start(bf16[4,128,512]{2,1,0:T(8,128)(2,1)} %get-tuple-element.125), channel_id=1, source_target_pairs={{0,8},{4,12},{8,0},{12,4},{16,24},{20,28},{24,16},{28,20},{1,9},{5... | collective-permute-start | bytes 1572872 | tf_op jit(solution)/shard_map/ppermute | solution.py:21
  8.9 54.2 %collective-permute-start.13 = (bf16[4,128,512]{2,1,0:T(8,128)(2,1)S(1)}, bf16[4,128,512]{2,1,0:T(8,128)(2,1)S(1)}, u32[]{:S(2)}, u32[]{:S(2)}) collective-permute-start(bf16[4,128,512]{2,1,0:T(8,128)(2,1)S(1)} %get-tuple-element.126), channel_id=1, source_target_pairs={{0,16},{4,20},{8,24},{12,28},{16,0},{20,4},{24,8},{28,12},{1,17},{... | collective-permute-start | bytes 1572872 | tf_op jit(solution)/shard_map/ppermute | solution.py:21
  9.3 54.5 %collective-permute-start.3 = (bf16[4,128,512]{2,1,0:T(8,128)(2,1)S(1)}, bf16[4,128,512]{2,1,0:T(8,128)(2,1)S(1)}, u32[]{:S(2)}, u32[]{:S(2)}) collective-permute-start(bf16[4,128,512]{2,1,0:T(8,128)(2,1)S(1)} %get-tuple-element.126), channel_id=1, source_target_pairs={{0,8},{4,12},{8,0},{12,4},{16,24},{20,28},{24,16},{28,20},{1,9},{5... | collective-permute-start | bytes 1572872 | tf_op jit(solution)/shard_map/ppermute | solution.py:21
  9.8 44.6 %collective-permute-start.21 = (s32[4]{0:T(128)S(1)}, s32[4]{0:T(128)S(1)}, u32[]{:S(2)}, u32[]{:S(2)}) collective-permute-start(s32[4]{0:T(128)S(1)} %get-tuple-element.136), channel_id=1, source_target_pairs={{0,12},{4,8},{8,4},{12,0},{16,28},{20,24},{24,20},{28,16},{1,13},{... | collective-permute-start | bytes 56 | tf_op jit(solution)/shard_map/ppermute | solution.py:21
  61.6 14.8 %collective-permute-start.18 = (bf16[4,128,512]{2,1,0:T(8,128)(2,1)S(1)}, bf16[4,128,512]{2,1,0:T(8,128)(2,1)S(1)}, u32[]{:S(2)}, u32[]{:S(2)}) collective-permute-start(bf16[4,128,512]{2,1,0:T(8,128)(2,1)S(1)} %collective-permute-done.17.refs_1_.refs_3_), channel_id=1, source_target_pairs={{0,2},{1,3},{2,0},{3,1},{4,6},{5,7},{6,4},{7,5},{8,10},{9,11},{10,... | collective-permute-start | bytes 1572872 | tf_op jit(solution)/shard_map/ppermute | solution.py:26
  63.2 24.5 %collective-permute-start.8 = (bf16[4,128,512]{2,1,0:T(8,128)(2,1)S(1)}, bf16[4,128,512]{2,1,0:T(8,128)(2,1)S(1)}, u32[]{:S(2)}, u32[]{:S(2)}) collective-permute-start(bf16[4,128,512]{2,1,0:T(8,128)(2,1)S(1)} %collective-permute-done.7.refs_1_), channel_id=1, source_target_pairs={{0,2},{1,3},{2,0},{3,1},{4,6},{5,7},{6,4},{7,5},{8,10},{9,11},{10,... | collective-permute-start | bytes 1572872 | tf_op jit(solution)/shard_map/ppermute | solution.py:26
  63.7 35.1 %collective-permute-start.14 = (bf16[4,128,512]{2,1,0:T(8,128)(2,1)S(1)}, bf16[4,128,512]{2,1,0:T(8,128)(2,1)S(1)}, u32[]{:S(2)}, u32[]{:S(2)}) collective-permute-start(bf16[4,128,512]{2,1,0:T(8,128)(2,1)S(1)} %collective-permute-done.13.refs_1_.refs_3_), channel_id=1, source_target_pairs={{0,2},{1,3},{2,0},{3,1},{4,6},{5,7},{6,4},{7,5},{8,10},{9,11},{10,... | collective-permute-start | bytes 1572872 | tf_op jit(solution)/shard_map/ppermute | solution.py:26
  65.3 41.2 %collective-permute-start.4 = (bf16[4,128,512]{2,1,0:T(8,128)(2,1)S(1)}, bf16[4,128,512]{2,1,0:T(8,128)(2,1)S(1)}, u32[]{:S(2)}, u32[]{:S(2)}) collective-permute-start(bf16[4,128,512]{2,1,0:T(8,128)(2,1)S(1)} %collective-permute-done.3.refs_1_), channel_id=1, source_target_pairs={{0,2},{1,3},{2,0},{3,1},{4,6},{5,7},{6,4},{7,5},{8,10},{9,11},{10,... | collective-permute-start | bytes 1572872 | tf_op jit(solution)/shard_map/ppermute | solution.py:26
  76.4 30.0 %collective-permute-start.20 = (bf16[4,128,512]{2,1,0:T(8,128)(2,1)S(1)}, bf16[4,128,512]{2,1,0:T(8,128)(2,1)S(1)}, u32[]{:S(2)}, u32[]{:S(2)}) collective-permute-start(bf16[4,128,512]{2,1,0:T(8,128)(2,1)S(1)} %collective-permute-done.18.refs_2_.refs_4_), channel_id=1, source_target_pairs={{0,1},{1,0},{2,3},{3,2},{4,5},{5,4},{6,7},{7,6},{8,9},{9,8},{10,11... | collective-permute-start | bytes 1572872 | tf_op jit(solution)/shard_map/ppermute | solution.py:26
  76.4 37.9 %collective-permute-start.15 = (bf16[4,128,512]{2,1,0:T(8,128)(2,1)S(1)}, bf16[4,128,512]{2,1,0:T(8,128)(2,1)S(1)}, u32[]{:S(2)}, u32[]{:S(2)}) collective-permute-start(bf16[4,128,512]{2,1,0:T(8,128)(2,1)S(1)} %collective-permute-done.13.refs_1_.refs_3_), channel_id=1, source_target_pairs={{0,1},{1,0},{2,3},{3,2},{4,5},{5,4},{6,7},{7,6},{8,9},{9,8},{10,11... | collective-permute-start | bytes 1572872 | tf_op jit(solution)/shard_map/ppermute | solution.py:26
  87.7 27.3 %collective-permute-start.5 = (bf16[4,128,512]{2,1,0:T(8,128)(2,1)S(1)}, bf16[4,128,512]{2,1,0:T(8,128)(2,1)S(1)}, u32[]{:S(2)}, u32[]{:S(2)}) collective-permute-start(bf16[4,128,512]{2,1,0:T(8,128)(2,1)S(1)} %collective-permute-done.3.refs_1_), channel_id=1, source_target_pairs={{0,1},{1,0},{2,3},{3,2},{4,5},{5,4},{6,7},{7,6},{8,9},{9,8},{10,11... | collective-permute-start | bytes 1572872 | tf_op jit(solution)/shard_map/ppermute | solution.py:26
  98.9 17.5 %collective-permute-start.10 = (bf16[4,128,512]{2,1,0:T(8,128)(2,1)S(1)}, bf16[4,128,512]{2,1,0:T(8,128)(2,1)S(1)}, u32[]{:S(2)}, u32[]{:S(2)}) collective-permute-start(bf16[4,128,512]{2,1,0:T(8,128)(2,1)S(1)} %collective-permute-done.8.refs_2_), channel_id=1, source_target_pairs={{0,1},{1,0},{2,3},{3,2},{4,5},{5,4},{6,7},{7,6},{8,9},{9,8},{10,11... | collective-permute-start | bytes 1572872 | tf_op jit(solution)/shard_map/ppermute | solution.py:26
  106.5 14.9 %collective-permute-start.16 = (bf16[4,128,512]{2,1,0:T(8,128)(2,1)S(1)}, bf16[4,128,512]{2,1,0:T(8,128)(2,1)S(1)}, u32[]{:S(2)}, u32[]{:S(2)}) collective-permute-start(bf16[4,128,512]{2,1,0:T(8,128)(2,1)S(1)} %collective-permute-done.14.refs_2_.refs_4_), channel_id=1, source_target_pairs={{0,1},{1,0},{2,3},{3,2},{4,5},{5,4},{6,7},{7,6},{8,9},{9,8},{10,11... | collective-permute-start | bytes 1572872 | tf_op jit(solution)/shard_map/ppermute | solution.py:26
  114.3 14.9 %collective-permute-start.1 = (bf16[4,128,512]{2,1,0:T(8,128)(2,1)S(1)}, bf16[4,128,512]{2,1,0:T(8,128)(2,1)S(1)}, u32[]{:S(2)}, u32[]{:S(2)}) collective-permute-start(bf16[4,128,512]{2,1,0:T(8,128)(2,1)S(1)} %get-tuple-element.61), channel_id=1, source_target_pairs={{0,4},{4,0},{8,12},{12,8},{16,20},{20,16},{24,28},{28,24},{1,5},{5... | collective-permute-start | bytes 1572872 | tf_op jit(solution)/shard_map/ppermute | solution.py:21
  114.9 25.5 %collective-permute-start.2 = (bf16[4,128,512]{2,1,0:T(8,128)(2,1)S(1)}, bf16[4,128,512]{2,1,0:T(8,128)(2,1)S(1)}, u32[]{:S(2)}, u32[]{:S(2)}) collective-permute-start(bf16[4,128,512]{2,1,0:T(8,128)(2,1)S(1)} %get-tuple-element.62), channel_id=1, source_target_pairs={{0,4},{4,0},{8,12},{12,8},{16,20},{20,16},{24,28},{28,24},{1,5},{5... | collective-permute-start | bytes 1572872 | tf_op jit(solution)/shard_map/ppermute | solution.py:21
  116.4 46.5 %collective-permute-start.24 = (bf16[4,128,512]{2,1,0:T(8,128)(2,1)S(1)}, bf16[4,128,512]{2,1,0:T(8,128)(2,1)S(1)}, u32[]{:S(2)}, u32[]{:S(2)}) collective-permute-start(bf16[4,128,512]{2,1,0:T(8,128)(2,1)S(1)} %get-tuple-element.67), channel_id=1, source_target_pairs={{0,4},{4,0},{8,12},{12,8},{16,20},{20,16},{24,28},{28,24},{1,5},{5... | collective-permute-start | bytes 1572872 | tf_op jit(solution)/shard_map/ppermute | solution.py:21
  118.4 55.8 %collective-permute-start.12 = (bf16[4,128,512]{2,1,0:T(8,128)(2,1)S(1)}, bf16[4,128,512]{2,1,0:T(8,128)(2,1)S(1)}, u32[]{:S(2)}, u32[]{:S(2)}) collective-permute-start(bf16[4,128,512]{2,1,0:T(8,128)(2,1)S(1)} %gather_held.11), channel_id=1, source_target_pairs={{0,4},{4,0},{8,12},{12,8},{16,20},{20,16},{24,28},{28,24},{1,5},{5... | collective-permute-start | bytes 1572872 | tf_op jit(solution)/shard_map/ppermute | solution.py:21
  121.4 64.0 %collective-permute-start.11 = (bf16[4,128,512]{2,1,0:T(8,128)(2,1)S(1)}, bf16[4,128,512]{2,1,0:T(8,128)(2,1)S(1)}, u32[]{:S(2)}, u32[]{:S(2)}) collective-permute-start(bf16[4,128,512]{2,1,0:T(8,128)(2,1)S(1)} %gather_held.10), channel_id=1, source_target_pairs={{0,4},{4,0},{8,12},{12,8},{16,20},{20,16},{24,28},{28,24},{1,5},{5... | collective-permute-start | bytes 1572872 | tf_op jit(solution)/shard_map/ppermute | solution.py:21
  129.2 76.0 %collective-permute-start.26 = (bf16[4,128,512]{2,1,0:T(8,128)(2,1)S(1)}, bf16[4,128,512]{2,1,0:T(8,128)(2,1)S(1)}, u32[]{:S(2)}, u32[]{:S(2)}) collective-permute-start(bf16[4,128,512]{2,1,0:T(8,128)(2,1)S(1)} %get-tuple-element.69), channel_id=1, source_target_pairs={{0,8},{4,12},{8,0},{12,4},{16,24},{20,28},{24,16},{28,20},{1,9},{5... | collective-permute-start | bytes 1572872 | tf_op jit(solution)/shard_map/ppermute | solution.py:21
  140.4 64.8 %collective-permute-start.28 = (bf16[4,128,512]{2,1,0:T(8,128)(2,1)S(1)}, bf16[4,128,512]{2,1,0:T(8,128)(2,1)S(1)}, u32[]{:S(2)}, u32[]{:S(2)}) collective-permute-start(bf16[4,128,512]{2,1,0:T(8,128)(2,1)S(1)} %get-tuple-element.71), channel_id=1, source_target_pairs={{0,12},{4,8},{8,4},{12,0},{16,28},{20,24},{24,20},{28,16},{1,13},{... | collective-permute-start | bytes 1572872 | tf_op jit(solution)/shard_map/ppermute | solution.py:21
  162.9 44.0 %collective-permute-start.23 = (bf16[4,128,512]{2,1,0:T(8,128)(2,1)S(1)}, bf16[4,128,512]{2,1,0:T(8,128)(2,1)S(1)}, u32[]{:S(2)}, u32[]{:S(2)}) collective-permute-start(bf16[4,128,512]{2,1,0:T(8,128)(2,1)S(1)} %get-tuple-element.66), channel_id=1, source_target_pairs={{0,4},{4,0},{8,12},{12,8},{16,20},{20,16},{24,28},{28,24},{1,5},{5... | collective-permute-start | bytes 1572872 | tf_op jit(solution)/shard_map/ppermute | solution.py:21
  174.1 32.7 %collective-permute-start.25 = (bf16[4,128,512]{2,1,0:T(8,128)(2,1)S(1)}, bf16[4,128,512]{2,1,0:T(8,128)(2,1)S(1)}, u32[]{:S(2)}, u32[]{:S(2)}) collective-permute-start(bf16[4,128,512]{2,1,0:T(8,128)(2,1)S(1)} %get-tuple-element.68), channel_id=1, source_target_pairs={{0,8},{4,12},{8,0},{12,4},{16,24},{20,28},{24,16},{28,20},{1,9},{5... | collective-permute-start | bytes 1572872 | tf_op jit(solution)/shard_map/ppermute | solution.py:21
  185.4 21.5 %collective-permute-start.27 = (bf16[4,128,512]{2,1,0:T(8,128)(2,1)S(1)}, bf16[4,128,512]{2,1,0:T(8,128)(2,1)S(1)}, u32[]{:S(2)}, u32[]{:S(2)}) collective-permute-start(bf16[4,128,512]{2,1,0:T(8,128)(2,1)S(1)} %get-tuple-element.70), channel_id=1, source_target_pairs={{0,12},{4,8},{8,4},{12,0},{16,28},{20,24},{24,20},{28,16},{1,13},{... | collective-permute-start | bytes 1572872 | tf_op jit(solution)/shard_map/ppermute | solution.py:21
  226.3 24.3 %collective-permute-start.32 = (bf16[512,512]{1,0:T(8,128)(2,1)S(1)}, bf16[512,512]{1,0:T(8,128)(2,1)S(1)}, u32[]{:S(2)}, u32[]{:S(2)}) collective-permute-start(bf16[512,512]{1,0:T(8,128)(2,1)S(1)} %get-tuple-element.92), channel_id=1, source_target_pairs={{0,4},{4,0},{8,12},{12,8},{16,20},{20,16},{24,28},{28,24},{1,5},{5... | collective-permute-start | bytes 1572872 | tf_op jit(solution)/shard_map/ppermute | solution.py:21
  226.8 28.8 %collective-permute-start.33 = (bf16[512,512]{1,0:T(8,128)(2,1)}, bf16[512,512]{1,0:T(8,128)(2,1)}, u32[]{:S(2)}, u32[]{:S(2)}) collective-permute-start(bf16[512,512]{1,0:T(8,128)(2,1)} %get-tuple-element.93), channel_id=1, source_target_pairs={{0,8},{4,12},{8,0},{12,4},{16,24},{20,28},{24,16},{28,20},{1,9},{5... | collective-permute-start | bytes 1572872 | tf_op jit(solution)/shard_map/ppermute | solution.py:21
  227.5 29.7 %collective-permute-start.34 = (bf16[512,512]{1,0:T(8,128)(2,1)}, bf16[512,512]{1,0:T(8,128)(2,1)}, u32[]{:S(2)}, u32[]{:S(2)}) collective-permute-start(bf16[512,512]{1,0:T(8,128)(2,1)} %get-tuple-element.94), channel_id=1, source_target_pairs={{0,12},{4,8},{8,4},{12,0},{16,28},{20,24},{24,20},{28,16},{1,13},{... | collective-permute-start | bytes 1572872 | tf_op jit(solution)/shard_map/ppermute | solution.py:21
  229.8 45.1 %collective-permute-start.45 = (bf16[512,512]{1,0:T(8,128)(2,1)}, bf16[512,512]{1,0:T(8,128)(2,1)}, u32[]{:S(2)}, u32[]{:S(2)}) collective-permute-start(bf16[512,512]{1,0:T(8,128)(2,1)} %get-tuple-element.106), channel_id=1, source_target_pairs={{0,4},{4,0},{8,12},{12,8},{16,20},{20,16},{24,28},{28,24},{1,5},{5... | collective-permute-start | bytes 1572872 | tf_op jit(solution)/shard_map/ppermute | solution.py:21
  230.3 45.1 %collective-permute-start.46 = (bf16[512,512]{1,0:T(8,128)(2,1)}, bf16[512,512]{1,0:T(8,128)(2,1)}, u32[]{:S(2)}, u32[]{:S(2)}) collective-permute-start(bf16[512,512]{1,0:T(8,128)(2,1)} %get-tuple-element.107), channel_id=1, source_target_pairs={{0,8},{4,12},{8,0},{12,4},{16,24},{20,28},{24,16},{28,20},{1,9},{5... | collective-permute-start | bytes 1572872 | tf_op jit(solution)/shard_map/ppermute | solution.py:21
  251.4 24.1 %collective-permute-start.47 = (bf16[512,512]{1,0:T(8,128)(2,1)}, bf16[512,512]{1,0:T(8,128)(2,1)}, u32[]{:S(2)}, u32[]{:S(2)}) collective-permute-start(bf16[512,512]{1,0:T(8,128)(2,1)} %get-tuple-element.108), channel_id=1, source_target_pairs={{0,12},{4,8},{8,4},{12,0},{16,28},{20,24},{24,20},{28,16},{1,13},{... | collective-permute-start | bytes 1572872 | tf_op jit(solution)/shard_map/ppermute | solution.py:21
  255.6 30.4 %collective-permute-start.42 = (bf16[512,512]{1,0:T(8,128)(2,1)S(1)}, bf16[512,512]{1,0:T(8,128)(2,1)S(1)}, u32[]{:S(2)}, u32[]{:S(2)}) collective-permute-start(bf16[512,512]{1,0:T(8,128)(2,1)S(1)} %get-tuple-element.102), channel_id=1, source_target_pairs={{0,4},{4,0},{8,12},{12,8},{16,20},{20,16},{24,28},{28,24},{1,5},{5... | collective-permute-start | bytes 1572872 | tf_op jit(solution)/shard_map/ppermute | solution.py:21
  259.7 59.5 %collective-permute-start.35 = (bf16[8,128,512]{2,1,0:T(8,128)(2,1)S(1)}, bf16[8,128,512]{2,1,0:T(8,128)(2,1)S(1)}, u32[]{:S(2)}, u32[]{:S(2)}) collective-permute-start(bf16[8,128,512]{2,1,0:T(8,128)(2,1)S(1)} %get-tuple-element.96), channel_id=1, source_target_pairs={{0,1},{1,0},{2,3},{3,2},{4,5},{5,4},{6,7},{7,6},{8,9},{9,8},{10,11... | collective-permute-start | bytes 3145736 | tf_op jit(solution)/shard_map/ppermute | solution.py:26
  274.9 22.4 %collective-permute-start.29 = (bf16[512,512]{1,0:T(8,128)(2,1)S(1)}, bf16[512,512]{1,0:T(8,128)(2,1)S(1)}, u32[]{:S(2)}, u32[]{:S(2)}) collective-permute-start(bf16[512,512]{1,0:T(8,128)(2,1)S(1)} %get-tuple-element.88), channel_id=1, source_target_pairs={{0,4},{4,0},{8,12},{12,8},{16,20},{20,16},{24,28},{28,24},{1,5},{5... | collective-permute-start | bytes 1572872 | tf_op jit(solution)/shard_map/ppermute | solution.py:21
  277.8 42.4 %collective-permute-start.48 = (bf16[8,128,512]{2,1,0:T(8,128)(2,1)S(1)}, bf16[8,128,512]{2,1,0:T(8,128)(2,1)S(1)}, u32[]{:S(2)}, u32[]{:S(2)}) collective-permute-start(bf16[8,128,512]{2,1,0:T(8,128)(2,1)S(1)} %get-tuple-element.110), channel_id=1, source_target_pairs={{0,1},{1,0},{2,3},{3,2},{4,5},{5,4},{6,7},{7,6},{8,9},{9,8},{10,11... | collective-permute-start | bytes 3145736 | tf_op jit(solution)/shard_map/ppermute | solution.py:26
  279.8 28.6 %collective-permute-start.51 = (bf16[512,512]{1,0:T(8,128)(2,1)S(1)}, bf16[512,512]{1,0:T(8,128)(2,1)S(1)}, u32[]{:S(2)}, u32[]{:S(2)}) collective-permute-start(bf16[512,512]{1,0:T(8,128)(2,1)S(1)} %get-tuple-element.112), channel_id=1, source_target_pairs={{0,4},{4,0},{8,12},{12,8},{16,20},{20,16},{24,28},{28,24},{1,5},{5... | collective-permute-start | bytes 1572872 | tf_op jit(solution)/shard_map/ppermute | solution.py:21
  286.0 31.9 %collective-permute-start.38 = (bf16[512,512]{1,0:T(8,128)(2,1)S(1)}, bf16[512,512]{1,0:T(8,128)(2,1)S(1)}, u32[]{:S(2)}, u32[]{:S(2)}) collective-permute-start(bf16[512,512]{1,0:T(8,128)(2,1)S(1)} %get-tuple-element.98), channel_id=1, source_target_pairs={{0,4},{4,0},{8,12},{12,8},{16,20},{20,16},{24,28},{28,24},{1,5},{5... | collective-permute-start | bytes 1572872 | tf_op jit(solution)/shard_map/ppermute | solution.py:21
  297.2 25.0 %collective-permute-start.43 = (bf16[8,128,512]{2,1,0:T(8,128)(2,1)S(1)}, bf16[8,128,512]{2,1,0:T(8,128)(2,1)S(1)}, u32[]{:S(2)}, u32[]{:S(2)}) collective-permute-start(bf16[8,128,512]{2,1,0:T(8,128)(2,1)S(1)} %get-tuple-element.104), channel_id=1, source_target_pairs={{0,1},{1,0},{2,3},{3,2},{4,5},{5,4},{6,7},{7,6},{8,9},{9,8},{10,11... | collective-permute-start | bytes 3145736 | tf_op jit(solution)/shard_map/ppermute | solution.py:26
  308.5 14.8 %collective-permute-start.30 = (bf16[8,128,512]{2,1,0:T(8,128)(2,1)S(1)}, bf16[8,128,512]{2,1,0:T(8,128)(2,1)S(1)}, u32[]{:S(2)}, u32[]{:S(2)}) collective-permute-start(bf16[8,128,512]{2,1,0:T(8,128)(2,1)S(1)} %get-tuple-element.90), channel_id=1, source_target_pairs={{0,1},{1,0},{2,3},{3,2},{4,5},{5,4},{6,7},{7,6},{8,9},{9,8},{10,11... | collective-permute-start | bytes 3145736 | tf_op jit(solution)/shard_map/ppermute | solution.py:26
  320.2 60.5 %collective-permute-start.36 = (bf16[4,128,512]{2,1,0:T(8,128)(2,1)S(1)}, bf16[4,128,512]{2,1,0:T(8,128)(2,1)S(1)}, u32[]{:S(2)}, u32[]{:S(2)}) collective-permute-start(bf16[4,128,512]{2,1,0:T(8,128)(2,1)S(1)} %slice.143), channel_id=1, source_target_pairs={{0,2},{1,3},{2,0},{3,1},{4,6},{5,7},{6,4},{7,5},{8,10},{9,11},{10,... | collective-permute-start | bytes 1572872 | tf_op jit(solution)/shard_map/ppermute | solution.py:26
  322.3 24.1 %collective-permute-start.49 = (bf16[4,128,512]{2,1,0:T(8,128)(2,1)S(1)}, bf16[4,128,512]{2,1,0:T(8,128)(2,1)S(1)}, u32[]{:S(2)}, u32[]{:S(2)}) collective-permute-start(bf16[4,128,512]{2,1,0:T(8,128)(2,1)S(1)} %slice.140), channel_id=1, source_target_pairs={{0,2},{1,3},{2,0},{3,1},{4,6},{5,7},{6,4},{7,5},{8,10},{9,11},{10,... | collective-permute-start | bytes 1572872 | tf_op jit(solution)/shard_map/ppermute | solution.py:26
  323.3 67.7 %collective-permute-start.44 = (bf16[4,128,512]{2,1,0:T(8,128)(2,1)S(1)}, bf16[4,128,512]{2,1,0:T(8,128)(2,1)S(1)}, u32[]{:S(2)}, u32[]{:S(2)}) collective-permute-start(bf16[4,128,512]{2,1,0:T(8,128)(2,1)S(1)} %slice.141), channel_id=1, source_target_pairs={{0,2},{1,3},{2,0},{3,1},{4,6},{5,7},{6,4},{7,5},{8,10},{9,11},{10,... | collective-permute-start | bytes 1572872 | tf_op jit(solution)/shard_map/ppermute | solution.py:26
  326.2 82.0 %collective-permute-start.31 = (bf16[4,128,512]{2,1,0:T(8,128)(2,1)}, bf16[4,128,512]{2,1,0:T(8,128)(2,1)S(1)}, u32[]{:S(2)}, u32[]{:S(2)}) collective-permute-start(bf16[4,128,512]{2,1,0:T(8,128)(2,1)} %slice.144), channel_id=1, source_target_pairs={{0,2},{1,3},{2,0},{3,1},{4,6},{5,7},{6,4},{7,5},{8,10},{9,11},{10,... | collective-permute-start | bytes 1572872 | tf_op jit(solution)/shard_map/ppermute | solution.py:26
  327.4 52.6 %collective-permute-start.53 = (bf16[4,128,512]{2,1,0:T(8,128)(2,1)S(1)}, bf16[4,128,512]{2,1,0:T(8,128)(2,1)S(1)}, u32[]{:S(2)}, u32[]{:S(2)}) collective-permute-start(bf16[4,128,512]{2,1,0:T(8,128)(2,1)S(1)} %slice.139), channel_id=1, source_target_pairs={{0,2},{1,3},{2,0},{3,1},{4,6},{5,7},{6,4},{7,5},{8,10},{9,11},{10,... | collective-permute-start | bytes 1572872 | tf_op jit(solution)/shard_map/ppermute | solution.py:26
  346.3 44.0 %collective-permute-start.40 = (bf16[4,128,512]{2,1,0:T(8,128)(2,1)S(1)}, bf16[4,128,512]{2,1,0:T(8,128)(2,1)S(1)}, u32[]{:S(2)}, u32[]{:S(2)}) collective-permute-start(bf16[4,128,512]{2,1,0:T(8,128)(2,1)S(1)} %slice.142), channel_id=1, source_target_pairs={{0,2},{1,3},{2,0},{3,1},{4,6},{5,7},{6,4},{7,5},{8,10},{9,11},{10,... | collective-permute-start | bytes 1572872 | tf_op jit(solution)/shard_map/ppermute | solution.py:26
  380.0 27.2 %collective-permute-start.50 = (bf16[4,128,512]{2,1,0:T(8,128)(2,1)S(1)}, bf16[4,128,512]{2,1,0:T(8,128)(2,1)S(1)}, u32[]{:S(2)}, u32[]{:S(2)}) collective-permute-start(bf16[4,128,512]{2,1,0:T(8,128)(2,1)S(1)} %fusion.1), channel_id=1, source_target_pairs={{0,16},{4,20},{8,24},{12,28},{16,0},{20,4},{24,8},{28,12},{1,17},{... | collective-permute-start | bytes 1572872 | tf_op jit(solution)/shard_map/ppermute | solution.py:21
  380.7 26.5 %collective-permute-start.54 = (bf16[4,128,512]{2,1,0:T(8,128)(2,1)S(1)}, bf16[4,128,512]{2,1,0:T(8,128)(2,1)S(1)}, u32[]{:S(2)}, u32[]{:S(2)}) collective-permute-start(bf16[4,128,512]{2,1,0:T(8,128)(2,1)S(1)} %fusion), channel_id=1, source_target_pairs={{0,8},{4,12},{8,0},{12,4},{16,24},{20,28},{24,16},{28,20},{1,9},{5... | collective-permute-start | bytes 1572872 | tf_op jit(solution)/shard_map/ppermute | solution.py:21
  390.3 36.4 %collective-permute-start.37 = (bf16[4,128,512]{2,1,0:T(8,128)(2,1)S(1)}, bf16[4,128,512]{2,1,0:T(8,128)(2,1)S(1)}, u32[]{:S(2)}, u32[]{:S(2)}) collective-permute-start(bf16[4,128,512]{2,1,0:T(8,128)(2,1)S(1)} %fusion.5), channel_id=1, source_target_pairs={{0,16},{4,20},{8,24},{12,28},{16,0},{20,4},{24,8},{28,12},{1,17},{... | collective-permute-start | bytes 1572872 | tf_op jit(solution)/shard_map/ppermute | solution.py:21
  391.0 35.8 %collective-permute-start.41 = (bf16[4,128,512]{2,1,0:T(8,128)(2,1)S(1)}, bf16[4,128,512]{2,1,0:T(8,128)(2,1)S(1)}, u32[]{:S(2)}, u32[]{:S(2)}) collective-permute-start(bf16[4,128,512]{2,1,0:T(8,128)(2,1)S(1)} %fusion.4), channel_id=1, source_target_pairs={{0,8},{4,12},{8,0},{12,4},{16,24},{20,28},{24,16},{28,20},{1,9},{5... | collective-permute-start | bytes 1572872 | tf_op jit(solution)/shard_map/ppermute | solution.py:21
  (71 other events, 994.7 us)
where the time goes:
time: 433 us; the launch traced here: 429 us
  waiting for transfers between devices  285 us (66%)
  Pallas kernels  67.4 us (16%)
  starting transfers between devices  46 us (11%)
  local copies, waits for them, and re-layouts  21.4 us (5%)
  other arithmetic  7.4 us (2%)
    ppermute x31, waiting for transfers between devices, xor_proto(): return lax.ppermute(x, 'proto', [(i, i ^ shift) for i in range(count)])  187 us
    ppermute x24, waiting for transfers between devices, xor_design(): return lax.ppermute(x, 'design', [(i, i ^ shift) for i in range(count)])  97.1 us
    ppermute x31, starting transfers between devices, xor_proto(): return lax.ppermute(x, 'proto', [(i, i ^ shift) for i in range(count)])  32.7 us
    unnamed x128, local copies, waits for them, and re-layouts  17.4 us
    pallas_call x8, Pallas kernels, gather_held(): pl.pallas_call(functools.partial(gather_held_kernel, len(srcs), n, quarte...  15.1 us
    pallas_call x1, Pallas kernels, far_grads(): pl.pallas_call(functools.partial(far_kernel, group, cap, lanes, parts), o...  13.7 us
    ppermute x24, starting transfers between devices, xor_design(): return lax.ppermute(x, 'design', [(i, i ^ shift) for i in range(count)])  13.3 us
    pallas_call x2, Pallas kernels, design_grad(): pl.pallas_call(functools.partial(design_grad_kernel, n), out_shape=jax.Sh...  12.7 us
  transfers between devices with their start and end apart: 55, of which 24 were waited for; matrix products, arithmetic and copies ran while one was open for 2% of the time, Pallas kernels for 13%

commit v1 on v0

--- a/solution.py
+++ b/solution.py
@@ -41,8 +41,11 @@
 HBM = pl.BlockSpec(memory_space=pl.ANY)
 VM = pl.BlockSpec(memory_space=pltpu.VMEM)
 SM = pl.BlockSpec(memory_space=pltpu.SMEM)
-WIDE = pltpu.CompilerParams(vmem_limit_bytes=40 << 20)
-PARAMS = pltpu.CompilerParams(vmem_limit_bytes=16 << 20)
+FIXED = pl.BlockSpec(memory_space=pltpu.HBM)
+
+
+def grant(mib):
+    return pltpu.CompilerParams(vmem_limit_bytes=mib << 20)
 
 
 def gather_round_kernel(parts, table, src, *refs):
@@ -66,13 +69,13 @@
     return pl.pallas_call(
         functools.partial(gather_round_kernel, parts),
         out_shape=[jax.ShapeDtypeStruct((cap, tile, width // parts), BF)] * parts,
-        in_specs=[SM, HBM],
+        in_specs=[SM, FIXED],
         out_specs=[VM] * parts,
         scratch_shapes=[
             pltpu.VMEM((cap, tile, width), F32),
             pltpu.SemaphoreType.DMA((cap,)),
         ],
-        compiler_params=PARAMS,
+        compiler_params=grant(6),
         name="gather_round",
     )(table, shard)
 
@@ -82,20 +85,26 @@
     outs, sems = refs[n_out + n_src : -1], refs[-1]
     cap = outs[0].shape[0]
     y, c = me[0] // 2, me[0] % 2
-    for i in range(n_out * cap):
-        row = jnp.maximum(tables[i // cap][i % cap], 0)
-        owner, inside = row // quarter, row % quarter
-        which = ((owner % 2) ^ c) * lanes + ((owner // 2) ^ y)
-        for a in range(n_src):
-
-            @pl.when(which == a)
-            def _():
-                pltpu.make_async_copy(
-                    srcs[a].at[inside], outs[i // cap].at[i % cap], sems.at[i]
-                ).start()
-
-    for i in range(n_out * cap):
-        pltpu.make_async_copy(srcs[0].at[0], outs[i // cap].at[i % cap], sems.at[i]).wait()
+    for n in range(n_out):
+
+        @pl.loop(0, cap)
+        def _(k):
+            row = jnp.maximum(tables[n][k], 0)
+            owner, inside = row // quarter, row % quarter
+            which = ((owner % 2) ^ c) * lanes + ((owner // 2) ^ y)
+            for a in range(n_src):
+
+                @pl.when(which == a)
+                def _():
+                    pltpu.make_async_copy(
+                        srcs[a].at[inside], outs[n].at[k], sems.at[n * cap + k]
+                    ).start()
+
+    for n in range(n_out):
+
+        @pl.loop(0, cap)
+        def _(k):
+            pltpu.make_async_copy(srcs[0].at[0], outs[n].at[k], sems.at[n * cap + k]).wait()
 
 
 def gather_held(me, tables, srcs, lanes):
@@ -109,7 +118,7 @@
         in_specs=[SM] * (n + 1) + [HBM] * len(srcs),
         out_specs=[VM] * n,
         scratch_shapes=[pltpu.SemaphoreType.DMA((n * cap,))],
-        compiler_params=PARAMS,
+        compiler_params=grant(2),
         name="gather_held",
     )(me, *tables, *srcs)
 
@@ -161,15 +170,22 @@
 
 def own_kernel(group, cap, lanes, parts, base, x, pos, *refs):
     rows = [refs[s * parts : (s + 1) * parts] for s in range(group)]
-    logits = refs[group * parts : group * (parts + 1)]
-    top_out, sum_out, hit_out = refs[group * (parts + 1) :]
+    kept = refs[group * parts : group * (parts + 1)]
+    top_out, sum_out, hit_out, logits, sems = refs[group * (parts + 1) :]
     count = x.shape[0]
-    for j in range(0, count, lanes):
-        at = pl.ds(j, lanes)
+
+    def copy_out(s, j):
+        at = pl.ds(pl.multiple_of(j * lanes, lanes), lanes)
+        return pltpu.make_async_copy(logits.at[s, :, at], kept[s].at[:, at], sems.at[s, j])
+
+    @pl.loop(0, count // lanes)
+    def _(j):
+        at = pl.ds(pl.multiple_of(j * lanes, lanes), lanes)
         for s in range(group):
-            logits[s][:, at] = contract(rows[s], x, slice(j, j + lanes))
+            logits[s, :, at] = contract(rows[s], x, at)
+            copy_out(s, j).start()
         slots = [
-            (s * cap + k, logits[s].at[pl.ds(k * TILE, TILE), at])
+            (s * cap + k, logits.at[s, pl.ds(k * TILE, TILE), at])
             for s in range(group)
             for k in range(cap)
         ]
@@ -182,6 +198,11 @@
         hit_out[:, at] = hit
         sum_out[:, at] = jnp.sum(total, axis=0, keepdims=True)
 
+    @pl.loop(0, count // lanes)
+    def _(j):
+        for s in range(group):
+            copy_out(s, j).wait()
+
 
 def own_logits(base, x, pos, rows, cap, lanes=256):
     group, parts = len(rows), len(rows[0])
@@ -194,19 +215,24 @@
         out_shape=[jax.ShapeDtypeStruct(shape, F32)] * group
         + [jax.ShapeDtypeStruct(line, F32)] * 3,
         in_specs=[SM] + [VM] * (2 + len(rows)),
-        out_specs=[VM] * (group + 3),
-        compiler_params=PARAMS,
+        out_specs=[FIXED] * group + [VM] * 3,
+        scratch_shapes=[
+            pltpu.VMEM((group,) + shape, F32),
+            pltpu.SemaphoreType.DMA((group, count // lanes)),
+        ],
+        compiler_params=grant(12),
         name="own_logits",
     )(base, x, pos, *rows)
 
 
-def far_kernel(group, cap, lanes, parts, base, x, pos, top_own, sum_own, hit_own, *refs):
+def far_kernel(group, cap, lanes, parts, n_stats, base, x, pos, *refs):
+    stats = [refs[3 * i : 3 * i + 3] for i in range(n_stats)]
+    refs = refs[3 * n_stats :]
     rows = [refs[s * parts : (s + 1) * parts] for s in range(group)]
     refs = refs[group * parts :]
     losses, top_out, inv_out = refs[:3]
-    grads = refs[3 : group + 3]
-    tiles = refs[group + 3 : -1]
-    logits = refs[-1]
+    kept = refs[3:-4]
+    logits, grads, tiles, sems = refs[-4:]
     count, width = x.shape
     scale = D ** (-0.5)
     for j in range(0, count, lanes):
@@ -214,15 +240,16 @@
         at = pl.ds(j, lanes)
         for s in range(group):
             logits[turn, s * cap * TILE : (s + 1) * cap * TILE, :] = contract(
-                rows[s], x, slice(j, j + lanes)
+                rows[s], x, pl.ds(j, lanes)
             )
         slots = [
             (n, logits.at[turn, pl.ds(n * TILE, TILE), :]) for n in range(group * cap)
         ]
         rel = relative(pos[:, at], lanes)
         top, hit = slot_stats(base, rel, slots)
-        mine = top_own[:, at]
-        both = jnp.maximum(top, mine)
+        both = top
+        for top_own, _, _ in stats:
+            both = jnp.maximum(both, top_own[:, at])
         total = None
         for n, ref in slots:
             power = slot_power(base, n, ref, both)
@@ -230,21 +257,32 @@
             part = fold(power, jnp.sum)
             total = part if total is None else total + part
         total = jnp.sum(total, axis=0, keepdims=True)
-        total = total + sum_own[:, at] * jnp.exp2((mine - both) * EXP_SCALE)
-        losses[:, at] = both * scale + jnp.log(total) - (hit + hit_own[:, at]) * scale
+        for top_own, sum_own, hit_own in stats:
+            total = total + sum_own[:, at] * jnp.exp2((top_own[:, at] - both) * EXP_SCALE)
+            hit = hit + hit_own[:, at]
+        losses[:, at] = both * scale + jnp.log(total) - hit * scale
         inv = 1.0 / total
         top_out[:, at] = both
         inv_out[:, at] = inv
         for n, ref in slots:
             s, k = n // cap, n % cap
             target = jnp.where(rel == base[n], 1.0, 0.0)
-            grads[s][k * TILE : (k + 1) * TILE, at] = (ref[...] * inv - target).astype(BF)
+            grads[s, k * TILE : (k + 1) * TILE, at] = (ref[...] * inv - target).astype(BF)
     step = width // parts
+    sources = [grads.at[s] for s in range(group)]
+    sources += [tiles.at[n] for n in range(parts * group)]
+    copies = [pltpu.make_async_copy(a, b, sems.at[n]) for n, (a, b) in enumerate(zip(sources, kept))]
+    for copy in copies[:group]:
+        copy.start()
     for i in range(parts):
         for s in range(group):
-            tiles[i * group + s][...] = jnp.dot(
-                grads[s][...], x[:, i * step : (i + 1) * step], preferred_element_type=F32
+            n = i * group + s
+            tiles[n] = jnp.dot(
+                grads[s], x[:, i * step : (i + 1) * step], preferred_element_type=F32
             ).astype(BF)
+            copies[group + n].start()
+    for copy in copies:
+        copy.wait()
 
 
 def far_grads(base, x, pos, stats, rows, cap, parts, lanes=256):
@@ -255,12 +293,17 @@
     outs = [((1, count), F32)] * 3 + [((size, count), BF)] * group
     outs += [((size, width // parts), BF)] * (group * parts)
     got = pl.pallas_call(
-        functools.partial(far_kernel, group, cap, lanes, parts),
+        functools.partial(far_kernel, group, cap, lanes, parts, len(stats) // 3),
         out_shape=[jax.ShapeDtypeStruct(*o) for o in outs],
-        in_specs=[SM] + [VM] * (5 + len(rows)),
-        out_specs=[VM] * len(outs),
-        scratch_shapes=[pltpu.VMEM((2, group * size, lanes), F32)],
-        compiler_params=PARAMS,
+        in_specs=[SM] + [VM] * (2 + len(stats) + len(rows)),
+        out_specs=[VM] * 3 + [FIXED] * (len(outs) - 3),
+        scratch_shapes=[
+            pltpu.VMEM((2, group * size, lanes), F32),
+            pltpu.VMEM((group, size, count), BF),
+            pltpu.VMEM((group * parts, size, width // parts), BF),
+            pltpu.SemaphoreType.DMA((group * (1 + parts),)),
+        ],
+        compiler_params=grant(20),
         name="far_grads",
     )(base, x, pos, *stats, *rows)
     tiles = got[3 + group :]
@@ -291,35 +334,35 @@
         out_shape=[jax.ShapeDtypeStruct(*o) for o in outs],
         in_specs=[SM] + [VM] * 5,
         out_specs=[VM] * len(outs),
-        compiler_params=PARAMS,
+        compiler_params=grant(6),
         name="own_grad",
     )(base, x, pos, top, inv, logits)
     return got[0], got[1:]
 
 
-def design_grad_kernel(n, *refs):
+def design_grad_kernel(n, chunk, *refs):
     grads, rows, out = refs[:n], refs[n : 2 * n], refs[2 * n]
-    acc = None
-    for g, r in zip(grads, rows):
-        part = lax.dot_general(
-            g[...], r[...], (((0,), (0,)), ((), ())), preferred_element_type=F32
-        )
-        acc = part if acc is None else acc + part
-    out[...] = acc.astype(BF)
+
+    @pl.loop(0, out.shape[0] // chunk)
+    def _(j):
+        at = pl.ds(pl.multiple_of(j * chunk, chunk), chunk)
+        acc = None
+        for g, r in zip(grads, rows):
+            part = lax.dot_general(
+                g[:, at], r[...], (((0,), (0,)), ((), ())), preferred_element_type=F32
+            )
+            acc = part if acc is None else acc + part
+        out[at, :] = acc.astype(BF)
 
 
 def design_grad(grads, rows, chunk=256):
     n = len(grads)
-    cols, count = grads[0].shape
-    width = rows[0].shape[1]
     return pl.pallas_call(
-        functools.partial(design_grad_kernel, n),
-        out_shape=jax.ShapeDtypeStruct((count, width), BF),
-        grid=(count // chunk,),
-        in_specs=[pl.BlockSpec((cols, chunk), lambda i: (0, i))] * n
-        + [pl.BlockSpec((cols, width), lambda i: (0, 0))] * n,
-        out_specs=pl.BlockSpec((chunk, width), lambda i: (i, 0)),
-        compiler_params=WIDE,
+        functools.partial(design_grad_kernel, n, chunk),
+        out_shape=jax.ShapeDtypeStruct((grads[0].shape[1], rows[0].shape[1]), BF),
+        in_specs=[VM] * (2 * n),
+        out_specs=VM,
+        compiler_params=grant(8),
         name="design_grad",
     )(*grads, *rows)
 
@@ -350,7 +393,7 @@
         in_specs=[SM] + [VM] * n,
         out_specs=[VM] * 2,
         scratch_shapes=[pltpu.VMEM((2 * kept, TILE, width), F32)],
-        compiler_params=PARAMS,
+        compiler_params=grant(8),
         name="collect",
     )(spot, *parts)
 
@@ -433,24 +476,30 @@
         (out,) = gather_held(me, [asking[0]], held, lanes)
         far_rows[0][i] = flat(out)
 
-    def bases(lists, which_half):
+    def bases(lists, which_half, group):
         out = []
-        for s in range(half):
+        for s in group:
             first = (which_half * half + (q ^ s)) * blocks_dev
             out.append(jnp.where(lists[s] >= 0, (first + lists[s]) * TILE, -(2**30)))
         return jnp.concatenate(out)
 
     pos = positives.reshape(1, count)
-    own_base = bases(near, h)
-    *logits, top, total, hit = own_logits(own_base, designs, pos, own_rows, cap)
+    logits, sums = {}, []
+    for group in groups_of(half).values():
+        *got, top, total, hit = own_logits(
+            bases(near, h, group), designs, pos, [own_rows[s] for s in group], cap
+        )
+        logits.update(zip(group, got))
+        sums += [top, total, hit]
     stats, far_g, far_tiles = far_grads(
-        bases(other, 1 - h), designs, pos, (top, total, hit), far_rows, cap, parts
+        bases(other, 1 - h, range(half)), designs, pos, sums, far_rows, cap, parts
     )
     losses, top, inv = stats
-    own_base = own_base.reshape(half, cap)
     own_g, own_tiles = [], []
     for s in range(half):
-        g, t = own_grad(own_base[s], designs, pos, top, inv, logits[s], cap, parts)
+        g, t = own_grad(
+            bases(near, h, [s]), designs, pos, top, inv, logits[s], cap, parts
+        )
         own_g.append(g)
         own_tiles.append(t)
 
@@ -497,6 +546,11 @@
     return (losses.reshape(count), jnp.concatenate(dgrad, axis=-1), result)
 
 
+def groups_of(half):
+    late = list(range(3, half, 2))
+    return {"own_a": [s for s in range(half) if s not in late], "own_b": late}
+
+
 def solution(mesh):
     return jax.shard_map(
         body,

time: 433 us -> 433 us (level)
  Pallas kernels: 67.4 us -> 76 us
  local copies, waits for them, and re-layouts: 21.4 us -> 16.5 us
    pallas_call x1 -> x2, Pallas kernels: 6.58 us -> 15.8 us  [own_logits(): pl.pallas_call(functools.partial(own_kernel, group, cap, lanes, parts), o...]
    unnamed x128 -> x120, local copies, waits for them, and re-layouts: 17.4 us -> 14.2 us
  transfers between devices with their start and end apart: 55 -> 55, of which waited for: 24 -> 23; matrix products, arithmetic and copies ran while one was open for 2% -> 1% of each run, Pallas kernels for 13% -> 14%
where the time goes in v1:
time: 433 us
  waiting for transfers between devices  282 us (65%)
  Pallas kernels  76 us (18%)
  starting transfers between devices  49.1 us (11%)
  local copies, waits for them, and re-layouts  16.5 us (4%)
  other arithmetic  7.38 us (2%)
    ppermute x31, waiting for transfers between devices, xor_proto(): return lax.ppermute(x, 'proto', [(i, i ^ shift) for i in range(count)])  184 us
    ppermute x24, waiting for transfers between devices, xor_design(): return lax.ppermute(x, 'design', [(i, i ^ shift) for i in range(count)])  97.9 us
    ppermute x31, starting transfers between devices, xor_proto(): return lax.ppermute(x, 'proto', [(i, i ^ shift) for i in range(count)])  35.8 us
    pallas_call x2, Pallas kernels, own_logits(): pl.pallas_call(functools.partial(own_kernel, group, cap, lanes, parts), o...  15.8 us
    pallas_call x1, Pallas kernels, far_grads(): pl.pallas_call(functools.partial(far_kernel, group, cap, lanes, parts, le...  15.1 us
    pallas_call x8, Pallas kernels, gather_held(): pl.pallas_call(functools.partial(gather_held_kernel, len(srcs), n, quarte...  15.1 us
    unnamed x120, local copies, waits for them, and re-layouts  14.2 us
    ppermute x24, starting transfers between devices, xor_design(): return lax.ppermute(x, 'design', [(i, i ^ shift) for i in range(count)])  13.3 us
  transfers between devices with their start and end apart: 55, of which 23 were waited for; matrix products, arithmetic and copies ran while one was open for 1% of the time, Pallas kernels for 14%

profile of v1, /device:TPU:0, one launch (start us, length us, event | category | flops | bytes accessed | tf_op | source)
XLA Modules:
  0.0 432.7 jit_solution(16920468140775680026)
XLA Ops:
  0.6 1.7 dynamic-slice_convert_fusion
  2.5 4.1 collective-permute-start.17
  6.6 1.6 collective-permute-start.7
  9.2 2.8 collective-permute-start.21
  12.0 41.5 %collective-permute-done.21.refs_0_ = s32[4]{0:T(128)S(1)} collective-permute-done((s32[4]{0:T(128)S(1)}, s32[4]{0:T(128)S(1)}, u32[]{:S(2)}, u32[]{:S(2)}) %collective-permute-start.21) | collective-permute-done | bytes 48 | tf_op jit(solution)/shard_map/ppermute | solution.py:21
  55.0 2.1 collective-permute-done.22.refs_1_
  57.6 3.1 collective-permute-done
  64.8 10.6 %collective-permute-done.18.refs_2_.refs_4_ = bf16[4,128,512]{2,1,0:T(8,128)(2,1)S(1)} collective-permute-done((bf16[4,128,512]{2,1,0:T(8,128)(2,1)S(1)}, bf16[4,128,512]{2,1,0:T(8,128)(2,1)S(1)}, u32[]{:S(2)}, u32[]{:S(2)}) %collective-permute-start.18) | collective-permute-done | bytes 524320 | tf_op jit(solution)/shard_map/ppermute | solution.py:26
  76.0 10.7 %collective-permute-done.8.refs_2_ = bf16[4,128,512]{2,1,0:T(8,128)(2,1)S(1)} collective-permute-done((bf16[4,128,512]{2,1,0:T(8,128)(2,1)S(1)}, bf16[4,128,512]{2,1,0:T(8,128)(2,1)S(1)}, u32[]{:S(2)}, u32[]{:S(2)}) %collective-permute-start.8) | collective-permute-done | bytes 524320 | tf_op jit(solution)/shard_map/ppermute | solution.py:26
  86.7 11.2 %collective-permute-done.14.refs_2_.refs_4_ = bf16[4,128,512]{2,1,0:T(8,128)(2,1)S(1)} collective-permute-done((bf16[4,128,512]{2,1,0:T(8,128)(2,1)S(1)}, bf16[4,128,512]{2,1,0:T(8,128)(2,1)S(1)}, u32[]{:S(2)}, u32[]{:S(2)}) %collective-permute-start.14) | collective-permute-done | bytes 524320 | tf_op jit(solution)/shard_map/ppermute | solution.py:26
  98.0 7.5 %collective-permute-done.4.refs_2_ = bf16[4,128,512]{2,1,0:T(8,128)(2,1)S(1)} collective-permute-done((bf16[4,128,512]{2,1,0:T(8,128)(2,1)S(1)}, bf16[4,128,512]{2,1,0:T(8,128)(2,1)S(1)}, u32[]{:S(2)}, u32[]{:S(2)}) %collective-permute-start.4) | collective-permute-done | bytes 524320 | tf_op jit(solution)/shard_map/ppermute | solution.py:26
  106.0 3.4 copy-done.1
  110.3 3.2 gather_held.15
  117.6 1.6 collective-permute-start.12
  121.2 3.2 gather_held.14
  124.5 3.9 collective-permute-done.1
  129.1 10.5 %collective-permute-done.2 = bf16[4,128,512]{2,1,0:T(8,128)(2,1)S(1)} collective-permute-done((bf16[4,128,512]{2,1,0:T(8,128)(2,1)S(1)}, bf16[4,128,512]{2,1,0:T(8,128)(2,1)S(1)}, u32[]{:S(2)}, u32[]{:S(2)}) %collective-permute-start.2) | collective-permute-done | bytes 524320 | tf_op jit(solution)/shard_map/ppermute | solution.py:21
  140.3 21.8 %collective-permute-done.24 = bf16[4,128,512]{2,1,0:T(8,128)(2,1)S(1)} collective-permute-done((bf16[4,128,512]{2,1,0:T(8,128)(2,1)S(1)}, bf16[4,128,512]{2,1,0:T(8,128)(2,1)S(1)}, u32[]{:S(2)}, u32[]{:S(2)}) %collective-permute-start.24) | collective-permute-done | bytes 524320 | tf_op jit(solution)/shard_map/ppermute | solution.py:21
  162.6 10.7 %collective-permute-done.12 = bf16[4,128,512]{2,1,0:T(8,128)(2,1)S(1)} collective-permute-done((bf16[4,128,512]{2,1,0:T(8,128)(2,1)S(1)}, bf16[4,128,512]{2,1,0:T(8,128)(2,1)S(1)}, u32[]{:S(2)}, u32[]{:S(2)}) %collective-permute-start.12) | collective-permute-done | bytes 524320 | tf_op jit(solution)/shard_map/ppermute | solution.py:21
  174.1 10.5 %collective-permute-done.11 = bf16[4,128,512]{2,1,0:T(8,128)(2,1)S(1)} collective-permute-done((bf16[4,128,512]{2,1,0:T(8,128)(2,1)S(1)}, bf16[4,128,512]{2,1,0:T(8,128)(2,1)S(1)}, u32[]{:S(2)}, u32[]{:S(2)}) %collective-permute-start.11) | collective-permute-done | bytes 524320 | tf_op jit(solution)/shard_map/ppermute | solution.py:21
  189.3 12.0 %own_logits.2 = (f32[512,1024]{1,0:T(8,128)S(1)}, f32[512,1024]{1,0:T(8,128)S(1)}, f32[512,1024]{1,0:T(8,128)S(1)}, f32[1,1024]{1,0:T(1,128)S(1)}, f32[1,1024]{1,0:T(1,128)S(1)}, /*index=5*/f32[1,1024]{1,0:T(1,128)S(1)}) custom-call(s32[12]{0:T(128)S(1)} %pad_add_fusion.2.base, bf16[1024,1024]{1,0:T(8,128)(2,1)S(1)} %copy-done, s32[1,1024]{1,0:T(1,128)S(1)} %bitcast.106, ...), custom_call_target="tpu_custom_call" | custom-call | tf_op jit(solution)/shard_map/own_logits/pallas_call | solution.py:213
  205.6 3.9 own_logits.3
  210.9 15.1 %far_grads.1 = (f32[1,1024]{1,0:T(1,128)}, f32[1,1024]{1,0:T(1,128)S(1)}, f32[1,1024]{1,0:T(1,128)S(1)}, bf16[512,1024]{1,0:T(8,128)(2,1)S(1)}, bf16[512,1024]{1...) custom-call(s32[16]{0:T(128)S(1)} %pad_add_fusion.1.base, ...), custom_call_target="tpu_custom_call" | custom-call | tf_op jit(solution)/shard_map/far_grads/pallas_call | solution.py:295
  238.0 18.0 %collective-permute-done.32.refs_1_ = bf16[512,512]{1,0:T(8,128)(2,1)S(1)} collective-permute-done((bf16[512,512]{1,0:T(8,128)(2,1)S(1)}, bf16[512,512]{1,0:T(8,128)(2,1)S(1)}, u32[]{:S(2)}, u32[]{:S(2)}) %collective-permute-start.32) | collective-permute-done | bytes 524320 | tf_op jit(solution)/shard_map/ppermute | solution.py:21
  256.8 2.2 collective-permute-start.47
  259.0 1.6 copy-done.27
  260.6 2.0 own_grad.5
  263.3 2.3 collect.7
  265.7 14.6 %collective-permute-done.45.refs_1_ = bf16[512,512]{1,0:T(8,128)(2,1)} collective-permute-done((bf16[512,512]{1,0:T(8,128)(2,1)}, bf16[512,512]{1,0:T(8,128)(2,1)}, u32[]{:S(2)}, u32[]{:S(2)}) %collective-permute-start.45) | collective-permute-done | bytes 524320 | tf_op jit(solution)/shard_map/ppermute | solution.py:21
  281.8 2.3 collect.10
  284.2 2.0 own_grad.7
  286.7 4.7 %collective-permute-done.42.refs_1_ = bf16[512,512]{1,0:T(8,128)(2,1)S(1)} collective-permute-done((bf16[512,512]{1,0:T(8,128)(2,1)S(1)}, bf16[512,512]{1,0:T(8,128)(2,1)S(1)}, u32[]{:S(2)}, u32[]{:S(2)}) %collective-permute-start.42) | collective-permute-done | bytes 524320 | tf_op jit(solution)/shard_map/ppermute | solution.py:21
  293.0 2.0 own_grad.4
  296.3 6.4 %collective-permute-done.29.refs_1_ = bf16[512,512]{1,0:T(8,128)(2,1)S(1)} collective-permute-done((bf16[512,512]{1,0:T(8,128)(2,1)S(1)}, bf16[512,512]{1,0:T(8,128)(2,1)S(1)}, u32[]{:S(2)}, u32[]{:S(2)}) %collective-permute-start.29) | collective-permute-done | bytes 524320 | tf_op jit(solution)/shard_map/ppermute | solution.py:21
  302.8 2.0 own_grad.6
  306.2 7.7 %collective-permute-done.51.refs_1_ = bf16[512,512]{1,0:T(8,128)(2,1)S(1)} collective-permute-done((bf16[512,512]{1,0:T(8,128)(2,1)S(1)}, bf16[512,512]{1,0:T(8,128)(2,1)S(1)}, u32[]{:S(2)}, u32[]{:S(2)}) %collective-permute-start.51) | collective-permute-done | bytes 524320 | tf_op jit(solution)/shard_map/ppermute | solution.py:21
  315.2 6.9 %collective-permute-done.38.refs_1_ = bf16[512,512]{1,0:T(8,128)(2,1)S(1)} collective-permute-done((bf16[512,512]{1,0:T(8,128)(2,1)S(1)}, bf16[512,512]{1,0:T(8,128)(2,1)S(1)}, u32[]{:S(2)}, u32[]{:S(2)}) %collective-permute-start.38) | collective-permute-done | bytes 524320 | tf_op jit(solution)/shard_map/ppermute | solution.py:21
  324.4 1.6 collective-permute-start.36
  327.5 1.6 collective-permute-start.44
  330.6 1.6 collective-permute-start.53
  332.6 17.9 %collective-permute-done.49 = bf16[4,128,512]{2,1,0:T(8,128)(2,1)S(1)} collective-permute-done((bf16[4,128,512]{2,1,0:T(8,128)(2,1)S(1)}, bf16[4,128,512]{2,1,0:T(8,128)(2,1)S(1)}, u32[]{:S(2)}, u32[]{:S(2)}) %collective-permute-start.49) | collective-permute-done | bytes 524320 | tf_op jit(solution)/shard_map/ppermute | solution.py:26
  352.2 32.0 %collective-permute-done.53 = bf16[4,128,512]{2,1,0:T(8,128)(2,1)S(1)} collective-permute-done((bf16[4,128,512]{2,1,0:T(8,128)(2,1)S(1)}, bf16[4,128,512]{2,1,0:T(8,128)(2,1)S(1)}, u32[]{:S(2)}, u32[]{:S(2)}) %collective-permute-start.53) | collective-permute-done | bytes 524320 | tf_op jit(solution)/shard_map/ppermute | solution.py:26
  386.6 7.9 %collective-permute-done.40 = bf16[4,128,512]{2,1,0:T(8,128)(2,1)S(1)} collective-permute-done((bf16[4,128,512]{2,1,0:T(8,128)(2,1)S(1)}, bf16[4,128,512]{2,1,0:T(8,128)(2,1)S(1)}, u32[]{:S(2)}, u32[]{:S(2)}) %collective-permute-start.40) | collective-permute-done | bytes 524320 | tf_op jit(solution)/shard_map/ppermute | solution.py:26
  396.8 5.2 %design_grad.3 = bf16[1024,512]{1,0:T(8,128)(2,1)S(1)} custom-call(bf16[512,1024]{1,0:T(8,128)(2,1)S(1)} %get-tuple-element.82.refs_0_, bf16[512,1024]{1,0:T(8,128)(2,1)S(1)} %get-tuple-element.84.refs_1_, bf16[512,1024]{1,0:T(8,128)(2,1)S(1)} %get-tuple-element.86.refs_2_, bf16[512,1024]{1,0:T(8,128)(2,1)S(1)} %get-tuple-element.88.refs_3_, ...), custom_call_target="tpu_custom_call" | custom-call | tf_op jit(solution)/shard_map/design_grad/pallas_call | solution.py:360
  402.1 5.2 %design_grad.2 = bf16[1024,512]{1,0:T(8,128)(2,1)S(1)} custom-call(bf16[512,1024]{1,0:T(8,128)(2,1)S(1)} %get-tuple-element.82.refs_0_, bf16[512,1024]{1,0:T(8,128)(2,1)S(1)} %get-tuple-element.84.refs_1_, bf16[512,1024]{1,0:T(8,128)(2,1)S(1)} %get-tuple-element.86.refs_2_, bf16[512,1024]{1,0:T(8,128)(2,1)S(1)} %get-tuple-element.88.refs_3_, ...), custom_call_target="tpu_custom_call" | custom-call | tf_op jit(solution)/shard_map/design_grad/pallas_call | solution.py:360
  407.4 1.6 pad_maximum_fusion
  408.9 3.0 collective-permute-done.50
  412.3 18.6 %collective-permute-done.37 = bf16[4,128,512]{2,1,0:T(8,128)(2,1)S(1)} collective-permute-done((bf16[4,128,512]{2,1,0:T(8,128)(2,1)S(1)}, bf16[4,128,512]{2,1,0:T(8,128)(2,1)S(1)}, u32[]{:S(2)}, u32[]{:S(2)}) %collective-permute-start.37) | collective-permute-done | bytes 524320 | tf_op jit(solution)/shard_map/ppermute | solution.py:21
  (245 shorter events, 63.3 us)
Async XLA Ops:
  2.5 52.5 %collective-permute-start.17 = (bf16[4,128,512]{2,1,0:T(8,128)(2,1)S(1)}, bf16[4,128,512]{2,1,0:T(8,128)(2,1)S(1)}, u32[]{:S(2)}, u32[]{:S(2)}) collective-permute-start(bf16[4,128,512]{2,1,0:T(8,128)(2,1)S(1)} %get-tuple-element.131), channel_id=1, source_target_pairs={{0,16},{4,20},{8,24},{12,28},{16,0},{20,4},{24,8},{28,12},{1,17},{... | collective-permute-start | bytes 1572872 | tf_op jit(solution)/shard_map/ppermute | solution.py:21
  6.6 55.6 %collective-permute-start.7 = (bf16[4,128,512]{2,1,0:T(8,128)(2,1)S(1)}, bf16[4,128,512]{2,1,0:T(8,128)(2,1)S(1)}, u32[]{:S(2)}, u32[]{:S(2)}) collective-permute-start(bf16[4,128,512]{2,1,0:T(8,128)(2,1)S(1)} %get-tuple-element.131), channel_id=1, source_target_pairs={{0,8},{4,12},{8,0},{12,4},{16,24},{20,28},{24,16},{28,20},{1,9},{5... | collective-permute-start | bytes 1572872 | tf_op jit(solution)/shard_map/ppermute | solution.py:21
  8.2 54.0 %collective-permute-start.13 = (bf16[4,128,512]{2,1,0:T(8,128)(2,1)S(1)}, bf16[4,128,512]{2,1,0:T(8,128)(2,1)S(1)}, u32[]{:S(2)}, u32[]{:S(2)}) collective-permute-start(bf16[4,128,512]{2,1,0:T(8,128)(2,1)S(1)} %get-tuple-element.132), channel_id=1, source_target_pairs={{0,16},{4,20},{8,24},{12,28},{16,0},{20,4},{24,8},{28,12},{1,17},{... | collective-permute-start | bytes 1572872 | tf_op jit(solution)/shard_map/ppermute | solution.py:21
  8.5 54.3 %collective-permute-start.3 = (bf16[4,128,512]{2,1,0:T(8,128)(2,1)S(1)}, bf16[4,128,512]{2,1,0:T(8,128)(2,1)S(1)}, u32[]{:S(2)}, u32[]{:S(2)}) collective-permute-start(bf16[4,128,512]{2,1,0:T(8,128)(2,1)S(1)} %get-tuple-element.132), channel_id=1, source_target_pairs={{0,8},{4,12},{8,0},{12,4},{16,24},{20,28},{24,16},{28,20},{1,9},{5... | collective-permute-start | bytes 1572872 | tf_op jit(solution)/shard_map/ppermute | solution.py:21
  9.2 44.4 %collective-permute-start.21 = (s32[4]{0:T(128)S(1)}, s32[4]{0:T(128)S(1)}, u32[]{:S(2)}, u32[]{:S(2)}) collective-permute-start(s32[4]{0:T(128)S(1)} %get-tuple-element.142), channel_id=1, source_target_pairs={{0,12},{4,8},{8,4},{12,0},{16,28},{20,24},{24,20},{28,16},{1,13},{... | collective-permute-start | bytes 56 | tf_op jit(solution)/shard_map/ppermute | solution.py:21
  60.7 14.8 %collective-permute-start.18 = (bf16[4,128,512]{2,1,0:T(8,128)(2,1)S(1)}, bf16[4,128,512]{2,1,0:T(8,128)(2,1)S(1)}, u32[]{:S(2)}, u32[]{:S(2)}) collective-permute-start(bf16[4,128,512]{2,1,0:T(8,128)(2,1)S(1)} %collective-permute-done.17.refs_1_.refs_3_), channel_id=1, source_target_pairs={{0,2},{1,3},{2,0},{3,1},{4,6},{5,7},{6,4},{7,5},{8,10},{9,11},{10,... | collective-permute-start | bytes 1572872 | tf_op jit(solution)/shard_map/ppermute | solution.py:26
  62.2 24.5 %collective-permute-start.8 = (bf16[4,128,512]{2,1,0:T(8,128)(2,1)S(1)}, bf16[4,128,512]{2,1,0:T(8,128)(2,1)S(1)}, u32[]{:S(2)}, u32[]{:S(2)}) collective-permute-start(bf16[4,128,512]{2,1,0:T(8,128)(2,1)S(1)} %collective-permute-done.7.refs_1_), channel_id=1, source_target_pairs={{0,2},{1,3},{2,0},{3,1},{4,6},{5,7},{6,4},{7,5},{8,10},{9,11},{10,... | collective-permute-start | bytes 1572872 | tf_op jit(solution)/shard_map/ppermute | solution.py:26
  62.8 35.1 %collective-permute-start.14 = (bf16[4,128,512]{2,1,0:T(8,128)(2,1)S(1)}, bf16[4,128,512]{2,1,0:T(8,128)(2,1)S(1)}, u32[]{:S(2)}, u32[]{:S(2)}) collective-permute-start(bf16[4,128,512]{2,1,0:T(8,128)(2,1)S(1)} %collective-permute-done.13.refs_1_.refs_3_), channel_id=1, source_target_pairs={{0,2},{1,3},{2,0},{3,1},{4,6},{5,7},{6,4},{7,5},{8,10},{9,11},{10,... | collective-permute-start | bytes 1572872 | tf_op jit(solution)/shard_map/ppermute | solution.py:26
  64.3 41.2 %collective-permute-start.4 = (bf16[4,128,512]{2,1,0:T(8,128)(2,1)S(1)}, bf16[4,128,512]{2,1,0:T(8,128)(2,1)S(1)}, u32[]{:S(2)}, u32[]{:S(2)}) collective-permute-start(bf16[4,128,512]{2,1,0:T(8,128)(2,1)S(1)} %collective-permute-done.3.refs_1_), channel_id=1, source_target_pairs={{0,2},{1,3},{2,0},{3,1},{4,6},{5,7},{6,4},{7,5},{8,10},{9,11},{10,... | collective-permute-start | bytes 1572872 | tf_op jit(solution)/shard_map/ppermute | solution.py:26
  75.5 30.0 %collective-permute-start.20 = (bf16[4,128,512]{2,1,0:T(8,128)(2,1)S(1)}, bf16[4,128,512]{2,1,0:T(8,128)(2,1)S(1)}, u32[]{:S(2)}, u32[]{:S(2)}) collective-permute-start(bf16[4,128,512]{2,1,0:T(8,128)(2,1)S(1)} %collective-permute-done.18.refs_2_.refs_4_), channel_id=1, source_target_pairs={{0,1},{1,0},{2,3},{3,2},{4,5},{5,4},{6,7},{7,6},{8,9},{9,8},{10,11... | collective-permute-start | bytes 1572872 | tf_op jit(solution)/shard_map/ppermute | solution.py:26
  75.5 38.0 %collective-permute-start.15 = (bf16[4,128,512]{2,1,0:T(8,128)(2,1)S(1)}, bf16[4,128,512]{2,1,0:T(8,128)(2,1)S(1)}, u32[]{:S(2)}, u32[]{:S(2)}) collective-permute-start(bf16[4,128,512]{2,1,0:T(8,128)(2,1)S(1)} %collective-permute-done.13.refs_1_.refs_3_), channel_id=1, source_target_pairs={{0,1},{1,0},{2,3},{3,2},{4,5},{5,4},{6,7},{7,6},{8,9},{9,8},{10,11... | collective-permute-start | bytes 1572872 | tf_op jit(solution)/shard_map/ppermute | solution.py:26
  86.7 27.4 %collective-permute-start.5 = (bf16[4,128,512]{2,1,0:T(8,128)(2,1)S(1)}, bf16[4,128,512]{2,1,0:T(8,128)(2,1)S(1)}, u32[]{:S(2)}, u32[]{:S(2)}) collective-permute-start(bf16[4,128,512]{2,1,0:T(8,128)(2,1)S(1)} %collective-permute-done.3.refs_1_), channel_id=1, source_target_pairs={{0,1},{1,0},{2,3},{3,2},{4,5},{5,4},{6,7},{7,6},{8,9},{9,8},{10,11... | collective-permute-start | bytes 1572872 | tf_op jit(solution)/shard_map/ppermute | solution.py:26
  98.0 17.7 %collective-permute-start.10 = (bf16[4,128,512]{2,1,0:T(8,128)(2,1)S(1)}, bf16[4,128,512]{2,1,0:T(8,128)(2,1)S(1)}, u32[]{:S(2)}, u32[]{:S(2)}) collective-permute-start(bf16[4,128,512]{2,1,0:T(8,128)(2,1)S(1)} %collective-permute-done.8.refs_2_), channel_id=1, source_target_pairs={{0,1},{1,0},{2,3},{3,2},{4,5},{5,4},{6,7},{7,6},{8,9},{9,8},{10,11... | collective-permute-start | bytes 1572872 | tf_op jit(solution)/shard_map/ppermute | solution.py:26
  105.5 15.1 %collective-permute-start.16 = (bf16[4,128,512]{2,1,0:T(8,128)(2,1)S(1)}, bf16[4,128,512]{2,1,0:T(8,128)(2,1)S(1)}, u32[]{:S(2)}, u32[]{:S(2)}) collective-permute-start(bf16[4,128,512]{2,1,0:T(8,128)(2,1)S(1)} %collective-permute-done.14.refs_2_.refs_4_), channel_id=1, source_target_pairs={{0,1},{1,0},{2,3},{3,2},{4,5},{5,4},{6,7},{7,6},{8,9},{9,8},{10,11... | collective-permute-start | bytes 1572872 | tf_op jit(solution)/shard_map/ppermute | solution.py:26
  113.5 14.9 %collective-permute-start.1 = (bf16[4,128,512]{2,1,0:T(8,128)(2,1)S(1)}, bf16[4,128,512]{2,1,0:T(8,128)(2,1)S(1)}, u32[]{:S(2)}, u32[]{:S(2)}) collective-permute-start(bf16[4,128,512]{2,1,0:T(8,128)(2,1)S(1)} %get-tuple-element.64), channel_id=1, source_target_pairs={{0,4},{4,0},{8,12},{12,8},{16,20},{20,16},{24,28},{28,24},{1,5},{5... | collective-permute-start | bytes 1572872 | tf_op jit(solution)/shard_map/ppermute | solution.py:21
  114.1 25.5 %collective-permute-start.2 = (bf16[4,128,512]{2,1,0:T(8,128)(2,1)S(1)}, bf16[4,128,512]{2,1,0:T(8,128)(2,1)S(1)}, u32[]{:S(2)}, u32[]{:S(2)}) collective-permute-start(bf16[4,128,512]{2,1,0:T(8,128)(2,1)S(1)} %get-tuple-element.65), channel_id=1, source_target_pairs={{0,4},{4,0},{8,12},{12,8},{16,20},{20,16},{24,28},{28,24},{1,5},{5... | collective-permute-start | bytes 1572872 | tf_op jit(solution)/shard_map/ppermute | solution.py:21
  115.6 46.5 %collective-permute-start.24 = (bf16[4,128,512]{2,1,0:T(8,128)(2,1)S(1)}, bf16[4,128,512]{2,1,0:T(8,128)(2,1)S(1)}, u32[]{:S(2)}, u32[]{:S(2)}) collective-permute-start(bf16[4,128,512]{2,1,0:T(8,128)(2,1)S(1)} %get-tuple-element.73), channel_id=1, source_target_pairs={{0,4},{4,0},{8,12},{12,8},{16,20},{20,16},{24,28},{28,24},{1,5},{5... | collective-permute-start | bytes 1572872 | tf_op jit(solution)/shard_map/ppermute | solution.py:21
  117.6 55.7 %collective-permute-start.12 = (bf16[4,128,512]{2,1,0:T(8,128)(2,1)S(1)}, bf16[4,128,512]{2,1,0:T(8,128)(2,1)S(1)}, u32[]{:S(2)}, u32[]{:S(2)}) collective-permute-start(bf16[4,128,512]{2,1,0:T(8,128)(2,1)S(1)} %gather_held.11), channel_id=1, source_target_pairs={{0,4},{4,0},{8,12},{12,8},{16,20},{20,16},{24,28},{28,24},{1,5},{5... | collective-permute-start | bytes 1572872 | tf_op jit(solution)/shard_map/ppermute | solution.py:21
  120.6 63.9 %collective-permute-start.11 = (bf16[4,128,512]{2,1,0:T(8,128)(2,1)S(1)}, bf16[4,128,512]{2,1,0:T(8,128)(2,1)S(1)}, u32[]{:S(2)}, u32[]{:S(2)}) collective-permute-start(bf16[4,128,512]{2,1,0:T(8,128)(2,1)S(1)} %gather_held.10), channel_id=1, source_target_pairs={{0,4},{4,0},{8,12},{12,8},{16,20},{20,16},{24,28},{28,24},{1,5},{5... | collective-permute-start | bytes 1572872 | tf_op jit(solution)/shard_map/ppermute | solution.py:21
  128.4 82.4 %collective-permute-start.26 = (bf16[4,128,512]{2,1,0:T(8,128)(2,1)S(1)}, bf16[4,128,512]{2,1,0:T(8,128)(2,1)S(1)}, u32[]{:S(2)}, u32[]{:S(2)}) collective-permute-start(bf16[4,128,512]{2,1,0:T(8,128)(2,1)S(1)} %get-tuple-element.75), channel_id=1, source_target_pairs={{0,8},{4,12},{8,0},{12,4},{16,24},{20,28},{24,16},{28,20},{1,9},{5... | collective-permute-start | bytes 1572872 | tf_op jit(solution)/shard_map/ppermute | solution.py:21
  139.6 71.1 %collective-permute-start.28 = (bf16[4,128,512]{2,1,0:T(8,128)(2,1)S(1)}, bf16[4,128,512]{2,1,0:T(8,128)(2,1)S(1)}, u32[]{:S(2)}, u32[]{:S(2)}) collective-permute-start(bf16[4,128,512]{2,1,0:T(8,128)(2,1)S(1)} %get-tuple-element.77), channel_id=1, source_target_pairs={{0,12},{4,8},{8,4},{12,0},{16,28},{20,24},{24,20},{28,16},{1,13},{... | collective-permute-start | bytes 1572872 | tf_op jit(solution)/shard_map/ppermute | solution.py:21
  162.1 48.7 %collective-permute-start.23 = (bf16[4,128,512]{2,1,0:T(8,128)(2,1)S(1)}, bf16[4,128,512]{2,1,0:T(8,128)(2,1)S(1)}, u32[]{:S(2)}, u32[]{:S(2)}) collective-permute-start(bf16[4,128,512]{2,1,0:T(8,128)(2,1)S(1)} %get-tuple-element.72), channel_id=1, source_target_pairs={{0,4},{4,0},{8,12},{12,8},{16,20},{20,16},{24,28},{28,24},{1,5},{5... | collective-permute-start | bytes 1572872 | tf_op jit(solution)/shard_map/ppermute | solution.py:21
  173.3 37.5 %collective-permute-start.25 = (bf16[4,128,512]{2,1,0:T(8,128)(2,1)S(1)}, bf16[4,128,512]{2,1,0:T(8,128)(2,1)S(1)}, u32[]{:S(2)}, u32[]{:S(2)}) collective-permute-start(bf16[4,128,512]{2,1,0:T(8,128)(2,1)S(1)} %get-tuple-element.74), channel_id=1, source_target_pairs={{0,8},{4,12},{8,0},{12,4},{16,24},{20,28},{24,16},{28,20},{1,9},{5... | collective-permute-start | bytes 1572872 | tf_op jit(solution)/shard_map/ppermute | solution.py:21
  184.6 26.2 %collective-permute-start.27 = (bf16[4,128,512]{2,1,0:T(8,128)(2,1)S(1)}, bf16[4,128,512]{2,1,0:T(8,128)(2,1)S(1)}, u32[]{:S(2)}, u32[]{:S(2)}) collective-permute-start(bf16[4,128,512]{2,1,0:T(8,128)(2,1)S(1)} %get-tuple-element.76), channel_id=1, source_target_pairs={{0,12},{4,8},{8,4},{12,0},{16,28},{20,24},{24,20},{28,16},{1,13},{... | collective-permute-start | bytes 1572872 | tf_op jit(solution)/shard_map/ppermute | solution.py:21
  231.7 24.3 %collective-permute-start.32 = (bf16[512,512]{1,0:T(8,128)(2,1)S(1)}, bf16[512,512]{1,0:T(8,128)(2,1)S(1)}, u32[]{:S(2)}, u32[]{:S(2)}) collective-permute-start(bf16[512,512]{1,0:T(8,128)(2,1)S(1)} %get-tuple-element.98), channel_id=1, source_target_pairs={{0,4},{4,0},{8,12},{12,8},{16,20},{20,16},{24,28},{28,24},{1,5},{5... | collective-permute-start | bytes 1572872 | tf_op jit(solution)/shard_map/ppermute | solution.py:21
  233.2 29.4 %collective-permute-start.33 = (bf16[512,512]{1,0:T(8,128)(2,1)}, bf16[512,512]{1,0:T(8,128)(2,1)}, u32[]{:S(2)}, u32[]{:S(2)}) collective-permute-start(bf16[512,512]{1,0:T(8,128)(2,1)} %get-tuple-element.99), channel_id=1, source_target_pairs={{0,8},{4,12},{8,0},{12,4},{16,24},{20,28},{24,16},{28,20},{1,9},{5... | collective-permute-start | bytes 1572872 | tf_op jit(solution)/shard_map/ppermute | solution.py:21
  234.5 28.8 %collective-permute-start.34 = (bf16[512,512]{1,0:T(8,128)(2,1)}, bf16[512,512]{1,0:T(8,128)(2,1)}, u32[]{:S(2)}, u32[]{:S(2)}) collective-permute-start(bf16[512,512]{1,0:T(8,128)(2,1)} %get-tuple-element.100), channel_id=1, source_target_pairs={{0,12},{4,8},{8,4},{12,0},{16,28},{20,24},{24,20},{28,16},{1,13},{... | collective-permute-start | bytes 1572872 | tf_op jit(solution)/shard_map/ppermute | solution.py:21
  235.2 45.1 %collective-permute-start.45 = (bf16[512,512]{1,0:T(8,128)(2,1)}, bf16[512,512]{1,0:T(8,128)(2,1)}, u32[]{:S(2)}, u32[]{:S(2)}) collective-permute-start(bf16[512,512]{1,0:T(8,128)(2,1)} %get-tuple-element.112), channel_id=1, source_target_pairs={{0,4},{4,0},{8,12},{12,8},{16,20},{20,16},{24,28},{28,24},{1,5},{5... | collective-permute-start | bytes 1572872 | tf_op jit(solution)/shard_map/ppermute | solution.py:21
  236.7 45.1 %collective-permute-start.46 = (bf16[512,512]{1,0:T(8,128)(2,1)}, bf16[512,512]{1,0:T(8,128)(2,1)}, u32[]{:S(2)}, u32[]{:S(2)}) collective-permute-start(bf16[512,512]{1,0:T(8,128)(2,1)} %get-tuple-element.113), channel_id=1, source_target_pairs={{0,8},{4,12},{8,0},{12,4},{16,24},{20,28},{24,16},{28,20},{1,9},{5... | collective-permute-start | bytes 1572872 | tf_op jit(solution)/shard_map/ppermute | solution.py:21
  256.8 25.0 %collective-permute-start.47 = (bf16[512,512]{1,0:T(8,128)(2,1)}, bf16[512,512]{1,0:T(8,128)(2,1)}, u32[]{:S(2)}, u32[]{:S(2)}) collective-permute-start(bf16[512,512]{1,0:T(8,128)(2,1)} %get-tuple-element.114), channel_id=1, source_target_pairs={{0,12},{4,8},{8,4},{12,0},{16,28},{20,24},{24,20},{28,16},{1,13},{... | collective-permute-start | bytes 1572872 | tf_op jit(solution)/shard_map/ppermute | solution.py:21
  262.6 28.8 %collective-permute-start.42 = (bf16[512,512]{1,0:T(8,128)(2,1)S(1)}, bf16[512,512]{1,0:T(8,128)(2,1)S(1)}, u32[]{:S(2)}, u32[]{:S(2)}) collective-permute-start(bf16[512,512]{1,0:T(8,128)(2,1)S(1)} %get-tuple-element.108), channel_id=1, source_target_pairs={{0,4},{4,0},{8,12},{12,8},{16,20},{20,16},{24,28},{28,24},{1,5},{5... | collective-permute-start | bytes 1572872 | tf_op jit(solution)/shard_map/ppermute | solution.py:21
  265.6 57.7 %collective-permute-start.35 = (bf16[8,128,512]{2,1,0:T(8,128)(2,1)S(1)}, bf16[8,128,512]{2,1,0:T(8,128)(2,1)S(1)}, u32[]{:S(2)}, u32[]{:S(2)}) collective-permute-start(bf16[8,128,512]{2,1,0:T(8,128)(2,1)S(1)} %get-tuple-element.102), channel_id=1, source_target_pairs={{0,1},{1,0},{2,3},{3,2},{4,5},{5,4},{6,7},{7,6},{8,9},{9,8},{10,11... | collective-permute-start | bytes 3145736 | tf_op jit(solution)/shard_map/ppermute | solution.py:26
  280.3 22.4 %collective-permute-start.29 = (bf16[512,512]{1,0:T(8,128)(2,1)S(1)}, bf16[512,512]{1,0:T(8,128)(2,1)S(1)}, u32[]{:S(2)}, u32[]{:S(2)}) collective-permute-start(bf16[512,512]{1,0:T(8,128)(2,1)S(1)} %get-tuple-element.94), channel_id=1, source_target_pairs={{0,4},{4,0},{8,12},{12,8},{16,20},{20,16},{24,28},{28,24},{1,5},{5... | collective-permute-start | bytes 1572872 | tf_op jit(solution)/shard_map/ppermute | solution.py:21
  284.1 40.3 %collective-permute-start.48 = (bf16[8,128,512]{2,1,0:T(8,128)(2,1)S(1)}, bf16[8,128,512]{2,1,0:T(8,128)(2,1)S(1)}, u32[]{:S(2)}, u32[]{:S(2)}) collective-permute-start(bf16[8,128,512]{2,1,0:T(8,128)(2,1)S(1)} %get-tuple-element.116), channel_id=1, source_target_pairs={{0,1},{1,0},{2,3},{3,2},{4,5},{5,4},{6,7},{7,6},{8,9},{9,8},{10,11... | collective-permute-start | bytes 3145736 | tf_op jit(solution)/shard_map/ppermute | solution.py:26
  286.2 27.7 %collective-permute-start.51 = (bf16[512,512]{1,0:T(8,128)(2,1)S(1)}, bf16[512,512]{1,0:T(8,128)(2,1)S(1)}, u32[]{:S(2)}, u32[]{:S(2)}) collective-permute-start(bf16[512,512]{1,0:T(8,128)(2,1)S(1)} %get-tuple-element.118), channel_id=1, source_target_pairs={{0,4},{4,0},{8,12},{12,8},{16,20},{20,16},{24,28},{28,24},{1,5},{5... | collective-permute-start | bytes 1572872 | tf_op jit(solution)/shard_map/ppermute | solution.py:21
  291.4 30.7 %collective-permute-start.38 = (bf16[512,512]{1,0:T(8,128)(2,1)S(1)}, bf16[512,512]{1,0:T(8,128)(2,1)S(1)}, u32[]{:S(2)}, u32[]{:S(2)}) collective-permute-start(bf16[512,512]{1,0:T(8,128)(2,1)S(1)} %get-tuple-element.104), channel_id=1, source_target_pairs={{0,4},{4,0},{8,12},{12,8},{16,20},{20,16},{24,28},{28,24},{1,5},{5... | collective-permute-start | bytes 1572872 | tf_op jit(solution)/shard_map/ppermute | solution.py:21
  302.7 23.8 %collective-permute-start.43 = (bf16[8,128,512]{2,1,0:T(8,128)(2,1)S(1)}, bf16[8,128,512]{2,1,0:T(8,128)(2,1)S(1)}, u32[]{:S(2)}, u32[]{:S(2)}) collective-permute-start(bf16[8,128,512]{2,1,0:T(8,128)(2,1)S(1)} %get-tuple-element.110), channel_id=1, source_target_pairs={{0,1},{1,0},{2,3},{3,2},{4,5},{5,4},{6,7},{7,6},{8,9},{9,8},{10,11... | collective-permute-start | bytes 3145736 | tf_op jit(solution)/shard_map/ppermute | solution.py:26
  313.9 13.6 %collective-permute-start.30 = (bf16[8,128,512]{2,1,0:T(8,128)(2,1)S(1)}, bf16[8,128,512]{2,1,0:T(8,128)(2,1)S(1)}, u32[]{:S(2)}, u32[]{:S(2)}) collective-permute-start(bf16[8,128,512]{2,1,0:T(8,128)(2,1)S(1)} %get-tuple-element.96), channel_id=1, source_target_pairs={{0,1},{1,0},{2,3},{3,2},{4,5},{5,4},{6,7},{7,6},{8,9},{9,8},{10,11... | collective-permute-start | bytes 3145736 | tf_op jit(solution)/shard_map/ppermute | solution.py:26
  324.4 61.1 %collective-permute-start.36 = (bf16[4,128,512]{2,1,0:T(8,128)(2,1)S(1)}, bf16[4,128,512]{2,1,0:T(8,128)(2,1)S(1)}, u32[]{:S(2)}, u32[]{:S(2)}) collective-permute-start(bf16[4,128,512]{2,1,0:T(8,128)(2,1)S(1)} %slice.135), channel_id=1, source_target_pairs={{0,2},{1,3},{2,0},{3,1},{4,6},{5,7},{6,4},{7,5},{8,10},{9,11},{10,... | collective-permute-start | bytes 1572872 | tf_op jit(solution)/shard_map/ppermute | solution.py:26
  326.5 24.0 %collective-permute-start.49 = (bf16[4,128,512]{2,1,0:T(8,128)(2,1)S(1)}, bf16[4,128,512]{2,1,0:T(8,128)(2,1)S(1)}, u32[]{:S(2)}, u32[]{:S(2)}) collective-permute-start(bf16[4,128,512]{2,1,0:T(8,128)(2,1)S(1)} %slice.132), channel_id=1, source_target_pairs={{0,2},{1,3},{2,0},{3,1},{4,6},{5,7},{6,4},{7,5},{8,10},{9,11},{10,... | collective-permute-start | bytes 1572872 | tf_op jit(solution)/shard_map/ppermute | solution.py:26
  327.5 68.2 %collective-permute-start.44 = (bf16[4,128,512]{2,1,0:T(8,128)(2,1)S(1)}, bf16[4,128,512]{2,1,0:T(8,128)(2,1)S(1)}, u32[]{:S(2)}, u32[]{:S(2)}) collective-permute-start(bf16[4,128,512]{2,1,0:T(8,128)(2,1)S(1)} %slice.133), channel_id=1, source_target_pairs={{0,2},{1,3},{2,0},{3,1},{4,6},{5,7},{6,4},{7,5},{8,10},{9,11},{10,... | collective-permute-start | bytes 1572872 | tf_op jit(solution)/shard_map/ppermute | solution.py:26
  329.6 82.7 %collective-permute-start.31 = (bf16[4,128,512]{2,1,0:T(8,128)(2,1)S(1)}, bf16[4,128,512]{2,1,0:T(8,128)(2,1)S(1)}, u32[]{:S(2)}, u32[]{:S(2)}) collective-permute-start(bf16[4,128,512]{2,1,0:T(8,128)(2,1)S(1)} %slice.136), channel_id=1, source_target_pairs={{0,2},{1,3},{2,0},{3,1},{4,6},{5,7},{6,4},{7,5},{8,10},{9,11},{10,... | collective-permute-start | bytes 1572872 | tf_op jit(solution)/shard_map/ppermute | solution.py:26
  330.6 53.6 %collective-permute-start.53 = (bf16[4,128,512]{2,1,0:T(8,128)(2,1)S(1)}, bf16[4,128,512]{2,1,0:T(8,128)(2,1)S(1)}, u32[]{:S(2)}, u32[]{:S(2)}) collective-permute-start(bf16[4,128,512]{2,1,0:T(8,128)(2,1)S(1)} %slice.131), channel_id=1, source_target_pairs={{0,2},{1,3},{2,0},{3,1},{4,6},{5,7},{6,4},{7,5},{8,10},{9,11},{10,... | collective-permute-start | bytes 1572872 | tf_op jit(solution)/shard_map/ppermute | solution.py:26
  350.5 44.0 %collective-permute-start.40 = (bf16[4,128,512]{2,1,0:T(8,128)(2,1)S(1)}, bf16[4,128,512]{2,1,0:T(8,128)(2,1)S(1)}, u32[]{:S(2)}, u32[]{:S(2)}) collective-permute-start(bf16[4,128,512]{2,1,0:T(8,128)(2,1)S(1)} %slice.134), channel_id=1, source_target_pairs={{0,2},{1,3},{2,0},{3,1},{4,6},{5,7},{6,4},{7,5},{8,10},{9,11},{10,... | collective-permute-start | bytes 1572872 | tf_op jit(solution)/shard_map/ppermute | solution.py:26
  384.2 27.8 %collective-permute-start.50 = (bf16[4,128,512]{2,1,0:T(8,128)(2,1)S(1)}, bf16[4,128,512]{2,1,0:T(8,128)(2,1)S(1)}, u32[]{:S(2)}, u32[]{:S(2)}) collective-permute-start(bf16[4,128,512]{2,1,0:T(8,128)(2,1)S(1)} %fusion.1), channel_id=1, source_target_pairs={{0,16},{4,20},{8,24},{12,28},{16,0},{20,4},{24,8},{28,12},{1,17},{... | collective-permute-start | bytes 1572872 | tf_op jit(solution)/shard_map/ppermute | solution.py:21
  385.5 26.5 %collective-permute-start.54 = (bf16[4,128,512]{2,1,0:T(8,128)(2,1)S(1)}, bf16[4,128,512]{2,1,0:T(8,128)(2,1)S(1)}, u32[]{:S(2)}, u32[]{:S(2)}) collective-permute-start(bf16[4,128,512]{2,1,0:T(8,128)(2,1)S(1)} %fusion), channel_id=1, source_target_pairs={{0,8},{4,12},{8,0},{12,4},{16,24},{20,28},{24,16},{28,20},{1,9},{5... | collective-permute-start | bytes 1572872 | tf_op jit(solution)/shard_map/ppermute | solution.py:21
  394.5 36.4 %collective-permute-start.37 = (bf16[4,128,512]{2,1,0:T(8,128)(2,1)S(1)}, bf16[4,128,512]{2,1,0:T(8,128)(2,1)S(1)}, u32[]{:S(2)}, u32[]{:S(2)}) collective-permute-start(bf16[4,128,512]{2,1,0:T(8,128)(2,1)S(1)} %fusion.5), channel_id=1, source_target_pairs={{0,16},{4,20},{8,24},{12,28},{16,0},{20,4},{24,8},{28,12},{1,17},{... | collective-permute-start | bytes 1572872 | tf_op jit(solution)/shard_map/ppermute | solution.py:21
  395.7 35.2 %collective-permute-start.41 = (bf16[4,128,512]{2,1,0:T(8,128)(2,1)S(1)}, bf16[4,128,512]{2,1,0:T(8,128)(2,1)S(1)}, u32[]{:S(2)}, u32[]{:S(2)}) collective-permute-start(bf16[4,128,512]{2,1,0:T(8,128)(2,1)S(1)} %fusion.4), channel_id=1, source_target_pairs={{0,8},{4,12},{8,0},{12,4},{16,24},{20,28},{24,16},{28,20},{1,9},{5... | collective-permute-start | bytes 1572872 | tf_op jit(solution)/shard_map/ppermute | solution.py:21
  (67 other events, 925.5 us)

commit v2 on v1

--- a/solution.py
+++ b/solution.py
@@ -212,8 +212,7 @@
     shape = (rows[0].shape[0], count)
     return pl.pallas_call(
         functools.partial(own_kernel, group, cap, lanes, parts),
-        out_shape=[jax.ShapeDtypeStruct(shape, F32)] * group
-        + [jax.ShapeDtypeStruct(line, F32)] * 3,
+        out_shape=[pltpu.HBM(shape, F32)] * group + [jax.ShapeDtypeStruct(line, F32)] * 3,
         in_specs=[SM] + [VM] * (2 + len(rows)),
         out_specs=[FIXED] * group + [VM] * 3,
         scratch_shapes=[
@@ -294,7 +293,8 @@
     outs += [((size, width // parts), BF)] * (group * parts)
     got = pl.pallas_call(
         functools.partial(far_kernel, group, cap, lanes, parts, len(stats) // 3),
-        out_shape=[jax.ShapeDtypeStruct(*o) for o in outs],
+        out_shape=[jax.ShapeDtypeStruct(*o) for o in outs[:3]]
+        + [pltpu.HBM(*o) for o in outs[3:]],
         in_specs=[SM] + [VM] * (2 + len(stats) + len(rows)),
         out_specs=[VM] * 3 + [FIXED] * (len(outs) - 3),
         scratch_shapes=[

time: 433 us -> 423 us (0.977)
  local copies, waits for them, and re-layouts: 16.5 us -> 8.29 us
  waiting for transfers between devices: 282 us -> 290 us
  Pallas kernels: 76 us -> 69.9 us
    unnamed x120 -> x100, local copies, waits for them, and re-layouts: 14.2 us -> 5.96 us
    ppermute x31, waiting for transfers between devices: 184 us -> 192 us  [xor_proto(): return lax.ppermute(x, 'proto', [(i, i ^ shift) for i in range(count)])]
    pallas_call x2, Pallas kernels: 15.8 us -> 10.5 us  [own_logits(): pl.pallas_call(functools.partial(own_kernel, group, cap, lanes, parts), o...]
  transfers between devices with their start and end apart: 55 -> 55, of which waited for: 23 -> 24; matrix products, arithmetic and copies ran while one was open for 1% -> 1% of each run, Pallas kernels for 14% -> 13%
where the time goes in v2:
time: 423 us
  waiting for transfers between devices  290 us (69%)
  Pallas kernels  69.9 us (17%)
  starting transfers between devices  46.2 us (11%)
  local copies, waits for them, and re-layouts  8.29 us (2%)
  other arithmetic  7.38 us (2%)
    ppermute x31, waiting for transfers between devices, xor_proto(): return lax.ppermute(x, 'proto', [(i, i ^ shift) for i in range(count)])  192 us
    ppermute x24, waiting for transfers between devices, xor_design(): return lax.ppermute(x, 'design', [(i, i ^ shift) for i in range(count)])  97.9 us
    ppermute x31, starting transfers between devices, xor_proto(): return lax.ppermute(x, 'proto', [(i, i ^ shift) for i in range(count)])  32.9 us
    pallas_call x8, Pallas kernels, gather_held(): pl.pallas_call(functools.partial(gather_held_kernel, len(srcs), n, quarte...  15.1 us
    pallas_call x1, Pallas kernels, far_grads(): pl.pallas_call(functools.partial(far_kernel, group, cap, lanes, parts, le...  14.1 us
    ppermute x24, starting transfers between devices, xor_design(): return lax.ppermute(x, 'design', [(i, i ^ shift) for i in range(count)])  13.3 us
    pallas_call x2, Pallas kernels, own_logits(): pl.pallas_call(functools.partial(own_kernel, group, cap, lanes, parts), o...  10.5 us
    pallas_call x2, Pallas kernels, design_grad(): pl.pallas_call(functools.partial(design_grad_kernel, n, chunk), out_shape...  10.4 us
  transfers between devices with their start and end apart: 55, of which 24 were waited for; matrix products, arithmetic and copies ran while one was open for 1% of the time, Pallas kernels for 13%

profile of v2, /device:TPU:0, one launch (start us, length us, event | category | flops | bytes accessed | tf_op | source)
XLA Modules:
  0.0 423.1 jit_solution(9675238406115610660)
XLA Ops:
  0.6 1.7 dynamic-slice_convert_fusion
  2.5 4.1 collective-permute-start.17
  6.6 1.6 collective-permute-start.7
  9.2 2.8 collective-permute-start.21
  12.0 41.5 %collective-permute-done.21.refs_0_ = s32[4]{0:T(128)S(1)} collective-permute-done((s32[4]{0:T(128)S(1)}, s32[4]{0:T(128)S(1)}, u32[]{:S(2)}, u32[]{:S(2)}) %collective-permute-start.21) | collective-permute-done | bytes 48 | tf_op jit(solution)/shard_map/ppermute | solution.py:21
  55.0 2.1 collective-permute-done.22.refs_1_
  57.6 3.1 collective-permute-done
  64.8 10.6 %collective-permute-done.18.refs_2_.refs_4_ = bf16[4,128,512]{2,1,0:T(8,128)(2,1)S(1)} collective-permute-done((bf16[4,128,512]{2,1,0:T(8,128)(2,1)S(1)}, bf16[4,128,512]{2,1,0:T(8,128)(2,1)S(1)}, u32[]{:S(2)}, u32[]{:S(2)}) %collective-permute-start.18) | collective-permute-done | bytes 524320 | tf_op jit(solution)/shard_map/ppermute | solution.py:26
  76.0 10.7 %collective-permute-done.8.refs_2_ = bf16[4,128,512]{2,1,0:T(8,128)(2,1)S(1)} collective-permute-done((bf16[4,128,512]{2,1,0:T(8,128)(2,1)S(1)}, bf16[4,128,512]{2,1,0:T(8,128)(2,1)S(1)}, u32[]{:S(2)}, u32[]{:S(2)}) %collective-permute-start.8) | collective-permute-done | bytes 524320 | tf_op jit(solution)/shard_map/ppermute | solution.py:26
  86.7 11.2 %collective-permute-done.14.refs_2_.refs_4_ = bf16[4,128,512]{2,1,0:T(8,128)(2,1)S(1)} collective-permute-done((bf16[4,128,512]{2,1,0:T(8,128)(2,1)S(1)}, bf16[4,128,512]{2,1,0:T(8,128)(2,1)S(1)}, u32[]{:S(2)}, u32[]{:S(2)}) %collective-permute-start.14) | collective-permute-done | bytes 524320 | tf_op jit(solution)/shard_map/ppermute | solution.py:26
  98.0 7.5 %collective-permute-done.4.refs_2_ = bf16[4,128,512]{2,1,0:T(8,128)(2,1)S(1)} collective-permute-done((bf16[4,128,512]{2,1,0:T(8,128)(2,1)S(1)}, bf16[4,128,512]{2,1,0:T(8,128)(2,1)S(1)}, u32[]{:S(2)}, u32[]{:S(2)}) %collective-permute-start.4) | collective-permute-done | bytes 524320 | tf_op jit(solution)/shard_map/ppermute | solution.py:26
  106.0 3.4 copy-done.1
  110.3 3.2 gather_held.15
  121.2 3.2 gather_held.14
  124.5 3.9 collective-permute-done.1
  129.1 10.5 %collective-permute-done.2 = bf16[4,128,512]{2,1,0:T(8,128)(2,1)S(1)} collective-permute-done((bf16[4,128,512]{2,1,0:T(8,128)(2,1)S(1)}, bf16[4,128,512]{2,1,0:T(8,128)(2,1)S(1)}, u32[]{:S(2)}, u32[]{:S(2)}) %collective-permute-start.2) | collective-permute-done | bytes 524320 | tf_op jit(solution)/shard_map/ppermute | solution.py:21
  140.3 21.8 %collective-permute-done.24 = bf16[4,128,512]{2,1,0:T(8,128)(2,1)S(1)} collective-permute-done((bf16[4,128,512]{2,1,0:T(8,128)(2,1)S(1)}, bf16[4,128,512]{2,1,0:T(8,128)(2,1)S(1)}, u32[]{:S(2)}, u32[]{:S(2)}) %collective-permute-start.24) | collective-permute-done | bytes 524320 | tf_op jit(solution)/shard_map/ppermute | solution.py:21
  162.6 10.7 %collective-permute-done.12 = bf16[4,128,512]{2,1,0:T(8,128)(2,1)S(1)} collective-permute-done((bf16[4,128,512]{2,1,0:T(8,128)(2,1)S(1)}, bf16[4,128,512]{2,1,0:T(8,128)(2,1)S(1)}, u32[]{:S(2)}, u32[]{:S(2)}) %collective-permute-start.12) | collective-permute-done | bytes 524320 | tf_op jit(solution)/shard_map/ppermute | solution.py:21
  174.1 10.5 %collective-permute-done.11 = bf16[4,128,512]{2,1,0:T(8,128)(2,1)S(1)} collective-permute-done((bf16[4,128,512]{2,1,0:T(8,128)(2,1)S(1)}, bf16[4,128,512]{2,1,0:T(8,128)(2,1)S(1)}, u32[]{:S(2)}, u32[]{:S(2)}) %collective-permute-start.11) | collective-permute-done | bytes 524320 | tf_op jit(solution)/shard_map/ppermute | solution.py:21
  189.3 6.9 %own_logits.2 = (f32[512,1024]{1,0:T(8,128)}, f32[512,1024]{1,0:T(8,128)}, f32[512,1024]{1,0:T(8,128)}, f32[1,1024]{1,0:T(1,128)S(1)}, f32[1,1024]{1,0:T(1,128)S(1)}, /*index=5*/f32[1,1024]{1,0:T(1,128)S(1)}) custom-call(s32[12]{0:T(128)S(1)} %pad_add_fusion.2.base, bf16[1024,1024]{1,0:T(8,128)(2,1)S(1)} %copy-done, s32[1,1024]{1,0:T(1,128)S(1)} %bitcast.106, ...), custom_call_target="tpu_custom_call" | custom-call | tf_op jit(solution)/shard_map/own_logits/pallas_call | solution.py:213
  199.1 3.6 own_logits.3
  202.8 3.3 collective-permute-done.23
  206.1 14.1 %far_grads.1 = (f32[1,1024]{1,0:T(1,128)}, f32[1,1024]{1,0:T(1,128)S(1)}, f32[1,1024]{1,0:T(1,128)S(1)}, bf16[512,1024]{1,0:T(8,128)(2,1)}, bf16[512,1024]{1,0:T...) custom-call(s32[16]{0:T(128)S(1)} %pad_add_fusion.1.base, ...), custom_call_target="tpu_custom_call" | custom-call | tf_op jit(solution)/shard_map/far_grads/pallas_call | solution.py:294
  221.7 2.2 collective-permute-start.34
  225.2 20.0 %collective-permute-done.32.refs_1_ = bf16[512,512]{1,0:T(8,128)(2,1)S(1)} collective-permute-done((bf16[512,512]{1,0:T(8,128)(2,1)}, bf16[512,512]{1,0:T(8,128)(2,1)S(1)}, u32[]{:S(2)}, u32[]{:S(2)}) %collective-permute-start.32) | collective-permute-done | bytes 524320 | tf_op jit(solution)/shard_map/ppermute | solution.py:21
  246.6 1.6 copy-done.19
  248.2 1.9 own_grad.5
  251.9 2.5 collect.7
  254.5 14.7 %collective-permute-done.45.refs_1_ = bf16[512,512]{1,0:T(8,128)(2,1)} collective-permute-done((bf16[512,512]{1,0:T(8,128)(2,1)}, bf16[512,512]{1,0:T(8,128)(2,1)}, u32[]{:S(2)}, u32[]{:S(2)}) %collective-permute-start.45) | collective-permute-done | bytes 524320 | tf_op jit(solution)/shard_map/ppermute | solution.py:21
  269.8 2.3 collect.10
  272.2 2.0 own_grad.7
  275.6 4.7 %collective-permute-done.42.refs_1_ = bf16[512,512]{1,0:T(8,128)(2,1)S(1)} collective-permute-done((bf16[512,512]{1,0:T(8,128)(2,1)S(1)}, bf16[512,512]{1,0:T(8,128)(2,1)S(1)}, u32[]{:S(2)}, u32[]{:S(2)}) %collective-permute-start.42) | collective-permute-done | bytes 524320 | tf_op jit(solution)/shard_map/ppermute | solution.py:21
  281.0 2.0 own_grad.4
  284.3 7.3 %collective-permute-done.29.refs_1_ = bf16[512,512]{1,0:T(8,128)(2,1)S(1)} collective-permute-done((bf16[512,512]{1,0:T(8,128)(2,1)S(1)}, bf16[512,512]{1,0:T(8,128)(2,1)S(1)}, u32[]{:S(2)}, u32[]{:S(2)}) %collective-permute-start.29) | collective-permute-done | bytes 524320 | tf_op jit(solution)/shard_map/ppermute | solution.py:21
  291.7 2.0 own_grad.6
  294.9 7.9 %collective-permute-done.51.refs_1_ = bf16[512,512]{1,0:T(8,128)(2,1)S(1)} collective-permute-done((bf16[512,512]{1,0:T(8,128)(2,1)S(1)}, bf16[512,512]{1,0:T(8,128)(2,1)S(1)}, u32[]{:S(2)}, u32[]{:S(2)}) %collective-permute-start.51) | collective-permute-done | bytes 524320 | tf_op jit(solution)/shard_map/ppermute | solution.py:21
  304.1 8.1 %collective-permute-done.38.refs_1_ = bf16[512,512]{1,0:T(8,128)(2,1)S(1)} collective-permute-done((bf16[512,512]{1,0:T(8,128)(2,1)S(1)}, bf16[512,512]{1,0:T(8,128)(2,1)S(1)}, u32[]{:S(2)}, u32[]{:S(2)}) %collective-permute-start.38) | collective-permute-done | bytes 524320 | tf_op jit(solution)/shard_map/ppermute | solution.py:21
  314.8 1.6 collective-permute-start.36
  317.9 1.6 collective-permute-start.44
  321.0 1.6 collective-permute-start.53
  323.0 17.9 %collective-permute-done.49 = bf16[4,128,512]{2,1,0:T(8,128)(2,1)S(1)} collective-permute-done((bf16[4,128,512]{2,1,0:T(8,128)(2,1)S(1)}, bf16[4,128,512]{2,1,0:T(8,128)(2,1)S(1)}, u32[]{:S(2)}, u32[]{:S(2)}) %collective-permute-start.49) | collective-permute-done | bytes 524320 | tf_op jit(solution)/shard_map/ppermute | solution.py:26
  342.7 32.0 %collective-permute-done.53 = bf16[4,128,512]{2,1,0:T(8,128)(2,1)S(1)} collective-permute-done((bf16[4,128,512]{2,1,0:T(8,128)(2,1)S(1)}, bf16[4,128,512]{2,1,0:T(8,128)(2,1)S(1)}, u32[]{:S(2)}, u32[]{:S(2)}) %collective-permute-start.53) | collective-permute-done | bytes 524320 | tf_op jit(solution)/shard_map/ppermute | solution.py:26
  377.1 7.8 %collective-permute-done.40 = bf16[4,128,512]{2,1,0:T(8,128)(2,1)S(1)} collective-permute-done((bf16[4,128,512]{2,1,0:T(8,128)(2,1)S(1)}, bf16[4,128,512]{2,1,0:T(8,128)(2,1)S(1)}, u32[]{:S(2)}, u32[]{:S(2)}) %collective-permute-start.40) | collective-permute-done | bytes 524320 | tf_op jit(solution)/shard_map/ppermute | solution.py:26
  387.3 5.2 %design_grad.3 = bf16[1024,512]{1,0:T(8,128)(2,1)S(1)} custom-call(bf16[512,1024]{1,0:T(8,128)(2,1)S(1)} %get-tuple-element.82.refs_0_, bf16[512,1024]{1,0:T(8,128)(2,1)S(1)} %get-tuple-element.84.refs_1_, bf16[512,1024]{1,0:T(8,128)(2,1)S(1)} %get-tuple-element.86.refs_2_, bf16[512,1024]{1,0:T(8,128)(2,1)S(1)} %get-tuple-element.88.refs_3_, ...), custom_call_target="tpu_custom_call" | custom-call | tf_op jit(solution)/shard_map/design_grad/pallas_call | solution.py:360
  392.6 5.2 %design_grad.2 = bf16[1024,512]{1,0:T(8,128)(2,1)S(1)} custom-call(bf16[512,1024]{1,0:T(8,128)(2,1)S(1)} %get-tuple-element.82.refs_0_, bf16[512,1024]{1,0:T(8,128)(2,1)S(1)} %get-tuple-element.84.refs_1_, bf16[512,1024]{1,0:T(8,128)(2,1)S(1)} %get-tuple-element.86.refs_2_, bf16[512,1024]{1,0:T(8,128)(2,1)S(1)} %get-tuple-element.88.refs_3_, ...), custom_call_target="tpu_custom_call" | custom-call | tf_op jit(solution)/shard_map/design_grad/pallas_call | solution.py:360
  397.8 1.6 pad_maximum_fusion
  399.4 2.5 collective-permute-done.50
  402.1 19.2 %collective-permute-done.37 = bf16[4,128,512]{2,1,0:T(8,128)(2,1)S(1)} collective-permute-done((bf16[4,128,512]{2,1,0:T(8,128)(2,1)S(1)}, bf16[4,128,512]{2,1,0:T(8,128)(2,1)S(1)}, u32[]{:S(2)}, u32[]{:S(2)}) %collective-permute-start.37) | collective-permute-done | bytes 524320 | tf_op jit(solution)/shard_map/ppermute | solution.py:21
  (225 shorter events, 53.7 us)
Async XLA Ops:
  2.5 52.5 %collective-permute-start.17 = (bf16[4,128,512]{2,1,0:T(8,128)(2,1)S(1)}, bf16[4,128,512]{2,1,0:T(8,128)(2,1)S(1)}, u32[]{:S(2)}, u32[]{:S(2)}) collective-permute-start(bf16[4,128,512]{2,1,0:T(8,128)(2,1)S(1)} %get-tuple-element.131), channel_id=1, source_target_pairs={{0,16},{4,20},{8,24},{12,28},{16,0},{20,4},{24,8},{28,12},{1,17},{... | collective-permute-start | bytes 1572872 | tf_op jit(solution)/shard_map/ppermute | solution.py:21
  6.6 55.6 %collective-permute-start.7 = (bf16[4,128,512]{2,1,0:T(8,128)(2,1)S(1)}, bf16[4,128,512]{2,1,0:T(8,128)(2,1)S(1)}, u32[]{:S(2)}, u32[]{:S(2)}) collective-permute-start(bf16[4,128,512]{2,1,0:T(8,128)(2,1)S(1)} %get-tuple-element.131), channel_id=1, source_target_pairs={{0,8},{4,12},{8,0},{12,4},{16,24},{20,28},{24,16},{28,20},{1,9},{5... | collective-permute-start | bytes 1572872 | tf_op jit(solution)/shard_map/ppermute | solution.py:21
  8.2 54.0 %collective-permute-start.13 = (bf16[4,128,512]{2,1,0:T(8,128)(2,1)S(1)}, bf16[4,128,512]{2,1,0:T(8,128)(2,1)S(1)}, u32[]{:S(2)}, u32[]{:S(2)}) collective-permute-start(bf16[4,128,512]{2,1,0:T(8,128)(2,1)S(1)} %get-tuple-element.132), channel_id=1, source_target_pairs={{0,16},{4,20},{8,24},{12,28},{16,0},{20,4},{24,8},{28,12},{1,17},{... | collective-permute-start | bytes 1572872 | tf_op jit(solution)/shard_map/ppermute | solution.py:21
  8.5 54.3 %collective-permute-start.3 = (bf16[4,128,512]{2,1,0:T(8,128)(2,1)S(1)}, bf16[4,128,512]{2,1,0:T(8,128)(2,1)S(1)}, u32[]{:S(2)}, u32[]{:S(2)}) collective-permute-start(bf16[4,128,512]{2,1,0:T(8,128)(2,1)S(1)} %get-tuple-element.132), channel_id=1, source_target_pairs={{0,8},{4,12},{8,0},{12,4},{16,24},{20,28},{24,16},{28,20},{1,9},{5... | collective-permute-start | bytes 1572872 | tf_op jit(solution)/shard_map/ppermute | solution.py:21
  9.2 44.4 %collective-permute-start.21 = (s32[4]{0:T(128)S(1)}, s32[4]{0:T(128)S(1)}, u32[]{:S(2)}, u32[]{:S(2)}) collective-permute-start(s32[4]{0:T(128)S(1)} %get-tuple-element.142), channel_id=1, source_target_pairs={{0,12},{4,8},{8,4},{12,0},{16,28},{20,24},{24,20},{28,16},{1,13},{... | collective-permute-start | bytes 56 | tf_op jit(solution)/shard_map/ppermute | solution.py:21
  60.7 14.8 %collective-permute-start.18 = (bf16[4,128,512]{2,1,0:T(8,128)(2,1)S(1)}, bf16[4,128,512]{2,1,0:T(8,128)(2,1)S(1)}, u32[]{:S(2)}, u32[]{:S(2)}) collective-permute-start(bf16[4,128,512]{2,1,0:T(8,128)(2,1)S(1)} %collective-permute-done.17.refs_1_.refs_3_), channel_id=1, source_target_pairs={{0,2},{1,3},{2,0},{3,1},{4,6},{5,7},{6,4},{7,5},{8,10},{9,11},{10,... | collective-permute-start | bytes 1572872 | tf_op jit(solution)/shard_map/ppermute | solution.py:26
  62.2 24.5 %collective-permute-start.8 = (bf16[4,128,512]{2,1,0:T(8,128)(2,1)S(1)}, bf16[4,128,512]{2,1,0:T(8,128)(2,1)S(1)}, u32[]{:S(2)}, u32[]{:S(2)}) collective-permute-start(bf16[4,128,512]{2,1,0:T(8,128)(2,1)S(1)} %collective-permute-done.7.refs_1_), channel_id=1, source_target_pairs={{0,2},{1,3},{2,0},{3,1},{4,6},{5,7},{6,4},{7,5},{8,10},{9,11},{10,... | collective-permute-start | bytes 1572872 | tf_op jit(solution)/shard_map/ppermute | solution.py:26
  62.8 35.1 %collective-permute-start.14 = (bf16[4,128,512]{2,1,0:T(8,128)(2,1)S(1)}, bf16[4,128,512]{2,1,0:T(8,128)(2,1)S(1)}, u32[]{:S(2)}, u32[]{:S(2)}) collective-permute-start(bf16[4,128,512]{2,1,0:T(8,128)(2,1)S(1)} %collective-permute-done.13.refs_1_.refs_3_), channel_id=1, source_target_pairs={{0,2},{1,3},{2,0},{3,1},{4,6},{5,7},{6,4},{7,5},{8,10},{9,11},{10,... | collective-permute-start | bytes 1572872 | tf_op jit(solution)/shard_map/ppermute | solution.py:26
  64.3 41.2 %collective-permute-start.4 = (bf16[4,128,512]{2,1,0:T(8,128)(2,1)S(1)}, bf16[4,128,512]{2,1,0:T(8,128)(2,1)S(1)}, u32[]{:S(2)}, u32[]{:S(2)}) collective-permute-start(bf16[4,128,512]{2,1,0:T(8,128)(2,1)S(1)} %collective-permute-done.3.refs_1_), channel_id=1, source_target_pairs={{0,2},{1,3},{2,0},{3,1},{4,6},{5,7},{6,4},{7,5},{8,10},{9,11},{10,... | collective-permute-start | bytes 1572872 | tf_op jit(solution)/shard_map/ppermute | solution.py:26
  75.5 30.0 %collective-permute-start.20 = (bf16[4,128,512]{2,1,0:T(8,128)(2,1)S(1)}, bf16[4,128,512]{2,1,0:T(8,128)(2,1)S(1)}, u32[]{:S(2)}, u32[]{:S(2)}) collective-permute-start(bf16[4,128,512]{2,1,0:T(8,128)(2,1)S(1)} %collective-permute-done.18.refs_2_.refs_4_), channel_id=1, source_target_pairs={{0,1},{1,0},{2,3},{3,2},{4,5},{5,4},{6,7},{7,6},{8,9},{9,8},{10,11... | collective-permute-start | bytes 1572872 | tf_op jit(solution)/shard_map/ppermute | solution.py:26
  75.5 38.0 %collective-permute-start.15 = (bf16[4,128,512]{2,1,0:T(8,128)(2,1)S(1)}, bf16[4,128,512]{2,1,0:T(8,128)(2,1)S(1)}, u32[]{:S(2)}, u32[]{:S(2)}) collective-permute-start(bf16[4,128,512]{2,1,0:T(8,128)(2,1)S(1)} %collective-permute-done.13.refs_1_.refs_3_), channel_id=1, source_target_pairs={{0,1},{1,0},{2,3},{3,2},{4,5},{5,4},{6,7},{7,6},{8,9},{9,8},{10,11... | collective-permute-start | bytes 1572872 | tf_op jit(solution)/shard_map/ppermute | solution.py:26
  86.7 27.4 %collective-permute-start.5 = (bf16[4,128,512]{2,1,0:T(8,128)(2,1)S(1)}, bf16[4,128,512]{2,1,0:T(8,128)(2,1)S(1)}, u32[]{:S(2)}, u32[]{:S(2)}) collective-permute-start(bf16[4,128,512]{2,1,0:T(8,128)(2,1)S(1)} %collective-permute-done.3.refs_1_), channel_id=1, source_target_pairs={{0,1},{1,0},{2,3},{3,2},{4,5},{5,4},{6,7},{7,6},{8,9},{9,8},{10,11... | collective-permute-start | bytes 1572872 | tf_op jit(solution)/shard_map/ppermute | solution.py:26
  98.0 17.7 %collective-permute-start.10 = (bf16[4,128,512]{2,1,0:T(8,128)(2,1)S(1)}, bf16[4,128,512]{2,1,0:T(8,128)(2,1)S(1)}, u32[]{:S(2)}, u32[]{:S(2)}) collective-permute-start(bf16[4,128,512]{2,1,0:T(8,128)(2,1)S(1)} %collective-permute-done.8.refs_2_), channel_id=1, source_target_pairs={{0,1},{1,0},{2,3},{3,2},{4,5},{5,4},{6,7},{7,6},{8,9},{9,8},{10,11... | collective-permute-start | bytes 1572872 | tf_op jit(solution)/shard_map/ppermute | solution.py:26
  105.5 15.1 %collective-permute-start.16 = (bf16[4,128,512]{2,1,0:T(8,128)(2,1)S(1)}, bf16[4,128,512]{2,1,0:T(8,128)(2,1)S(1)}, u32[]{:S(2)}, u32[]{:S(2)}) collective-permute-start(bf16[4,128,512]{2,1,0:T(8,128)(2,1)S(1)} %collective-permute-done.14.refs_2_.refs_4_), channel_id=1, source_target_pairs={{0,1},{1,0},{2,3},{3,2},{4,5},{5,4},{6,7},{7,6},{8,9},{9,8},{10,11... | collective-permute-start | bytes 1572872 | tf_op jit(solution)/shard_map/ppermute | solution.py:26
  113.5 14.9 %collective-permute-start.1 = (bf16[4,128,512]{2,1,0:T(8,128)(2,1)S(1)}, bf16[4,128,512]{2,1,0:T(8,128)(2,1)S(1)}, u32[]{:S(2)}, u32[]{:S(2)}) collective-permute-start(bf16[4,128,512]{2,1,0:T(8,128)(2,1)S(1)} %get-tuple-element.64), channel_id=1, source_target_pairs={{0,4},{4,0},{8,12},{12,8},{16,20},{20,16},{24,28},{28,24},{1,5},{5... | collective-permute-start | bytes 1572872 | tf_op jit(solution)/shard_map/ppermute | solution.py:21
  114.1 25.5 %collective-permute-start.2 = (bf16[4,128,512]{2,1,0:T(8,128)(2,1)S(1)}, bf16[4,128,512]{2,1,0:T(8,128)(2,1)S(1)}, u32[]{:S(2)}, u32[]{:S(2)}) collective-permute-start(bf16[4,128,512]{2,1,0:T(8,128)(2,1)S(1)} %get-tuple-element.65), channel_id=1, source_target_pairs={{0,4},{4,0},{8,12},{12,8},{16,20},{20,16},{24,28},{28,24},{1,5},{5... | collective-permute-start | bytes 1572872 | tf_op jit(solution)/shard_map/ppermute | solution.py:21
  115.6 46.5 %collective-permute-start.24 = (bf16[4,128,512]{2,1,0:T(8,128)(2,1)S(1)}, bf16[4,128,512]{2,1,0:T(8,128)(2,1)S(1)}, u32[]{:S(2)}, u32[]{:S(2)}) collective-permute-start(bf16[4,128,512]{2,1,0:T(8,128)(2,1)S(1)} %get-tuple-element.73), channel_id=1, source_target_pairs={{0,4},{4,0},{8,12},{12,8},{16,20},{20,16},{24,28},{28,24},{1,5},{5... | collective-permute-start | bytes 1572872 | tf_op jit(solution)/shard_map/ppermute | solution.py:21
  117.6 55.7 %collective-permute-start.12 = (bf16[4,128,512]{2,1,0:T(8,128)(2,1)S(1)}, bf16[4,128,512]{2,1,0:T(8,128)(2,1)S(1)}, u32[]{:S(2)}, u32[]{:S(2)}) collective-permute-start(bf16[4,128,512]{2,1,0:T(8,128)(2,1)S(1)} %gather_held.11), channel_id=1, source_target_pairs={{0,4},{4,0},{8,12},{12,8},{16,20},{20,16},{24,28},{28,24},{1,5},{5... | collective-permute-start | bytes 1572872 | tf_op jit(solution)/shard_map/ppermute | solution.py:21
  120.6 63.9 %collective-permute-start.11 = (bf16[4,128,512]{2,1,0:T(8,128)(2,1)S(1)}, bf16[4,128,512]{2,1,0:T(8,128)(2,1)S(1)}, u32[]{:S(2)}, u32[]{:S(2)}) collective-permute-start(bf16[4,128,512]{2,1,0:T(8,128)(2,1)S(1)} %gather_held.10), channel_id=1, source_target_pairs={{0,4},{4,0},{8,12},{12,8},{16,20},{20,16},{24,28},{28,24},{1,5},{5... | collective-permute-start | bytes 1572872 | tf_op jit(solution)/shard_map/ppermute | solution.py:21
  128.4 74.3 %collective-permute-start.26 = (bf16[4,128,512]{2,1,0:T(8,128)(2,1)S(1)}, bf16[4,128,512]{2,1,0:T(8,128)(2,1)S(1)}, u32[]{:S(2)}, u32[]{:S(2)}) collective-permute-start(bf16[4,128,512]{2,1,0:T(8,128)(2,1)S(1)} %get-tuple-element.75), channel_id=1, source_target_pairs={{0,8},{4,12},{8,0},{12,4},{16,24},{20,28},{24,16},{28,20},{1,9},{5... | collective-permute-start | bytes 1572872 | tf_op jit(solution)/shard_map/ppermute | solution.py:21
  139.6 63.1 %collective-permute-start.28 = (bf16[4,128,512]{2,1,0:T(8,128)(2,1)S(1)}, bf16[4,128,512]{2,1,0:T(8,128)(2,1)S(1)}, u32[]{:S(2)}, u32[]{:S(2)}) collective-permute-start(bf16[4,128,512]{2,1,0:T(8,128)(2,1)S(1)} %get-tuple-element.77), channel_id=1, source_target_pairs={{0,12},{4,8},{8,4},{12,0},{16,28},{20,24},{24,20},{28,16},{1,13},{... | collective-permute-start | bytes 1572872 | tf_op jit(solution)/shard_map/ppermute | solution.py:21
  162.1 44.0 %collective-permute-start.23 = (bf16[4,128,512]{2,1,0:T(8,128)(2,1)S(1)}, bf16[4,128,512]{2,1,0:T(8,128)(2,1)S(1)}, u32[]{:S(2)}, u32[]{:S(2)}) collective-permute-start(bf16[4,128,512]{2,1,0:T(8,128)(2,1)S(1)} %get-tuple-element.72), channel_id=1, source_target_pairs={{0,4},{4,0},{8,12},{12,8},{16,20},{20,16},{24,28},{28,24},{1,5},{5... | collective-permute-start | bytes 1572872 | tf_op jit(solution)/shard_map/ppermute | solution.py:21
  173.3 32.7 %collective-permute-start.25 = (bf16[4,128,512]{2,1,0:T(8,128)(2,1)S(1)}, bf16[4,128,512]{2,1,0:T(8,128)(2,1)S(1)}, u32[]{:S(2)}, u32[]{:S(2)}) collective-permute-start(bf16[4,128,512]{2,1,0:T(8,128)(2,1)S(1)} %get-tuple-element.74), channel_id=1, source_target_pairs={{0,8},{4,12},{8,0},{12,4},{16,24},{20,28},{24,16},{28,20},{1,9},{5... | collective-permute-start | bytes 1572872 | tf_op jit(solution)/shard_map/ppermute | solution.py:21
  184.6 21.5 %collective-permute-start.27 = (bf16[4,128,512]{2,1,0:T(8,128)(2,1)S(1)}, bf16[4,128,512]{2,1,0:T(8,128)(2,1)S(1)}, u32[]{:S(2)}, u32[]{:S(2)}) collective-permute-start(bf16[4,128,512]{2,1,0:T(8,128)(2,1)S(1)} %get-tuple-element.76), channel_id=1, source_target_pairs={{0,12},{4,8},{8,4},{12,0},{16,28},{20,24},{24,20},{28,16},{1,13},{... | collective-permute-start | bytes 1572872 | tf_op jit(solution)/shard_map/ppermute | solution.py:21
  220.3 24.8 %collective-permute-start.32 = (bf16[512,512]{1,0:T(8,128)(2,1)}, bf16[512,512]{1,0:T(8,128)(2,1)S(1)}, u32[]{:S(2)}, u32[]{:S(2)}) collective-permute-start(bf16[512,512]{1,0:T(8,128)(2,1)} %get-tuple-element.98), channel_id=1, source_target_pairs={{0,4},{4,0},{8,12},{12,8},{16,20},{20,16},{24,28},{28,24},{1,5},{5... | collective-permute-start | bytes 1572872 | tf_op jit(solution)/shard_map/ppermute | solution.py:21
  221.0 29.3 %collective-permute-start.33 = (bf16[512,512]{1,0:T(8,128)(2,1)}, bf16[512,512]{1,0:T(8,128)(2,1)}, u32[]{:S(2)}, u32[]{:S(2)}) collective-permute-start(bf16[512,512]{1,0:T(8,128)(2,1)} %get-tuple-element.99), channel_id=1, source_target_pairs={{0,8},{4,12},{8,0},{12,4},{16,24},{20,28},{24,16},{28,20},{1,9},{5... | collective-permute-start | bytes 1572872 | tf_op jit(solution)/shard_map/ppermute | solution.py:21
  221.7 30.2 %collective-permute-start.34 = (bf16[512,512]{1,0:T(8,128)(2,1)}, bf16[512,512]{1,0:T(8,128)(2,1)}, u32[]{:S(2)}, u32[]{:S(2)}) collective-permute-start(bf16[512,512]{1,0:T(8,128)(2,1)} %get-tuple-element.100), channel_id=1, source_target_pairs={{0,12},{4,8},{8,4},{12,0},{16,28},{20,24},{24,20},{28,16},{1,13},{... | collective-permute-start | bytes 1572872 | tf_op jit(solution)/shard_map/ppermute | solution.py:21
  223.9 45.3 %collective-permute-start.45 = (bf16[512,512]{1,0:T(8,128)(2,1)}, bf16[512,512]{1,0:T(8,128)(2,1)}, u32[]{:S(2)}, u32[]{:S(2)}) collective-permute-start(bf16[512,512]{1,0:T(8,128)(2,1)} %get-tuple-element.112), channel_id=1, source_target_pairs={{0,4},{4,0},{8,12},{12,8},{16,20},{20,16},{24,28},{28,24},{1,5},{5... | collective-permute-start | bytes 1572872 | tf_op jit(solution)/shard_map/ppermute | solution.py:21
  224.4 45.3 %collective-permute-start.46 = (bf16[512,512]{1,0:T(8,128)(2,1)}, bf16[512,512]{1,0:T(8,128)(2,1)}, u32[]{:S(2)}, u32[]{:S(2)}) collective-permute-start(bf16[512,512]{1,0:T(8,128)(2,1)} %get-tuple-element.113), channel_id=1, source_target_pairs={{0,8},{4,12},{8,0},{12,4},{16,24},{20,28},{24,16},{28,20},{1,9},{5... | collective-permute-start | bytes 1572872 | tf_op jit(solution)/shard_map/ppermute | solution.py:21
  245.9 23.9 %collective-permute-start.47 = (bf16[512,512]{1,0:T(8,128)(2,1)}, bf16[512,512]{1,0:T(8,128)(2,1)}, u32[]{:S(2)}, u32[]{:S(2)}) collective-permute-start(bf16[512,512]{1,0:T(8,128)(2,1)} %get-tuple-element.114), channel_id=1, source_target_pairs={{0,12},{4,8},{8,4},{12,0},{16,28},{20,24},{24,20},{28,16},{1,13},{... | collective-permute-start | bytes 1572872 | tf_op jit(solution)/shard_map/ppermute | solution.py:21
  250.2 30.1 %collective-permute-start.42 = (bf16[512,512]{1,0:T(8,128)(2,1)S(1)}, bf16[512,512]{1,0:T(8,128)(2,1)S(1)}, u32[]{:S(2)}, u32[]{:S(2)}) collective-permute-start(bf16[512,512]{1,0:T(8,128)(2,1)S(1)} %get-tuple-element.108), channel_id=1, source_target_pairs={{0,4},{4,0},{8,12},{12,8},{16,20},{20,16},{24,28},{28,24},{1,5},{5... | collective-permute-start | bytes 1572872 | tf_op jit(solution)/shard_map/ppermute | solution.py:21
  254.5 59.3 %collective-permute-start.35 = (bf16[8,128,512]{2,1,0:T(8,128)(2,1)S(1)}, bf16[8,128,512]{2,1,0:T(8,128)(2,1)S(1)}, u32[]{:S(2)}, u32[]{:S(2)}) collective-permute-start(bf16[8,128,512]{2,1,0:T(8,128)(2,1)S(1)} %get-tuple-element.102), channel_id=1, source_target_pairs={{0,1},{1,0},{2,3},{3,2},{4,5},{5,4},{6,7},{7,6},{8,9},{9,8},{10,11... | collective-permute-start | bytes 3145736 | tf_op jit(solution)/shard_map/ppermute | solution.py:26
  269.2 22.4 %collective-permute-start.29 = (bf16[512,512]{1,0:T(8,128)(2,1)S(1)}, bf16[512,512]{1,0:T(8,128)(2,1)S(1)}, u32[]{:S(2)}, u32[]{:S(2)}) collective-permute-start(bf16[512,512]{1,0:T(8,128)(2,1)S(1)} %get-tuple-element.94), channel_id=1, source_target_pairs={{0,4},{4,0},{8,12},{12,8},{16,20},{20,16},{24,28},{28,24},{1,5},{5... | collective-permute-start | bytes 1572872 | tf_op jit(solution)/shard_map/ppermute | solution.py:21
  272.1 42.7 %collective-permute-start.48 = (bf16[8,128,512]{2,1,0:T(8,128)(2,1)S(1)}, bf16[8,128,512]{2,1,0:T(8,128)(2,1)S(1)}, u32[]{:S(2)}, u32[]{:S(2)}) collective-permute-start(bf16[8,128,512]{2,1,0:T(8,128)(2,1)S(1)} %get-tuple-element.116), channel_id=1, source_target_pairs={{0,1},{1,0},{2,3},{3,2},{4,5},{5,4},{6,7},{7,6},{8,9},{9,8},{10,11... | collective-permute-start | bytes 3145736 | tf_op jit(solution)/shard_map/ppermute | solution.py:26
  274.2 28.6 %collective-permute-start.51 = (bf16[512,512]{1,0:T(8,128)(2,1)S(1)}, bf16[512,512]{1,0:T(8,128)(2,1)S(1)}, u32[]{:S(2)}, u32[]{:S(2)}) collective-permute-start(bf16[512,512]{1,0:T(8,128)(2,1)S(1)} %get-tuple-element.118), channel_id=1, source_target_pairs={{0,4},{4,0},{8,12},{12,8},{16,20},{20,16},{24,28},{28,24},{1,5},{5... | collective-permute-start | bytes 1572872 | tf_op jit(solution)/shard_map/ppermute | solution.py:21
  280.3 31.9 %collective-permute-start.38 = (bf16[512,512]{1,0:T(8,128)(2,1)S(1)}, bf16[512,512]{1,0:T(8,128)(2,1)S(1)}, u32[]{:S(2)}, u32[]{:S(2)}) collective-permute-start(bf16[512,512]{1,0:T(8,128)(2,1)S(1)} %get-tuple-element.104), channel_id=1, source_target_pairs={{0,4},{4,0},{8,12},{12,8},{16,20},{20,16},{24,28},{28,24},{1,5},{5... | collective-permute-start | bytes 1572872 | tf_op jit(solution)/shard_map/ppermute | solution.py:21
  291.6 25.3 %collective-permute-start.43 = (bf16[8,128,512]{2,1,0:T(8,128)(2,1)S(1)}, bf16[8,128,512]{2,1,0:T(8,128)(2,1)S(1)}, u32[]{:S(2)}, u32[]{:S(2)}) collective-permute-start(bf16[8,128,512]{2,1,0:T(8,128)(2,1)S(1)} %get-tuple-element.110), channel_id=1, source_target_pairs={{0,1},{1,0},{2,3},{3,2},{4,5},{5,4},{6,7},{7,6},{8,9},{9,8},{10,11... | collective-permute-start | bytes 3145736 | tf_op jit(solution)/shard_map/ppermute | solution.py:26
  302.8 15.1 %collective-permute-start.30 = (bf16[8,128,512]{2,1,0:T(8,128)(2,1)S(1)}, bf16[8,128,512]{2,1,0:T(8,128)(2,1)S(1)}, u32[]{:S(2)}, u32[]{:S(2)}) collective-permute-start(bf16[8,128,512]{2,1,0:T(8,128)(2,1)S(1)} %get-tuple-element.96), channel_id=1, source_target_pairs={{0,1},{1,0},{2,3},{3,2},{4,5},{5,4},{6,7},{7,6},{8,9},{9,8},{10,11... | collective-permute-start | bytes 3145736 | tf_op jit(solution)/shard_map/ppermute | solution.py:26
  314.8 60.5 %collective-permute-start.36 = (bf16[4,128,512]{2,1,0:T(8,128)(2,1)S(1)}, bf16[4,128,512]{2,1,0:T(8,128)(2,1)S(1)}, u32[]{:S(2)}, u32[]{:S(2)}) collective-permute-start(bf16[4,128,512]{2,1,0:T(8,128)(2,1)S(1)} %slice.135), channel_id=1, source_target_pairs={{0,2},{1,3},{2,0},{3,1},{4,6},{5,7},{6,4},{7,5},{8,10},{9,11},{10,... | collective-permute-start | bytes 1572872 | tf_op jit(solution)/shard_map/ppermute | solution.py:26
  316.9 24.0 %collective-permute-start.49 = (bf16[4,128,512]{2,1,0:T(8,128)(2,1)S(1)}, bf16[4,128,512]{2,1,0:T(8,128)(2,1)S(1)}, u32[]{:S(2)}, u32[]{:S(2)}) collective-permute-start(bf16[4,128,512]{2,1,0:T(8,128)(2,1)S(1)} %slice.132), channel_id=1, source_target_pairs={{0,2},{1,3},{2,0},{3,1},{4,6},{5,7},{6,4},{7,5},{8,10},{9,11},{10,... | collective-permute-start | bytes 1572872 | tf_op jit(solution)/shard_map/ppermute | solution.py:26
  317.9 67.7 %collective-permute-start.44 = (bf16[4,128,512]{2,1,0:T(8,128)(2,1)S(1)}, bf16[4,128,512]{2,1,0:T(8,128)(2,1)S(1)}, u32[]{:S(2)}, u32[]{:S(2)}) collective-permute-start(bf16[4,128,512]{2,1,0:T(8,128)(2,1)S(1)} %slice.133), channel_id=1, source_target_pairs={{0,2},{1,3},{2,0},{3,1},{4,6},{5,7},{6,4},{7,5},{8,10},{9,11},{10,... | collective-permute-start | bytes 1572872 | tf_op jit(solution)/shard_map/ppermute | solution.py:26
  320.0 82.1 %collective-permute-start.31 = (bf16[4,128,512]{2,1,0:T(8,128)(2,1)S(1)}, bf16[4,128,512]{2,1,0:T(8,128)(2,1)S(1)}, u32[]{:S(2)}, u32[]{:S(2)}) collective-permute-start(bf16[4,128,512]{2,1,0:T(8,128)(2,1)S(1)} %slice.136), channel_id=1, source_target_pairs={{0,2},{1,3},{2,0},{3,1},{4,6},{5,7},{6,4},{7,5},{8,10},{9,11},{10,... | collective-permute-start | bytes 1572872 | tf_op jit(solution)/shard_map/ppermute | solution.py:26
  321.0 53.6 %collective-permute-start.53 = (bf16[4,128,512]{2,1,0:T(8,128)(2,1)S(1)}, bf16[4,128,512]{2,1,0:T(8,128)(2,1)S(1)}, u32[]{:S(2)}, u32[]{:S(2)}) collective-permute-start(bf16[4,128,512]{2,1,0:T(8,128)(2,1)S(1)} %slice.131), channel_id=1, source_target_pairs={{0,2},{1,3},{2,0},{3,1},{4,6},{5,7},{6,4},{7,5},{8,10},{9,11},{10,... | collective-permute-start | bytes 1572872 | tf_op jit(solution)/shard_map/ppermute | solution.py:26
  340.9 44.0 %collective-permute-start.40 = (bf16[4,128,512]{2,1,0:T(8,128)(2,1)S(1)}, bf16[4,128,512]{2,1,0:T(8,128)(2,1)S(1)}, u32[]{:S(2)}, u32[]{:S(2)}) collective-permute-start(bf16[4,128,512]{2,1,0:T(8,128)(2,1)S(1)} %slice.134), channel_id=1, source_target_pairs={{0,2},{1,3},{2,0},{3,1},{4,6},{5,7},{6,4},{7,5},{8,10},{9,11},{10,... | collective-permute-start | bytes 1572872 | tf_op jit(solution)/shard_map/ppermute | solution.py:26
  374.6 27.2 %collective-permute-start.50 = (bf16[4,128,512]{2,1,0:T(8,128)(2,1)S(1)}, bf16[4,128,512]{2,1,0:T(8,128)(2,1)S(1)}, u32[]{:S(2)}, u32[]{:S(2)}) collective-permute-start(bf16[4,128,512]{2,1,0:T(8,128)(2,1)S(1)} %fusion.1), channel_id=1, source_target_pairs={{0,16},{4,20},{8,24},{12,28},{16,0},{20,4},{24,8},{28,12},{1,17},{... | collective-permute-start | bytes 1572872 | tf_op jit(solution)/shard_map/ppermute | solution.py:21
  375.4 26.5 %collective-permute-start.54 = (bf16[4,128,512]{2,1,0:T(8,128)(2,1)S(1)}, bf16[4,128,512]{2,1,0:T(8,128)(2,1)S(1)}, u32[]{:S(2)}, u32[]{:S(2)}) collective-permute-start(bf16[4,128,512]{2,1,0:T(8,128)(2,1)S(1)} %fusion), channel_id=1, source_target_pairs={{0,8},{4,12},{8,0},{12,4},{16,24},{20,28},{24,16},{28,20},{1,9},{5... | collective-permute-start | bytes 1572872 | tf_op jit(solution)/shard_map/ppermute | solution.py:21
  384.9 36.4 %collective-permute-start.37 = (bf16[4,128,512]{2,1,0:T(8,128)(2,1)S(1)}, bf16[4,128,512]{2,1,0:T(8,128)(2,1)S(1)}, u32[]{:S(2)}, u32[]{:S(2)}) collective-permute-start(bf16[4,128,512]{2,1,0:T(8,128)(2,1)S(1)} %fusion.5), channel_id=1, source_target_pairs={{0,16},{4,20},{8,24},{12,28},{16,0},{20,4},{24,8},{28,12},{1,17},{... | collective-permute-start | bytes 1572872 | tf_op jit(solution)/shard_map/ppermute | solution.py:21
  385.6 35.7 %collective-permute-start.41 = (bf16[4,128,512]{2,1,0:T(8,128)(2,1)S(1)}, bf16[4,128,512]{2,1,0:T(8,128)(2,1)S(1)}, u32[]{:S(2)}, u32[]{:S(2)}) collective-permute-start(bf16[4,128,512]{2,1,0:T(8,128)(2,1)S(1)} %fusion.4), channel_id=1, source_target_pairs={{0,8},{4,12},{8,0},{12,4},{16,24},{20,28},{24,16},{28,20},{1,9},{5... | collective-permute-start | bytes 1572872 | tf_op jit(solution)/shard_map/ppermute | solution.py:21
  (57 other events, 898.8 us)

commit v3 on v2

--- a/solution.py
+++ b/solution.py
@@ -268,18 +268,15 @@
             target = jnp.where(rel == base[n], 1.0, 0.0)
             grads[s, k * TILE : (k + 1) * TILE, at] = (ref[...] * inv - target).astype(BF)
     step = width // parts
-    sources = [grads.at[s] for s in range(group)]
-    sources += [tiles.at[n] for n in range(parts * group)]
-    copies = [pltpu.make_async_copy(a, b, sems.at[n]) for n, (a, b) in enumerate(zip(sources, kept))]
+    sources = [grads.at[s] for s in range(group)] + [tiles.at[s] for s in range(group)]
+    copies = [
+        pltpu.make_async_copy(a, b, sems.at[n]) for n, (a, b) in enumerate(zip(sources, kept))
+    ]
     for copy in copies[:group]:
         copy.start()
-    for i in range(parts):
-        for s in range(group):
-            n = i * group + s
-            tiles[n] = jnp.dot(
-                grads[s], x[:, i * step : (i + 1) * step], preferred_element_type=F32
-            ).astype(BF)
-            copies[group + n].start()
+    for s in reversed(range(group)):
+        tiles[s] = jnp.dot(grads[s], x[:, :step], preferred_element_type=F32).astype(BF)
+        copies[group + s].start()
     for copy in copies:
         copy.wait()
 
@@ -290,7 +287,7 @@
     count, width = x.shape
     size = rows[0].shape[0]
     outs = [((1, count), F32)] * 3 + [((size, count), BF)] * group
-    outs += [((size, width // parts), BF)] * (group * parts)
+    outs += [((size, width // parts), BF)] * group
     got = pl.pallas_call(
         functools.partial(far_kernel, group, cap, lanes, parts, len(stats) // 3),
         out_shape=[jax.ShapeDtypeStruct(*o) for o in outs[:3]]
@@ -300,14 +297,37 @@
         scratch_shapes=[
             pltpu.VMEM((2, group * size, lanes), F32),
             pltpu.VMEM((group, size, count), BF),
-            pltpu.VMEM((group * parts, size, width // parts), BF),
-            pltpu.SemaphoreType.DMA((group * (1 + parts),)),
+            pltpu.VMEM((group, size, width // parts), BF),
+            pltpu.SemaphoreType.DMA((2 * group,)),
         ],
         compiler_params=grant(20),
         name="far_grads",
     )(base, x, pos, *stats, *rows)
-    tiles = got[3 + group :]
-    return got[:3], got[3 : 3 + group], [tiles[i * group : (i + 1) * group] for i in range(parts)]
+    return got[:3], got[3 : 3 + group], got[3 + group :]
+
+
+def far_tiles_kernel(group, first, x, *refs):
+    grads, tiles = refs[:group], refs[group:]
+    step = tiles[0].shape[1]
+    for n, tile in enumerate(tiles):
+        i = first + n // group
+        tile[...] = jnp.dot(
+            grads[n % group][...], x[:, i * step : (i + 1) * step], preferred_element_type=F32
+        ).astype(BF)
+
+
+def far_tiles(x, grads, parts):
+    group = len(grads)
+    shape = (grads[0].shape[0], x.shape[1] // parts)
+    got = pl.pallas_call(
+        functools.partial(far_tiles_kernel, group, 1),
+        out_shape=[jax.ShapeDtypeStruct(shape, BF)] * (group * (parts - 1)),
+        in_specs=[VM] * (1 + group),
+        out_specs=[VM] * (group * (parts - 1)),
+        compiler_params=grant(6),
+        name="far_tiles",
+    )(x, *grads)
+    return [got[i : i + group] for i in range(0, len(got), group)]
 
 
 def own_grad_kernel(cap, parts, base, x, pos, top, inv, logits, grad, *tiles):
@@ -491,9 +511,10 @@
         )
         logits.update(zip(group, got))
         sums += [top, total, hit]
-    stats, far_g, far_tiles = far_grads(
+    stats, far_g, first = far_grads(
         bases(other, 1 - h, range(half)), designs, pos, sums, far_rows, cap, parts
     )
+    back_tiles = [first] + far_tiles(designs, far_g, parts)
     losses, top, inv = stats
     own_g, own_tiles = [], []
     for s in range(half):
@@ -526,8 +547,8 @@
     dgrad = []
     far_tables = [asking[s] for s in range(half)]
     for i in range(parts):
-        tiles = [far_tiles[i][0]]
-        tiles += [xor_proto(far_tiles[i][s], s) for s in range(1, half)]
+        tiles = [back_tiles[i][0]]
+        tiles += [xor_proto(back_tiles[i][s], s) for s in range(1, half)]
         total = reduce_shard(far_tables, tiles)
         landed = [xor_proto(total.astype(BF), half)]
         for u in evens:

time: 423 us -> 422 us (level)
  waiting for transfers between devices: 290 us -> 282 us
  local copies, waits for them, and re-layouts: 8.29 us -> 14 us
    ppermute x31, waiting for transfers between devices: 192 us -> 184 us  [xor_proto(): return lax.ppermute(x, 'proto', [(i, i ^ shift) for i in range(count)])]
    unnamed x100 -> x110, local copies, waits for them, and re-layouts: 5.96 us -> 11.7 us
  transfers between devices with their start and end apart: 55 -> 55, of which waited for: 24 -> 26; matrix products, arithmetic and copies ran while one was open for 1% -> 1% of each run, Pallas kernels for 13% -> 14%
where the time goes in v3:
time: 422 us; the launch traced here: 421 us
  waiting for transfers between devices  282 us (67%)
  Pallas kernels  71.3 us (17%)
  starting transfers between devices  45.1 us (11%)
  local copies, waits for them, and re-layouts  14 us (3%)
  other arithmetic  7.23 us (2%)
    ppermute x31, waiting for transfers between devices, xor_proto(): return lax.ppermute(x, 'proto', [(i, i ^ shift) for i in range(count)])  184 us
    ppermute x24, waiting for transfers between devices, xor_design(): return lax.ppermute(x, 'design', [(i, i ^ shift) for i in range(count)])  98 us
    ppermute x31, starting transfers between devices, xor_proto(): return lax.ppermute(x, 'proto', [(i, i ^ shift) for i in range(count)])  31.8 us
    pallas_call x8, Pallas kernels, gather_held(): pl.pallas_call(functools.partial(gather_held_kernel, len(srcs), n, quarte...  15.1 us
    ppermute x24, starting transfers between devices, xor_design(): return lax.ppermute(x, 'design', [(i, i ^ shift) for i in range(count)])  13.3 us
    pallas_call x1, Pallas kernels, far_grads(): pl.pallas_call(functools.partial(far_kernel, group, cap, lanes, parts, le...  12.5 us
    unnamed x110, local copies, waits for them, and re-layouts  11.7 us
    pallas_call x2, Pallas kernels, own_logits(): pl.pallas_call(functools.partial(own_kernel, group, cap, lanes, parts), o...  10.5 us
  transfers between devices with their start and end apart: 55, of which 26 were waited for; matrix products, arithmetic and copies ran while one was open for 1% of the time, Pallas kernels for 14%

profile of v3, /device:TPU:0, one launch (start us, length us, event | category | flops | bytes accessed | tf_op | source)
XLA Modules:
  0.0 421.3 jit_solution(14011520155101566707)
XLA Ops:
  0.6 1.7 dynamic-slice_convert_fusion
  2.5 4.1 collective-permute-start.17
  9.2 2.8 collective-permute-start.21
  12.0 41.5 %collective-permute-done.21.refs_0_ = s32[4]{0:T(128)S(1)} collective-permute-done((s32[4]{0:T(128)S(1)}, s32[4]{0:T(128)S(1)}, u32[]{:S(2)}, u32[]{:S(2)}) %collective-permute-start.21) | collective-permute-done | bytes 48 | tf_op jit(solution)/shard_map/ppermute | solution.py:21
  55.0 2.1 collective-permute-done.22.refs_1_
  57.6 3.1 collective-permute-done
  64.8 10.6 %collective-permute-done.18.refs_2_.refs_4_ = bf16[4,128,512]{2,1,0:T(8,128)(2,1)S(1)} collective-permute-done((bf16[4,128,512]{2,1,0:T(8,128)(2,1)S(1)}, bf16[4,128,512]{2,1,0:T(8,128)(2,1)S(1)}, u32[]{:S(2)}, u32[]{:S(2)}) %collective-permute-start.18) | collective-permute-done | bytes 524320 | tf_op jit(solution)/shard_map/ppermute | solution.py:26
  76.0 10.7 %collective-permute-done.8.refs_2_ = bf16[4,128,512]{2,1,0:T(8,128)(2,1)S(1)} collective-permute-done((bf16[4,128,512]{2,1,0:T(8,128)(2,1)S(1)}, bf16[4,128,512]{2,1,0:T(8,128)(2,1)S(1)}, u32[]{:S(2)}, u32[]{:S(2)}) %collective-permute-start.8) | collective-permute-done | bytes 524320 | tf_op jit(solution)/shard_map/ppermute | solution.py:26
  86.7 11.2 %collective-permute-done.14.refs_2_.refs_4_ = bf16[4,128,512]{2,1,0:T(8,128)(2,1)S(1)} collective-permute-done((bf16[4,128,512]{2,1,0:T(8,128)(2,1)S(1)}, bf16[4,128,512]{2,1,0:T(8,128)(2,1)S(1)}, u32[]{:S(2)}, u32[]{:S(2)}) %collective-permute-start.14) | collective-permute-done | bytes 524320 | tf_op jit(solution)/shard_map/ppermute | solution.py:26
  98.0 7.5 %collective-permute-done.4.refs_2_ = bf16[4,128,512]{2,1,0:T(8,128)(2,1)S(1)} collective-permute-done((bf16[4,128,512]{2,1,0:T(8,128)(2,1)S(1)}, bf16[4,128,512]{2,1,0:T(8,128)(2,1)S(1)}, u32[]{:S(2)}, u32[]{:S(2)}) %collective-permute-start.4) | collective-permute-done | bytes 524320 | tf_op jit(solution)/shard_map/ppermute | solution.py:26
  106.0 3.4 copy-done.1
  110.3 3.2 gather_held.15
  121.2 3.2 gather_held.14
  124.5 3.9 collective-permute-done.1
  129.1 10.5 %collective-permute-done.2 = bf16[4,128,512]{2,1,0:T(8,128)(2,1)S(1)} collective-permute-done((bf16[4,128,512]{2,1,0:T(8,128)(2,1)S(1)}, bf16[4,128,512]{2,1,0:T(8,128)(2,1)S(1)}, u32[]{:S(2)}, u32[]{:S(2)}) %collective-permute-start.2) | collective-permute-done | bytes 524320 | tf_op jit(solution)/shard_map/ppermute | solution.py:21
  140.3 21.8 %collective-permute-done.24 = bf16[4,128,512]{2,1,0:T(8,128)(2,1)S(1)} collective-permute-done((bf16[4,128,512]{2,1,0:T(8,128)(2,1)S(1)}, bf16[4,128,512]{2,1,0:T(8,128)(2,1)S(1)}, u32[]{:S(2)}, u32[]{:S(2)}) %collective-permute-start.24) | collective-permute-done | bytes 524320 | tf_op jit(solution)/shard_map/ppermute | solution.py:21
  162.6 10.7 %collective-permute-done.12 = bf16[4,128,512]{2,1,0:T(8,128)(2,1)S(1)} collective-permute-done((bf16[4,128,512]{2,1,0:T(8,128)(2,1)S(1)}, bf16[4,128,512]{2,1,0:T(8,128)(2,1)S(1)}, u32[]{:S(2)}, u32[]{:S(2)}) %collective-permute-start.12) | collective-permute-done | bytes 524320 | tf_op jit(solution)/shard_map/ppermute | solution.py:21
  174.1 10.5 %collective-permute-done.11 = bf16[4,128,512]{2,1,0:T(8,128)(2,1)S(1)} collective-permute-done((bf16[4,128,512]{2,1,0:T(8,128)(2,1)S(1)}, bf16[4,128,512]{2,1,0:T(8,128)(2,1)S(1)}, u32[]{:S(2)}, u32[]{:S(2)}) %collective-permute-start.11) | collective-permute-done | bytes 524320 | tf_op jit(solution)/shard_map/ppermute | solution.py:21
  189.3 6.8 %own_logits.2 = (f32[512,1024]{1,0:T(8,128)}, f32[512,1024]{1,0:T(8,128)}, f32[512,1024]{1,0:T(8,128)}, f32[1,1024]{1,0:T(1,128)S(1)}, f32[1,1024]{1,0:T(1,128)S(1)}, /*index=5*/f32[1,1024]{1,0:T(1,128)S(1)}) custom-call(s32[12]{0:T(128)S(1)} %pad_add_fusion.2.base, bf16[1024,1024]{1,0:T(8,128)(2,1)S(1)} %copy-done, s32[1,1024]{1,0:T(1,128)S(1)} %bitcast.106, ...), custom_call_target="tpu_custom_call" | custom-call | tf_op jit(solution)/shard_map/own_logits/pallas_call | solution.py:213
  199.1 3.6 own_logits.3
  202.7 3.3 collective-permute-done.23
  206.1 12.5 %far_grads.1 = (f32[1,1024]{1,0:T(1,128)}, f32[1,1024]{1,0:T(1,128)S(1)}, f32[1,1024]{1,0:T(1,128)S(1)}, bf16[512,1024]{1,0:T(8,128)(2,1)}, bf16[512,1024]{1,0:T...) custom-call(s32[16]{0:T(128)S(1)} %pad_add_fusion.1.base, ...), custom_call_target="tpu_custom_call" | custom-call | tf_op jit(solution)/shard_map/far_grads/pallas_call | solution.py:291
  220.0 2.2 collective-permute-start.34
  227.1 3.1 far_tiles.1
  235.3 1.6 copy-done.23
  236.9 1.9 own_grad.5
  240.2 6.4 %collective-permute-done.34.refs_3_ = bf16[512,512]{1,0:T(8,128)(2,1)} collective-permute-done((bf16[512,512]{1,0:T(8,128)(2,1)}, bf16[512,512]{1,0:T(8,128)(2,1)}, u32[]{:S(2)}, u32[]{:S(2)}) %collective-permute-start.34) | collective-permute-done | bytes 524320 | tf_op jit(solution)/shard_map/ppermute | solution.py:21
  246.6 2.5 collect.7
  249.2 8.2 %collective-permute-done.45.refs_1_ = bf16[512,512]{1,0:T(8,128)(2,1)} collective-permute-done((bf16[512,512]{1,0:T(8,128)(2,1)}, bf16[512,512]{1,0:T(8,128)(2,1)}, u32[]{:S(2)}, u32[]{:S(2)}) %collective-permute-start.45) | collective-permute-done | bytes 524320 | tf_op jit(solution)/shard_map/ppermute | solution.py:21
  257.9 9.1 %collective-permute-done.47.refs_3_ = bf16[512,512]{1,0:T(8,128)(2,1)} collective-permute-done((bf16[512,512]{1,0:T(8,128)(2,1)}, bf16[512,512]{1,0:T(8,128)(2,1)}, u32[]{:S(2)}, u32[]{:S(2)}) %collective-permute-start.47) | collective-permute-done | bytes 524320 | tf_op jit(solution)/shard_map/ppermute | solution.py:21
  267.0 2.3 collect.10
  269.5 2.0 own_grad.7
  272.0 5.9 %collective-permute-done.42.refs_1_ = bf16[512,512]{1,0:T(8,128)(2,1)S(1)} collective-permute-done((bf16[512,512]{1,0:T(8,128)(2,1)S(1)}, bf16[512,512]{1,0:T(8,128)(2,1)S(1)}, u32[]{:S(2)}, u32[]{:S(2)}) %collective-permute-start.42) | collective-permute-done | bytes 524320 | tf_op jit(solution)/shard_map/ppermute | solution.py:21
  278.5 1.9 own_grad.4
  281.7 7.3 %collective-permute-done.29.refs_1_ = bf16[512,512]{1,0:T(8,128)(2,1)S(1)} collective-permute-done((bf16[512,512]{1,0:T(8,128)(2,1)S(1)}, bf16[512,512]{1,0:T(8,128)(2,1)S(1)}, u32[]{:S(2)}, u32[]{:S(2)}) %collective-permute-start.29) | collective-permute-done | bytes 524320 | tf_op jit(solution)/shard_map/ppermute | solution.py:21
  289.2 2.0 own_grad.6
  292.4 7.9 %collective-permute-done.51.refs_1_ = bf16[512,512]{1,0:T(8,128)(2,1)S(1)} collective-permute-done((bf16[512,512]{1,0:T(8,128)(2,1)S(1)}, bf16[512,512]{1,0:T(8,128)(2,1)S(1)}, u32[]{:S(2)}, u32[]{:S(2)}) %collective-permute-start.51) | collective-permute-done | bytes 524320 | tf_op jit(solution)/shard_map/ppermute | solution.py:21
  301.6 9.0 %collective-permute-done.38.refs_1_ = bf16[512,512]{1,0:T(8,128)(2,1)S(1)} collective-permute-done((bf16[512,512]{1,0:T(8,128)(2,1)S(1)}, bf16[512,512]{1,0:T(8,128)(2,1)S(1)}, u32[]{:S(2)}, u32[]{:S(2)}) %collective-permute-start.38) | collective-permute-done | bytes 524320 | tf_op jit(solution)/shard_map/ppermute | solution.py:21
  313.1 1.6 collective-permute-start.36
  319.2 1.6 collective-permute-start.53
  321.2 17.9 %collective-permute-done.49 = bf16[4,128,512]{2,1,0:T(8,128)(2,1)S(1)} collective-permute-done((bf16[4,128,512]{2,1,0:T(8,128)(2,1)S(1)}, bf16[4,128,512]{2,1,0:T(8,128)(2,1)S(1)}, u32[]{:S(2)}, u32[]{:S(2)}) %collective-permute-start.49) | collective-permute-done | bytes 524320 | tf_op jit(solution)/shard_map/ppermute | solution.py:26
  340.9 32.0 %collective-permute-done.53 = bf16[4,128,512]{2,1,0:T(8,128)(2,1)S(1)} collective-permute-done((bf16[4,128,512]{2,1,0:T(8,128)(2,1)S(1)}, bf16[4,128,512]{2,1,0:T(8,128)(2,1)S(1)}, u32[]{:S(2)}, u32[]{:S(2)}) %collective-permute-start.53) | collective-permute-done | bytes 524320 | tf_op jit(solution)/shard_map/ppermute | solution.py:26
  375.3 7.9 %collective-permute-done.40 = bf16[4,128,512]{2,1,0:T(8,128)(2,1)S(1)} collective-permute-done((bf16[4,128,512]{2,1,0:T(8,128)(2,1)S(1)}, bf16[4,128,512]{2,1,0:T(8,128)(2,1)S(1)}, u32[]{:S(2)}, u32[]{:S(2)}) %collective-permute-start.40) | collective-permute-done | bytes 524320 | tf_op jit(solution)/shard_map/ppermute | solution.py:26
  385.5 5.2 %design_grad.3 = bf16[1024,512]{1,0:T(8,128)(2,1)S(1)} custom-call(bf16[512,1024]{1,0:T(8,128)(2,1)S(1)} %get-tuple-element.82.refs_0_, bf16[512,1024]{1,0:T(8,128)(2,1)S(1)} %get-tuple-element.84.refs_1_, bf16[512,1024]{1,0:T(8,128)(2,1)S(1)} %get-tuple-element.86.refs_2_, bf16[512,1024]{1,0:T(8,128)(2,1)S(1)} %get-tuple-element.88.refs_3_, ...), custom_call_target="tpu_custom_call" | custom-call | tf_op jit(solution)/shard_map/design_grad/pallas_call | solution.py:380
  390.8 5.2 %design_grad.2 = bf16[1024,512]{1,0:T(8,128)(2,1)S(1)} custom-call(bf16[512,1024]{1,0:T(8,128)(2,1)S(1)} %get-tuple-element.82.refs_0_, bf16[512,1024]{1,0:T(8,128)(2,1)S(1)} %get-tuple-element.84.refs_1_, bf16[512,1024]{1,0:T(8,128)(2,1)S(1)} %get-tuple-element.86.refs_2_, bf16[512,1024]{1,0:T(8,128)(2,1)S(1)} %get-tuple-element.88.refs_3_, ...), custom_call_target="tpu_custom_call" | custom-call | tf_op jit(solution)/shard_map/design_grad/pallas_call | solution.py:380
  396.0 1.6 pad_maximum_fusion
  397.7 2.4 collective-permute-done.50
  400.4 19.2 %collective-permute-done.37 = bf16[4,128,512]{2,1,0:T(8,128)(2,1)S(1)} collective-permute-done((bf16[4,128,512]{2,1,0:T(8,128)(2,1)S(1)}, bf16[4,128,512]{2,1,0:T(8,128)(2,1)S(1)}, u32[]{:S(2)}, u32[]{:S(2)}) %collective-permute-start.37) | collective-permute-done | bytes 524320 | tf_op jit(solution)/shard_map/ppermute | solution.py:21
  (236 shorter events, 62.5 us)
Async XLA Ops:
  2.5 52.5 %collective-permute-start.17 = (bf16[4,128,512]{2,1,0:T(8,128)(2,1)S(1)}, bf16[4,128,512]{2,1,0:T(8,128)(2,1)S(1)}, u32[]{:S(2)}, u32[]{:S(2)}) collective-permute-start(bf16[4,128,512]{2,1,0:T(8,128)(2,1)S(1)} %get-tuple-element.131), channel_id=1, source_target_pairs={{0,16},{4,20},{8,24},{12,28},{16,0},{20,4},{24,8},{28,12},{1,17},{... | collective-permute-start | bytes 1572872 | tf_op jit(solution)/shard_map/ppermute | solution.py:21
  6.6 55.6 %collective-permute-start.7 = (bf16[4,128,512]{2,1,0:T(8,128)(2,1)S(1)}, bf16[4,128,512]{2,1,0:T(8,128)(2,1)S(1)}, u32[]{:S(2)}, u32[]{:S(2)}) collective-permute-start(bf16[4,128,512]{2,1,0:T(8,128)(2,1)S(1)} %get-tuple-element.131), channel_id=1, source_target_pairs={{0,8},{4,12},{8,0},{12,4},{16,24},{20,28},{24,16},{28,20},{1,9},{5... | collective-permute-start | bytes 1572872 | tf_op jit(solution)/shard_map/ppermute | solution.py:21
  8.2 54.0 %collective-permute-start.13 = (bf16[4,128,512]{2,1,0:T(8,128)(2,1)S(1)}, bf16[4,128,512]{2,1,0:T(8,128)(2,1)S(1)}, u32[]{:S(2)}, u32[]{:S(2)}) collective-permute-start(bf16[4,128,512]{2,1,0:T(8,128)(2,1)S(1)} %get-tuple-element.132), channel_id=1, source_target_pairs={{0,16},{4,20},{8,24},{12,28},{16,0},{20,4},{24,8},{28,12},{1,17},{... | collective-permute-start | bytes 1572872 | tf_op jit(solution)/shard_map/ppermute | solution.py:21
  8.5 54.3 %collective-permute-start.3 = (bf16[4,128,512]{2,1,0:T(8,128)(2,1)S(1)}, bf16[4,128,512]{2,1,0:T(8,128)(2,1)S(1)}, u32[]{:S(2)}, u32[]{:S(2)}) collective-permute-start(bf16[4,128,512]{2,1,0:T(8,128)(2,1)S(1)} %get-tuple-element.132), channel_id=1, source_target_pairs={{0,8},{4,12},{8,0},{12,4},{16,24},{20,28},{24,16},{28,20},{1,9},{5... | collective-permute-start | bytes 1572872 | tf_op jit(solution)/shard_map/ppermute | solution.py:21
  9.2 44.4 %collective-permute-start.21 = (s32[4]{0:T(128)S(1)}, s32[4]{0:T(128)S(1)}, u32[]{:S(2)}, u32[]{:S(2)}) collective-permute-start(s32[4]{0:T(128)S(1)} %get-tuple-element.142), channel_id=1, source_target_pairs={{0,12},{4,8},{8,4},{12,0},{16,28},{20,24},{24,20},{28,16},{1,13},{... | collective-permute-start | bytes 56 | tf_op jit(solution)/shard_map/ppermute | solution.py:21
  60.7 14.8 %collective-permute-start.18 = (bf16[4,128,512]{2,1,0:T(8,128)(2,1)S(1)}, bf16[4,128,512]{2,1,0:T(8,128)(2,1)S(1)}, u32[]{:S(2)}, u32[]{:S(2)}) collective-permute-start(bf16[4,128,512]{2,1,0:T(8,128)(2,1)S(1)} %collective-permute-done.17.refs_1_.refs_3_), channel_id=1, source_target_pairs={{0,2},{1,3},{2,0},{3,1},{4,6},{5,7},{6,4},{7,5},{8,10},{9,11},{10,... | collective-permute-start | bytes 1572872 | tf_op jit(solution)/shard_map/ppermute | solution.py:26
  62.2 24.5 %collective-permute-start.8 = (bf16[4,128,512]{2,1,0:T(8,128)(2,1)S(1)}, bf16[4,128,512]{2,1,0:T(8,128)(2,1)S(1)}, u32[]{:S(2)}, u32[]{:S(2)}) collective-permute-start(bf16[4,128,512]{2,1,0:T(8,128)(2,1)S(1)} %collective-permute-done.7.refs_1_), channel_id=1, source_target_pairs={{0,2},{1,3},{2,0},{3,1},{4,6},{5,7},{6,4},{7,5},{8,10},{9,11},{10,... | collective-permute-start | bytes 1572872 | tf_op jit(solution)/shard_map/ppermute | solution.py:26
  62.8 35.1 %collective-permute-start.14 = (bf16[4,128,512]{2,1,0:T(8,128)(2,1)S(1)}, bf16[4,128,512]{2,1,0:T(8,128)(2,1)S(1)}, u32[]{:S(2)}, u32[]{:S(2)}) collective-permute-start(bf16[4,128,512]{2,1,0:T(8,128)(2,1)S(1)} %collective-permute-done.13.refs_1_.refs_3_), channel_id=1, source_target_pairs={{0,2},{1,3},{2,0},{3,1},{4,6},{5,7},{6,4},{7,5},{8,10},{9,11},{10,... | collective-permute-start | bytes 1572872 | tf_op jit(solution)/shard_map/ppermute | solution.py:26
  64.3 41.2 %collective-permute-start.4 = (bf16[4,128,512]{2,1,0:T(8,128)(2,1)S(1)}, bf16[4,128,512]{2,1,0:T(8,128)(2,1)S(1)}, u32[]{:S(2)}, u32[]{:S(2)}) collective-permute-start(bf16[4,128,512]{2,1,0:T(8,128)(2,1)S(1)} %collective-permute-done.3.refs_1_), channel_id=1, source_target_pairs={{0,2},{1,3},{2,0},{3,1},{4,6},{5,7},{6,4},{7,5},{8,10},{9,11},{10,... | collective-permute-start | bytes 1572872 | tf_op jit(solution)/shard_map/ppermute | solution.py:26
  75.5 30.0 %collective-permute-start.20 = (bf16[4,128,512]{2,1,0:T(8,128)(2,1)S(1)}, bf16[4,128,512]{2,1,0:T(8,128)(2,1)S(1)}, u32[]{:S(2)}, u32[]{:S(2)}) collective-permute-start(bf16[4,128,512]{2,1,0:T(8,128)(2,1)S(1)} %collective-permute-done.18.refs_2_.refs_4_), channel_id=1, source_target_pairs={{0,1},{1,0},{2,3},{3,2},{4,5},{5,4},{6,7},{7,6},{8,9},{9,8},{10,11... | collective-permute-start | bytes 1572872 | tf_op jit(solution)/shard_map/ppermute | solution.py:26
  75.5 38.0 %collective-permute-start.15 = (bf16[4,128,512]{2,1,0:T(8,128)(2,1)S(1)}, bf16[4,128,512]{2,1,0:T(8,128)(2,1)S(1)}, u32[]{:S(2)}, u32[]{:S(2)}) collective-permute-start(bf16[4,128,512]{2,1,0:T(8,128)(2,1)S(1)} %collective-permute-done.13.refs_1_.refs_3_), channel_id=1, source_target_pairs={{0,1},{1,0},{2,3},{3,2},{4,5},{5,4},{6,7},{7,6},{8,9},{9,8},{10,11... | collective-permute-start | bytes 1572872 | tf_op jit(solution)/shard_map/ppermute | solution.py:26
  86.7 27.4 %collective-permute-start.5 = (bf16[4,128,512]{2,1,0:T(8,128)(2,1)S(1)}, bf16[4,128,512]{2,1,0:T(8,128)(2,1)S(1)}, u32[]{:S(2)}, u32[]{:S(2)}) collective-permute-start(bf16[4,128,512]{2,1,0:T(8,128)(2,1)S(1)} %collective-permute-done.3.refs_1_), channel_id=1, source_target_pairs={{0,1},{1,0},{2,3},{3,2},{4,5},{5,4},{6,7},{7,6},{8,9},{9,8},{10,11... | collective-permute-start | bytes 1572872 | tf_op jit(solution)/shard_map/ppermute | solution.py:26
  98.0 17.7 %collective-permute-start.10 = (bf16[4,128,512]{2,1,0:T(8,128)(2,1)S(1)}, bf16[4,128,512]{2,1,0:T(8,128)(2,1)S(1)}, u32[]{:S(2)}, u32[]{:S(2)}) collective-permute-start(bf16[4,128,512]{2,1,0:T(8,128)(2,1)S(1)} %collective-permute-done.8.refs_2_), channel_id=1, source_target_pairs={{0,1},{1,0},{2,3},{3,2},{4,5},{5,4},{6,7},{7,6},{8,9},{9,8},{10,11... | collective-permute-start | bytes 1572872 | tf_op jit(solution)/shard_map/ppermute | solution.py:26
  105.5 15.1 %collective-permute-start.16 = (bf16[4,128,512]{2,1,0:T(8,128)(2,1)S(1)}, bf16[4,128,512]{2,1,0:T(8,128)(2,1)S(1)}, u32[]{:S(2)}, u32[]{:S(2)}) collective-permute-start(bf16[4,128,512]{2,1,0:T(8,128)(2,1)S(1)} %collective-permute-done.14.refs_2_.refs_4_), channel_id=1, source_target_pairs={{0,1},{1,0},{2,3},{3,2},{4,5},{5,4},{6,7},{7,6},{8,9},{9,8},{10,11... | collective-permute-start | bytes 1572872 | tf_op jit(solution)/shard_map/ppermute | solution.py:26
  113.5 14.9 %collective-permute-start.1 = (bf16[4,128,512]{2,1,0:T(8,128)(2,1)S(1)}, bf16[4,128,512]{2,1,0:T(8,128)(2,1)S(1)}, u32[]{:S(2)}, u32[]{:S(2)}) collective-permute-start(bf16[4,128,512]{2,1,0:T(8,128)(2,1)S(1)} %get-tuple-element.64), channel_id=1, source_target_pairs={{0,4},{4,0},{8,12},{12,8},{16,20},{20,16},{24,28},{28,24},{1,5},{5... | collective-permute-start | bytes 1572872 | tf_op jit(solution)/shard_map/ppermute | solution.py:21
  114.1 25.5 %collective-permute-start.2 = (bf16[4,128,512]{2,1,0:T(8,128)(2,1)S(1)}, bf16[4,128,512]{2,1,0:T(8,128)(2,1)S(1)}, u32[]{:S(2)}, u32[]{:S(2)}) collective-permute-start(bf16[4,128,512]{2,1,0:T(8,128)(2,1)S(1)} %get-tuple-element.65), channel_id=1, source_target_pairs={{0,4},{4,0},{8,12},{12,8},{16,20},{20,16},{24,28},{28,24},{1,5},{5... | collective-permute-start | bytes 1572872 | tf_op jit(solution)/shard_map/ppermute | solution.py:21
  115.6 46.5 %collective-permute-start.24 = (bf16[4,128,512]{2,1,0:T(8,128)(2,1)S(1)}, bf16[4,128,512]{2,1,0:T(8,128)(2,1)S(1)}, u32[]{:S(2)}, u32[]{:S(2)}) collective-permute-start(bf16[4,128,512]{2,1,0:T(8,128)(2,1)S(1)} %get-tuple-element.73), channel_id=1, source_target_pairs={{0,4},{4,0},{8,12},{12,8},{16,20},{20,16},{24,28},{28,24},{1,5},{5... | collective-permute-start | bytes 1572872 | tf_op jit(solution)/shard_map/ppermute | solution.py:21
  117.6 55.7 %collective-permute-start.12 = (bf16[4,128,512]{2,1,0:T(8,128)(2,1)S(1)}, bf16[4,128,512]{2,1,0:T(8,128)(2,1)S(1)}, u32[]{:S(2)}, u32[]{:S(2)}) collective-permute-start(bf16[4,128,512]{2,1,0:T(8,128)(2,1)S(1)} %gather_held.11), channel_id=1, source_target_pairs={{0,4},{4,0},{8,12},{12,8},{16,20},{20,16},{24,28},{28,24},{1,5},{5... | collective-permute-start | bytes 1572872 | tf_op jit(solution)/shard_map/ppermute | solution.py:21
  120.6 63.9 %collective-permute-start.11 = (bf16[4,128,512]{2,1,0:T(8,128)(2,1)S(1)}, bf16[4,128,512]{2,1,0:T(8,128)(2,1)S(1)}, u32[]{:S(2)}, u32[]{:S(2)}) collective-permute-start(bf16[4,128,512]{2,1,0:T(8,128)(2,1)S(1)} %gather_held.10), channel_id=1, source_target_pairs={{0,4},{4,0},{8,12},{12,8},{16,20},{20,16},{24,28},{28,24},{1,5},{5... | collective-permute-start | bytes 1572872 | tf_op jit(solution)/shard_map/ppermute | solution.py:21
  128.4 74.3 %collective-permute-start.26 = (bf16[4,128,512]{2,1,0:T(8,128)(2,1)S(1)}, bf16[4,128,512]{2,1,0:T(8,128)(2,1)S(1)}, u32[]{:S(2)}, u32[]{:S(2)}) collective-permute-start(bf16[4,128,512]{2,1,0:T(8,128)(2,1)S(1)} %get-tuple-element.75), channel_id=1, source_target_pairs={{0,8},{4,12},{8,0},{12,4},{16,24},{20,28},{24,16},{28,20},{1,9},{5... | collective-permute-start | bytes 1572872 | tf_op jit(solution)/shard_map/ppermute | solution.py:21
  139.6 63.1 %collective-permute-start.28 = (bf16[4,128,512]{2,1,0:T(8,128)(2,1)S(1)}, bf16[4,128,512]{2,1,0:T(8,128)(2,1)S(1)}, u32[]{:S(2)}, u32[]{:S(2)}) collective-permute-start(bf16[4,128,512]{2,1,0:T(8,128)(2,1)S(1)} %get-tuple-element.77), channel_id=1, source_target_pairs={{0,12},{4,8},{8,4},{12,0},{16,28},{20,24},{24,20},{28,16},{1,13},{... | collective-permute-start | bytes 1572872 | tf_op jit(solution)/shard_map/ppermute | solution.py:21
  162.1 44.0 %collective-permute-start.23 = (bf16[4,128,512]{2,1,0:T(8,128)(2,1)S(1)}, bf16[4,128,512]{2,1,0:T(8,128)(2,1)S(1)}, u32[]{:S(2)}, u32[]{:S(2)}) collective-permute-start(bf16[4,128,512]{2,1,0:T(8,128)(2,1)S(1)} %get-tuple-element.72), channel_id=1, source_target_pairs={{0,4},{4,0},{8,12},{12,8},{16,20},{20,16},{24,28},{28,24},{1,5},{5... | collective-permute-start | bytes 1572872 | tf_op jit(solution)/shard_map/ppermute | solution.py:21
  173.3 32.7 %collective-permute-start.25 = (bf16[4,128,512]{2,1,0:T(8,128)(2,1)S(1)}, bf16[4,128,512]{2,1,0:T(8,128)(2,1)S(1)}, u32[]{:S(2)}, u32[]{:S(2)}) collective-permute-start(bf16[4,128,512]{2,1,0:T(8,128)(2,1)S(1)} %get-tuple-element.74), channel_id=1, source_target_pairs={{0,8},{4,12},{8,0},{12,4},{16,24},{20,28},{24,16},{28,20},{1,9},{5... | collective-permute-start | bytes 1572872 | tf_op jit(solution)/shard_map/ppermute | solution.py:21
  184.6 21.5 %collective-permute-start.27 = (bf16[4,128,512]{2,1,0:T(8,128)(2,1)S(1)}, bf16[4,128,512]{2,1,0:T(8,128)(2,1)S(1)}, u32[]{:S(2)}, u32[]{:S(2)}) collective-permute-start(bf16[4,128,512]{2,1,0:T(8,128)(2,1)S(1)} %get-tuple-element.76), channel_id=1, source_target_pairs={{0,12},{4,8},{8,4},{12,0},{16,28},{20,24},{24,20},{28,16},{1,13},{... | collective-permute-start | bytes 1572872 | tf_op jit(solution)/shard_map/ppermute | solution.py:21
  218.6 14.8 %collective-permute-start.32 = (bf16[512,512]{1,0:T(8,128)(2,1)}, bf16[512,512]{1,0:T(8,128)(2,1)S(1)}, u32[]{:S(2)}, u32[]{:S(2)}) collective-permute-start(bf16[512,512]{1,0:T(8,128)(2,1)} %get-tuple-element.98), channel_id=1, source_target_pairs={{0,4},{4,0},{8,12},{12,8},{16,20},{20,16},{24,28},{28,24},{1,5},{5... | collective-permute-start | bytes 1572872 | tf_op jit(solution)/shard_map/ppermute | solution.py:21
  219.3 19.6 %collective-permute-start.33 = (bf16[512,512]{1,0:T(8,128)(2,1)}, bf16[512,512]{1,0:T(8,128)(2,1)}, u32[]{:S(2)}, u32[]{:S(2)}) collective-permute-start(bf16[512,512]{1,0:T(8,128)(2,1)} %get-tuple-element.99), channel_id=1, source_target_pairs={{0,8},{4,12},{8,0},{12,4},{16,24},{20,28},{24,16},{28,20},{1,9},{5... | collective-permute-start | bytes 1572872 | tf_op jit(solution)/shard_map/ppermute | solution.py:21
  220.0 26.6 %collective-permute-start.34 = (bf16[512,512]{1,0:T(8,128)(2,1)}, bf16[512,512]{1,0:T(8,128)(2,1)}, u32[]{:S(2)}, u32[]{:S(2)}) collective-permute-start(bf16[512,512]{1,0:T(8,128)(2,1)} %get-tuple-element.100), channel_id=1, source_target_pairs={{0,12},{4,8},{8,4},{12,0},{16,28},{20,24},{24,20},{28,16},{1,13},{... | collective-permute-start | bytes 1572872 | tf_op jit(solution)/shard_map/ppermute | solution.py:21
  231.1 26.3 %collective-permute-start.45 = (bf16[512,512]{1,0:T(8,128)(2,1)}, bf16[512,512]{1,0:T(8,128)(2,1)}, u32[]{:S(2)}, u32[]{:S(2)}) collective-permute-start(bf16[512,512]{1,0:T(8,128)(2,1)} %get-tuple-element.112), channel_id=1, source_target_pairs={{0,4},{4,0},{8,12},{12,8},{16,20},{20,16},{24,28},{28,24},{1,5},{5... | collective-permute-start | bytes 1572872 | tf_op jit(solution)/shard_map/ppermute | solution.py:21
  231.6 26.3 %collective-permute-start.46 = (bf16[512,512]{1,0:T(8,128)(2,1)}, bf16[512,512]{1,0:T(8,128)(2,1)}, u32[]{:S(2)}, u32[]{:S(2)}) collective-permute-start(bf16[512,512]{1,0:T(8,128)(2,1)} %get-tuple-element.113), channel_id=1, source_target_pairs={{0,8},{4,12},{8,0},{12,4},{16,24},{20,28},{24,16},{28,20},{1,9},{5... | collective-permute-start | bytes 1572872 | tf_op jit(solution)/shard_map/ppermute | solution.py:21
  234.3 32.8 %collective-permute-start.47 = (bf16[512,512]{1,0:T(8,128)(2,1)}, bf16[512,512]{1,0:T(8,128)(2,1)}, u32[]{:S(2)}, u32[]{:S(2)}) collective-permute-start(bf16[512,512]{1,0:T(8,128)(2,1)} %get-tuple-element.114), channel_id=1, source_target_pairs={{0,12},{4,8},{8,4},{12,0},{16,28},{20,24},{24,20},{28,16},{1,13},{... | collective-permute-start | bytes 1572872 | tf_op jit(solution)/shard_map/ppermute | solution.py:21
  238.9 38.9 %collective-permute-start.42 = (bf16[512,512]{1,0:T(8,128)(2,1)S(1)}, bf16[512,512]{1,0:T(8,128)(2,1)S(1)}, u32[]{:S(2)}, u32[]{:S(2)}) collective-permute-start(bf16[512,512]{1,0:T(8,128)(2,1)S(1)} %get-tuple-element.108), channel_id=1, source_target_pairs={{0,4},{4,0},{8,12},{12,8},{16,20},{20,16},{24,28},{28,24},{1,5},{5... | collective-permute-start | bytes 1572872 | tf_op jit(solution)/shard_map/ppermute | solution.py:21
  249.1 63.0 %collective-permute-start.35 = (bf16[8,128,512]{2,1,0:T(8,128)(2,1)S(1)}, bf16[8,128,512]{2,1,0:T(8,128)(2,1)S(1)}, u32[]{:S(2)}, u32[]{:S(2)}) collective-permute-start(bf16[8,128,512]{2,1,0:T(8,128)(2,1)S(1)} %get-tuple-element.102), channel_id=1, source_target_pairs={{0,1},{1,0},{2,3},{3,2},{4,5},{5,4},{6,7},{7,6},{8,9},{9,8},{10,11... | collective-permute-start | bytes 3145736 | tf_op jit(solution)/shard_map/ppermute | solution.py:26
  257.4 31.7 %collective-permute-start.29 = (bf16[512,512]{1,0:T(8,128)(2,1)S(1)}, bf16[512,512]{1,0:T(8,128)(2,1)S(1)}, u32[]{:S(2)}, u32[]{:S(2)}) collective-permute-start(bf16[512,512]{1,0:T(8,128)(2,1)S(1)} %get-tuple-element.94), channel_id=1, source_target_pairs={{0,4},{4,0},{8,12},{12,8},{16,20},{20,16},{24,28},{28,24},{1,5},{5... | collective-permute-start | bytes 1572872 | tf_op jit(solution)/shard_map/ppermute | solution.py:21
  269.4 43.7 %collective-permute-start.48 = (bf16[8,128,512]{2,1,0:T(8,128)(2,1)S(1)}, bf16[8,128,512]{2,1,0:T(8,128)(2,1)S(1)}, u32[]{:S(2)}, u32[]{:S(2)}) collective-permute-start(bf16[8,128,512]{2,1,0:T(8,128)(2,1)S(1)} %get-tuple-element.116), channel_id=1, source_target_pairs={{0,1},{1,0},{2,3},{3,2},{4,5},{5,4},{6,7},{7,6},{8,9},{9,8},{10,11... | collective-permute-start | bytes 3145736 | tf_op jit(solution)/shard_map/ppermute | solution.py:26
  271.4 28.9 %collective-permute-start.51 = (bf16[512,512]{1,0:T(8,128)(2,1)S(1)}, bf16[512,512]{1,0:T(8,128)(2,1)S(1)}, u32[]{:S(2)}, u32[]{:S(2)}) collective-permute-start(bf16[512,512]{1,0:T(8,128)(2,1)S(1)} %get-tuple-element.118), channel_id=1, source_target_pairs={{0,4},{4,0},{8,12},{12,8},{16,20},{20,16},{24,28},{28,24},{1,5},{5... | collective-permute-start | bytes 1572872 | tf_op jit(solution)/shard_map/ppermute | solution.py:21
  277.8 32.7 %collective-permute-start.38 = (bf16[512,512]{1,0:T(8,128)(2,1)S(1)}, bf16[512,512]{1,0:T(8,128)(2,1)S(1)}, u32[]{:S(2)}, u32[]{:S(2)}) collective-permute-start(bf16[512,512]{1,0:T(8,128)(2,1)S(1)} %get-tuple-element.104), channel_id=1, source_target_pairs={{0,4},{4,0},{8,12},{12,8},{16,20},{20,16},{24,28},{28,24},{1,5},{5... | collective-permute-start | bytes 1572872 | tf_op jit(solution)/shard_map/ppermute | solution.py:21
  289.1 26.0 %collective-permute-start.43 = (bf16[8,128,512]{2,1,0:T(8,128)(2,1)S(1)}, bf16[8,128,512]{2,1,0:T(8,128)(2,1)S(1)}, u32[]{:S(2)}, u32[]{:S(2)}) collective-permute-start(bf16[8,128,512]{2,1,0:T(8,128)(2,1)S(1)} %get-tuple-element.110), channel_id=1, source_target_pairs={{0,1},{1,0},{2,3},{3,2},{4,5},{5,4},{6,7},{7,6},{8,9},{9,8},{10,11... | collective-permute-start | bytes 3145736 | tf_op jit(solution)/shard_map/ppermute | solution.py:26
  300.3 15.7 %collective-permute-start.30 = (bf16[8,128,512]{2,1,0:T(8,128)(2,1)S(1)}, bf16[8,128,512]{2,1,0:T(8,128)(2,1)S(1)}, u32[]{:S(2)}, u32[]{:S(2)}) collective-permute-start(bf16[8,128,512]{2,1,0:T(8,128)(2,1)S(1)} %get-tuple-element.96), channel_id=1, source_target_pairs={{0,1},{1,0},{2,3},{3,2},{4,5},{5,4},{6,7},{7,6},{8,9},{9,8},{10,11... | collective-permute-start | bytes 3145736 | tf_op jit(solution)/shard_map/ppermute | solution.py:26
  313.1 60.5 %collective-permute-start.36 = (bf16[4,128,512]{2,1,0:T(8,128)(2,1)S(1)}, bf16[4,128,512]{2,1,0:T(8,128)(2,1)S(1)}, u32[]{:S(2)}, u32[]{:S(2)}) collective-permute-start(bf16[4,128,512]{2,1,0:T(8,128)(2,1)S(1)} %slice.135), channel_id=1, source_target_pairs={{0,2},{1,3},{2,0},{3,1},{4,6},{5,7},{6,4},{7,5},{8,10},{9,11},{10,... | collective-permute-start | bytes 1572872 | tf_op jit(solution)/shard_map/ppermute | solution.py:26
  315.1 24.1 %collective-permute-start.49 = (bf16[4,128,512]{2,1,0:T(8,128)(2,1)S(1)}, bf16[4,128,512]{2,1,0:T(8,128)(2,1)S(1)}, u32[]{:S(2)}, u32[]{:S(2)}) collective-permute-start(bf16[4,128,512]{2,1,0:T(8,128)(2,1)S(1)} %slice.132), channel_id=1, source_target_pairs={{0,2},{1,3},{2,0},{3,1},{4,6},{5,7},{6,4},{7,5},{8,10},{9,11},{10,... | collective-permute-start | bytes 1572872 | tf_op jit(solution)/shard_map/ppermute | solution.py:26
  316.1 67.7 %collective-permute-start.44 = (bf16[4,128,512]{2,1,0:T(8,128)(2,1)S(1)}, bf16[4,128,512]{2,1,0:T(8,128)(2,1)S(1)}, u32[]{:S(2)}, u32[]{:S(2)}) collective-permute-start(bf16[4,128,512]{2,1,0:T(8,128)(2,1)S(1)} %slice.133), channel_id=1, source_target_pairs={{0,2},{1,3},{2,0},{3,1},{4,6},{5,7},{6,4},{7,5},{8,10},{9,11},{10,... | collective-permute-start | bytes 1572872 | tf_op jit(solution)/shard_map/ppermute | solution.py:26
  318.1 82.2 %collective-permute-start.31 = (bf16[4,128,512]{2,1,0:T(8,128)(2,1)S(1)}, bf16[4,128,512]{2,1,0:T(8,128)(2,1)S(1)}, u32[]{:S(2)}, u32[]{:S(2)}) collective-permute-start(bf16[4,128,512]{2,1,0:T(8,128)(2,1)S(1)} %slice.136), channel_id=1, source_target_pairs={{0,2},{1,3},{2,0},{3,1},{4,6},{5,7},{6,4},{7,5},{8,10},{9,11},{10,... | collective-permute-start | bytes 1572872 | tf_op jit(solution)/shard_map/ppermute | solution.py:26
  319.2 53.7 %collective-permute-start.53 = (bf16[4,128,512]{2,1,0:T(8,128)(2,1)S(1)}, bf16[4,128,512]{2,1,0:T(8,128)(2,1)S(1)}, u32[]{:S(2)}, u32[]{:S(2)}) collective-permute-start(bf16[4,128,512]{2,1,0:T(8,128)(2,1)S(1)} %slice.131), channel_id=1, source_target_pairs={{0,2},{1,3},{2,0},{3,1},{4,6},{5,7},{6,4},{7,5},{8,10},{9,11},{10,... | collective-permute-start | bytes 1572872 | tf_op jit(solution)/shard_map/ppermute | solution.py:26
  339.2 44.0 %collective-permute-start.40 = (bf16[4,128,512]{2,1,0:T(8,128)(2,1)S(1)}, bf16[4,128,512]{2,1,0:T(8,128)(2,1)S(1)}, u32[]{:S(2)}, u32[]{:S(2)}) collective-permute-start(bf16[4,128,512]{2,1,0:T(8,128)(2,1)S(1)} %slice.134), channel_id=1, source_target_pairs={{0,2},{1,3},{2,0},{3,1},{4,6},{5,7},{6,4},{7,5},{8,10},{9,11},{10,... | collective-permute-start | bytes 1572872 | tf_op jit(solution)/shard_map/ppermute | solution.py:26
  372.9 27.2 %collective-permute-start.50 = (bf16[4,128,512]{2,1,0:T(8,128)(2,1)S(1)}, bf16[4,128,512]{2,1,0:T(8,128)(2,1)S(1)}, u32[]{:S(2)}, u32[]{:S(2)}) collective-permute-start(bf16[4,128,512]{2,1,0:T(8,128)(2,1)S(1)} %fusion.1), channel_id=1, source_target_pairs={{0,16},{4,20},{8,24},{12,28},{16,0},{20,4},{24,8},{28,12},{1,17},{... | collective-permute-start | bytes 1572872 | tf_op jit(solution)/shard_map/ppermute | solution.py:21
  373.6 26.5 %collective-permute-start.54 = (bf16[4,128,512]{2,1,0:T(8,128)(2,1)S(1)}, bf16[4,128,512]{2,1,0:T(8,128)(2,1)S(1)}, u32[]{:S(2)}, u32[]{:S(2)}) collective-permute-start(bf16[4,128,512]{2,1,0:T(8,128)(2,1)S(1)} %fusion), channel_id=1, source_target_pairs={{0,8},{4,12},{8,0},{12,4},{16,24},{20,28},{24,16},{28,20},{1,9},{5... | collective-permute-start | bytes 1572872 | tf_op jit(solution)/shard_map/ppermute | solution.py:21
  383.2 36.4 %collective-permute-start.37 = (bf16[4,128,512]{2,1,0:T(8,128)(2,1)S(1)}, bf16[4,128,512]{2,1,0:T(8,128)(2,1)S(1)}, u32[]{:S(2)}, u32[]{:S(2)}) collective-permute-start(bf16[4,128,512]{2,1,0:T(8,128)(2,1)S(1)} %fusion.5), channel_id=1, source_target_pairs={{0,16},{4,20},{8,24},{12,28},{16,0},{20,4},{24,8},{28,12},{1,17},{... | collective-permute-start | bytes 1572872 | tf_op jit(solution)/shard_map/ppermute | solution.py:21
  383.8 35.8 %collective-permute-start.41 = (bf16[4,128,512]{2,1,0:T(8,128)(2,1)S(1)}, bf16[4,128,512]{2,1,0:T(8,128)(2,1)S(1)}, u32[]{:S(2)}, u32[]{:S(2)}) collective-permute-start(bf16[4,128,512]{2,1,0:T(8,128)(2,1)S(1)} %fusion.4), channel_id=1, source_target_pairs={{0,8},{4,12},{8,0},{12,4},{16,24},{20,28},{24,16},{28,20},{1,9},{5... | collective-permute-start | bytes 1572872 | tf_op jit(solution)/shard_map/ppermute | solution.py:21
  (62 other events, 917.4 us)

commit v4 on v3

--- a/solution.py
+++ b/solution.py
@@ -535,11 +535,13 @@
 
     def reduce_shard(tables, tiles):
         keep, give = collect(spots(tables), tiles, cap, kept)
-        keep = keep + xor_design(give, 1).astype(F32)
+        came = xor_design(give, 1)
+        keep = keep + came.astype(F32)
         keep = keep.reshape(lanes, quarter, TILE, step)
+        onward = [keep[ys].astype(BF) for ys in range(1, lanes)]
         total = keep[0]
         for ys in range(1, lanes):
-            back = xor_design(keep[ys].astype(BF), 2 * ys)
+            back = xor_design(onward[ys - 1], 2 * ys)
             total = total + back.astype(F32)
         return total
 

time: 422 us -> 422 us (level)
  no operation moved by 1% of the time
where the time goes in v4:
time: 422 us; the launch traced here: 421 us
  waiting for transfers between devices  282 us (67%)
  Pallas kernels  71.3 us (17%)
  starting transfers between devices  45.1 us (11%)
  local copies, waits for them, and re-layouts  14 us (3%)
  other arithmetic  7.23 us (2%)
    ppermute x31, waiting for transfers between devices, xor_proto(): return lax.ppermute(x, 'proto', [(i, i ^ shift) for i in range(count)])  184 us
    ppermute x24, waiting for transfers between devices, xor_design(): return lax.ppermute(x, 'design', [(i, i ^ shift) for i in range(count)])  98 us
    ppermute x31, starting transfers between devices, xor_proto(): return lax.ppermute(x, 'proto', [(i, i ^ shift) for i in range(count)])  31.8 us
    pallas_call x8, Pallas kernels, gather_held(): pl.pallas_call(functools.partial(gather_held_kernel, len(srcs), n, quarte...  15.1 us
    ppermute x24, starting transfers between devices, xor_design(): return lax.ppermute(x, 'design', [(i, i ^ shift) for i in range(count)])  13.3 us
    pallas_call x1, Pallas kernels, far_grads(): pl.pallas_call(functools.partial(far_kernel, group, cap, lanes, parts, le...  12.5 us
    unnamed x110, local copies, waits for them, and re-layouts  11.7 us
    pallas_call x2, Pallas kernels, own_logits(): pl.pallas_call(functools.partial(own_kernel, group, cap, lanes, parts), o...  10.5 us
  transfers between devices with their start and end apart: 55, of which 26 were waited for; matrix products, arithmetic and copies ran while one was open for 1% of the time, Pallas kernels for 14%

profile of v4, /device:TPU:0, one launch (start us, length us, event | category | flops | bytes accessed | tf_op | source)
XLA Modules:
  0.0 421.3 jit_solution(14011520155101566707)
XLA Ops:
  0.6 1.7 dynamic-slice_convert_fusion
  2.5 4.1 collective-permute-start.17
  9.2 2.8 collective-permute-start.21
  12.0 41.5 %collective-permute-done.21.refs_0_ = s32[4]{0:T(128)S(1)} collective-permute-done((s32[4]{0:T(128)S(1)}, s32[4]{0:T(128)S(1)}, u32[]{:S(2)}, u32[]{:S(2)}) %collective-permute-start.21) | collective-permute-done | bytes 48 | tf_op jit(solution)/shard_map/ppermute | solution.py:21
  55.0 2.1 collective-permute-done.22.refs_1_
  57.6 3.1 collective-permute-done
  64.8 10.6 %collective-permute-done.18.refs_2_.refs_4_ = bf16[4,128,512]{2,1,0:T(8,128)(2,1)S(1)} collective-permute-done((bf16[4,128,512]{2,1,0:T(8,128)(2,1)S(1)}, bf16[4,128,512]{2,1,0:T(8,128)(2,1)S(1)}, u32[]{:S(2)}, u32[]{:S(2)}) %collective-permute-start.18) | collective-permute-done | bytes 524320 | tf_op jit(solution)/shard_map/ppermute | solution.py:26
  76.0 10.7 %collective-permute-done.8.refs_2_ = bf16[4,128,512]{2,1,0:T(8,128)(2,1)S(1)} collective-permute-done((bf16[4,128,512]{2,1,0:T(8,128)(2,1)S(1)}, bf16[4,128,512]{2,1,0:T(8,128)(2,1)S(1)}, u32[]{:S(2)}, u32[]{:S(2)}) %collective-permute-start.8) | collective-permute-done | bytes 524320 | tf_op jit(solution)/shard_map/ppermute | solution.py:26
  86.7 11.2 %collective-permute-done.14.refs_2_.refs_4_ = bf16[4,128,512]{2,1,0:T(8,128)(2,1)S(1)} collective-permute-done((bf16[4,128,512]{2,1,0:T(8,128)(2,1)S(1)}, bf16[4,128,512]{2,1,0:T(8,128)(2,1)S(1)}, u32[]{:S(2)}, u32[]{:S(2)}) %collective-permute-start.14) | collective-permute-done | bytes 524320 | tf_op jit(solution)/shard_map/ppermute | solution.py:26
  98.0 7.5 %collective-permute-done.4.refs_2_ = bf16[4,128,512]{2,1,0:T(8,128)(2,1)S(1)} collective-permute-done((bf16[4,128,512]{2,1,0:T(8,128)(2,1)S(1)}, bf16[4,128,512]{2,1,0:T(8,128)(2,1)S(1)}, u32[]{:S(2)}, u32[]{:S(2)}) %collective-permute-start.4) | collective-permute-done | bytes 524320 | tf_op jit(solution)/shard_map/ppermute | solution.py:26
  106.0 3.4 copy-done.1
  110.3 3.2 gather_held.15
  121.2 3.2 gather_held.14
  124.5 3.9 collective-permute-done.1
  129.1 10.5 %collective-permute-done.2 = bf16[4,128,512]{2,1,0:T(8,128)(2,1)S(1)} collective-permute-done((bf16[4,128,512]{2,1,0:T(8,128)(2,1)S(1)}, bf16[4,128,512]{2,1,0:T(8,128)(2,1)S(1)}, u32[]{:S(2)}, u32[]{:S(2)}) %collective-permute-start.2) | collective-permute-done | bytes 524320 | tf_op jit(solution)/shard_map/ppermute | solution.py:21
  140.3 21.8 %collective-permute-done.24 = bf16[4,128,512]{2,1,0:T(8,128)(2,1)S(1)} collective-permute-done((bf16[4,128,512]{2,1,0:T(8,128)(2,1)S(1)}, bf16[4,128,512]{2,1,0:T(8,128)(2,1)S(1)}, u32[]{:S(2)}, u32[]{:S(2)}) %collective-permute-start.24) | collective-permute-done | bytes 524320 | tf_op jit(solution)/shard_map/ppermute | solution.py:21
  162.6 10.7 %collective-permute-done.12 = bf16[4,128,512]{2,1,0:T(8,128)(2,1)S(1)} collective-permute-done((bf16[4,128,512]{2,1,0:T(8,128)(2,1)S(1)}, bf16[4,128,512]{2,1,0:T(8,128)(2,1)S(1)}, u32[]{:S(2)}, u32[]{:S(2)}) %collective-permute-start.12) | collective-permute-done | bytes 524320 | tf_op jit(solution)/shard_map/ppermute | solution.py:21
  174.1 10.5 %collective-permute-done.11 = bf16[4,128,512]{2,1,0:T(8,128)(2,1)S(1)} collective-permute-done((bf16[4,128,512]{2,1,0:T(8,128)(2,1)S(1)}, bf16[4,128,512]{2,1,0:T(8,128)(2,1)S(1)}, u32[]{:S(2)}, u32[]{:S(2)}) %collective-permute-start.11) | collective-permute-done | bytes 524320 | tf_op jit(solution)/shard_map/ppermute | solution.py:21
  189.3 6.8 %own_logits.2 = (f32[512,1024]{1,0:T(8,128)}, f32[512,1024]{1,0:T(8,128)}, f32[512,1024]{1,0:T(8,128)}, f32[1,1024]{1,0:T(1,128)S(1)}, f32[1,1024]{1,0:T(1,128)S(1)}, /*index=5*/f32[1,1024]{1,0:T(1,128)S(1)}) custom-call(s32[12]{0:T(128)S(1)} %pad_add_fusion.2.base, bf16[1024,1024]{1,0:T(8,128)(2,1)S(1)} %copy-done, s32[1,1024]{1,0:T(1,128)S(1)} %bitcast.106, ...), custom_call_target="tpu_custom_call" | custom-call | tf_op jit(solution)/shard_map/own_logits/pallas_call | solution.py:213
  199.1 3.6 own_logits.3
  202.7 3.3 collective-permute-done.23
  206.1 12.5 %far_grads.1 = (f32[1,1024]{1,0:T(1,128)}, f32[1,1024]{1,0:T(1,128)S(1)}, f32[1,1024]{1,0:T(1,128)S(1)}, bf16[512,1024]{1,0:T(8,128)(2,1)}, bf16[512,1024]{1,0:T...) custom-call(s32[16]{0:T(128)S(1)} %pad_add_fusion.1.base, ...), custom_call_target="tpu_custom_call" | custom-call | tf_op jit(solution)/shard_map/far_grads/pallas_call | solution.py:291
  220.0 2.2 collective-permute-start.34
  227.1 3.1 far_tiles.1
  235.3 1.6 copy-done.23
  236.9 1.9 own_grad.5
  240.2 6.4 %collective-permute-done.34.refs_3_ = bf16[512,512]{1,0:T(8,128)(2,1)} collective-permute-done((bf16[512,512]{1,0:T(8,128)(2,1)}, bf16[512,512]{1,0:T(8,128)(2,1)}, u32[]{:S(2)}, u32[]{:S(2)}) %collective-permute-start.34) | collective-permute-done | bytes 524320 | tf_op jit(solution)/shard_map/ppermute | solution.py:21
  246.6 2.5 collect.7
  249.2 8.2 %collective-permute-done.45.refs_1_ = bf16[512,512]{1,0:T(8,128)(2,1)} collective-permute-done((bf16[512,512]{1,0:T(8,128)(2,1)}, bf16[512,512]{1,0:T(8,128)(2,1)}, u32[]{:S(2)}, u32[]{:S(2)}) %collective-permute-start.45) | collective-permute-done | bytes 524320 | tf_op jit(solution)/shard_map/ppermute | solution.py:21
  257.9 9.1 %collective-permute-done.47.refs_3_ = bf16[512,512]{1,0:T(8,128)(2,1)} collective-permute-done((bf16[512,512]{1,0:T(8,128)(2,1)}, bf16[512,512]{1,0:T(8,128)(2,1)}, u32[]{:S(2)}, u32[]{:S(2)}) %collective-permute-start.47) | collective-permute-done | bytes 524320 | tf_op jit(solution)/shard_map/ppermute | solution.py:21
  267.0 2.3 collect.10
  269.5 2.0 own_grad.7
  272.0 5.9 %collective-permute-done.42.refs_1_ = bf16[512,512]{1,0:T(8,128)(2,1)S(1)} collective-permute-done((bf16[512,512]{1,0:T(8,128)(2,1)S(1)}, bf16[512,512]{1,0:T(8,128)(2,1)S(1)}, u32[]{:S(2)}, u32[]{:S(2)}) %collective-permute-start.42) | collective-permute-done | bytes 524320 | tf_op jit(solution)/shard_map/ppermute | solution.py:21
  278.5 1.9 own_grad.4
  281.7 7.3 %collective-permute-done.29.refs_1_ = bf16[512,512]{1,0:T(8,128)(2,1)S(1)} collective-permute-done((bf16[512,512]{1,0:T(8,128)(2,1)S(1)}, bf16[512,512]{1,0:T(8,128)(2,1)S(1)}, u32[]{:S(2)}, u32[]{:S(2)}) %collective-permute-start.29) | collective-permute-done | bytes 524320 | tf_op jit(solution)/shard_map/ppermute | solution.py:21
  289.2 2.0 own_grad.6
  292.4 7.9 %collective-permute-done.51.refs_1_ = bf16[512,512]{1,0:T(8,128)(2,1)S(1)} collective-permute-done((bf16[512,512]{1,0:T(8,128)(2,1)S(1)}, bf16[512,512]{1,0:T(8,128)(2,1)S(1)}, u32[]{:S(2)}, u32[]{:S(2)}) %collective-permute-start.51) | collective-permute-done | bytes 524320 | tf_op jit(solution)/shard_map/ppermute | solution.py:21
  301.6 9.0 %collective-permute-done.38.refs_1_ = bf16[512,512]{1,0:T(8,128)(2,1)S(1)} collective-permute-done((bf16[512,512]{1,0:T(8,128)(2,1)S(1)}, bf16[512,512]{1,0:T(8,128)(2,1)S(1)}, u32[]{:S(2)}, u32[]{:S(2)}) %collective-permute-start.38) | collective-permute-done | bytes 524320 | tf_op jit(solution)/shard_map/ppermute | solution.py:21
  313.1 1.6 collective-permute-start.36
  319.2 1.6 collective-permute-start.53
  321.2 17.9 %collective-permute-done.49 = bf16[4,128,512]{2,1,0:T(8,128)(2,1)S(1)} collective-permute-done((bf16[4,128,512]{2,1,0:T(8,128)(2,1)S(1)}, bf16[4,128,512]{2,1,0:T(8,128)(2,1)S(1)}, u32[]{:S(2)}, u32[]{:S(2)}) %collective-permute-start.49) | collective-permute-done | bytes 524320 | tf_op jit(solution)/shard_map/ppermute | solution.py:26
  340.9 32.0 %collective-permute-done.53 = bf16[4,128,512]{2,1,0:T(8,128)(2,1)S(1)} collective-permute-done((bf16[4,128,512]{2,1,0:T(8,128)(2,1)S(1)}, bf16[4,128,512]{2,1,0:T(8,128)(2,1)S(1)}, u32[]{:S(2)}, u32[]{:S(2)}) %collective-permute-start.53) | collective-permute-done | bytes 524320 | tf_op jit(solution)/shard_map/ppermute | solution.py:26
  375.3 7.9 %collective-permute-done.40 = bf16[4,128,512]{2,1,0:T(8,128)(2,1)S(1)} collective-permute-done((bf16[4,128,512]{2,1,0:T(8,128)(2,1)S(1)}, bf16[4,128,512]{2,1,0:T(8,128)(2,1)S(1)}, u32[]{:S(2)}, u32[]{:S(2)}) %collective-permute-start.40) | collective-permute-done | bytes 524320 | tf_op jit(solution)/shard_map/ppermute | solution.py:26
  385.5 5.2 %design_grad.3 = bf16[1024,512]{1,0:T(8,128)(2,1)S(1)} custom-call(bf16[512,1024]{1,0:T(8,128)(2,1)S(1)} %get-tuple-element.82.refs_0_, bf16[512,1024]{1,0:T(8,128)(2,1)S(1)} %get-tuple-element.84.refs_1_, bf16[512,1024]{1,0:T(8,128)(2,1)S(1)} %get-tuple-element.86.refs_2_, bf16[512,1024]{1,0:T(8,128)(2,1)S(1)} %get-tuple-element.88.refs_3_, ...), custom_call_target="tpu_custom_call" | custom-call | tf_op jit(solution)/shard_map/design_grad/pallas_call | solution.py:380
  390.8 5.2 %design_grad.2 = bf16[1024,512]{1,0:T(8,128)(2,1)S(1)} custom-call(bf16[512,1024]{1,0:T(8,128)(2,1)S(1)} %get-tuple-element.82.refs_0_, bf16[512,1024]{1,0:T(8,128)(2,1)S(1)} %get-tuple-element.84.refs_1_, bf16[512,1024]{1,0:T(8,128)(2,1)S(1)} %get-tuple-element.86.refs_2_, bf16[512,1024]{1,0:T(8,128)(2,1)S(1)} %get-tuple-element.88.refs_3_, ...), custom_call_target="tpu_custom_call" | custom-call | tf_op jit(solution)/shard_map/design_grad/pallas_call | solution.py:380
  396.0 1.6 pad_maximum_fusion
  397.7 2.4 collective-permute-done.50
  400.4 19.2 %collective-permute-done.37 = bf16[4,128,512]{2,1,0:T(8,128)(2,1)S(1)} collective-permute-done((bf16[4,128,512]{2,1,0:T(8,128)(2,1)S(1)}, bf16[4,128,512]{2,1,0:T(8,128)(2,1)S(1)}, u32[]{:S(2)}, u32[]{:S(2)}) %collective-permute-start.37) | collective-permute-done | bytes 524320 | tf_op jit(solution)/shard_map/ppermute | solution.py:21
  (236 shorter events, 62.5 us)
Async XLA Ops:
  2.5 52.5 %collective-permute-start.17 = (bf16[4,128,512]{2,1,0:T(8,128)(2,1)S(1)}, bf16[4,128,512]{2,1,0:T(8,128)(2,1)S(1)}, u32[]{:S(2)}, u32[]{:S(2)}) collective-permute-start(bf16[4,128,512]{2,1,0:T(8,128)(2,1)S(1)} %get-tuple-element.131), channel_id=1, source_target_pairs={{0,16},{4,20},{8,24},{12,28},{16,0},{20,4},{24,8},{28,12},{1,17},{... | collective-permute-start | bytes 1572872 | tf_op jit(solution)/shard_map/ppermute | solution.py:21
  6.6 55.6 %collective-permute-start.7 = (bf16[4,128,512]{2,1,0:T(8,128)(2,1)S(1)}, bf16[4,128,512]{2,1,0:T(8,128)(2,1)S(1)}, u32[]{:S(2)}, u32[]{:S(2)}) collective-permute-start(bf16[4,128,512]{2,1,0:T(8,128)(2,1)S(1)} %get-tuple-element.131), channel_id=1, source_target_pairs={{0,8},{4,12},{8,0},{12,4},{16,24},{20,28},{24,16},{28,20},{1,9},{5... | collective-permute-start | bytes 1572872 | tf_op jit(solution)/shard_map/ppermute | solution.py:21
  8.2 54.0 %collective-permute-start.13 = (bf16[4,128,512]{2,1,0:T(8,128)(2,1)S(1)}, bf16[4,128,512]{2,1,0:T(8,128)(2,1)S(1)}, u32[]{:S(2)}, u32[]{:S(2)}) collective-permute-start(bf16[4,128,512]{2,1,0:T(8,128)(2,1)S(1)} %get-tuple-element.132), channel_id=1, source_target_pairs={{0,16},{4,20},{8,24},{12,28},{16,0},{20,4},{24,8},{28,12},{1,17},{... | collective-permute-start | bytes 1572872 | tf_op jit(solution)/shard_map/ppermute | solution.py:21
  8.5 54.3 %collective-permute-start.3 = (bf16[4,128,512]{2,1,0:T(8,128)(2,1)S(1)}, bf16[4,128,512]{2,1,0:T(8,128)(2,1)S(1)}, u32[]{:S(2)}, u32[]{:S(2)}) collective-permute-start(bf16[4,128,512]{2,1,0:T(8,128)(2,1)S(1)} %get-tuple-element.132), channel_id=1, source_target_pairs={{0,8},{4,12},{8,0},{12,4},{16,24},{20,28},{24,16},{28,20},{1,9},{5... | collective-permute-start | bytes 1572872 | tf_op jit(solution)/shard_map/ppermute | solution.py:21
  9.2 44.4 %collective-permute-start.21 = (s32[4]{0:T(128)S(1)}, s32[4]{0:T(128)S(1)}, u32[]{:S(2)}, u32[]{:S(2)}) collective-permute-start(s32[4]{0:T(128)S(1)} %get-tuple-element.142), channel_id=1, source_target_pairs={{0,12},{4,8},{8,4},{12,0},{16,28},{20,24},{24,20},{28,16},{1,13},{... | collective-permute-start | bytes 56 | tf_op jit(solution)/shard_map/ppermute | solution.py:21
  60.7 14.8 %collective-permute-start.18 = (bf16[4,128,512]{2,1,0:T(8,128)(2,1)S(1)}, bf16[4,128,512]{2,1,0:T(8,128)(2,1)S(1)}, u32[]{:S(2)}, u32[]{:S(2)}) collective-permute-start(bf16[4,128,512]{2,1,0:T(8,128)(2,1)S(1)} %collective-permute-done.17.refs_1_.refs_3_), channel_id=1, source_target_pairs={{0,2},{1,3},{2,0},{3,1},{4,6},{5,7},{6,4},{7,5},{8,10},{9,11},{10,... | collective-permute-start | bytes 1572872 | tf_op jit(solution)/shard_map/ppermute | solution.py:26
  62.2 24.5 %collective-permute-start.8 = (bf16[4,128,512]{2,1,0:T(8,128)(2,1)S(1)}, bf16[4,128,512]{2,1,0:T(8,128)(2,1)S(1)}, u32[]{:S(2)}, u32[]{:S(2)}) collective-permute-start(bf16[4,128,512]{2,1,0:T(8,128)(2,1)S(1)} %collective-permute-done.7.refs_1_), channel_id=1, source_target_pairs={{0,2},{1,3},{2,0},{3,1},{4,6},{5,7},{6,4},{7,5},{8,10},{9,11},{10,... | collective-permute-start | bytes 1572872 | tf_op jit(solution)/shard_map/ppermute | solution.py:26
  62.8 35.1 %collective-permute-start.14 = (bf16[4,128,512]{2,1,0:T(8,128)(2,1)S(1)}, bf16[4,128,512]{2,1,0:T(8,128)(2,1)S(1)}, u32[]{:S(2)}, u32[]{:S(2)}) collective-permute-start(bf16[4,128,512]{2,1,0:T(8,128)(2,1)S(1)} %collective-permute-done.13.refs_1_.refs_3_), channel_id=1, source_target_pairs={{0,2},{1,3},{2,0},{3,1},{4,6},{5,7},{6,4},{7,5},{8,10},{9,11},{10,... | collective-permute-start | bytes 1572872 | tf_op jit(solution)/shard_map/ppermute | solution.py:26
  64.3 41.2 %collective-permute-start.4 = (bf16[4,128,512]{2,1,0:T(8,128)(2,1)S(1)}, bf16[4,128,512]{2,1,0:T(8,128)(2,1)S(1)}, u32[]{:S(2)}, u32[]{:S(2)}) collective-permute-start(bf16[4,128,512]{2,1,0:T(8,128)(2,1)S(1)} %collective-permute-done.3.refs_1_), channel_id=1, source_target_pairs={{0,2},{1,3},{2,0},{3,1},{4,6},{5,7},{6,4},{7,5},{8,10},{9,11},{10,... | collective-permute-start | bytes 1572872 | tf_op jit(solution)/shard_map/ppermute | solution.py:26
  75.5 30.0 %collective-permute-start.20 = (bf16[4,128,512]{2,1,0:T(8,128)(2,1)S(1)}, bf16[4,128,512]{2,1,0:T(8,128)(2,1)S(1)}, u32[]{:S(2)}, u32[]{:S(2)}) collective-permute-start(bf16[4,128,512]{2,1,0:T(8,128)(2,1)S(1)} %collective-permute-done.18.refs_2_.refs_4_), channel_id=1, source_target_pairs={{0,1},{1,0},{2,3},{3,2},{4,5},{5,4},{6,7},{7,6},{8,9},{9,8},{10,11... | collective-permute-start | bytes 1572872 | tf_op jit(solution)/shard_map/ppermute | solution.py:26
  75.5 38.0 %collective-permute-start.15 = (bf16[4,128,512]{2,1,0:T(8,128)(2,1)S(1)}, bf16[4,128,512]{2,1,0:T(8,128)(2,1)S(1)}, u32[]{:S(2)}, u32[]{:S(2)}) collective-permute-start(bf16[4,128,512]{2,1,0:T(8,128)(2,1)S(1)} %collective-permute-done.13.refs_1_.refs_3_), channel_id=1, source_target_pairs={{0,1},{1,0},{2,3},{3,2},{4,5},{5,4},{6,7},{7,6},{8,9},{9,8},{10,11... | collective-permute-start | bytes 1572872 | tf_op jit(solution)/shard_map/ppermute | solution.py:26
  86.7 27.4 %collective-permute-start.5 = (bf16[4,128,512]{2,1,0:T(8,128)(2,1)S(1)}, bf16[4,128,512]{2,1,0:T(8,128)(2,1)S(1)}, u32[]{:S(2)}, u32[]{:S(2)}) collective-permute-start(bf16[4,128,512]{2,1,0:T(8,128)(2,1)S(1)} %collective-permute-done.3.refs_1_), channel_id=1, source_target_pairs={{0,1},{1,0},{2,3},{3,2},{4,5},{5,4},{6,7},{7,6},{8,9},{9,8},{10,11... | collective-permute-start | bytes 1572872 | tf_op jit(solution)/shard_map/ppermute | solution.py:26
  98.0 17.7 %collective-permute-start.10 = (bf16[4,128,512]{2,1,0:T(8,128)(2,1)S(1)}, bf16[4,128,512]{2,1,0:T(8,128)(2,1)S(1)}, u32[]{:S(2)}, u32[]{:S(2)}) collective-permute-start(bf16[4,128,512]{2,1,0:T(8,128)(2,1)S(1)} %collective-permute-done.8.refs_2_), channel_id=1, source_target_pairs={{0,1},{1,0},{2,3},{3,2},{4,5},{5,4},{6,7},{7,6},{8,9},{9,8},{10,11... | collective-permute-start | bytes 1572872 | tf_op jit(solution)/shard_map/ppermute | solution.py:26
  105.5 15.1 %collective-permute-start.16 = (bf16[4,128,512]{2,1,0:T(8,128)(2,1)S(1)}, bf16[4,128,512]{2,1,0:T(8,128)(2,1)S(1)}, u32[]{:S(2)}, u32[]{:S(2)}) collective-permute-start(bf16[4,128,512]{2,1,0:T(8,128)(2,1)S(1)} %collective-permute-done.14.refs_2_.refs_4_), channel_id=1, source_target_pairs={{0,1},{1,0},{2,3},{3,2},{4,5},{5,4},{6,7},{7,6},{8,9},{9,8},{10,11... | collective-permute-start | bytes 1572872 | tf_op jit(solution)/shard_map/ppermute | solution.py:26
  113.5 14.9 %collective-permute-start.1 = (bf16[4,128,512]{2,1,0:T(8,128)(2,1)S(1)}, bf16[4,128,512]{2,1,0:T(8,128)(2,1)S(1)}, u32[]{:S(2)}, u32[]{:S(2)}) collective-permute-start(bf16[4,128,512]{2,1,0:T(8,128)(2,1)S(1)} %get-tuple-element.64), channel_id=1, source_target_pairs={{0,4},{4,0},{8,12},{12,8},{16,20},{20,16},{24,28},{28,24},{1,5},{5... | collective-permute-start | bytes 1572872 | tf_op jit(solution)/shard_map/ppermute | solution.py:21
  114.1 25.5 %collective-permute-start.2 = (bf16[4,128,512]{2,1,0:T(8,128)(2,1)S(1)}, bf16[4,128,512]{2,1,0:T(8,128)(2,1)S(1)}, u32[]{:S(2)}, u32[]{:S(2)}) collective-permute-start(bf16[4,128,512]{2,1,0:T(8,128)(2,1)S(1)} %get-tuple-element.65), channel_id=1, source_target_pairs={{0,4},{4,0},{8,12},{12,8},{16,20},{20,16},{24,28},{28,24},{1,5},{5... | collective-permute-start | bytes 1572872 | tf_op jit(solution)/shard_map/ppermute | solution.py:21
  115.6 46.5 %collective-permute-start.24 = (bf16[4,128,512]{2,1,0:T(8,128)(2,1)S(1)}, bf16[4,128,512]{2,1,0:T(8,128)(2,1)S(1)}, u32[]{:S(2)}, u32[]{:S(2)}) collective-permute-start(bf16[4,128,512]{2,1,0:T(8,128)(2,1)S(1)} %get-tuple-element.73), channel_id=1, source_target_pairs={{0,4},{4,0},{8,12},{12,8},{16,20},{20,16},{24,28},{28,24},{1,5},{5... | collective-permute-start | bytes 1572872 | tf_op jit(solution)/shard_map/ppermute | solution.py:21
  117.6 55.7 %collective-permute-start.12 = (bf16[4,128,512]{2,1,0:T(8,128)(2,1)S(1)}, bf16[4,128,512]{2,1,0:T(8,128)(2,1)S(1)}, u32[]{:S(2)}, u32[]{:S(2)}) collective-permute-start(bf16[4,128,512]{2,1,0:T(8,128)(2,1)S(1)} %gather_held.11), channel_id=1, source_target_pairs={{0,4},{4,0},{8,12},{12,8},{16,20},{20,16},{24,28},{28,24},{1,5},{5... | collective-permute-start | bytes 1572872 | tf_op jit(solution)/shard_map/ppermute | solution.py:21
  120.6 63.9 %collective-permute-start.11 = (bf16[4,128,512]{2,1,0:T(8,128)(2,1)S(1)}, bf16[4,128,512]{2,1,0:T(8,128)(2,1)S(1)}, u32[]{:S(2)}, u32[]{:S(2)}) collective-permute-start(bf16[4,128,512]{2,1,0:T(8,128)(2,1)S(1)} %gather_held.10), channel_id=1, source_target_pairs={{0,4},{4,0},{8,12},{12,8},{16,20},{20,16},{24,28},{28,24},{1,5},{5... | collective-permute-start | bytes 1572872 | tf_op jit(solution)/shard_map/ppermute | solution.py:21
  128.4 74.3 %collective-permute-start.26 = (bf16[4,128,512]{2,1,0:T(8,128)(2,1)S(1)}, bf16[4,128,512]{2,1,0:T(8,128)(2,1)S(1)}, u32[]{:S(2)}, u32[]{:S(2)}) collective-permute-start(bf16[4,128,512]{2,1,0:T(8,128)(2,1)S(1)} %get-tuple-element.75), channel_id=1, source_target_pairs={{0,8},{4,12},{8,0},{12,4},{16,24},{20,28},{24,16},{28,20},{1,9},{5... | collective-permute-start | bytes 1572872 | tf_op jit(solution)/shard_map/ppermute | solution.py:21
  139.6 63.1 %collective-permute-start.28 = (bf16[4,128,512]{2,1,0:T(8,128)(2,1)S(1)}, bf16[4,128,512]{2,1,0:T(8,128)(2,1)S(1)}, u32[]{:S(2)}, u32[]{:S(2)}) collective-permute-start(bf16[4,128,512]{2,1,0:T(8,128)(2,1)S(1)} %get-tuple-element.77), channel_id=1, source_target_pairs={{0,12},{4,8},{8,4},{12,0},{16,28},{20,24},{24,20},{28,16},{1,13},{... | collective-permute-start | bytes 1572872 | tf_op jit(solution)/shard_map/ppermute | solution.py:21
  162.1 44.0 %collective-permute-start.23 = (bf16[4,128,512]{2,1,0:T(8,128)(2,1)S(1)}, bf16[4,128,512]{2,1,0:T(8,128)(2,1)S(1)}, u32[]{:S(2)}, u32[]{:S(2)}) collective-permute-start(bf16[4,128,512]{2,1,0:T(8,128)(2,1)S(1)} %get-tuple-element.72), channel_id=1, source_target_pairs={{0,4},{4,0},{8,12},{12,8},{16,20},{20,16},{24,28},{28,24},{1,5},{5... | collective-permute-start | bytes 1572872 | tf_op jit(solution)/shard_map/ppermute | solution.py:21
  173.3 32.7 %collective-permute-start.25 = (bf16[4,128,512]{2,1,0:T(8,128)(2,1)S(1)}, bf16[4,128,512]{2,1,0:T(8,128)(2,1)S(1)}, u32[]{:S(2)}, u32[]{:S(2)}) collective-permute-start(bf16[4,128,512]{2,1,0:T(8,128)(2,1)S(1)} %get-tuple-element.74), channel_id=1, source_target_pairs={{0,8},{4,12},{8,0},{12,4},{16,24},{20,28},{24,16},{28,20},{1,9},{5... | collective-permute-start | bytes 1572872 | tf_op jit(solution)/shard_map/ppermute | solution.py:21
  184.6 21.5 %collective-permute-start.27 = (bf16[4,128,512]{2,1,0:T(8,128)(2,1)S(1)}, bf16[4,128,512]{2,1,0:T(8,128)(2,1)S(1)}, u32[]{:S(2)}, u32[]{:S(2)}) collective-permute-start(bf16[4,128,512]{2,1,0:T(8,128)(2,1)S(1)} %get-tuple-element.76), channel_id=1, source_target_pairs={{0,12},{4,8},{8,4},{12,0},{16,28},{20,24},{24,20},{28,16},{1,13},{... | collective-permute-start | bytes 1572872 | tf_op jit(solution)/shard_map/ppermute | solution.py:21
  218.6 14.8 %collective-permute-start.32 = (bf16[512,512]{1,0:T(8,128)(2,1)}, bf16[512,512]{1,0:T(8,128)(2,1)S(1)}, u32[]{:S(2)}, u32[]{:S(2)}) collective-permute-start(bf16[512,512]{1,0:T(8,128)(2,1)} %get-tuple-element.98), channel_id=1, source_target_pairs={{0,4},{4,0},{8,12},{12,8},{16,20},{20,16},{24,28},{28,24},{1,5},{5... | collective-permute-start | bytes 1572872 | tf_op jit(solution)/shard_map/ppermute | solution.py:21
  219.3 19.6 %collective-permute-start.33 = (bf16[512,512]{1,0:T(8,128)(2,1)}, bf16[512,512]{1,0:T(8,128)(2,1)}, u32[]{:S(2)}, u32[]{:S(2)}) collective-permute-start(bf16[512,512]{1,0:T(8,128)(2,1)} %get-tuple-element.99), channel_id=1, source_target_pairs={{0,8},{4,12},{8,0},{12,4},{16,24},{20,28},{24,16},{28,20},{1,9},{5... | collective-permute-start | bytes 1572872 | tf_op jit(solution)/shard_map/ppermute | solution.py:21
  220.0 26.6 %collective-permute-start.34 = (bf16[512,512]{1,0:T(8,128)(2,1)}, bf16[512,512]{1,0:T(8,128)(2,1)}, u32[]{:S(2)}, u32[]{:S(2)}) collective-permute-start(bf16[512,512]{1,0:T(8,128)(2,1)} %get-tuple-element.100), channel_id=1, source_target_pairs={{0,12},{4,8},{8,4},{12,0},{16,28},{20,24},{24,20},{28,16},{1,13},{... | collective-permute-start | bytes 1572872 | tf_op jit(solution)/shard_map/ppermute | solution.py:21
  231.1 26.3 %collective-permute-start.45 = (bf16[512,512]{1,0:T(8,128)(2,1)}, bf16[512,512]{1,0:T(8,128)(2,1)}, u32[]{:S(2)}, u32[]{:S(2)}) collective-permute-start(bf16[512,512]{1,0:T(8,128)(2,1)} %get-tuple-element.112), channel_id=1, source_target_pairs={{0,4},{4,0},{8,12},{12,8},{16,20},{20,16},{24,28},{28,24},{1,5},{5... | collective-permute-start | bytes 1572872 | tf_op jit(solution)/shard_map/ppermute | solution.py:21
  231.6 26.3 %collective-permute-start.46 = (bf16[512,512]{1,0:T(8,128)(2,1)}, bf16[512,512]{1,0:T(8,128)(2,1)}, u32[]{:S(2)}, u32[]{:S(2)}) collective-permute-start(bf16[512,512]{1,0:T(8,128)(2,1)} %get-tuple-element.113), channel_id=1, source_target_pairs={{0,8},{4,12},{8,0},{12,4},{16,24},{20,28},{24,16},{28,20},{1,9},{5... | collective-permute-start | bytes 1572872 | tf_op jit(solution)/shard_map/ppermute | solution.py:21
  234.3 32.8 %collective-permute-start.47 = (bf16[512,512]{1,0:T(8,128)(2,1)}, bf16[512,512]{1,0:T(8,128)(2,1)}, u32[]{:S(2)}, u32[]{:S(2)}) collective-permute-start(bf16[512,512]{1,0:T(8,128)(2,1)} %get-tuple-element.114), channel_id=1, source_target_pairs={{0,12},{4,8},{8,4},{12,0},{16,28},{20,24},{24,20},{28,16},{1,13},{... | collective-permute-start | bytes 1572872 | tf_op jit(solution)/shard_map/ppermute | solution.py:21
  238.9 38.9 %collective-permute-start.42 = (bf16[512,512]{1,0:T(8,128)(2,1)S(1)}, bf16[512,512]{1,0:T(8,128)(2,1)S(1)}, u32[]{:S(2)}, u32[]{:S(2)}) collective-permute-start(bf16[512,512]{1,0:T(8,128)(2,1)S(1)} %get-tuple-element.108), channel_id=1, source_target_pairs={{0,4},{4,0},{8,12},{12,8},{16,20},{20,16},{24,28},{28,24},{1,5},{5... | collective-permute-start | bytes 1572872 | tf_op jit(solution)/shard_map/ppermute | solution.py:21
  249.1 63.0 %collective-permute-start.35 = (bf16[8,128,512]{2,1,0:T(8,128)(2,1)S(1)}, bf16[8,128,512]{2,1,0:T(8,128)(2,1)S(1)}, u32[]{:S(2)}, u32[]{:S(2)}) collective-permute-start(bf16[8,128,512]{2,1,0:T(8,128)(2,1)S(1)} %get-tuple-element.102), channel_id=1, source_target_pairs={{0,1},{1,0},{2,3},{3,2},{4,5},{5,4},{6,7},{7,6},{8,9},{9,8},{10,11... | collective-permute-start | bytes 3145736 | tf_op jit(solution)/shard_map/ppermute | solution.py:26
  257.4 31.7 %collective-permute-start.29 = (bf16[512,512]{1,0:T(8,128)(2,1)S(1)}, bf16[512,512]{1,0:T(8,128)(2,1)S(1)}, u32[]{:S(2)}, u32[]{:S(2)}) collective-permute-start(bf16[512,512]{1,0:T(8,128)(2,1)S(1)} %get-tuple-element.94), channel_id=1, source_target_pairs={{0,4},{4,0},{8,12},{12,8},{16,20},{20,16},{24,28},{28,24},{1,5},{5... | collective-permute-start | bytes 1572872 | tf_op jit(solution)/shard_map/ppermute | solution.py:21
  269.4 43.7 %collective-permute-start.48 = (bf16[8,128,512]{2,1,0:T(8,128)(2,1)S(1)}, bf16[8,128,512]{2,1,0:T(8,128)(2,1)S(1)}, u32[]{:S(2)}, u32[]{:S(2)}) collective-permute-start(bf16[8,128,512]{2,1,0:T(8,128)(2,1)S(1)} %get-tuple-element.116), channel_id=1, source_target_pairs={{0,1},{1,0},{2,3},{3,2},{4,5},{5,4},{6,7},{7,6},{8,9},{9,8},{10,11... | collective-permute-start | bytes 3145736 | tf_op jit(solution)/shard_map/ppermute | solution.py:26
  271.4 28.9 %collective-permute-start.51 = (bf16[512,512]{1,0:T(8,128)(2,1)S(1)}, bf16[512,512]{1,0:T(8,128)(2,1)S(1)}, u32[]{:S(2)}, u32[]{:S(2)}) collective-permute-start(bf16[512,512]{1,0:T(8,128)(2,1)S(1)} %get-tuple-element.118), channel_id=1, source_target_pairs={{0,4},{4,0},{8,12},{12,8},{16,20},{20,16},{24,28},{28,24},{1,5},{5... | collective-permute-start | bytes 1572872 | tf_op jit(solution)/shard_map/ppermute | solution.py:21
  277.8 32.7 %collective-permute-start.38 = (bf16[512,512]{1,0:T(8,128)(2,1)S(1)}, bf16[512,512]{1,0:T(8,128)(2,1)S(1)}, u32[]{:S(2)}, u32[]{:S(2)}) collective-permute-start(bf16[512,512]{1,0:T(8,128)(2,1)S(1)} %get-tuple-element.104), channel_id=1, source_target_pairs={{0,4},{4,0},{8,12},{12,8},{16,20},{20,16},{24,28},{28,24},{1,5},{5... | collective-permute-start | bytes 1572872 | tf_op jit(solution)/shard_map/ppermute | solution.py:21
  289.1 26.0 %collective-permute-start.43 = (bf16[8,128,512]{2,1,0:T(8,128)(2,1)S(1)}, bf16[8,128,512]{2,1,0:T(8,128)(2,1)S(1)}, u32[]{:S(2)}, u32[]{:S(2)}) collective-permute-start(bf16[8,128,512]{2,1,0:T(8,128)(2,1)S(1)} %get-tuple-element.110), channel_id=1, source_target_pairs={{0,1},{1,0},{2,3},{3,2},{4,5},{5,4},{6,7},{7,6},{8,9},{9,8},{10,11... | collective-permute-start | bytes 3145736 | tf_op jit(solution)/shard_map/ppermute | solution.py:26
  300.3 15.7 %collective-permute-start.30 = (bf16[8,128,512]{2,1,0:T(8,128)(2,1)S(1)}, bf16[8,128,512]{2,1,0:T(8,128)(2,1)S(1)}, u32[]{:S(2)}, u32[]{:S(2)}) collective-permute-start(bf16[8,128,512]{2,1,0:T(8,128)(2,1)S(1)} %get-tuple-element.96), channel_id=1, source_target_pairs={{0,1},{1,0},{2,3},{3,2},{4,5},{5,4},{6,7},{7,6},{8,9},{9,8},{10,11... | collective-permute-start | bytes 3145736 | tf_op jit(solution)/shard_map/ppermute | solution.py:26
  313.1 60.5 %collective-permute-start.36 = (bf16[4,128,512]{2,1,0:T(8,128)(2,1)S(1)}, bf16[4,128,512]{2,1,0:T(8,128)(2,1)S(1)}, u32[]{:S(2)}, u32[]{:S(2)}) collective-permute-start(bf16[4,128,512]{2,1,0:T(8,128)(2,1)S(1)} %slice.135), channel_id=1, source_target_pairs={{0,2},{1,3},{2,0},{3,1},{4,6},{5,7},{6,4},{7,5},{8,10},{9,11},{10,... | collective-permute-start | bytes 1572872 | tf_op jit(solution)/shard_map/ppermute | solution.py:26
  315.1 24.1 %collective-permute-start.49 = (bf16[4,128,512]{2,1,0:T(8,128)(2,1)S(1)}, bf16[4,128,512]{2,1,0:T(8,128)(2,1)S(1)}, u32[]{:S(2)}, u32[]{:S(2)}) collective-permute-start(bf16[4,128,512]{2,1,0:T(8,128)(2,1)S(1)} %slice.132), channel_id=1, source_target_pairs={{0,2},{1,3},{2,0},{3,1},{4,6},{5,7},{6,4},{7,5},{8,10},{9,11},{10,... | collective-permute-start | bytes 1572872 | tf_op jit(solution)/shard_map/ppermute | solution.py:26
  316.1 67.7 %collective-permute-start.44 = (bf16[4,128,512]{2,1,0:T(8,128)(2,1)S(1)}, bf16[4,128,512]{2,1,0:T(8,128)(2,1)S(1)}, u32[]{:S(2)}, u32[]{:S(2)}) collective-permute-start(bf16[4,128,512]{2,1,0:T(8,128)(2,1)S(1)} %slice.133), channel_id=1, source_target_pairs={{0,2},{1,3},{2,0},{3,1},{4,6},{5,7},{6,4},{7,5},{8,10},{9,11},{10,... | collective-permute-start | bytes 1572872 | tf_op jit(solution)/shard_map/ppermute | solution.py:26
  318.1 82.2 %collective-permute-start.31 = (bf16[4,128,512]{2,1,0:T(8,128)(2,1)S(1)}, bf16[4,128,512]{2,1,0:T(8,128)(2,1)S(1)}, u32[]{:S(2)}, u32[]{:S(2)}) collective-permute-start(bf16[4,128,512]{2,1,0:T(8,128)(2,1)S(1)} %slice.136), channel_id=1, source_target_pairs={{0,2},{1,3},{2,0},{3,1},{4,6},{5,7},{6,4},{7,5},{8,10},{9,11},{10,... | collective-permute-start | bytes 1572872 | tf_op jit(solution)/shard_map/ppermute | solution.py:26
  319.2 53.7 %collective-permute-start.53 = (bf16[4,128,512]{2,1,0:T(8,128)(2,1)S(1)}, bf16[4,128,512]{2,1,0:T(8,128)(2,1)S(1)}, u32[]{:S(2)}, u32[]{:S(2)}) collective-permute-start(bf16[4,128,512]{2,1,0:T(8,128)(2,1)S(1)} %slice.131), channel_id=1, source_target_pairs={{0,2},{1,3},{2,0},{3,1},{4,6},{5,7},{6,4},{7,5},{8,10},{9,11},{10,... | collective-permute-start | bytes 1572872 | tf_op jit(solution)/shard_map/ppermute | solution.py:26
  339.2 44.0 %collective-permute-start.40 = (bf16[4,128,512]{2,1,0:T(8,128)(2,1)S(1)}, bf16[4,128,512]{2,1,0:T(8,128)(2,1)S(1)}, u32[]{:S(2)}, u32[]{:S(2)}) collective-permute-start(bf16[4,128,512]{2,1,0:T(8,128)(2,1)S(1)} %slice.134), channel_id=1, source_target_pairs={{0,2},{1,3},{2,0},{3,1},{4,6},{5,7},{6,4},{7,5},{8,10},{9,11},{10,... | collective-permute-start | bytes 1572872 | tf_op jit(solution)/shard_map/ppermute | solution.py:26
  372.9 27.2 %collective-permute-start.50 = (bf16[4,128,512]{2,1,0:T(8,128)(2,1)S(1)}, bf16[4,128,512]{2,1,0:T(8,128)(2,1)S(1)}, u32[]{:S(2)}, u32[]{:S(2)}) collective-permute-start(bf16[4,128,512]{2,1,0:T(8,128)(2,1)S(1)} %fusion.1), channel_id=1, source_target_pairs={{0,16},{4,20},{8,24},{12,28},{16,0},{20,4},{24,8},{28,12},{1,17},{... | collective-permute-start | bytes 1572872 | tf_op jit(solution)/shard_map/ppermute | solution.py:21
  373.6 26.5 %collective-permute-start.54 = (bf16[4,128,512]{2,1,0:T(8,128)(2,1)S(1)}, bf16[4,128,512]{2,1,0:T(8,128)(2,1)S(1)}, u32[]{:S(2)}, u32[]{:S(2)}) collective-permute-start(bf16[4,128,512]{2,1,0:T(8,128)(2,1)S(1)} %fusion), channel_id=1, source_target_pairs={{0,8},{4,12},{8,0},{12,4},{16,24},{20,28},{24,16},{28,20},{1,9},{5... | collective-permute-start | bytes 1572872 | tf_op jit(solution)/shard_map/ppermute | solution.py:21
  383.2 36.4 %collective-permute-start.37 = (bf16[4,128,512]{2,1,0:T(8,128)(2,1)S(1)}, bf16[4,128,512]{2,1,0:T(8,128)(2,1)S(1)}, u32[]{:S(2)}, u32[]{:S(2)}) collective-permute-start(bf16[4,128,512]{2,1,0:T(8,128)(2,1)S(1)} %fusion.5), channel_id=1, source_target_pairs={{0,16},{4,20},{8,24},{12,28},{16,0},{20,4},{24,8},{28,12},{1,17},{... | collective-permute-start | bytes 1572872 | tf_op jit(solution)/shard_map/ppermute | solution.py:21
  383.8 35.8 %collective-permute-start.41 = (bf16[4,128,512]{2,1,0:T(8,128)(2,1)S(1)}, bf16[4,128,512]{2,1,0:T(8,128)(2,1)S(1)}, u32[]{:S(2)}, u32[]{:S(2)}) collective-permute-start(bf16[4,128,512]{2,1,0:T(8,128)(2,1)S(1)} %fusion.4), channel_id=1, source_target_pairs={{0,8},{4,12},{8,0},{12,4},{16,24},{20,28},{24,16},{28,20},{1,9},{5... | collective-permute-start | bytes 1572872 | tf_op jit(solution)/shard_map/ppermute | solution.py:21
  (62 other events, 917.4 us)

commit v5 on v4

--- a/solution.py
+++ b/solution.py
@@ -440,12 +440,14 @@
     me = d.reshape(1)
     shifts = list(range(half - 1, 0, -1))
     evens = list(range(2, half, 2))
+    flip = half // 2
+    across = half + flip
     columns = [slice(i * step, (i + 1) * step) for i in range(parts)]
 
     wanted = request_table(candidates[0], blocks_dev, cap, proto_count)
     wanted = wanted.reshape(2, half, cap)
     near = [wanted[h, q ^ s] for s in range(half)]
-    other = [wanted[1 - h, q ^ s] for s in range(half)]
+    other = [wanted[1 - h, q ^ s ^ flip] for s in range(half)]
     asking = {0: other[0]}
     for s in shifts:
         if s == 1:
@@ -463,7 +465,7 @@
         piece = mine[:, :, columns[i]]
         for u in evens:
             sent[u, i] = xor_proto(piece, u)
-        sent["far", i] = xor_proto(piece, half)
+        sent["far", i] = xor_proto(piece, across)
 
     def share(piece):
         held = [piece]
@@ -496,10 +498,10 @@
         (out,) = gather_held(me, [asking[0]], held, lanes)
         far_rows[0][i] = flat(out)
 
-    def bases(lists, which_half, group):
+    def bases(lists, which_half, group, turn=0):
         out = []
         for s in group:
-            first = (which_half * half + (q ^ s)) * blocks_dev
+            first = (which_half * half + (q ^ s ^ turn)) * blocks_dev
             out.append(jnp.where(lists[s] >= 0, (first + lists[s]) * TILE, -(2**30)))
         return jnp.concatenate(out)
 
@@ -512,7 +514,7 @@
         logits.update(zip(group, got))
         sums += [top, total, hit]
     stats, far_g, first = far_grads(
-        bases(other, 1 - h, range(half)), designs, pos, sums, far_rows, cap, parts
+        bases(other, 1 - h, range(half), flip), designs, pos, sums, far_rows, cap, parts
     )
     back_tiles = [first] + far_tiles(designs, far_g, parts)
     losses, top, inv = stats
@@ -552,7 +554,7 @@
         tiles = [back_tiles[i][0]]
         tiles += [xor_proto(back_tiles[i][s], s) for s in range(1, half)]
         total = reduce_shard(far_tables, tiles)
-        landed = [xor_proto(total.astype(BF), half)]
+        landed = [xor_proto(total.astype(BF), across)]
         for u in evens:
             tile = xor_proto(own_tiles[u ^ 1][i], 1)
             total = reduce_shard([near[u], beside[u]], [own_tiles[u][i], tile])

time: 422 us -> 423 us (level)
  transfers between devices with their start and end apart: 55 -> 55, of which waited for: 26 -> 27; matrix products, arithmetic and copies ran while one was open for 1% -> 1% of each run, Pallas kernels for 14% -> 14%
where the time goes in v5:
time: 423 us; the launch traced here: 422 us
  waiting for transfers between devices  285 us (67%)
  Pallas kernels  70.6 us (17%)
  starting transfers between devices  43.9 us (10%)
  local copies, waits for them, and re-layouts  14 us (3%)
  other arithmetic  7.23 us (2%)
    ppermute x31, waiting for transfers between devices, xor_proto(): return lax.ppermute(x, 'proto', [(i, i ^ shift) for i in range(count)])  185 us
    ppermute x24, waiting for transfers between devices, xor_design(): return lax.ppermute(x, 'design', [(i, i ^ shift) for i in range(count)])  99.3 us
    ppermute x31, starting transfers between devices, xor_proto(): return lax.ppermute(x, 'proto', [(i, i ^ shift) for i in range(count)])  30.7 us
    pallas_call x8, Pallas kernels, gather_held(): pl.pallas_call(functools.partial(gather_held_kernel, len(srcs), n, quarte...  15.1 us
    ppermute x24, starting transfers between devices, xor_design(): return lax.ppermute(x, 'design', [(i, i ^ shift) for i in range(count)])  13.3 us
    pallas_call x1, Pallas kernels, far_grads(): pl.pallas_call(functools.partial(far_kernel, group, cap, lanes, parts, le...  12.4 us
    unnamed x110, local copies, waits for them, and re-layouts  11.7 us
    pallas_call x2, Pallas kernels, own_logits(): pl.pallas_call(functools.partial(own_kernel, group, cap, lanes, parts), o...  10.4 us
  transfers between devices with their start and end apart: 55, of which 27 were waited for; matrix products, arithmetic and copies ran while one was open for 1% of the time, Pallas kernels for 14%

profile of v5, /device:TPU:0, one launch (start us, length us, event | category | flops | bytes accessed | tf_op | source)
XLA Modules:
  0.0 422.1 jit_solution(16350131667360675955)
XLA Ops:
  0.6 1.7 dynamic-slice_convert_fusion
  2.5 5.1 %collective-permute-start.17 = (bf16[4,128,512]{2,1,0:T(8,128)(2,1)S(1)}, bf16[4,128,512]{2,1,0:T(8,128)(2,1)S(1)}, u32[]{:S(2)}, u32[]{:S(2)}) collective-permute-start(bf16[4,128,512]{2,1,0:T(8,128)(2,1)S(1)} %get-tuple-element.131), channel_id=1, source_target_pairs={{0,24},{4,28},{8,16},{12,20},{16,8},{20,12},{24,0},{28,4},{1,25},{... | collective-permute-start | bytes 1572872 | tf_op jit(solution)/shard_map/ppermute | solution.py:21
  10.1 1.9 collective-permute-start.21
  12.0 42.3 %collective-permute-done.21.refs_0_ = s32[4]{0:T(128)S(1)} collective-permute-done((s32[4]{0:T(128)S(1)}, s32[4]{0:T(128)S(1)}, u32[]{:S(2)}, u32[]{:S(2)}) %collective-permute-start.21) | collective-permute-done | bytes 48 | tf_op jit(solution)/shard_map/ppermute | solution.py:21
  54.3 1.7 collective-permute-start.22
  56.0 1.8 collective-permute-done.22.refs_1_
  58.4 3.0 collective-permute-done
  65.6 10.6 %collective-permute-done.18.refs_2_.refs_4_ = bf16[4,128,512]{2,1,0:T(8,128)(2,1)S(1)} collective-permute-done((bf16[4,128,512]{2,1,0:T(8,128)(2,1)S(1)}, bf16[4,128,512]{2,1,0:T(8,128)(2,1)S(1)}, u32[]{:S(2)}, u32[]{:S(2)}) %collective-permute-start.18) | collective-permute-done | bytes 524320 | tf_op jit(solution)/shard_map/ppermute | solution.py:26
  76.8 10.7 %collective-permute-done.8.refs_2_ = bf16[4,128,512]{2,1,0:T(8,128)(2,1)S(1)} collective-permute-done((bf16[4,128,512]{2,1,0:T(8,128)(2,1)S(1)}, bf16[4,128,512]{2,1,0:T(8,128)(2,1)S(1)}, u32[]{:S(2)}, u32[]{:S(2)}) %collective-permute-start.8) | collective-permute-done | bytes 524320 | tf_op jit(solution)/shard_map/ppermute | solution.py:26
  87.5 11.2 %collective-permute-done.14.refs_2_.refs_4_ = bf16[4,128,512]{2,1,0:T(8,128)(2,1)S(1)} collective-permute-done((bf16[4,128,512]{2,1,0:T(8,128)(2,1)S(1)}, bf16[4,128,512]{2,1,0:T(8,128)(2,1)S(1)}, u32[]{:S(2)}, u32[]{:S(2)}) %collective-permute-start.14) | collective-permute-done | bytes 524320 | tf_op jit(solution)/shard_map/ppermute | solution.py:26
  98.7 7.8 %collective-permute-done.4.refs_2_ = bf16[4,128,512]{2,1,0:T(8,128)(2,1)S(1)} collective-permute-done((bf16[4,128,512]{2,1,0:T(8,128)(2,1)S(1)}, bf16[4,128,512]{2,1,0:T(8,128)(2,1)S(1)}, u32[]{:S(2)}, u32[]{:S(2)}) %collective-permute-start.4) | collective-permute-done | bytes 524320 | tf_op jit(solution)/shard_map/ppermute | solution.py:26
  107.0 3.4 copy-done.1
  111.3 3.2 gather_held.15
  122.2 3.2 gather_held.14
  125.5 3.9 collective-permute-done.1
  130.1 10.5 %collective-permute-done.2 = bf16[4,128,512]{2,1,0:T(8,128)(2,1)S(1)} collective-permute-done((bf16[4,128,512]{2,1,0:T(8,128)(2,1)S(1)}, bf16[4,128,512]{2,1,0:T(8,128)(2,1)S(1)}, u32[]{:S(2)}, u32[]{:S(2)}) %collective-permute-start.2) | collective-permute-done | bytes 524320 | tf_op jit(solution)/shard_map/ppermute | solution.py:21
  141.3 21.8 %collective-permute-done.24 = bf16[4,128,512]{2,1,0:T(8,128)(2,1)S(1)} collective-permute-done((bf16[4,128,512]{2,1,0:T(8,128)(2,1)S(1)}, bf16[4,128,512]{2,1,0:T(8,128)(2,1)S(1)}, u32[]{:S(2)}, u32[]{:S(2)}) %collective-permute-start.24) | collective-permute-done | bytes 524320 | tf_op jit(solution)/shard_map/ppermute | solution.py:21
  163.6 10.7 %collective-permute-done.12 = bf16[4,128,512]{2,1,0:T(8,128)(2,1)S(1)} collective-permute-done((bf16[4,128,512]{2,1,0:T(8,128)(2,1)S(1)}, bf16[4,128,512]{2,1,0:T(8,128)(2,1)S(1)}, u32[]{:S(2)}, u32[]{:S(2)}) %collective-permute-start.12) | collective-permute-done | bytes 524320 | tf_op jit(solution)/shard_map/ppermute | solution.py:21
  175.1 10.5 %collective-permute-done.11 = bf16[4,128,512]{2,1,0:T(8,128)(2,1)S(1)} collective-permute-done((bf16[4,128,512]{2,1,0:T(8,128)(2,1)S(1)}, bf16[4,128,512]{2,1,0:T(8,128)(2,1)S(1)}, u32[]{:S(2)}, u32[]{:S(2)}) %collective-permute-start.11) | collective-permute-done | bytes 524320 | tf_op jit(solution)/shard_map/ppermute | solution.py:21
  190.3 6.8 %own_logits.2 = (f32[512,1024]{1,0:T(8,128)}, f32[512,1024]{1,0:T(8,128)}, f32[512,1024]{1,0:T(8,128)}, f32[1,1024]{1,0:T(1,128)S(1)}, f32[1,1024]{1,0:T(1,128)S(1)}, /*index=5*/f32[1,1024]{1,0:T(1,128)S(1)}) custom-call(s32[12]{0:T(128)S(1)} %pad_add_fusion.2.base, bf16[1024,1024]{1,0:T(8,128)(2,1)S(1)} %copy-done, s32[1,1024]{1,0:T(1,128)S(1)} %bitcast.106, ...), custom_call_target="tpu_custom_call" | custom-call | tf_op jit(solution)/shard_map/own_logits/pallas_call | solution.py:213
  200.1 3.6 own_logits.3
  203.8 3.3 collective-permute-done.23
  207.1 12.4 %far_grads.1 = (f32[1,1024]{1,0:T(1,128)}, f32[1,1024]{1,0:T(1,128)S(1)}, f32[1,1024]{1,0:T(1,128)S(1)}, bf16[512,1024]{1,0:T(8,128)(2,1)}, bf16[512,1024]{1,0:T...) custom-call(s32[16]{0:T(128)S(1)} %pad_add_fusion.1.base, ...), custom_call_target="tpu_custom_call" | custom-call | tf_op jit(solution)/shard_map/far_grads/pallas_call | solution.py:291
  221.0 2.2 collective-permute-start.34
  228.1 3.1 far_tiles.1
  236.3 1.6 copy-done.23
  237.9 1.9 own_grad.5
  241.2 6.4 %collective-permute-done.34.refs_3_ = bf16[512,512]{1,0:T(8,128)(2,1)} collective-permute-done((bf16[512,512]{1,0:T(8,128)(2,1)}, bf16[512,512]{1,0:T(8,128)(2,1)}, u32[]{:S(2)}, u32[]{:S(2)}) %collective-permute-start.34) | collective-permute-done | bytes 524320 | tf_op jit(solution)/shard_map/ppermute | solution.py:21
  247.6 2.2 collect.7
  249.9 8.5 %collective-permute-done.45.refs_1_ = bf16[512,512]{1,0:T(8,128)(2,1)} collective-permute-done((bf16[512,512]{1,0:T(8,128)(2,1)}, bf16[512,512]{1,0:T(8,128)(2,1)}, u32[]{:S(2)}, u32[]{:S(2)}) %collective-permute-start.45) | collective-permute-done | bytes 524320 | tf_op jit(solution)/shard_map/ppermute | solution.py:21
  258.9 9.1 %collective-permute-done.47.refs_3_ = bf16[512,512]{1,0:T(8,128)(2,1)} collective-permute-done((bf16[512,512]{1,0:T(8,128)(2,1)}, bf16[512,512]{1,0:T(8,128)(2,1)}, u32[]{:S(2)}, u32[]{:S(2)}) %collective-permute-start.47) | collective-permute-done | bytes 524320 | tf_op jit(solution)/shard_map/ppermute | solution.py:21
  268.1 2.0 collect.10
  270.2 1.9 own_grad.7
  273.1 5.8 %collective-permute-done.42.refs_1_ = bf16[512,512]{1,0:T(8,128)(2,1)S(1)} collective-permute-done((bf16[512,512]{1,0:T(8,128)(2,1)S(1)}, bf16[512,512]{1,0:T(8,128)(2,1)S(1)}, u32[]{:S(2)}, u32[]{:S(2)}) %collective-permute-start.42) | collective-permute-done | bytes 524320 | tf_op jit(solution)/shard_map/ppermute | solution.py:21
  279.5 1.9 own_grad.4
  282.8 7.3 %collective-permute-done.29.refs_1_ = bf16[512,512]{1,0:T(8,128)(2,1)S(1)} collective-permute-done((bf16[512,512]{1,0:T(8,128)(2,1)S(1)}, bf16[512,512]{1,0:T(8,128)(2,1)S(1)}, u32[]{:S(2)}, u32[]{:S(2)}) %collective-permute-start.29) | collective-permute-done | bytes 524320 | tf_op jit(solution)/shard_map/ppermute | solution.py:21
  290.2 2.0 own_grad.6
  293.4 7.9 %collective-permute-done.51.refs_1_ = bf16[512,512]{1,0:T(8,128)(2,1)S(1)} collective-permute-done((bf16[512,512]{1,0:T(8,128)(2,1)S(1)}, bf16[512,512]{1,0:T(8,128)(2,1)S(1)}, u32[]{:S(2)}, u32[]{:S(2)}) %collective-permute-start.51) | collective-permute-done | bytes 524320 | tf_op jit(solution)/shard_map/ppermute | solution.py:21
  302.6 9.0 %collective-permute-done.38.refs_1_ = bf16[512,512]{1,0:T(8,128)(2,1)S(1)} collective-permute-done((bf16[512,512]{1,0:T(8,128)(2,1)S(1)}, bf16[512,512]{1,0:T(8,128)(2,1)S(1)}, u32[]{:S(2)}, u32[]{:S(2)}) %collective-permute-start.38) | collective-permute-done | bytes 524320 | tf_op jit(solution)/shard_map/ppermute | solution.py:21
  322.3 17.9 %collective-permute-done.49 = bf16[4,128,512]{2,1,0:T(8,128)(2,1)S(1)} collective-permute-done((bf16[4,128,512]{2,1,0:T(8,128)(2,1)S(1)}, bf16[4,128,512]{2,1,0:T(8,128)(2,1)S(1)}, u32[]{:S(2)}, u32[]{:S(2)}) %collective-permute-start.49) | collective-permute-done | bytes 524320 | tf_op jit(solution)/shard_map/ppermute | solution.py:26
  341.9 32.0 %collective-permute-done.53 = bf16[4,128,512]{2,1,0:T(8,128)(2,1)S(1)} collective-permute-done((bf16[4,128,512]{2,1,0:T(8,128)(2,1)S(1)}, bf16[4,128,512]{2,1,0:T(8,128)(2,1)S(1)}, u32[]{:S(2)}, u32[]{:S(2)}) %collective-permute-start.53) | collective-permute-done | bytes 524320 | tf_op jit(solution)/shard_map/ppermute | solution.py:26
  375.3 8.9 %collective-permute-done.40 = bf16[4,128,512]{2,1,0:T(8,128)(2,1)S(1)} collective-permute-done((bf16[4,128,512]{2,1,0:T(8,128)(2,1)S(1)}, bf16[4,128,512]{2,1,0:T(8,128)(2,1)S(1)}, u32[]{:S(2)}, u32[]{:S(2)}) %collective-permute-start.40) | collective-permute-done | bytes 524320 | tf_op jit(solution)/shard_map/ppermute | solution.py:26
  385.5 5.2 %design_grad.3 = bf16[1024,512]{1,0:T(8,128)(2,1)S(1)} custom-call(bf16[512,1024]{1,0:T(8,128)(2,1)S(1)} %get-tuple-element.82.refs_0_, bf16[512,1024]{1,0:T(8,128)(2,1)S(1)} %get-tuple-element.84.refs_1_, bf16[512,1024]{1,0:T(8,128)(2,1)S(1)} %get-tuple-element.86.refs_2_, bf16[512,1024]{1,0:T(8,128)(2,1)S(1)} %get-tuple-element.88.refs_3_, ...), custom_call_target="tpu_custom_call" | custom-call | tf_op jit(solution)/shard_map/design_grad/pallas_call | solution.py:380
  390.8 5.2 %design_grad.2 = bf16[1024,512]{1,0:T(8,128)(2,1)S(1)} custom-call(bf16[512,1024]{1,0:T(8,128)(2,1)S(1)} %get-tuple-element.82.refs_0_, bf16[512,1024]{1,0:T(8,128)(2,1)S(1)} %get-tuple-element.84.refs_1_, bf16[512,1024]{1,0:T(8,128)(2,1)S(1)} %get-tuple-element.86.refs_2_, bf16[512,1024]{1,0:T(8,128)(2,1)S(1)} %get-tuple-element.88.refs_3_, ...), custom_call_target="tpu_custom_call" | custom-call | tf_op jit(solution)/shard_map/design_grad/pallas_call | solution.py:380
  396.1 1.6 pad_maximum_fusion
  397.7 4.1 collective-permute-done.54
  402.1 10.9 %collective-permute-done.37 = bf16[4,128,512]{2,1,0:T(8,128)(2,1)S(1)} collective-permute-done((bf16[4,128,512]{2,1,0:T(8,128)(2,1)S(1)}, bf16[4,128,512]{2,1,0:T(8,128)(2,1)S(1)}, u32[]{:S(2)}, u32[]{:S(2)}) %collective-permute-start.37) | collective-permute-done | bytes 524320 | tf_op jit(solution)/shard_map/ppermute | solution.py:21
  413.0 7.4 %collective-permute-done.41 = bf16[4,128,512]{2,1,0:T(8,128)(2,1)S(1)} collective-permute-done((bf16[4,128,512]{2,1,0:T(8,128)(2,1)S(1)}, bf16[4,128,512]{2,1,0:T(8,128)(2,1)S(1)}, u32[]{:S(2)}, u32[]{:S(2)}) %collective-permute-start.41) | collective-permute-done | bytes 524320 | tf_op jit(solution)/shard_map/ppermute | solution.py:21
  (236 shorter events, 62.6 us)
Async XLA Ops:
  2.5 53.5 %collective-permute-start.17 = (bf16[4,128,512]{2,1,0:T(8,128)(2,1)S(1)}, bf16[4,128,512]{2,1,0:T(8,128)(2,1)S(1)}, u32[]{:S(2)}, u32[]{:S(2)}) collective-permute-start(bf16[4,128,512]{2,1,0:T(8,128)(2,1)S(1)} %get-tuple-element.131), channel_id=1, source_target_pairs={{0,24},{4,28},{8,16},{12,20},{16,8},{20,12},{24,0},{28,4},{1,25},{... | collective-permute-start | bytes 1572872 | tf_op jit(solution)/shard_map/ppermute | solution.py:21
  7.6 55.3 %collective-permute-start.7 = (bf16[4,128,512]{2,1,0:T(8,128)(2,1)S(1)}, bf16[4,128,512]{2,1,0:T(8,128)(2,1)S(1)}, u32[]{:S(2)}, u32[]{:S(2)}) collective-permute-start(bf16[4,128,512]{2,1,0:T(8,128)(2,1)S(1)} %get-tuple-element.131), channel_id=1, source_target_pairs={{0,8},{4,12},{8,0},{12,4},{16,24},{20,28},{24,16},{28,20},{1,9},{5... | collective-permute-start | bytes 1572872 | tf_op jit(solution)/shard_map/ppermute | solution.py:21
  7.6 55.3 %collective-permute-start.13 = (bf16[4,128,512]{2,1,0:T(8,128)(2,1)S(1)}, bf16[4,128,512]{2,1,0:T(8,128)(2,1)S(1)}, u32[]{:S(2)}, u32[]{:S(2)}) collective-permute-start(bf16[4,128,512]{2,1,0:T(8,128)(2,1)S(1)} %get-tuple-element.132), channel_id=1, source_target_pairs={{0,24},{4,28},{8,16},{12,20},{16,8},{20,12},{24,0},{28,4},{1,25},{... | collective-permute-start | bytes 1572872 | tf_op jit(solution)/shard_map/ppermute | solution.py:21
  8.5 55.0 %collective-permute-start.3 = (bf16[4,128,512]{2,1,0:T(8,128)(2,1)S(1)}, bf16[4,128,512]{2,1,0:T(8,128)(2,1)S(1)}, u32[]{:S(2)}, u32[]{:S(2)}) collective-permute-start(bf16[4,128,512]{2,1,0:T(8,128)(2,1)S(1)} %get-tuple-element.132), channel_id=1, source_target_pairs={{0,8},{4,12},{8,0},{12,4},{16,24},{20,28},{24,16},{28,20},{1,9},{5... | collective-permute-start | bytes 1572872 | tf_op jit(solution)/shard_map/ppermute | solution.py:21
  10.1 44.2 %collective-permute-start.21 = (s32[4]{0:T(128)S(1)}, s32[4]{0:T(128)S(1)}, u32[]{:S(2)}, u32[]{:S(2)}) collective-permute-start(s32[4]{0:T(128)S(1)} %get-tuple-element.142), channel_id=1, source_target_pairs={{0,12},{4,8},{8,4},{12,0},{16,28},{20,24},{24,20},{28,16},{1,13},{... | collective-permute-start | bytes 56 | tf_op jit(solution)/shard_map/ppermute | solution.py:21
  61.5 14.8 %collective-permute-start.18 = (bf16[4,128,512]{2,1,0:T(8,128)(2,1)S(1)}, bf16[4,128,512]{2,1,0:T(8,128)(2,1)S(1)}, u32[]{:S(2)}, u32[]{:S(2)}) collective-permute-start(bf16[4,128,512]{2,1,0:T(8,128)(2,1)S(1)} %collective-permute-done.17.refs_1_.refs_3_), channel_id=1, source_target_pairs={{0,2},{1,3},{2,0},{3,1},{4,6},{5,7},{6,4},{7,5},{8,10},{9,11},{10,... | collective-permute-start | bytes 1572872 | tf_op jit(solution)/shard_map/ppermute | solution.py:26
  63.0 24.5 %collective-permute-start.8 = (bf16[4,128,512]{2,1,0:T(8,128)(2,1)S(1)}, bf16[4,128,512]{2,1,0:T(8,128)(2,1)S(1)}, u32[]{:S(2)}, u32[]{:S(2)}) collective-permute-start(bf16[4,128,512]{2,1,0:T(8,128)(2,1)S(1)} %collective-permute-done.7.refs_1_), channel_id=1, source_target_pairs={{0,2},{1,3},{2,0},{3,1},{4,6},{5,7},{6,4},{7,5},{8,10},{9,11},{10,... | collective-permute-start | bytes 1572872 | tf_op jit(solution)/shard_map/ppermute | solution.py:26
  63.6 35.1 %collective-permute-start.14 = (bf16[4,128,512]{2,1,0:T(8,128)(2,1)S(1)}, bf16[4,128,512]{2,1,0:T(8,128)(2,1)S(1)}, u32[]{:S(2)}, u32[]{:S(2)}) collective-permute-start(bf16[4,128,512]{2,1,0:T(8,128)(2,1)S(1)} %collective-permute-done.13.refs_1_.refs_3_), channel_id=1, source_target_pairs={{0,2},{1,3},{2,0},{3,1},{4,6},{5,7},{6,4},{7,5},{8,10},{9,11},{10,... | collective-permute-start | bytes 1572872 | tf_op jit(solution)/shard_map/ppermute | solution.py:26
  65.1 41.4 %collective-permute-start.4 = (bf16[4,128,512]{2,1,0:T(8,128)(2,1)S(1)}, bf16[4,128,512]{2,1,0:T(8,128)(2,1)S(1)}, u32[]{:S(2)}, u32[]{:S(2)}) collective-permute-start(bf16[4,128,512]{2,1,0:T(8,128)(2,1)S(1)} %collective-permute-done.3.refs_1_), channel_id=1, source_target_pairs={{0,2},{1,3},{2,0},{3,1},{4,6},{5,7},{6,4},{7,5},{8,10},{9,11},{10,... | collective-permute-start | bytes 1572872 | tf_op jit(solution)/shard_map/ppermute | solution.py:26
  76.3 30.3 %collective-permute-start.20 = (bf16[4,128,512]{2,1,0:T(8,128)(2,1)S(1)}, bf16[4,128,512]{2,1,0:T(8,128)(2,1)S(1)}, u32[]{:S(2)}, u32[]{:S(2)}) collective-permute-start(bf16[4,128,512]{2,1,0:T(8,128)(2,1)S(1)} %collective-permute-done.18.refs_2_.refs_4_), channel_id=1, source_target_pairs={{0,1},{1,0},{2,3},{3,2},{4,5},{5,4},{6,7},{7,6},{8,9},{9,8},{10,11... | collective-permute-start | bytes 1572872 | tf_op jit(solution)/shard_map/ppermute | solution.py:26
  76.3 38.3 %collective-permute-start.15 = (bf16[4,128,512]{2,1,0:T(8,128)(2,1)S(1)}, bf16[4,128,512]{2,1,0:T(8,128)(2,1)S(1)}, u32[]{:S(2)}, u32[]{:S(2)}) collective-permute-start(bf16[4,128,512]{2,1,0:T(8,128)(2,1)S(1)} %collective-permute-done.13.refs_1_.refs_3_), channel_id=1, source_target_pairs={{0,1},{1,0},{2,3},{3,2},{4,5},{5,4},{6,7},{7,6},{8,9},{9,8},{10,11... | collective-permute-start | bytes 1572872 | tf_op jit(solution)/shard_map/ppermute | solution.py:26
  87.5 27.7 %collective-permute-start.5 = (bf16[4,128,512]{2,1,0:T(8,128)(2,1)S(1)}, bf16[4,128,512]{2,1,0:T(8,128)(2,1)S(1)}, u32[]{:S(2)}, u32[]{:S(2)}) collective-permute-start(bf16[4,128,512]{2,1,0:T(8,128)(2,1)S(1)} %collective-permute-done.3.refs_1_), channel_id=1, source_target_pairs={{0,1},{1,0},{2,3},{3,2},{4,5},{5,4},{6,7},{7,6},{8,9},{9,8},{10,11... | collective-permute-start | bytes 1572872 | tf_op jit(solution)/shard_map/ppermute | solution.py:26
  98.7 17.9 %collective-permute-start.10 = (bf16[4,128,512]{2,1,0:T(8,128)(2,1)S(1)}, bf16[4,128,512]{2,1,0:T(8,128)(2,1)S(1)}, u32[]{:S(2)}, u32[]{:S(2)}) collective-permute-start(bf16[4,128,512]{2,1,0:T(8,128)(2,1)S(1)} %collective-permute-done.8.refs_2_), channel_id=1, source_target_pairs={{0,1},{1,0},{2,3},{3,2},{4,5},{5,4},{6,7},{7,6},{8,9},{9,8},{10,11... | collective-permute-start | bytes 1572872 | tf_op jit(solution)/shard_map/ppermute | solution.py:26
  106.5 15.1 %collective-permute-start.16 = (bf16[4,128,512]{2,1,0:T(8,128)(2,1)S(1)}, bf16[4,128,512]{2,1,0:T(8,128)(2,1)S(1)}, u32[]{:S(2)}, u32[]{:S(2)}) collective-permute-start(bf16[4,128,512]{2,1,0:T(8,128)(2,1)S(1)} %collective-permute-done.14.refs_2_.refs_4_), channel_id=1, source_target_pairs={{0,1},{1,0},{2,3},{3,2},{4,5},{5,4},{6,7},{7,6},{8,9},{9,8},{10,11... | collective-permute-start | bytes 1572872 | tf_op jit(solution)/shard_map/ppermute | solution.py:26
  114.5 14.9 %collective-permute-start.1 = (bf16[4,128,512]{2,1,0:T(8,128)(2,1)S(1)}, bf16[4,128,512]{2,1,0:T(8,128)(2,1)S(1)}, u32[]{:S(2)}, u32[]{:S(2)}) collective-permute-start(bf16[4,128,512]{2,1,0:T(8,128)(2,1)S(1)} %get-tuple-element.64), channel_id=1, source_target_pairs={{0,4},{4,0},{8,12},{12,8},{16,20},{20,16},{24,28},{28,24},{1,5},{5... | collective-permute-start | bytes 1572872 | tf_op jit(solution)/shard_map/ppermute | solution.py:21
  115.1 25.5 %collective-permute-start.2 = (bf16[4,128,512]{2,1,0:T(8,128)(2,1)S(1)}, bf16[4,128,512]{2,1,0:T(8,128)(2,1)S(1)}, u32[]{:S(2)}, u32[]{:S(2)}) collective-permute-start(bf16[4,128,512]{2,1,0:T(8,128)(2,1)S(1)} %get-tuple-element.65), channel_id=1, source_target_pairs={{0,4},{4,0},{8,12},{12,8},{16,20},{20,16},{24,28},{28,24},{1,5},{5... | collective-permute-start | bytes 1572872 | tf_op jit(solution)/shard_map/ppermute | solution.py:21
  116.6 46.5 %collective-permute-start.24 = (bf16[4,128,512]{2,1,0:T(8,128)(2,1)S(1)}, bf16[4,128,512]{2,1,0:T(8,128)(2,1)S(1)}, u32[]{:S(2)}, u32[]{:S(2)}) collective-permute-start(bf16[4,128,512]{2,1,0:T(8,128)(2,1)S(1)} %get-tuple-element.73), channel_id=1, source_target_pairs={{0,4},{4,0},{8,12},{12,8},{16,20},{20,16},{24,28},{28,24},{1,5},{5... | collective-permute-start | bytes 1572872 | tf_op jit(solution)/shard_map/ppermute | solution.py:21
  118.6 55.7 %collective-permute-start.12 = (bf16[4,128,512]{2,1,0:T(8,128)(2,1)S(1)}, bf16[4,128,512]{2,1,0:T(8,128)(2,1)S(1)}, u32[]{:S(2)}, u32[]{:S(2)}) collective-permute-start(bf16[4,128,512]{2,1,0:T(8,128)(2,1)S(1)} %gather_held.11), channel_id=1, source_target_pairs={{0,4},{4,0},{8,12},{12,8},{16,20},{20,16},{24,28},{28,24},{1,5},{5... | collective-permute-start | bytes 1572872 | tf_op jit(solution)/shard_map/ppermute | solution.py:21
  121.6 63.9 %collective-permute-start.11 = (bf16[4,128,512]{2,1,0:T(8,128)(2,1)S(1)}, bf16[4,128,512]{2,1,0:T(8,128)(2,1)S(1)}, u32[]{:S(2)}, u32[]{:S(2)}) collective-permute-start(bf16[4,128,512]{2,1,0:T(8,128)(2,1)S(1)} %gather_held.10), channel_id=1, source_target_pairs={{0,4},{4,0},{8,12},{12,8},{16,20},{20,16},{24,28},{28,24},{1,5},{5... | collective-permute-start | bytes 1572872 | tf_op jit(solution)/shard_map/ppermute | solution.py:21
  129.4 74.3 %collective-permute-start.26 = (bf16[4,128,512]{2,1,0:T(8,128)(2,1)S(1)}, bf16[4,128,512]{2,1,0:T(8,128)(2,1)S(1)}, u32[]{:S(2)}, u32[]{:S(2)}) collective-permute-start(bf16[4,128,512]{2,1,0:T(8,128)(2,1)S(1)} %get-tuple-element.75), channel_id=1, source_target_pairs={{0,8},{4,12},{8,0},{12,4},{16,24},{20,28},{24,16},{28,20},{1,9},{5... | collective-permute-start | bytes 1572872 | tf_op jit(solution)/shard_map/ppermute | solution.py:21
  140.6 63.1 %collective-permute-start.28 = (bf16[4,128,512]{2,1,0:T(8,128)(2,1)S(1)}, bf16[4,128,512]{2,1,0:T(8,128)(2,1)S(1)}, u32[]{:S(2)}, u32[]{:S(2)}) collective-permute-start(bf16[4,128,512]{2,1,0:T(8,128)(2,1)S(1)} %get-tuple-element.77), channel_id=1, source_target_pairs={{0,12},{4,8},{8,4},{12,0},{16,28},{20,24},{24,20},{28,16},{1,13},{... | collective-permute-start | bytes 1572872 | tf_op jit(solution)/shard_map/ppermute | solution.py:21
  163.1 44.0 %collective-permute-start.23 = (bf16[4,128,512]{2,1,0:T(8,128)(2,1)S(1)}, bf16[4,128,512]{2,1,0:T(8,128)(2,1)S(1)}, u32[]{:S(2)}, u32[]{:S(2)}) collective-permute-start(bf16[4,128,512]{2,1,0:T(8,128)(2,1)S(1)} %get-tuple-element.72), channel_id=1, source_target_pairs={{0,4},{4,0},{8,12},{12,8},{16,20},{20,16},{24,28},{28,24},{1,5},{5... | collective-permute-start | bytes 1572872 | tf_op jit(solution)/shard_map/ppermute | solution.py:21
  174.3 32.7 %collective-permute-start.25 = (bf16[4,128,512]{2,1,0:T(8,128)(2,1)S(1)}, bf16[4,128,512]{2,1,0:T(8,128)(2,1)S(1)}, u32[]{:S(2)}, u32[]{:S(2)}) collective-permute-start(bf16[4,128,512]{2,1,0:T(8,128)(2,1)S(1)} %get-tuple-element.74), channel_id=1, source_target_pairs={{0,8},{4,12},{8,0},{12,4},{16,24},{20,28},{24,16},{28,20},{1,9},{5... | collective-permute-start | bytes 1572872 | tf_op jit(solution)/shard_map/ppermute | solution.py:21
  185.6 21.5 %collective-permute-start.27 = (bf16[4,128,512]{2,1,0:T(8,128)(2,1)S(1)}, bf16[4,128,512]{2,1,0:T(8,128)(2,1)S(1)}, u32[]{:S(2)}, u32[]{:S(2)}) collective-permute-start(bf16[4,128,512]{2,1,0:T(8,128)(2,1)S(1)} %get-tuple-element.76), channel_id=1, source_target_pairs={{0,12},{4,8},{8,4},{12,0},{16,28},{20,24},{24,20},{28,16},{1,13},{... | collective-permute-start | bytes 1572872 | tf_op jit(solution)/shard_map/ppermute | solution.py:21
  219.6 14.8 %collective-permute-start.32 = (bf16[512,512]{1,0:T(8,128)(2,1)}, bf16[512,512]{1,0:T(8,128)(2,1)S(1)}, u32[]{:S(2)}, u32[]{:S(2)}) collective-permute-start(bf16[512,512]{1,0:T(8,128)(2,1)} %get-tuple-element.98), channel_id=1, source_target_pairs={{0,4},{4,0},{8,12},{12,8},{16,20},{20,16},{24,28},{28,24},{1,5},{5... | collective-permute-start | bytes 1572872 | tf_op jit(solution)/shard_map/ppermute | solution.py:21
  220.3 19.6 %collective-permute-start.33 = (bf16[512,512]{1,0:T(8,128)(2,1)}, bf16[512,512]{1,0:T(8,128)(2,1)}, u32[]{:S(2)}, u32[]{:S(2)}) collective-permute-start(bf16[512,512]{1,0:T(8,128)(2,1)} %get-tuple-element.99), channel_id=1, source_target_pairs={{0,8},{4,12},{8,0},{12,4},{16,24},{20,28},{24,16},{28,20},{1,9},{5... | collective-permute-start | bytes 1572872 | tf_op jit(solution)/shard_map/ppermute | solution.py:21
  221.0 26.6 %collective-permute-start.34 = (bf16[512,512]{1,0:T(8,128)(2,1)}, bf16[512,512]{1,0:T(8,128)(2,1)}, u32[]{:S(2)}, u32[]{:S(2)}) collective-permute-start(bf16[512,512]{1,0:T(8,128)(2,1)} %get-tuple-element.100), channel_id=1, source_target_pairs={{0,12},{4,8},{8,4},{12,0},{16,28},{20,24},{24,20},{28,16},{1,13},{... | collective-permute-start | bytes 1572872 | tf_op jit(solution)/shard_map/ppermute | solution.py:21
  232.1 26.3 %collective-permute-start.45 = (bf16[512,512]{1,0:T(8,128)(2,1)}, bf16[512,512]{1,0:T(8,128)(2,1)}, u32[]{:S(2)}, u32[]{:S(2)}) collective-permute-start(bf16[512,512]{1,0:T(8,128)(2,1)} %get-tuple-element.112), channel_id=1, source_target_pairs={{0,4},{4,0},{8,12},{12,8},{16,20},{20,16},{24,28},{28,24},{1,5},{5... | collective-permute-start | bytes 1572872 | tf_op jit(solution)/shard_map/ppermute | solution.py:21
  232.6 26.3 %collective-permute-start.46 = (bf16[512,512]{1,0:T(8,128)(2,1)}, bf16[512,512]{1,0:T(8,128)(2,1)}, u32[]{:S(2)}, u32[]{:S(2)}) collective-permute-start(bf16[512,512]{1,0:T(8,128)(2,1)} %get-tuple-element.113), channel_id=1, source_target_pairs={{0,8},{4,12},{8,0},{12,4},{16,24},{20,28},{24,16},{28,20},{1,9},{5... | collective-permute-start | bytes 1572872 | tf_op jit(solution)/shard_map/ppermute | solution.py:21
  235.2 32.8 %collective-permute-start.47 = (bf16[512,512]{1,0:T(8,128)(2,1)}, bf16[512,512]{1,0:T(8,128)(2,1)}, u32[]{:S(2)}, u32[]{:S(2)}) collective-permute-start(bf16[512,512]{1,0:T(8,128)(2,1)} %get-tuple-element.114), channel_id=1, source_target_pairs={{0,12},{4,8},{8,4},{12,0},{16,28},{20,24},{24,20},{28,16},{1,13},{... | collective-permute-start | bytes 1572872 | tf_op jit(solution)/shard_map/ppermute | solution.py:21
  239.9 39.0 %collective-permute-start.42 = (bf16[512,512]{1,0:T(8,128)(2,1)S(1)}, bf16[512,512]{1,0:T(8,128)(2,1)S(1)}, u32[]{:S(2)}, u32[]{:S(2)}) collective-permute-start(bf16[512,512]{1,0:T(8,128)(2,1)S(1)} %get-tuple-element.108), channel_id=1, source_target_pairs={{0,4},{4,0},{8,12},{12,8},{16,20},{20,16},{24,28},{28,24},{1,5},{5... | collective-permute-start | bytes 1572872 | tf_op jit(solution)/shard_map/ppermute | solution.py:21
  249.8 63.3 %collective-permute-start.35 = (bf16[8,128,512]{2,1,0:T(8,128)(2,1)S(1)}, bf16[8,128,512]{2,1,0:T(8,128)(2,1)S(1)}, u32[]{:S(2)}, u32[]{:S(2)}) collective-permute-start(bf16[8,128,512]{2,1,0:T(8,128)(2,1)S(1)} %get-tuple-element.102), channel_id=1, source_target_pairs={{0,1},{1,0},{2,3},{3,2},{4,5},{5,4},{6,7},{7,6},{8,9},{9,8},{10,11... | collective-permute-start | bytes 3145736 | tf_op jit(solution)/shard_map/ppermute | solution.py:26
  258.4 31.7 %collective-permute-start.29 = (bf16[512,512]{1,0:T(8,128)(2,1)S(1)}, bf16[512,512]{1,0:T(8,128)(2,1)S(1)}, u32[]{:S(2)}, u32[]{:S(2)}) collective-permute-start(bf16[512,512]{1,0:T(8,128)(2,1)S(1)} %get-tuple-element.94), channel_id=1, source_target_pairs={{0,4},{4,0},{8,12},{12,8},{16,20},{20,16},{24,28},{28,24},{1,5},{5... | collective-permute-start | bytes 1572872 | tf_op jit(solution)/shard_map/ppermute | solution.py:21
  270.1 44.0 %collective-permute-start.48 = (bf16[8,128,512]{2,1,0:T(8,128)(2,1)S(1)}, bf16[8,128,512]{2,1,0:T(8,128)(2,1)S(1)}, u32[]{:S(2)}, u32[]{:S(2)}) collective-permute-start(bf16[8,128,512]{2,1,0:T(8,128)(2,1)S(1)} %get-tuple-element.116), channel_id=1, source_target_pairs={{0,1},{1,0},{2,3},{3,2},{4,5},{5,4},{6,7},{7,6},{8,9},{9,8},{10,11... | collective-permute-start | bytes 3145736 | tf_op jit(solution)/shard_map/ppermute | solution.py:26
  272.1 29.2 %collective-permute-start.51 = (bf16[512,512]{1,0:T(8,128)(2,1)S(1)}, bf16[512,512]{1,0:T(8,128)(2,1)S(1)}, u32[]{:S(2)}, u32[]{:S(2)}) collective-permute-start(bf16[512,512]{1,0:T(8,128)(2,1)S(1)} %get-tuple-element.118), channel_id=1, source_target_pairs={{0,4},{4,0},{8,12},{12,8},{16,20},{20,16},{24,28},{28,24},{1,5},{5... | collective-permute-start | bytes 1572872 | tf_op jit(solution)/shard_map/ppermute | solution.py:21
  278.9 32.7 %collective-permute-start.38 = (bf16[512,512]{1,0:T(8,128)(2,1)S(1)}, bf16[512,512]{1,0:T(8,128)(2,1)S(1)}, u32[]{:S(2)}, u32[]{:S(2)}) collective-permute-start(bf16[512,512]{1,0:T(8,128)(2,1)S(1)} %get-tuple-element.104), channel_id=1, source_target_pairs={{0,4},{4,0},{8,12},{12,8},{16,20},{20,16},{24,28},{28,24},{1,5},{5... | collective-permute-start | bytes 1572872 | tf_op jit(solution)/shard_map/ppermute | solution.py:21
  290.1 26.0 %collective-permute-start.43 = (bf16[8,128,512]{2,1,0:T(8,128)(2,1)S(1)}, bf16[8,128,512]{2,1,0:T(8,128)(2,1)S(1)}, u32[]{:S(2)}, u32[]{:S(2)}) collective-permute-start(bf16[8,128,512]{2,1,0:T(8,128)(2,1)S(1)} %get-tuple-element.110), channel_id=1, source_target_pairs={{0,1},{1,0},{2,3},{3,2},{4,5},{5,4},{6,7},{7,6},{8,9},{9,8},{10,11... | collective-permute-start | bytes 3145736 | tf_op jit(solution)/shard_map/ppermute | solution.py:26
  301.3 15.8 %collective-permute-start.30 = (bf16[8,128,512]{2,1,0:T(8,128)(2,1)S(1)}, bf16[8,128,512]{2,1,0:T(8,128)(2,1)S(1)}, u32[]{:S(2)}, u32[]{:S(2)}) collective-permute-start(bf16[8,128,512]{2,1,0:T(8,128)(2,1)S(1)} %get-tuple-element.96), channel_id=1, source_target_pairs={{0,1},{1,0},{2,3},{3,2},{4,5},{5,4},{6,7},{7,6},{8,9},{9,8},{10,11... | collective-permute-start | bytes 3145736 | tf_op jit(solution)/shard_map/ppermute | solution.py:26
  314.1 60.7 %collective-permute-start.36 = (bf16[4,128,512]{2,1,0:T(8,128)(2,1)S(1)}, bf16[4,128,512]{2,1,0:T(8,128)(2,1)S(1)}, u32[]{:S(2)}, u32[]{:S(2)}) collective-permute-start(bf16[4,128,512]{2,1,0:T(8,128)(2,1)S(1)} %slice.135), channel_id=1, source_target_pairs={{0,2},{1,3},{2,0},{3,1},{4,6},{5,7},{6,4},{7,5},{8,10},{9,11},{10,... | collective-permute-start | bytes 1572872 | tf_op jit(solution)/shard_map/ppermute | solution.py:26
  316.1 24.1 %collective-permute-start.49 = (bf16[4,128,512]{2,1,0:T(8,128)(2,1)S(1)}, bf16[4,128,512]{2,1,0:T(8,128)(2,1)S(1)}, u32[]{:S(2)}, u32[]{:S(2)}) collective-permute-start(bf16[4,128,512]{2,1,0:T(8,128)(2,1)S(1)} %slice.132), channel_id=1, source_target_pairs={{0,2},{1,3},{2,0},{3,1},{4,6},{5,7},{6,4},{7,5},{8,10},{9,11},{10,... | collective-permute-start | bytes 1572872 | tf_op jit(solution)/shard_map/ppermute | solution.py:26
  317.1 68.0 %collective-permute-start.44 = (bf16[4,128,512]{2,1,0:T(8,128)(2,1)S(1)}, bf16[4,128,512]{2,1,0:T(8,128)(2,1)S(1)}, u32[]{:S(2)}, u32[]{:S(2)}) collective-permute-start(bf16[4,128,512]{2,1,0:T(8,128)(2,1)S(1)} %slice.133), channel_id=1, source_target_pairs={{0,2},{1,3},{2,0},{3,1},{4,6},{5,7},{6,4},{7,5},{8,10},{9,11},{10,... | collective-permute-start | bytes 1572872 | tf_op jit(solution)/shard_map/ppermute | solution.py:26
  319.1 82.9 %collective-permute-start.31 = (bf16[4,128,512]{2,1,0:T(8,128)(2,1)S(1)}, bf16[4,128,512]{2,1,0:T(8,128)(2,1)S(1)}, u32[]{:S(2)}, u32[]{:S(2)}) collective-permute-start(bf16[4,128,512]{2,1,0:T(8,128)(2,1)S(1)} %slice.136), channel_id=1, source_target_pairs={{0,2},{1,3},{2,0},{3,1},{4,6},{5,7},{6,4},{7,5},{8,10},{9,11},{10,... | collective-permute-start | bytes 1572872 | tf_op jit(solution)/shard_map/ppermute | solution.py:26
  320.2 53.7 %collective-permute-start.53 = (bf16[4,128,512]{2,1,0:T(8,128)(2,1)S(1)}, bf16[4,128,512]{2,1,0:T(8,128)(2,1)S(1)}, u32[]{:S(2)}, u32[]{:S(2)}) collective-permute-start(bf16[4,128,512]{2,1,0:T(8,128)(2,1)S(1)} %slice.131), channel_id=1, source_target_pairs={{0,2},{1,3},{2,0},{3,1},{4,6},{5,7},{6,4},{7,5},{8,10},{9,11},{10,... | collective-permute-start | bytes 1572872 | tf_op jit(solution)/shard_map/ppermute | solution.py:26
  340.2 44.0 %collective-permute-start.40 = (bf16[4,128,512]{2,1,0:T(8,128)(2,1)S(1)}, bf16[4,128,512]{2,1,0:T(8,128)(2,1)S(1)}, u32[]{:S(2)}, u32[]{:S(2)}) collective-permute-start(bf16[4,128,512]{2,1,0:T(8,128)(2,1)S(1)} %slice.134), channel_id=1, source_target_pairs={{0,2},{1,3},{2,0},{3,1},{4,6},{5,7},{6,4},{7,5},{8,10},{9,11},{10,... | collective-permute-start | bytes 1572872 | tf_op jit(solution)/shard_map/ppermute | solution.py:26
  373.9 23.8 %collective-permute-start.50 = (bf16[4,128,512]{2,1,0:T(8,128)(2,1)S(1)}, bf16[4,128,512]{2,1,0:T(8,128)(2,1)S(1)}, u32[]{:S(2)}, u32[]{:S(2)}) collective-permute-start(bf16[4,128,512]{2,1,0:T(8,128)(2,1)S(1)} %fusion.1), channel_id=1, source_target_pairs={{0,24},{4,28},{8,16},{12,20},{16,8},{20,12},{24,0},{28,4},{1,25},{... | collective-permute-start | bytes 1572872 | tf_op jit(solution)/shard_map/ppermute | solution.py:21
  374.8 27.0 %collective-permute-start.54 = (bf16[4,128,512]{2,1,0:T(8,128)(2,1)S(1)}, bf16[4,128,512]{2,1,0:T(8,128)(2,1)S(1)}, u32[]{:S(2)}, u32[]{:S(2)}) collective-permute-start(bf16[4,128,512]{2,1,0:T(8,128)(2,1)S(1)} %fusion), channel_id=1, source_target_pairs={{0,8},{4,12},{8,0},{12,4},{16,24},{20,28},{24,16},{28,20},{1,9},{5... | collective-permute-start | bytes 1572872 | tf_op jit(solution)/shard_map/ppermute | solution.py:21
  384.2 28.8 %collective-permute-start.37 = (bf16[4,128,512]{2,1,0:T(8,128)(2,1)S(1)}, bf16[4,128,512]{2,1,0:T(8,128)(2,1)S(1)}, u32[]{:S(2)}, u32[]{:S(2)}) collective-permute-start(bf16[4,128,512]{2,1,0:T(8,128)(2,1)S(1)} %fusion.5), channel_id=1, source_target_pairs={{0,24},{4,28},{8,16},{12,20},{16,8},{20,12},{24,0},{28,4},{1,25},{... | collective-permute-start | bytes 1572872 | tf_op jit(solution)/shard_map/ppermute | solution.py:21
  385.1 35.3 %collective-permute-start.41 = (bf16[4,128,512]{2,1,0:T(8,128)(2,1)S(1)}, bf16[4,128,512]{2,1,0:T(8,128)(2,1)S(1)}, u32[]{:S(2)}, u32[]{:S(2)}) collective-permute-start(bf16[4,128,512]{2,1,0:T(8,128)(2,1)S(1)} %fusion.4), channel_id=1, source_target_pairs={{0,8},{4,12},{8,0},{12,4},{16,24},{20,28},{24,16},{28,20},{1,9},{5... | collective-permute-start | bytes 1572872 | tf_op jit(solution)/shard_map/ppermute | solution.py:21
  (62 other events, 905.8 us)

commit v6 on v5

--- a/solution.py
+++ b/solution.py
@@ -448,15 +448,15 @@
     wanted = wanted.reshape(2, half, cap)
     near = [wanted[h, q ^ s] for s in range(half)]
     other = [wanted[1 - h, q ^ s ^ flip] for s in range(half)]
-    asking = {0: other[0]}
+    asking, owed = {0: other[0]}, {0: other[flip]}
     for s in shifts:
+        note = [other[s], other[s ^ flip]]
         if s == 1:
-            note = jnp.stack([other[1]] + [near[u ^ 1] for u in [0] + evens])
-            note = xor_proto(note, 1)
-            asking[1] = note[0]
-            beside = {u: note[1 + n] for n, u in enumerate([0] + evens)}
-        else:
-            asking[s] = xor_proto(other[s], s)
+            note += [near[u ^ 1] for u in [0] + evens]
+        note = xor_proto(jnp.stack(note), s)
+        asking[s], owed[s] = note[0], note[1]
+        if s == 1:
+            beside = {u: note[2 + n] for n, u in enumerate([0] + evens)}
 
     shard = prototypes.reshape(blocks_dev, TILE, width)
     mine = lax.dynamic_slice_in_dim(shard, d * quarter, quarter, axis=0).astype(BF)
@@ -549,12 +549,12 @@
 
     result = []
     dgrad = []
-    far_tables = [asking[s] for s in range(half)]
+    far_tables = [owed[s] for s in range(half)]
     for i in range(parts):
-        tiles = [back_tiles[i][0]]
-        tiles += [xor_proto(back_tiles[i][s], s) for s in range(1, half)]
+        tiles = [back_tiles[i][flip]]
+        tiles += [xor_proto(back_tiles[i][s ^ flip], s) for s in range(1, half)]
         total = reduce_shard(far_tables, tiles)
-        landed = [xor_proto(total.astype(BF), across)]
+        landed = [xor_proto(total.astype(BF), half)]
         for u in evens:
             tile = xor_proto(own_tiles[u ^ 1][i], 1)
             total = reduce_shard([near[u], beside[u]], [own_tiles[u][i], tile])

time: 423 us -> 424 us (level)
  starting transfers between devices: 43.9 us -> 54.2 us
  waiting for transfers between devices: 285 us -> 275 us
    ppermute x31, starting transfers between devices: 30.7 us -> 40.9 us  [xor_proto(): return lax.ppermute(x, 'proto', [(i, i ^ shift) for i in range(count)])]
    ppermute x31, waiting for transfers between devices: 185 us -> 176 us  [xor_proto(): return lax.ppermute(x, 'proto', [(i, i ^ shift) for i in range(count)])]
  transfers between devices with their start and end apart: 55 -> 55, of which waited for: 27 -> 26; matrix products, arithmetic and copies ran while one was open for 1% -> 1% of each run, Pallas kernels for 14% -> 14%
where the time goes in v6:
time: 424 us; the launch traced here: 423 us
  waiting for transfers between devices  275 us (65%)
  Pallas kernels  71.3 us (17%)
  starting transfers between devices  54.2 us (13%)
  local copies, waits for them, and re-layouts  14 us (3%)
  other arithmetic  7.25 us (2%)
    ppermute x31, waiting for transfers between devices, xor_proto(): return lax.ppermute(x, 'proto', [(i, i ^ shift) for i in range(count)])  176 us
    ppermute x24, waiting for transfers between devices, xor_design(): return lax.ppermute(x, 'design', [(i, i ^ shift) for i in range(count)])  98.8 us
    ppermute x31, starting transfers between devices, xor_proto(): return lax.ppermute(x, 'proto', [(i, i ^ shift) for i in range(count)])  40.9 us
    pallas_call x8, Pallas kernels, gather_held(): pl.pallas_call(functools.partial(gather_held_kernel, len(srcs), n, quarte...  15.1 us
    ppermute x24, starting transfers between devices, xor_design(): return lax.ppermute(x, 'design', [(i, i ^ shift) for i in range(count)])  13.3 us
    pallas_call x1, Pallas kernels, far_grads(): pl.pallas_call(functools.partial(far_kernel, group, cap, lanes, parts, le...  12.4 us
    unnamed x110, local copies, waits for them, and re-layouts  11.7 us
    pallas_call x2, Pallas kernels, own_logits(): pl.pallas_call(functools.partial(own_kernel, group, cap, lanes, parts), o...  10.5 us
  transfers between devices with their start and end apart: 55, of which 26 were waited for; matrix products, arithmetic and copies ran while one was open for 1% of the time, Pallas kernels for 14%

profile of v6, /device:TPU:0, one launch (start us, length us, event | category | flops | bytes accessed | tf_op | source)
XLA Modules:
  0.0 423.3 jit_solution(9300390975515159471)
XLA Ops:
  0.6 1.7 dynamic-slice_convert_fusion
  2.5 5.1 %collective-permute-start.17 = (bf16[4,128,512]{2,1,0:T(8,128)(2,1)S(1)}, bf16[4,128,512]{2,1,0:T(8,128)(2,1)S(1)}, u32[]{:S(2)}, u32[]{:S(2)}) collective-permute-start(bf16[4,128,512]{2,1,0:T(8,128)(2,1)S(1)} %get-tuple-element.129), channel_id=1, source_target_pairs={{0,24},{4,28},{8,16},{12,20},{16,8},{20,12},{24,0},{28,4},{1,25},{... | collective-permute-start | bytes 1572872 | tf_op jit(solution)/shard_map/ppermute | solution.py:21
  11.1 42.3 %collective-permute-done.22 = s32[2,4]{1,0:T(2,128)S(1)} collective-permute-done((s32[2,4]{1,0:T(2,128)S(1)}, s32[2,4]{1,0:T(2,128)S(1)}, u32[]{:S(2)}, u32[]{:S(2)}) %collective-permute-start.22) | collective-permute-done | bytes 64 | tf_op jit(solution)/shard_map/ppermute | solution.py:21
  53.4 2.7 collective-permute-start.21
  56.1 1.8 collective-permute-done.21
  59.4 2.1 collective-permute-done
  65.6 10.6 %collective-permute-done.18.refs_2_.refs_4_ = bf16[4,128,512]{2,1,0:T(8,128)(2,1)S(1)} collective-permute-done((bf16[4,128,512]{2,1,0:T(8,128)(2,1)S(1)}, bf16[4,128,512]{2,1,0:T(8,128)(2,1)S(1)}, u32[]{:S(2)}, u32[]{:S(2)}) %collective-permute-start.18) | collective-permute-done | bytes 524320 | tf_op jit(solution)/shard_map/ppermute | solution.py:26
  76.8 10.7 %collective-permute-done.8.refs_2_ = bf16[4,128,512]{2,1,0:T(8,128)(2,1)S(1)} collective-permute-done((bf16[4,128,512]{2,1,0:T(8,128)(2,1)S(1)}, bf16[4,128,512]{2,1,0:T(8,128)(2,1)S(1)}, u32[]{:S(2)}, u32[]{:S(2)}) %collective-permute-start.8) | collective-permute-done | bytes 524320 | tf_op jit(solution)/shard_map/ppermute | solution.py:26
  87.5 11.2 %collective-permute-done.14.refs_2_.refs_4_ = bf16[4,128,512]{2,1,0:T(8,128)(2,1)S(1)} collective-permute-done((bf16[4,128,512]{2,1,0:T(8,128)(2,1)S(1)}, bf16[4,128,512]{2,1,0:T(8,128)(2,1)S(1)}, u32[]{:S(2)}, u32[]{:S(2)}) %collective-permute-start.14) | collective-permute-done | bytes 524320 | tf_op jit(solution)/shard_map/ppermute | solution.py:26
  98.8 8.7 %collective-permute-done.4.refs_2_ = bf16[4,128,512]{2,1,0:T(8,128)(2,1)S(1)} collective-permute-done((bf16[4,128,512]{2,1,0:T(8,128)(2,1)S(1)}, bf16[4,128,512]{2,1,0:T(8,128)(2,1)S(1)}, u32[]{:S(2)}, u32[]{:S(2)}) %collective-permute-start.4) | collective-permute-done | bytes 524320 | tf_op jit(solution)/shard_map/ppermute | solution.py:26
  108.0 3.4 copy-done.1
  112.2 3.2 gather_held.15
  123.4 3.2 gather_held.14
  126.6 3.7 collective-permute-done.1
  130.3 1.7 collective-permute-start.26
  132.1 9.5 %collective-permute-done.2 = bf16[4,128,512]{2,1,0:T(8,128)(2,1)S(1)} collective-permute-done((bf16[4,128,512]{2,1,0:T(8,128)(2,1)S(1)}, bf16[4,128,512]{2,1,0:T(8,128)(2,1)S(1)}, u32[]{:S(2)}, u32[]{:S(2)}) %collective-permute-start.2) | collective-permute-done | bytes 524320 | tf_op jit(solution)/shard_map/ppermute | solution.py:21
  141.6 1.7 collective-permute-start.28
  143.3 20.8 %collective-permute-done.24 = bf16[4,128,512]{2,1,0:T(8,128)(2,1)S(1)} collective-permute-done((bf16[4,128,512]{2,1,0:T(8,128)(2,1)S(1)}, bf16[4,128,512]{2,1,0:T(8,128)(2,1)S(1)}, u32[]{:S(2)}, u32[]{:S(2)}) %collective-permute-start.24) | collective-permute-done | bytes 524320 | tf_op jit(solution)/shard_map/ppermute | solution.py:21
  164.8 10.5 %collective-permute-done.12 = bf16[4,128,512]{2,1,0:T(8,128)(2,1)S(1)} collective-permute-done((bf16[4,128,512]{2,1,0:T(8,128)(2,1)S(1)}, bf16[4,128,512]{2,1,0:T(8,128)(2,1)S(1)}, u32[]{:S(2)}, u32[]{:S(2)}) %collective-permute-start.12) | collective-permute-done | bytes 524320 | tf_op jit(solution)/shard_map/ppermute | solution.py:21
  175.3 1.7 collective-permute-start.25
  177.0 9.5 %collective-permute-done.11 = bf16[4,128,512]{2,1,0:T(8,128)(2,1)S(1)} collective-permute-done((bf16[4,128,512]{2,1,0:T(8,128)(2,1)S(1)}, bf16[4,128,512]{2,1,0:T(8,128)(2,1)S(1)}, u32[]{:S(2)}, u32[]{:S(2)}) %collective-permute-start.11) | collective-permute-done | bytes 524320 | tf_op jit(solution)/shard_map/ppermute | solution.py:21
  192.2 6.9 %own_logits.2 = (f32[512,1024]{1,0:T(8,128)}, f32[512,1024]{1,0:T(8,128)}, f32[512,1024]{1,0:T(8,128)}, f32[1,1024]{1,0:T(1,128)S(1)}, f32[1,1024]{1,0:T(1,128)S(1)}, /*index=5*/f32[1,1024]{1,0:T(1,128)S(1)}) custom-call(s32[12]{0:T(128)S(1)} %pad_add_fusion.4.base, bf16[1024,1024]{1,0:T(8,128)(2,1)S(1)} %copy-done, s32[1,1024]{1,0:T(1,128)S(1)} %bitcast.117, ...), custom_call_target="tpu_custom_call" | custom-call | tf_op jit(solution)/shard_map/own_logits/pallas_call | solution.py:213
  202.1 3.6 own_logits.3
  205.7 2.3 collective-permute-done.23
  208.1 12.4 %far_grads.1 = (f32[1,1024]{1,0:T(1,128)}, f32[1,1024]{1,0:T(1,128)S(1)}, f32[1,1024]{1,0:T(1,128)S(1)}, bf16[512,1024]{1,0:T(8,128)(2,1)}, bf16[512,1024]{1,0:T...) custom-call(s32[16]{0:T(128)S(1)} %pad_add_fusion.3.base, ...), custom_call_target="tpu_custom_call" | custom-call | tf_op jit(solution)/shard_map/far_grads/pallas_call | solution.py:291
  229.1 3.1 far_tiles.1
  239.5 1.9 own_grad.5
  243.1 5.4 %collective-permute-done.34.refs_3_ = bf16[512,512]{1,0:T(8,128)(2,1)} collective-permute-done((bf16[512,512]{1,0:T(8,128)(2,1)}, bf16[512,512]{1,0:T(8,128)(2,1)}, u32[]{:S(2)}, u32[]{:S(2)}) %collective-permute-start.34) | collective-permute-done | bytes 524320 | tf_op jit(solution)/shard_map/ppermute | solution.py:21
  248.5 2.5 collect.7
  251.2 8.1 %collective-permute-done.45.refs_1_ = bf16[512,512]{1,0:T(8,128)(2,1)} collective-permute-done((bf16[512,512]{1,0:T(8,128)(2,1)}, bf16[512,512]{1,0:T(8,128)(2,1)}, u32[]{:S(2)}, u32[]{:S(2)}) %collective-permute-start.45) | collective-permute-done | bytes 524320 | tf_op jit(solution)/shard_map/ppermute | solution.py:21
  260.1 8.9 %collective-permute-done.47.refs_3_ = bf16[512,512]{1,0:T(8,128)(2,1)} collective-permute-done((bf16[512,512]{1,0:T(8,128)(2,1)}, bf16[512,512]{1,0:T(8,128)(2,1)}, u32[]{:S(2)}, u32[]{:S(2)}) %collective-permute-start.47) | collective-permute-done | bytes 524320 | tf_op jit(solution)/shard_map/ppermute | solution.py:21
  269.0 2.3 collect.10
  271.4 2.0 own_grad.7
  274.1 5.7 %collective-permute-done.42.refs_1_ = bf16[512,512]{1,0:T(8,128)(2,1)S(1)} collective-permute-done((bf16[512,512]{1,0:T(8,128)(2,1)S(1)}, bf16[512,512]{1,0:T(8,128)(2,1)S(1)}, u32[]{:S(2)}, u32[]{:S(2)}) %collective-permute-start.42) | collective-permute-done | bytes 524320 | tf_op jit(solution)/shard_map/ppermute | solution.py:21
  280.7 2.0 own_grad.4
  283.9 7.1 %collective-permute-done.29.refs_1_ = bf16[512,512]{1,0:T(8,128)(2,1)S(1)} collective-permute-done((bf16[512,512]{1,0:T(8,128)(2,1)S(1)}, bf16[512,512]{1,0:T(8,128)(2,1)S(1)}, u32[]{:S(2)}, u32[]{:S(2)}) %collective-permute-start.29) | collective-permute-done | bytes 524320 | tf_op jit(solution)/shard_map/ppermute | solution.py:21
  291.1 2.0 own_grad.6
  294.4 7.9 %collective-permute-done.51.refs_1_ = bf16[512,512]{1,0:T(8,128)(2,1)S(1)} collective-permute-done((bf16[512,512]{1,0:T(8,128)(2,1)S(1)}, bf16[512,512]{1,0:T(8,128)(2,1)S(1)}, u32[]{:S(2)}, u32[]{:S(2)}) %collective-permute-start.51) | collective-permute-done | bytes 524320 | tf_op jit(solution)/shard_map/ppermute | solution.py:21
  303.5 9.0 %collective-permute-done.38.refs_1_ = bf16[512,512]{1,0:T(8,128)(2,1)S(1)} collective-permute-done((bf16[512,512]{1,0:T(8,128)(2,1)S(1)}, bf16[512,512]{1,0:T(8,128)(2,1)S(1)}, u32[]{:S(2)}, u32[]{:S(2)}) %collective-permute-start.38) | collective-permute-done | bytes 524320 | tf_op jit(solution)/shard_map/ppermute | solution.py:21
  323.2 17.9 %collective-permute-done.49 = bf16[4,128,512]{2,1,0:T(8,128)(2,1)S(1)} collective-permute-done((bf16[4,128,512]{2,1,0:T(8,128)(2,1)S(1)}, bf16[4,128,512]{2,1,0:T(8,128)(2,1)S(1)}, u32[]{:S(2)}, u32[]{:S(2)}) %collective-permute-start.49) | collective-permute-done | bytes 524320 | tf_op jit(solution)/shard_map/ppermute | solution.py:26
  342.8 32.0 %collective-permute-done.53 = bf16[4,128,512]{2,1,0:T(8,128)(2,1)S(1)} collective-permute-done((bf16[4,128,512]{2,1,0:T(8,128)(2,1)S(1)}, bf16[4,128,512]{2,1,0:T(8,128)(2,1)S(1)}, u32[]{:S(2)}, u32[]{:S(2)}) %collective-permute-start.53) | collective-permute-done | bytes 524320 | tf_op jit(solution)/shard_map/ppermute | solution.py:26
  375.5 1.9 collective-permute-start.54
  377.6 7.5 %collective-permute-done.40 = bf16[4,128,512]{2,1,0:T(8,128)(2,1)S(1)} collective-permute-done((bf16[4,128,512]{2,1,0:T(8,128)(2,1)S(1)}, bf16[4,128,512]{2,1,0:T(8,128)(2,1)S(1)}, u32[]{:S(2)}, u32[]{:S(2)}) %collective-permute-start.40) | collective-permute-done | bytes 524320 | tf_op jit(solution)/shard_map/ppermute | solution.py:26
  385.7 1.9 collective-permute-start.41
  387.8 5.2 %design_grad.3 = bf16[1024,512]{1,0:T(8,128)(2,1)S(1)} custom-call(bf16[512,1024]{1,0:T(8,128)(2,1)S(1)} %get-tuple-element.82.refs_0_, bf16[512,1024]{1,0:T(8,128)(2,1)S(1)} %get-tuple-element.84.refs_1_, bf16[512,1024]{1,0:T(8,128)(2,1)S(1)} %get-tuple-element.86.refs_2_, bf16[512,1024]{1,0:T(8,128)(2,1)S(1)} %get-tuple-element.88.refs_3_, ...), custom_call_target="tpu_custom_call" | custom-call | tf_op jit(solution)/shard_map/design_grad/pallas_call | solution.py:380
  393.1 5.2 %design_grad.2 = bf16[1024,512]{1,0:T(8,128)(2,1)S(1)} custom-call(bf16[512,1024]{1,0:T(8,128)(2,1)S(1)} %get-tuple-element.82.refs_0_, bf16[512,1024]{1,0:T(8,128)(2,1)S(1)} %get-tuple-element.84.refs_1_, bf16[512,1024]{1,0:T(8,128)(2,1)S(1)} %get-tuple-element.86.refs_2_, bf16[512,1024]{1,0:T(8,128)(2,1)S(1)} %get-tuple-element.88.refs_3_, ...), custom_call_target="tpu_custom_call" | custom-call | tf_op jit(solution)/shard_map/design_grad/pallas_call | solution.py:380
  400.0 3.1 collective-permute-done.50
  403.4 18.2 %collective-permute-done.37 = bf16[4,128,512]{2,1,0:T(8,128)(2,1)S(1)} collective-permute-done((bf16[4,128,512]{2,1,0:T(8,128)(2,1)S(1)}, bf16[4,128,512]{2,1,0:T(8,128)(2,1)S(1)}, u32[]{:S(2)}, u32[]{:S(2)}) %collective-permute-start.37) | collective-permute-done | bytes 524320 | tf_op jit(solution)/shard_map/ppermute | solution.py:21
  (240 shorter events, 69.4 us)
Async XLA Ops:
  2.5 56.9 %collective-permute-start.17 = (bf16[4,128,512]{2,1,0:T(8,128)(2,1)S(1)}, bf16[4,128,512]{2,1,0:T(8,128)(2,1)S(1)}, u32[]{:S(2)}, u32[]{:S(2)}) collective-permute-start(bf16[4,128,512]{2,1,0:T(8,128)(2,1)S(1)} %get-tuple-element.129), channel_id=1, source_target_pairs={{0,24},{4,28},{8,16},{12,20},{16,8},{20,12},{24,0},{28,4},{1,25},{... | collective-permute-start | bytes 1572872 | tf_op jit(solution)/shard_map/ppermute | solution.py:21
  7.6 55.4 %collective-permute-start.7 = (bf16[4,128,512]{2,1,0:T(8,128)(2,1)S(1)}, bf16[4,128,512]{2,1,0:T(8,128)(2,1)S(1)}, u32[]{:S(2)}, u32[]{:S(2)}) collective-permute-start(bf16[4,128,512]{2,1,0:T(8,128)(2,1)S(1)} %get-tuple-element.129), channel_id=1, source_target_pairs={{0,8},{4,12},{8,0},{12,4},{16,24},{20,28},{24,16},{28,20},{1,9},{5... | collective-permute-start | bytes 1572872 | tf_op jit(solution)/shard_map/ppermute | solution.py:21
  7.6 55.4 %collective-permute-start.13 = (bf16[4,128,512]{2,1,0:T(8,128)(2,1)S(1)}, bf16[4,128,512]{2,1,0:T(8,128)(2,1)S(1)}, u32[]{:S(2)}, u32[]{:S(2)}) collective-permute-start(bf16[4,128,512]{2,1,0:T(8,128)(2,1)S(1)} %get-tuple-element.130), channel_id=1, source_target_pairs={{0,24},{4,28},{8,16},{12,20},{16,8},{20,12},{24,0},{28,4},{1,25},{... | collective-permute-start | bytes 1572872 | tf_op jit(solution)/shard_map/ppermute | solution.py:21
  8.5 55.1 %collective-permute-start.3 = (bf16[4,128,512]{2,1,0:T(8,128)(2,1)S(1)}, bf16[4,128,512]{2,1,0:T(8,128)(2,1)S(1)}, u32[]{:S(2)}, u32[]{:S(2)}) collective-permute-start(bf16[4,128,512]{2,1,0:T(8,128)(2,1)S(1)} %get-tuple-element.130), channel_id=1, source_target_pairs={{0,8},{4,12},{8,0},{12,4},{16,24},{20,28},{24,16},{28,20},{1,9},{5... | collective-permute-start | bytes 1572872 | tf_op jit(solution)/shard_map/ppermute | solution.py:21
  10.1 43.3 %collective-permute-start.22 = (s32[2,4]{1,0:T(2,128)S(1)}, s32[2,4]{1,0:T(2,128)S(1)}, u32[]{:S(2)}, u32[]{:S(2)}) collective-permute-start(s32[2,4]{1,0:T(2,128)S(1)} %pad_add_fusion.2), channel_id=1, source_target_pairs={{0,8},{4,12},{8,0},{12,4},{16,24},{20,28},{24,16},{28,20},{1,9},{5... | collective-permute-start | bytes 104 | tf_op jit(solution)/shard_map/ppermute | solution.py:21
  61.5 14.8 %collective-permute-start.18 = (bf16[4,128,512]{2,1,0:T(8,128)(2,1)S(1)}, bf16[4,128,512]{2,1,0:T(8,128)(2,1)S(1)}, u32[]{:S(2)}, u32[]{:S(2)}) collective-permute-start(bf16[4,128,512]{2,1,0:T(8,128)(2,1)S(1)} %collective-permute-done.17.refs_1_.refs_3_), channel_id=1, source_target_pairs={{0,2},{1,3},{2,0},{3,1},{4,6},{5,7},{6,4},{7,5},{8,10},{9,11},{10,... | collective-permute-start | bytes 1572872 | tf_op jit(solution)/shard_map/ppermute | solution.py:26
  63.0 24.5 %collective-permute-start.8 = (bf16[4,128,512]{2,1,0:T(8,128)(2,1)S(1)}, bf16[4,128,512]{2,1,0:T(8,128)(2,1)S(1)}, u32[]{:S(2)}, u32[]{:S(2)}) collective-permute-start(bf16[4,128,512]{2,1,0:T(8,128)(2,1)S(1)} %collective-permute-done.7.refs_1_), channel_id=1, source_target_pairs={{0,2},{1,3},{2,0},{3,1},{4,6},{5,7},{6,4},{7,5},{8,10},{9,11},{10,... | collective-permute-start | bytes 1572872 | tf_op jit(solution)/shard_map/ppermute | solution.py:26
  63.6 35.1 %collective-permute-start.14 = (bf16[4,128,512]{2,1,0:T(8,128)(2,1)S(1)}, bf16[4,128,512]{2,1,0:T(8,128)(2,1)S(1)}, u32[]{:S(2)}, u32[]{:S(2)}) collective-permute-start(bf16[4,128,512]{2,1,0:T(8,128)(2,1)S(1)} %collective-permute-done.13.refs_1_.refs_3_), channel_id=1, source_target_pairs={{0,2},{1,3},{2,0},{3,1},{4,6},{5,7},{6,4},{7,5},{8,10},{9,11},{10,... | collective-permute-start | bytes 1572872 | tf_op jit(solution)/shard_map/ppermute | solution.py:26
  65.1 42.3 %collective-permute-start.4 = (bf16[4,128,512]{2,1,0:T(8,128)(2,1)S(1)}, bf16[4,128,512]{2,1,0:T(8,128)(2,1)S(1)}, u32[]{:S(2)}, u32[]{:S(2)}) collective-permute-start(bf16[4,128,512]{2,1,0:T(8,128)(2,1)S(1)} %collective-permute-done.3.refs_1_), channel_id=1, source_target_pairs={{0,2},{1,3},{2,0},{3,1},{4,6},{5,7},{6,4},{7,5},{8,10},{9,11},{10,... | collective-permute-start | bytes 1572872 | tf_op jit(solution)/shard_map/ppermute | solution.py:26
  76.3 31.2 %collective-permute-start.20 = (bf16[4,128,512]{2,1,0:T(8,128)(2,1)S(1)}, bf16[4,128,512]{2,1,0:T(8,128)(2,1)S(1)}, u32[]{:S(2)}, u32[]{:S(2)}) collective-permute-start(bf16[4,128,512]{2,1,0:T(8,128)(2,1)S(1)} %collective-permute-done.18.refs_2_.refs_4_), channel_id=1, source_target_pairs={{0,1},{1,0},{2,3},{3,2},{4,5},{5,4},{6,7},{7,6},{8,9},{9,8},{10,11... | collective-permute-start | bytes 1572872 | tf_op jit(solution)/shard_map/ppermute | solution.py:26
  76.3 39.2 %collective-permute-start.15 = (bf16[4,128,512]{2,1,0:T(8,128)(2,1)S(1)}, bf16[4,128,512]{2,1,0:T(8,128)(2,1)S(1)}, u32[]{:S(2)}, u32[]{:S(2)}) collective-permute-start(bf16[4,128,512]{2,1,0:T(8,128)(2,1)S(1)} %collective-permute-done.13.refs_1_.refs_3_), channel_id=1, source_target_pairs={{0,1},{1,0},{2,3},{3,2},{4,5},{5,4},{6,7},{7,6},{8,9},{9,8},{10,11... | collective-permute-start | bytes 1572872 | tf_op jit(solution)/shard_map/ppermute | solution.py:26
  87.5 28.8 %collective-permute-start.5 = (bf16[4,128,512]{2,1,0:T(8,128)(2,1)S(1)}, bf16[4,128,512]{2,1,0:T(8,128)(2,1)S(1)}, u32[]{:S(2)}, u32[]{:S(2)}) collective-permute-start(bf16[4,128,512]{2,1,0:T(8,128)(2,1)S(1)} %collective-permute-done.3.refs_1_), channel_id=1, source_target_pairs={{0,1},{1,0},{2,3},{3,2},{4,5},{5,4},{6,7},{7,6},{8,9},{9,8},{10,11... | collective-permute-start | bytes 1572872 | tf_op jit(solution)/shard_map/ppermute | solution.py:26
  98.8 18.8 %collective-permute-start.10 = (bf16[4,128,512]{2,1,0:T(8,128)(2,1)S(1)}, bf16[4,128,512]{2,1,0:T(8,128)(2,1)S(1)}, u32[]{:S(2)}, u32[]{:S(2)}) collective-permute-start(bf16[4,128,512]{2,1,0:T(8,128)(2,1)S(1)} %collective-permute-done.8.refs_2_), channel_id=1, source_target_pairs={{0,1},{1,0},{2,3},{3,2},{4,5},{5,4},{6,7},{7,6},{8,9},{9,8},{10,11... | collective-permute-start | bytes 1572872 | tf_op jit(solution)/shard_map/ppermute | solution.py:26
  107.4 15.1 %collective-permute-start.16 = (bf16[4,128,512]{2,1,0:T(8,128)(2,1)S(1)}, bf16[4,128,512]{2,1,0:T(8,128)(2,1)S(1)}, u32[]{:S(2)}, u32[]{:S(2)}) collective-permute-start(bf16[4,128,512]{2,1,0:T(8,128)(2,1)S(1)} %collective-permute-done.14.refs_2_.refs_4_), channel_id=1, source_target_pairs={{0,1},{1,0},{2,3},{3,2},{4,5},{5,4},{6,7},{7,6},{8,9},{9,8},{10,11... | collective-permute-start | bytes 1572872 | tf_op jit(solution)/shard_map/ppermute | solution.py:26
  115.5 14.9 %collective-permute-start.1 = (bf16[4,128,512]{2,1,0:T(8,128)(2,1)S(1)}, bf16[4,128,512]{2,1,0:T(8,128)(2,1)S(1)}, u32[]{:S(2)}, u32[]{:S(2)}) collective-permute-start(bf16[4,128,512]{2,1,0:T(8,128)(2,1)S(1)} %get-tuple-element.64), channel_id=1, source_target_pairs={{0,4},{4,0},{8,12},{12,8},{16,20},{20,16},{24,28},{28,24},{1,5},{5... | collective-permute-start | bytes 1572872 | tf_op jit(solution)/shard_map/ppermute | solution.py:21
  116.3 25.3 %collective-permute-start.2 = (bf16[4,128,512]{2,1,0:T(8,128)(2,1)S(1)}, bf16[4,128,512]{2,1,0:T(8,128)(2,1)S(1)}, u32[]{:S(2)}, u32[]{:S(2)}) collective-permute-start(bf16[4,128,512]{2,1,0:T(8,128)(2,1)S(1)} %get-tuple-element.65), channel_id=1, source_target_pairs={{0,4},{4,0},{8,12},{12,8},{16,20},{20,16},{24,28},{28,24},{1,5},{5... | collective-permute-start | bytes 1572872 | tf_op jit(solution)/shard_map/ppermute | solution.py:21
  117.6 46.5 %collective-permute-start.24 = (bf16[4,128,512]{2,1,0:T(8,128)(2,1)S(1)}, bf16[4,128,512]{2,1,0:T(8,128)(2,1)S(1)}, u32[]{:S(2)}, u32[]{:S(2)}) collective-permute-start(bf16[4,128,512]{2,1,0:T(8,128)(2,1)S(1)} %get-tuple-element.73), channel_id=1, source_target_pairs={{0,4},{4,0},{8,12},{12,8},{16,20},{20,16},{24,28},{28,24},{1,5},{5... | collective-permute-start | bytes 1572872 | tf_op jit(solution)/shard_map/ppermute | solution.py:21
  119.8 55.5 %collective-permute-start.12 = (bf16[4,128,512]{2,1,0:T(8,128)(2,1)S(1)}, bf16[4,128,512]{2,1,0:T(8,128)(2,1)S(1)}, u32[]{:S(2)}, u32[]{:S(2)}) collective-permute-start(bf16[4,128,512]{2,1,0:T(8,128)(2,1)S(1)} %gather_held.11), channel_id=1, source_target_pairs={{0,4},{4,0},{8,12},{12,8},{16,20},{20,16},{24,28},{28,24},{1,5},{5... | collective-permute-start | bytes 1572872 | tf_op jit(solution)/shard_map/ppermute | solution.py:21
  122.6 63.9 %collective-permute-start.11 = (bf16[4,128,512]{2,1,0:T(8,128)(2,1)S(1)}, bf16[4,128,512]{2,1,0:T(8,128)(2,1)S(1)}, u32[]{:S(2)}, u32[]{:S(2)}) collective-permute-start(bf16[4,128,512]{2,1,0:T(8,128)(2,1)S(1)} %gather_held.10), channel_id=1, source_target_pairs={{0,4},{4,0},{8,12},{12,8},{16,20},{20,16},{24,28},{28,24},{1,5},{5... | collective-permute-start | bytes 1572872 | tf_op jit(solution)/shard_map/ppermute | solution.py:21
  130.3 75.3 %collective-permute-start.26 = (bf16[4,128,512]{2,1,0:T(8,128)(2,1)S(1)}, bf16[4,128,512]{2,1,0:T(8,128)(2,1)S(1)}, u32[]{:S(2)}, u32[]{:S(2)}) collective-permute-start(bf16[4,128,512]{2,1,0:T(8,128)(2,1)S(1)} %get-tuple-element.75), channel_id=1, source_target_pairs={{0,8},{4,12},{8,0},{12,4},{16,24},{20,28},{24,16},{28,20},{1,9},{5... | collective-permute-start | bytes 1572872 | tf_op jit(solution)/shard_map/ppermute | solution.py:21
  141.6 64.1 %collective-permute-start.28 = (bf16[4,128,512]{2,1,0:T(8,128)(2,1)S(1)}, bf16[4,128,512]{2,1,0:T(8,128)(2,1)S(1)}, u32[]{:S(2)}, u32[]{:S(2)}) collective-permute-start(bf16[4,128,512]{2,1,0:T(8,128)(2,1)S(1)} %get-tuple-element.77), channel_id=1, source_target_pairs={{0,12},{4,8},{8,4},{12,0},{16,28},{20,24},{24,20},{28,16},{1,13},{... | collective-permute-start | bytes 1572872 | tf_op jit(solution)/shard_map/ppermute | solution.py:21
  164.1 44.0 %collective-permute-start.23 = (bf16[4,128,512]{2,1,0:T(8,128)(2,1)S(1)}, bf16[4,128,512]{2,1,0:T(8,128)(2,1)S(1)}, u32[]{:S(2)}, u32[]{:S(2)}) collective-permute-start(bf16[4,128,512]{2,1,0:T(8,128)(2,1)S(1)} %get-tuple-element.72), channel_id=1, source_target_pairs={{0,4},{4,0},{8,12},{12,8},{16,20},{20,16},{24,28},{28,24},{1,5},{5... | collective-permute-start | bytes 1572872 | tf_op jit(solution)/shard_map/ppermute | solution.py:21
  175.3 32.8 %collective-permute-start.25 = (bf16[4,128,512]{2,1,0:T(8,128)(2,1)S(1)}, bf16[4,128,512]{2,1,0:T(8,128)(2,1)S(1)}, u32[]{:S(2)}, u32[]{:S(2)}) collective-permute-start(bf16[4,128,512]{2,1,0:T(8,128)(2,1)S(1)} %get-tuple-element.74), channel_id=1, source_target_pairs={{0,8},{4,12},{8,0},{12,4},{16,24},{20,28},{24,16},{28,20},{1,9},{5... | collective-permute-start | bytes 1572872 | tf_op jit(solution)/shard_map/ppermute | solution.py:21
  186.5 21.5 %collective-permute-start.27 = (bf16[4,128,512]{2,1,0:T(8,128)(2,1)S(1)}, bf16[4,128,512]{2,1,0:T(8,128)(2,1)S(1)}, u32[]{:S(2)}, u32[]{:S(2)}) collective-permute-start(bf16[4,128,512]{2,1,0:T(8,128)(2,1)S(1)} %get-tuple-element.76), channel_id=1, source_target_pairs={{0,12},{4,8},{8,4},{12,0},{16,28},{20,24},{24,20},{28,16},{1,13},{... | collective-permute-start | bytes 1572872 | tf_op jit(solution)/shard_map/ppermute | solution.py:21
  220.6 14.8 %collective-permute-start.32 = (bf16[512,512]{1,0:T(8,128)(2,1)}, bf16[512,512]{1,0:T(8,128)(2,1)S(1)}, u32[]{:S(2)}, u32[]{:S(2)}) collective-permute-start(bf16[512,512]{1,0:T(8,128)(2,1)} %get-tuple-element.98), channel_id=1, source_target_pairs={{0,4},{4,0},{8,12},{12,8},{16,20},{20,16},{24,28},{28,24},{1,5},{5... | collective-permute-start | bytes 1572872 | tf_op jit(solution)/shard_map/ppermute | solution.py:21
  221.4 20.0 %collective-permute-start.33 = (bf16[512,512]{1,0:T(8,128)(2,1)}, bf16[512,512]{1,0:T(8,128)(2,1)}, u32[]{:S(2)}, u32[]{:S(2)}) collective-permute-start(bf16[512,512]{1,0:T(8,128)(2,1)} %get-tuple-element.99), channel_id=1, source_target_pairs={{0,8},{4,12},{8,0},{12,4},{16,24},{20,28},{24,16},{28,20},{1,9},{5... | collective-permute-start | bytes 1572872 | tf_op jit(solution)/shard_map/ppermute | solution.py:21
  222.9 25.6 %collective-permute-start.34 = (bf16[512,512]{1,0:T(8,128)(2,1)}, bf16[512,512]{1,0:T(8,128)(2,1)}, u32[]{:S(2)}, u32[]{:S(2)}) collective-permute-start(bf16[512,512]{1,0:T(8,128)(2,1)} %get-tuple-element.100), channel_id=1, source_target_pairs={{0,12},{4,8},{8,4},{12,0},{16,28},{20,24},{24,20},{28,16},{1,13},{... | collective-permute-start | bytes 1572872 | tf_op jit(solution)/shard_map/ppermute | solution.py:21
  233.0 26.3 %collective-permute-start.45 = (bf16[512,512]{1,0:T(8,128)(2,1)}, bf16[512,512]{1,0:T(8,128)(2,1)}, u32[]{:S(2)}, u32[]{:S(2)}) collective-permute-start(bf16[512,512]{1,0:T(8,128)(2,1)} %get-tuple-element.112), channel_id=1, source_target_pairs={{0,4},{4,0},{8,12},{12,8},{16,20},{20,16},{24,28},{28,24},{1,5},{5... | collective-permute-start | bytes 1572872 | tf_op jit(solution)/shard_map/ppermute | solution.py:21
  233.7 26.3 %collective-permute-start.46 = (bf16[512,512]{1,0:T(8,128)(2,1)}, bf16[512,512]{1,0:T(8,128)(2,1)}, u32[]{:S(2)}, u32[]{:S(2)}) collective-permute-start(bf16[512,512]{1,0:T(8,128)(2,1)} %get-tuple-element.113), channel_id=1, source_target_pairs={{0,8},{4,12},{8,0},{12,4},{16,24},{20,28},{24,16},{28,20},{1,9},{5... | collective-permute-start | bytes 1572872 | tf_op jit(solution)/shard_map/ppermute | solution.py:21
  236.2 32.8 %collective-permute-start.47 = (bf16[512,512]{1,0:T(8,128)(2,1)}, bf16[512,512]{1,0:T(8,128)(2,1)}, u32[]{:S(2)}, u32[]{:S(2)}) collective-permute-start(bf16[512,512]{1,0:T(8,128)(2,1)} %get-tuple-element.114), channel_id=1, source_target_pairs={{0,12},{4,8},{8,4},{12,0},{16,28},{20,24},{24,20},{28,16},{1,13},{... | collective-permute-start | bytes 1572872 | tf_op jit(solution)/shard_map/ppermute | solution.py:21
  241.5 38.3 %collective-permute-start.42 = (bf16[512,512]{1,0:T(8,128)(2,1)S(1)}, bf16[512,512]{1,0:T(8,128)(2,1)S(1)}, u32[]{:S(2)}, u32[]{:S(2)}) collective-permute-start(bf16[512,512]{1,0:T(8,128)(2,1)S(1)} %get-tuple-element.108), channel_id=1, source_target_pairs={{0,4},{4,0},{8,12},{12,8},{16,20},{20,16},{24,28},{28,24},{1,5},{5... | collective-permute-start | bytes 1572872 | tf_op jit(solution)/shard_map/ppermute | solution.py:21
  251.1 63.0 %collective-permute-start.35 = (bf16[8,128,512]{2,1,0:T(8,128)(2,1)S(1)}, bf16[8,128,512]{2,1,0:T(8,128)(2,1)S(1)}, u32[]{:S(2)}, u32[]{:S(2)}) collective-permute-start(bf16[8,128,512]{2,1,0:T(8,128)(2,1)S(1)} %get-tuple-element.102), channel_id=1, source_target_pairs={{0,1},{1,0},{2,3},{3,2},{4,5},{5,4},{6,7},{7,6},{8,9},{9,8},{10,11... | collective-permute-start | bytes 3145736 | tf_op jit(solution)/shard_map/ppermute | solution.py:26
  259.3 31.7 %collective-permute-start.29 = (bf16[512,512]{1,0:T(8,128)(2,1)S(1)}, bf16[512,512]{1,0:T(8,128)(2,1)S(1)}, u32[]{:S(2)}, u32[]{:S(2)}) collective-permute-start(bf16[512,512]{1,0:T(8,128)(2,1)S(1)} %get-tuple-element.94), channel_id=1, source_target_pairs={{0,4},{4,0},{8,12},{12,8},{16,20},{20,16},{24,28},{28,24},{1,5},{5... | collective-permute-start | bytes 1572872 | tf_op jit(solution)/shard_map/ppermute | solution.py:21
  271.3 43.7 %collective-permute-start.48 = (bf16[8,128,512]{2,1,0:T(8,128)(2,1)S(1)}, bf16[8,128,512]{2,1,0:T(8,128)(2,1)S(1)}, u32[]{:S(2)}, u32[]{:S(2)}) collective-permute-start(bf16[8,128,512]{2,1,0:T(8,128)(2,1)S(1)} %get-tuple-element.116), channel_id=1, source_target_pairs={{0,1},{1,0},{2,3},{3,2},{4,5},{5,4},{6,7},{7,6},{8,9},{9,8},{10,11... | collective-permute-start | bytes 3145736 | tf_op jit(solution)/shard_map/ppermute | solution.py:26
  273.4 28.9 %collective-permute-start.51 = (bf16[512,512]{1,0:T(8,128)(2,1)S(1)}, bf16[512,512]{1,0:T(8,128)(2,1)S(1)}, u32[]{:S(2)}, u32[]{:S(2)}) collective-permute-start(bf16[512,512]{1,0:T(8,128)(2,1)S(1)} %get-tuple-element.118), channel_id=1, source_target_pairs={{0,4},{4,0},{8,12},{12,8},{16,20},{20,16},{24,28},{28,24},{1,5},{5... | collective-permute-start | bytes 1572872 | tf_op jit(solution)/shard_map/ppermute | solution.py:21
  279.8 32.7 %collective-permute-start.38 = (bf16[512,512]{1,0:T(8,128)(2,1)S(1)}, bf16[512,512]{1,0:T(8,128)(2,1)S(1)}, u32[]{:S(2)}, u32[]{:S(2)}) collective-permute-start(bf16[512,512]{1,0:T(8,128)(2,1)S(1)} %get-tuple-element.104), channel_id=1, source_target_pairs={{0,4},{4,0},{8,12},{12,8},{16,20},{20,16},{24,28},{28,24},{1,5},{5... | collective-permute-start | bytes 1572872 | tf_op jit(solution)/shard_map/ppermute | solution.py:21
  291.0 26.0 %collective-permute-start.43 = (bf16[8,128,512]{2,1,0:T(8,128)(2,1)S(1)}, bf16[8,128,512]{2,1,0:T(8,128)(2,1)S(1)}, u32[]{:S(2)}, u32[]{:S(2)}) collective-permute-start(bf16[8,128,512]{2,1,0:T(8,128)(2,1)S(1)} %get-tuple-element.110), channel_id=1, source_target_pairs={{0,1},{1,0},{2,3},{3,2},{4,5},{5,4},{6,7},{7,6},{8,9},{9,8},{10,11... | collective-permute-start | bytes 3145736 | tf_op jit(solution)/shard_map/ppermute | solution.py:26
  302.3 15.8 %collective-permute-start.30 = (bf16[8,128,512]{2,1,0:T(8,128)(2,1)S(1)}, bf16[8,128,512]{2,1,0:T(8,128)(2,1)S(1)}, u32[]{:S(2)}, u32[]{:S(2)}) collective-permute-start(bf16[8,128,512]{2,1,0:T(8,128)(2,1)S(1)} %get-tuple-element.96), channel_id=1, source_target_pairs={{0,1},{1,0},{2,3},{3,2},{4,5},{5,4},{6,7},{7,6},{8,9},{9,8},{10,11... | collective-permute-start | bytes 3145736 | tf_op jit(solution)/shard_map/ppermute | solution.py:26
  315.0 60.5 %collective-permute-start.36 = (bf16[4,128,512]{2,1,0:T(8,128)(2,1)S(1)}, bf16[4,128,512]{2,1,0:T(8,128)(2,1)S(1)}, u32[]{:S(2)}, u32[]{:S(2)}) collective-permute-start(bf16[4,128,512]{2,1,0:T(8,128)(2,1)S(1)} %slice.160), channel_id=1, source_target_pairs={{0,2},{1,3},{2,0},{3,1},{4,6},{5,7},{6,4},{7,5},{8,10},{9,11},{10,... | collective-permute-start | bytes 1572872 | tf_op jit(solution)/shard_map/ppermute | solution.py:26
  317.1 24.1 %collective-permute-start.49 = (bf16[4,128,512]{2,1,0:T(8,128)(2,1)S(1)}, bf16[4,128,512]{2,1,0:T(8,128)(2,1)S(1)}, u32[]{:S(2)}, u32[]{:S(2)}) collective-permute-start(bf16[4,128,512]{2,1,0:T(8,128)(2,1)S(1)} %slice.157), channel_id=1, source_target_pairs={{0,2},{1,3},{2,0},{3,1},{4,6},{5,7},{6,4},{7,5},{8,10},{9,11},{10,... | collective-permute-start | bytes 1572872 | tf_op jit(solution)/shard_map/ppermute | solution.py:26
  318.0 67.7 %collective-permute-start.44 = (bf16[4,128,512]{2,1,0:T(8,128)(2,1)S(1)}, bf16[4,128,512]{2,1,0:T(8,128)(2,1)S(1)}, u32[]{:S(2)}, u32[]{:S(2)}) collective-permute-start(bf16[4,128,512]{2,1,0:T(8,128)(2,1)S(1)} %slice.158), channel_id=1, source_target_pairs={{0,2},{1,3},{2,0},{3,1},{4,6},{5,7},{6,4},{7,5},{8,10},{9,11},{10,... | collective-permute-start | bytes 1572872 | tf_op jit(solution)/shard_map/ppermute | solution.py:26
  320.1 83.2 %collective-permute-start.31 = (bf16[4,128,512]{2,1,0:T(8,128)(2,1)S(1)}, bf16[4,128,512]{2,1,0:T(8,128)(2,1)S(1)}, u32[]{:S(2)}, u32[]{:S(2)}) collective-permute-start(bf16[4,128,512]{2,1,0:T(8,128)(2,1)S(1)} %slice.161), channel_id=1, source_target_pairs={{0,2},{1,3},{2,0},{3,1},{4,6},{5,7},{6,4},{7,5},{8,10},{9,11},{10,... | collective-permute-start | bytes 1572872 | tf_op jit(solution)/shard_map/ppermute | solution.py:26
  321.2 53.7 %collective-permute-start.53 = (bf16[4,128,512]{2,1,0:T(8,128)(2,1)S(1)}, bf16[4,128,512]{2,1,0:T(8,128)(2,1)S(1)}, u32[]{:S(2)}, u32[]{:S(2)}) collective-permute-start(bf16[4,128,512]{2,1,0:T(8,128)(2,1)S(1)} %slice.156), channel_id=1, source_target_pairs={{0,2},{1,3},{2,0},{3,1},{4,6},{5,7},{6,4},{7,5},{8,10},{9,11},{10,... | collective-permute-start | bytes 1572872 | tf_op jit(solution)/shard_map/ppermute | solution.py:26
  341.1 44.0 %collective-permute-start.40 = (bf16[4,128,512]{2,1,0:T(8,128)(2,1)S(1)}, bf16[4,128,512]{2,1,0:T(8,128)(2,1)S(1)}, u32[]{:S(2)}, u32[]{:S(2)}) collective-permute-start(bf16[4,128,512]{2,1,0:T(8,128)(2,1)S(1)} %slice.159), channel_id=1, source_target_pairs={{0,2},{1,3},{2,0},{3,1},{4,6},{5,7},{6,4},{7,5},{8,10},{9,11},{10,... | collective-permute-start | bytes 1572872 | tf_op jit(solution)/shard_map/ppermute | solution.py:26
  374.9 28.2 %collective-permute-start.50 = (bf16[4,128,512]{2,1,0:T(8,128)(2,1)S(1)}, bf16[4,128,512]{2,1,0:T(8,128)(2,1)S(1)}, u32[]{:S(2)}, u32[]{:S(2)}) collective-permute-start(bf16[4,128,512]{2,1,0:T(8,128)(2,1)S(1)} %fusion.1), channel_id=1, source_target_pairs={{0,16},{4,20},{8,24},{12,28},{16,0},{20,4},{24,8},{28,12},{1,17},{... | collective-permute-start | bytes 1572872 | tf_op jit(solution)/shard_map/ppermute | solution.py:21
  375.5 27.5 %collective-permute-start.54 = (bf16[4,128,512]{2,1,0:T(8,128)(2,1)S(1)}, bf16[4,128,512]{2,1,0:T(8,128)(2,1)S(1)}, u32[]{:S(2)}, u32[]{:S(2)}) collective-permute-start(bf16[4,128,512]{2,1,0:T(8,128)(2,1)S(1)} %fusion), channel_id=1, source_target_pairs={{0,8},{4,12},{8,0},{12,4},{16,24},{20,28},{24,16},{28,20},{1,9},{5... | collective-permute-start | bytes 1572872 | tf_op jit(solution)/shard_map/ppermute | solution.py:21
  385.1 36.4 %collective-permute-start.37 = (bf16[4,128,512]{2,1,0:T(8,128)(2,1)S(1)}, bf16[4,128,512]{2,1,0:T(8,128)(2,1)S(1)}, u32[]{:S(2)}, u32[]{:S(2)}) collective-permute-start(bf16[4,128,512]{2,1,0:T(8,128)(2,1)S(1)} %fusion.5), channel_id=1, source_target_pairs={{0,16},{4,20},{8,24},{12,28},{16,0},{20,4},{24,8},{28,12},{1,17},{... | collective-permute-start | bytes 1572872 | tf_op jit(solution)/shard_map/ppermute | solution.py:21
  385.7 35.8 %collective-permute-start.41 = (bf16[4,128,512]{2,1,0:T(8,128)(2,1)S(1)}, bf16[4,128,512]{2,1,0:T(8,128)(2,1)S(1)}, u32[]{:S(2)}, u32[]{:S(2)}) collective-permute-start(bf16[4,128,512]{2,1,0:T(8,128)(2,1)S(1)} %fusion.4), channel_id=1, source_target_pairs={{0,8},{4,12},{8,0},{12,4},{16,24},{20,28},{24,16},{28,20},{1,9},{5... | collective-permute-start | bytes 1572872 | tf_op jit(solution)/shard_map/ppermute | solution.py:21
  (62 other events, 918.3 us)

commit v7 on v4

--- a/solution.py
+++ b/solution.py
@@ -232,7 +232,7 @@
     losses, top_out, inv_out = refs[:3]
     kept = refs[3:-4]
     logits, grads, tiles, sems = refs[-4:]
-    count, width = x.shape
+    count, _ = x.shape
     scale = D ** (-0.5)
     for j in range(0, count, lanes):
         turn = (j // lanes) % 2
@@ -267,7 +267,7 @@
             s, k = n // cap, n % cap
             target = jnp.where(rel == base[n], 1.0, 0.0)
             grads[s, k * TILE : (k + 1) * TILE, at] = (ref[...] * inv - target).astype(BF)
-    step = width // parts
+    step = tiles.shape[-1]
     sources = [grads.at[s] for s in range(group)] + [tiles.at[s] for s in range(group)]
     copies = [
         pltpu.make_async_copy(a, b, sems.at[n]) for n, (a, b) in enumerate(zip(sources, kept))
@@ -281,13 +281,13 @@
         copy.wait()
 
 
-def far_grads(base, x, pos, stats, rows, cap, parts, lanes=256):
+def far_grads(base, x, pos, stats, rows, cap, parts, first, lanes=256):
     group = len(rows)
     rows = [r for row in rows for r in row]
-    count, width = x.shape
+    count, _ = x.shape
     size = rows[0].shape[0]
     outs = [((1, count), F32)] * 3 + [((size, count), BF)] * group
-    outs += [((size, width // parts), BF)] * group
+    outs += [((size, first), BF)] * group
     got = pl.pallas_call(
         functools.partial(far_kernel, group, cap, lanes, parts, len(stats) // 3),
         out_shape=[jax.ShapeDtypeStruct(*o) for o in outs[:3]]
@@ -297,7 +297,7 @@
         scratch_shapes=[
             pltpu.VMEM((2, group * size, lanes), F32),
             pltpu.VMEM((group, size, count), BF),
-            pltpu.VMEM((group, size, width // parts), BF),
+            pltpu.VMEM((group, size, first), BF),
             pltpu.SemaphoreType.DMA((2 * group,)),
         ],
         compiler_params=grant(20),
@@ -306,24 +306,31 @@
     return got[:3], got[3 : 3 + group], got[3 + group :]
 
 
+def far_widths(width):
+    most = width * 3 // 8
+    return [most, most, width - 2 * most]
+
+
 def far_tiles_kernel(group, first, x, *refs):
     grads, tiles = refs[:group], refs[group:]
-    step = tiles[0].shape[1]
+    at = first
     for n, tile in enumerate(tiles):
-        i = first + n // group
+        step = tile.shape[1]
         tile[...] = jnp.dot(
-            grads[n % group][...], x[:, i * step : (i + 1) * step], preferred_element_type=F32
+            grads[n % group][...], x[:, at : at + step], preferred_element_type=F32
         ).astype(BF)
-
-
-def far_tiles(x, grads, parts):
+        if n % group == group - 1:
+            at += step
+
+
+def far_tiles(x, grads, widths):
     group = len(grads)
-    shape = (grads[0].shape[0], x.shape[1] // parts)
+    shapes = [(grads[0].shape[0], w) for w in widths[1:] for _ in range(group)]
     got = pl.pallas_call(
-        functools.partial(far_tiles_kernel, group, 1),
-        out_shape=[jax.ShapeDtypeStruct(shape, BF)] * (group * (parts - 1)),
+        functools.partial(far_tiles_kernel, group, widths[0]),
+        out_shape=[jax.ShapeDtypeStruct(shape, BF) for shape in shapes],
         in_specs=[VM] * (1 + group),
-        out_specs=[VM] * (group * (parts - 1)),
+        out_specs=[VM] * len(shapes),
         compiler_params=grant(6),
         name="far_tiles",
     )(x, *grads)
@@ -440,6 +447,7 @@
     me = d.reshape(1)
     shifts = list(range(half - 1, 0, -1))
     evens = list(range(2, half, 2))
+    widths = far_widths(width)
     columns = [slice(i * step, (i + 1) * step) for i in range(parts)]
 
     wanted = request_table(candidates[0], blocks_dev, cap, proto_count)
@@ -512,9 +520,9 @@
         logits.update(zip(group, got))
         sums += [top, total, hit]
     stats, far_g, first = far_grads(
-        bases(other, 1 - h, range(half)), designs, pos, sums, far_rows, cap, parts
+        bases(other, 1 - h, range(half)), designs, pos, sums, far_rows, cap, parts, widths[0]
     )
-    back_tiles = [first] + far_tiles(designs, far_g, parts)
+    back_tiles = [first] + far_tiles(designs, far_g, widths)
     losses, top, inv = stats
     own_g, own_tiles = [], []
     for s in range(half):
@@ -537,7 +545,7 @@
         keep, give = collect(spots(tables), tiles, cap, kept)
         came = xor_design(give, 1)
         keep = keep + came.astype(F32)
-        keep = keep.reshape(lanes, quarter, TILE, step)
+        keep = keep.reshape(lanes, quarter, TILE, keep.shape[-1])
         onward = [keep[ys].astype(BF) for ys in range(1, lanes)]
         total = keep[0]
         for ys in range(1, lanes):
@@ -548,11 +556,14 @@
     result = []
     dgrad = []
     far_tables = [asking[s] for s in range(half)]
+    crossed = []
+    for tiles in back_tiles:
+        tiles = [tiles[0]] + [xor_proto(tiles[s], s) for s in range(1, half)]
+        total = reduce_shard(far_tables, tiles)
+        crossed.append(xor_proto(total.astype(BF), half))
+    crossed = jnp.concatenate(crossed, axis=-1)
     for i in range(parts):
-        tiles = [back_tiles[i][0]]
-        tiles += [xor_proto(back_tiles[i][s], s) for s in range(1, half)]
-        total = reduce_shard(far_tables, tiles)
-        landed = [xor_proto(total.astype(BF), half)]
+        landed = [crossed[:, :, columns[i]]]
         for u in evens:
             tile = xor_proto(own_tiles[u ^ 1][i], 1)
             total = reduce_shard([near[u], beside[u]], [own_tiles[u][i], tile])

time: 422 us -> 408 us (0.967)
  waiting for transfers between devices: 282 us -> 256 us
  starting transfers between devices: 45.1 us -> 52.6 us
    ppermute x24 -> x26, waiting for transfers between devices: 98 us -> 76 us  [xor_design(): return lax.ppermute(x, 'design', [(i, i ^ shift) for i in range(count)])]
    ppermute x31 -> x35, starting transfers between devices: 31.8 us -> 36.8 us  [xor_proto(): return lax.ppermute(x, 'proto', [(i, i ^ shift) for i in range(count)])]
    ppermute x31 -> x35, waiting for transfers between devices: 184 us -> 180 us  [xor_proto(): return lax.ppermute(x, 'proto', [(i, i ^ shift) for i in range(count)])]
    unnamed x110 -> x148, local copies, waits for them, and re-layouts: 11.7 us -> 14.7 us
    ppermute x24 -> x26, starting transfers between devices: 13.3 us -> 15.8 us  [xor_design(): return lax.ppermute(x, 'design', [(i, i ^ shift) for i in range(count)])]
    pallas_call x6 -> x7, Pallas kernels: 10.2 us -> 10.4 us  [collect(): pl.pallas_call(functools.partial(collect_kernel, n, cap), out_shape=[jax....]
  transfers between devices with their start and end apart: 55 -> 61, of which waited for: 26 -> 27; matrix products, arithmetic and copies ran while one was open for 1% -> 2% of each run, Pallas kernels for 14% -> 15%
where the time goes in v7:
time: 408 us
  waiting for transfers between devices  256 us (63%)
  Pallas kernels  72.8 us (18%)
  starting transfers between devices  52.6 us (13%)
  local copies, waits for them, and re-layouts  17 us (4%)
  other arithmetic  7.76 us (2%)
    ppermute x35, waiting for transfers between devices, xor_proto(): return lax.ppermute(x, 'proto', [(i, i ^ shift) for i in range(count)])  180 us
    ppermute x26, waiting for transfers between devices, xor_design(): return lax.ppermute(x, 'design', [(i, i ^ shift) for i in range(count)])  76 us
    ppermute x35, starting transfers between devices, xor_proto(): return lax.ppermute(x, 'proto', [(i, i ^ shift) for i in range(count)])  36.8 us
    ppermute x26, starting transfers between devices, xor_design(): return lax.ppermute(x, 'design', [(i, i ^ shift) for i in range(count)])  15.8 us
    pallas_call x8, Pallas kernels, gather_held(): pl.pallas_call(functools.partial(gather_held_kernel, len(srcs), n, quarte...  15.1 us
    unnamed x148, local copies, waits for them, and re-layouts  14.7 us
    pallas_call x1, Pallas kernels, far_grads(): pl.pallas_call(functools.partial(far_kernel, group, cap, lanes, parts, le...  12.6 us
    pallas_call x2, Pallas kernels, own_logits(): pl.pallas_call(functools.partial(own_kernel, group, cap, lanes, parts), o...  10.5 us
  transfers between devices with their start and end apart: 61, of which 27 were waited for; matrix products, arithmetic and copies ran while one was open for 2% of the time, Pallas kernels for 15%

profile of v7, /device:TPU:0, one launch (start us, length us, event | category | flops | bytes accessed | tf_op | source)
XLA Modules:
  0.0 407.6 jit_solution(10582258763407221377)
XLA Ops:
  0.6 1.7 dynamic-slice_convert_fusion
  2.5 4.1 %collective-permute-start.17 = (bf16[4,128,512]{2,1,0:T(8,128)(2,1)S(1)}, bf16[4,128,512]{2,1,0:T(8,128)(2,1)S(1)}, u32[]{:S(2)}, u32[]{:S(2)}) collective-permute-start(bf16[4,128,512]{2,1,0:T(8,128)(2,1)S(1)} %get-tuple-element.143), channel_id=1, source_target_pairs={{0,16},{4,20},{8,24},{12,28},{16,0},{20,4},{24,8},{28,12},{1,17},{... | collective-permute-start | bytes 1572872 | tf_op jit(solution)/shard_map/ppermute | solution.py:21
  9.2 2.8 collective-permute-start.21
  12.1 41.4 %collective-permute-done.21.refs_0_ = s32[4]{0:T(128)S(1)} collective-permute-done((s32[4]{0:T(128)S(1)}, s32[4]{0:T(128)S(1)}, u32[]{:S(2)}, u32[]{:S(2)}) %collective-permute-start.21) | collective-permute-done | bytes 48 | tf_op jit(solution)/shard_map/ppermute | solution.py:21
  55.0 2.1 collective-permute-done.22.refs_1_
  57.6 3.1 collective-permute-done
  64.8 10.6 %collective-permute-done.18.refs_2_.refs_4_ = bf16[4,128,512]{2,1,0:T(8,128)(2,1)S(1)} collective-permute-done((bf16[4,128,512]{2,1,0:T(8,128)(2,1)S(1)}, bf16[4,128,512]{2,1,0:T(8,128)(2,1)S(1)}, u32[]{:S(2)}, u32[]{:S(2)}) %collective-permute-start.18) | collective-permute-done | bytes 524320 | tf_op jit(solution)/shard_map/ppermute | solution.py:26
  76.0 10.7 %collective-permute-done.8.refs_2_ = bf16[4,128,512]{2,1,0:T(8,128)(2,1)S(1)} collective-permute-done((bf16[4,128,512]{2,1,0:T(8,128)(2,1)S(1)}, bf16[4,128,512]{2,1,0:T(8,128)(2,1)S(1)}, u32[]{:S(2)}, u32[]{:S(2)}) %collective-permute-start.8) | collective-permute-done | bytes 524320 | tf_op jit(solution)/shard_map/ppermute | solution.py:26
  86.7 11.2 %collective-permute-done.14.refs_2_.refs_4_ = bf16[4,128,512]{2,1,0:T(8,128)(2,1)S(1)} collective-permute-done((bf16[4,128,512]{2,1,0:T(8,128)(2,1)S(1)}, bf16[4,128,512]{2,1,0:T(8,128)(2,1)S(1)}, u32[]{:S(2)}, u32[]{:S(2)}) %collective-permute-start.14) | collective-permute-done | bytes 524320 | tf_op jit(solution)/shard_map/ppermute | solution.py:26
  98.0 7.5 %collective-permute-done.4.refs_2_ = bf16[4,128,512]{2,1,0:T(8,128)(2,1)S(1)} collective-permute-done((bf16[4,128,512]{2,1,0:T(8,128)(2,1)S(1)}, bf16[4,128,512]{2,1,0:T(8,128)(2,1)S(1)}, u32[]{:S(2)}, u32[]{:S(2)}) %collective-permute-start.4) | collective-permute-done | bytes 524320 | tf_op jit(solution)/shard_map/ppermute | solution.py:26
  106.1 3.4 copy-done.1
  110.3 3.2 gather_held.15
  121.3 3.2 gather_held.14
  124.5 3.9 collective-permute-done.1
  129.1 10.5 %collective-permute-done.2 = bf16[4,128,512]{2,1,0:T(8,128)(2,1)S(1)} collective-permute-done((bf16[4,128,512]{2,1,0:T(8,128)(2,1)S(1)}, bf16[4,128,512]{2,1,0:T(8,128)(2,1)S(1)}, u32[]{:S(2)}, u32[]{:S(2)}) %collective-permute-start.2) | collective-permute-done | bytes 524320 | tf_op jit(solution)/shard_map/ppermute | solution.py:21
  140.4 21.8 %collective-permute-done.24 = bf16[4,128,512]{2,1,0:T(8,128)(2,1)S(1)} collective-permute-done((bf16[4,128,512]{2,1,0:T(8,128)(2,1)S(1)}, bf16[4,128,512]{2,1,0:T(8,128)(2,1)S(1)}, u32[]{:S(2)}, u32[]{:S(2)}) %collective-permute-start.24) | collective-permute-done | bytes 524320 | tf_op jit(solution)/shard_map/ppermute | solution.py:21
  162.7 10.7 %collective-permute-done.12 = bf16[4,128,512]{2,1,0:T(8,128)(2,1)S(1)} collective-permute-done((bf16[4,128,512]{2,1,0:T(8,128)(2,1)S(1)}, bf16[4,128,512]{2,1,0:T(8,128)(2,1)S(1)}, u32[]{:S(2)}, u32[]{:S(2)}) %collective-permute-start.12) | collective-permute-done | bytes 524320 | tf_op jit(solution)/shard_map/ppermute | solution.py:21
  174.1 10.5 %collective-permute-done.11 = bf16[4,128,512]{2,1,0:T(8,128)(2,1)S(1)} collective-permute-done((bf16[4,128,512]{2,1,0:T(8,128)(2,1)S(1)}, bf16[4,128,512]{2,1,0:T(8,128)(2,1)S(1)}, u32[]{:S(2)}, u32[]{:S(2)}) %collective-permute-start.11) | collective-permute-done | bytes 524320 | tf_op jit(solution)/shard_map/ppermute | solution.py:21
  189.3 6.9 %own_logits.2 = (f32[512,1024]{1,0:T(8,128)}, f32[512,1024]{1,0:T(8,128)}, f32[512,1024]{1,0:T(8,128)}, f32[1,1024]{1,0:T(1,128)S(1)}, f32[1,1024]{1,0:T(1,128)S(1)}, /*index=5*/f32[1,1024]{1,0:T(1,128)S(1)}) custom-call(s32[12]{0:T(128)S(1)} %pad_add_fusion.2.base, bf16[1024,1024]{1,0:T(8,128)(2,1)S(1)} %copy-done, s32[1,1024]{1,0:T(1,128)S(1)} %bitcast.106, ...), custom_call_target="tpu_custom_call" | custom-call | tf_op jit(solution)/shard_map/own_logits/pallas_call | solution.py:213
  199.2 3.6 own_logits.3
  202.9 3.2 collective-permute-done.23
  206.2 12.6 %far_grads.1 = (f32[1,1024]{1,0:T(1,128)}, f32[1,1024]{1,0:T(1,128)S(1)}, f32[1,1024]{1,0:T(1,128)S(1)}, bf16[512,1024]{1,0:T(8,128)(2,1)}, bf16[512,1024]{1,0:T...) custom-call(s32[16]{0:T(128)S(1)} %pad_add_fusion.1.base, ...), custom_call_target="tpu_custom_call" | custom-call | tf_op jit(solution)/shard_map/far_grads/pallas_call | solution.py:291
  224.3 4.3 %far_tiles.1 = (bf16[512,384]{1,0:T(8,128)(2,1)S(1)}, bf16[512,384]{1,0:T(8,128)(2,1)S(1)}, bf16[512,384]{1,0:T(8,128)(2,1)S(1)}, bf16[512,384]{1,0:T(8,128)(2,1...) custom-call(bf16[1024,1024]{1,0:T(8,128)(2,1)S(1)} %copy-done, ...), custom_call_target="tpu_custom_call" | custom-call | tf_op jit(solution)/shard_map/far_tiles/pallas_call | solution.py:329
  235.8 3.2 collective-permute-done.51.refs_1_
  239.0 1.7 collective-permute-start.34
  240.6 1.9 collective-permute-done.52.refs_2_
  243.9 12.8 %collective-permute-done.53.refs_3_ = bf16[512,256]{1,0:T(8,128)(2,1)} collective-permute-done((bf16[512,256]{1,0:T(8,128)(2,1)}, bf16[512,256]{1,0:T(8,128)(2,1)}, u32[]{:S(2)}, u32[]{:S(2)}) %collective-permute-start.53) | collective-permute-done | bytes 262176 | tf_op jit(solution)/shard_map/ppermute | solution.py:21
  257.6 1.9 collect.12
  260.2 2.3 collective-permute-start.40
  262.6 1.6 copy-done.23
  264.8 2.0 own_grad.7
  266.8 2.0 own_grad.5
  273.3 1.9 collect.8
  275.2 5.5 %collective-permute-done.40.refs_3_ = bf16[512,384]{1,0:T(8,128)(2,1)S(1)} collective-permute-done((bf16[512,384]{1,0:T(8,128)(2,1)}, bf16[512,384]{1,0:T(8,128)(2,1)S(1)}, u32[]{:S(2)}, u32[]{:S(2)}) %collective-permute-start.40) | collective-permute-done | bytes 393248 | tf_op jit(solution)/shard_map/ppermute | solution.py:21
  282.9 8.8 %collective-permute-done.57.refs_1_ = bf16[512,512]{1,0:T(8,128)(2,1)S(1)} collective-permute-done((bf16[512,512]{1,0:T(8,128)(2,1)S(1)}, bf16[512,512]{1,0:T(8,128)(2,1)S(1)}, u32[]{:S(2)}, u32[]{:S(2)}) %collective-permute-start.57) | collective-permute-done | bytes 524320 | tf_op jit(solution)/shard_map/ppermute | solution.py:21
  291.7 11.2 %collective-permute-done.29.refs_1_ = bf16[512,512]{1,0:T(8,128)(2,1)S(1)} collective-permute-done((bf16[512,512]{1,0:T(8,128)(2,1)S(1)}, bf16[512,512]{1,0:T(8,128)(2,1)S(1)}, u32[]{:S(2)}, u32[]{:S(2)}) %collective-permute-start.29) | collective-permute-done | bytes 524320 | tf_op jit(solution)/shard_map/ppermute | solution.py:21
  304.6 2.0 own_grad.6
  307.8 6.3 %collective-permute-done.48.refs_1_ = bf16[512,512]{1,0:T(8,128)(2,1)S(1)} collective-permute-done((bf16[512,512]{1,0:T(8,128)(2,1)S(1)}, bf16[512,512]{1,0:T(8,128)(2,1)S(1)}, u32[]{:S(2)}, u32[]{:S(2)}) %collective-permute-start.48) | collective-permute-done | bytes 524320 | tf_op jit(solution)/shard_map/ppermute | solution.py:21
  314.3 2.0 own_grad.4
  318.8 5.8 %collective-permute-done.44.refs_1_ = bf16[512,512]{1,0:T(8,128)(2,1)S(1)} collective-permute-done((bf16[512,512]{1,0:T(8,128)(2,1)S(1)}, bf16[512,512]{1,0:T(8,128)(2,1)S(1)}, u32[]{:S(2)}, u32[]{:S(2)}) %collective-permute-start.44) | collective-permute-done | bytes 524320 | tf_op jit(solution)/shard_map/ppermute | solution.py:21
  330.0 8.8 %collective-permute-done.36 = bf16[4,128,384]{2,1,0:T(8,128)(2,1)S(1)} collective-permute-done((bf16[4,128,384]{2,1,0:T(8,128)(2,1)S(1)}, bf16[4,128,384]{2,1,0:T(8,128)(2,1)S(1)}, u32[]{:S(2)}, u32[]{:S(2)}) %collective-permute-start.36) | collective-permute-done | bytes 393248 | tf_op jit(solution)/shard_map/ppermute | solution.py:26
  344.5 17.5 %collective-permute-done.59 = bf16[4,128,512]{2,1,0:T(8,128)(2,1)S(1)} collective-permute-done((bf16[4,128,512]{2,1,0:T(8,128)(2,1)S(1)}, bf16[4,128,512]{2,1,0:T(8,128)(2,1)S(1)}, u32[]{:S(2)}, u32[]{:S(2)}) %collective-permute-start.59) | collective-permute-done | bytes 524320 | tf_op jit(solution)/shard_map/ppermute | solution.py:26
  363.7 9.5 %collective-permute-done.46 = bf16[4,128,512]{2,1,0:T(8,128)(2,1)S(1)} collective-permute-done((bf16[4,128,512]{2,1,0:T(8,128)(2,1)S(1)}, bf16[4,128,512]{2,1,0:T(8,128)(2,1)S(1)}, u32[]{:S(2)}, u32[]{:S(2)}) %collective-permute-start.46) | collective-permute-done | bytes 524320 | tf_op jit(solution)/shard_map/ppermute | solution.py:26
  377.7 5.2 %design_grad.3 = bf16[1024,512]{1,0:T(8,128)(2,1)S(1)} custom-call(bf16[512,1024]{1,0:T(8,128)(2,1)S(1)} %get-tuple-element.88.refs_0_, bf16[512,1024]{1,0:T(8,128)(2,1)S(1)} %get-tuple-element.90.refs_1_, bf16[512,1024]{1,0:T(8,128)(2,1)S(1)} %get-tuple-element.92.refs_2_, bf16[512,1024]{1,0:T(8,128)(2,1)S(1)} %get-tuple-element.94.refs_3_, ...), custom_call_target="tpu_custom_call" | custom-call | tf_op jit(solution)/shard_map/design_grad/pallas_call | solution.py:387
  383.0 5.2 %design_grad.2 = bf16[1024,512]{1,0:T(8,128)(2,1)S(1)} custom-call(bf16[512,1024]{1,0:T(8,128)(2,1)S(1)} %get-tuple-element.88.refs_0_, bf16[512,1024]{1,0:T(8,128)(2,1)S(1)} %get-tuple-element.90.refs_1_, bf16[512,1024]{1,0:T(8,128)(2,1)S(1)} %get-tuple-element.92.refs_2_, bf16[512,1024]{1,0:T(8,128)(2,1)S(1)} %get-tuple-element.94.refs_3_, ...), custom_call_target="tpu_custom_call" | custom-call | tf_op jit(solution)/shard_map/design_grad/pallas_call | solution.py:387
  388.3 1.6 pad_maximum_fusion
  389.9 14.0 %collective-permute-done.43 = bf16[4,128,384]{2,1,0:T(8,128)(2,1)S(1)} collective-permute-done((bf16[4,128,384]{2,1,0:T(8,128)(2,1)S(1)}, bf16[4,128,384]{2,1,0:T(8,128)(2,1)S(1)}, u32[]{:S(2)}, u32[]{:S(2)}) %collective-permute-start.43) | collective-permute-done | bytes 393248 | tf_op jit(solution)/shard_map/ppermute | solution.py:21
  403.9 1.7 collective-permute-done.47
  (289 shorter events, 76.1 us)
Async XLA Ops:
  2.5 52.5 %collective-permute-start.17 = (bf16[4,128,512]{2,1,0:T(8,128)(2,1)S(1)}, bf16[4,128,512]{2,1,0:T(8,128)(2,1)S(1)}, u32[]{:S(2)}, u32[]{:S(2)}) collective-permute-start(bf16[4,128,512]{2,1,0:T(8,128)(2,1)S(1)} %get-tuple-element.143), channel_id=1, source_target_pairs={{0,16},{4,20},{8,24},{12,28},{16,0},{20,4},{24,8},{28,12},{1,17},{... | collective-permute-start | bytes 1572872 | tf_op jit(solution)/shard_map/ppermute | solution.py:21
  6.6 55.6 %collective-permute-start.7 = (bf16[4,128,512]{2,1,0:T(8,128)(2,1)S(1)}, bf16[4,128,512]{2,1,0:T(8,128)(2,1)S(1)}, u32[]{:S(2)}, u32[]{:S(2)}) collective-permute-start(bf16[4,128,512]{2,1,0:T(8,128)(2,1)S(1)} %get-tuple-element.143), channel_id=1, source_target_pairs={{0,8},{4,12},{8,0},{12,4},{16,24},{20,28},{24,16},{28,20},{1,9},{5... | collective-permute-start | bytes 1572872 | tf_op jit(solution)/shard_map/ppermute | solution.py:21
  8.2 54.0 %collective-permute-start.13 = (bf16[4,128,512]{2,1,0:T(8,128)(2,1)S(1)}, bf16[4,128,512]{2,1,0:T(8,128)(2,1)S(1)}, u32[]{:S(2)}, u32[]{:S(2)}) collective-permute-start(bf16[4,128,512]{2,1,0:T(8,128)(2,1)S(1)} %get-tuple-element.144), channel_id=1, source_target_pairs={{0,16},{4,20},{8,24},{12,28},{16,0},{20,4},{24,8},{28,12},{1,17},{... | collective-permute-start | bytes 1572872 | tf_op jit(solution)/shard_map/ppermute | solution.py:21
  8.5 54.3 %collective-permute-start.3 = (bf16[4,128,512]{2,1,0:T(8,128)(2,1)S(1)}, bf16[4,128,512]{2,1,0:T(8,128)(2,1)S(1)}, u32[]{:S(2)}, u32[]{:S(2)}) collective-permute-start(bf16[4,128,512]{2,1,0:T(8,128)(2,1)S(1)} %get-tuple-element.144), channel_id=1, source_target_pairs={{0,8},{4,12},{8,0},{12,4},{16,24},{20,28},{24,16},{28,20},{1,9},{5... | collective-permute-start | bytes 1572872 | tf_op jit(solution)/shard_map/ppermute | solution.py:21
  9.2 44.3 %collective-permute-start.21 = (s32[4]{0:T(128)S(1)}, s32[4]{0:T(128)S(1)}, u32[]{:S(2)}, u32[]{:S(2)}) collective-permute-start(s32[4]{0:T(128)S(1)} %get-tuple-element.156), channel_id=1, source_target_pairs={{0,12},{4,8},{8,4},{12,0},{16,28},{20,24},{24,20},{28,16},{1,13},{... | collective-permute-start | bytes 56 | tf_op jit(solution)/shard_map/ppermute | solution.py:21
  62.2 24.5 %collective-permute-start.8 = (bf16[4,128,512]{2,1,0:T(8,128)(2,1)S(1)}, bf16[4,128,512]{2,1,0:T(8,128)(2,1)S(1)}, u32[]{:S(2)}, u32[]{:S(2)}) collective-permute-start(bf16[4,128,512]{2,1,0:T(8,128)(2,1)S(1)} %collective-permute-done.7.refs_1_), channel_id=1, source_target_pairs={{0,2},{1,3},{2,0},{3,1},{4,6},{5,7},{6,4},{7,5},{8,10},{9,11},{10,... | collective-permute-start | bytes 1572872 | tf_op jit(solution)/shard_map/ppermute | solution.py:26
  62.8 35.1 %collective-permute-start.14 = (bf16[4,128,512]{2,1,0:T(8,128)(2,1)S(1)}, bf16[4,128,512]{2,1,0:T(8,128)(2,1)S(1)}, u32[]{:S(2)}, u32[]{:S(2)}) collective-permute-start(bf16[4,128,512]{2,1,0:T(8,128)(2,1)S(1)} %collective-permute-done.13.refs_1_.refs_3_), channel_id=1, source_target_pairs={{0,2},{1,3},{2,0},{3,1},{4,6},{5,7},{6,4},{7,5},{8,10},{9,11},{10,... | collective-permute-start | bytes 1572872 | tf_op jit(solution)/shard_map/ppermute | solution.py:26
  64.3 41.2 %collective-permute-start.4 = (bf16[4,128,512]{2,1,0:T(8,128)(2,1)S(1)}, bf16[4,128,512]{2,1,0:T(8,128)(2,1)S(1)}, u32[]{:S(2)}, u32[]{:S(2)}) collective-permute-start(bf16[4,128,512]{2,1,0:T(8,128)(2,1)S(1)} %collective-permute-done.3.refs_1_), channel_id=1, source_target_pairs={{0,2},{1,3},{2,0},{3,1},{4,6},{5,7},{6,4},{7,5},{8,10},{9,11},{10,... | collective-permute-start | bytes 1572872 | tf_op jit(solution)/shard_map/ppermute | solution.py:26
  75.5 30.0 %collective-permute-start.20 = (bf16[4,128,512]{2,1,0:T(8,128)(2,1)S(1)}, bf16[4,128,512]{2,1,0:T(8,128)(2,1)S(1)}, u32[]{:S(2)}, u32[]{:S(2)}) collective-permute-start(bf16[4,128,512]{2,1,0:T(8,128)(2,1)S(1)} %collective-permute-done.18.refs_2_.refs_4_), channel_id=1, source_target_pairs={{0,1},{1,0},{2,3},{3,2},{4,5},{5,4},{6,7},{7,6},{8,9},{9,8},{10,11... | collective-permute-start | bytes 1572872 | tf_op jit(solution)/shard_map/ppermute | solution.py:26
  75.5 38.0 %collective-permute-start.15 = (bf16[4,128,512]{2,1,0:T(8,128)(2,1)S(1)}, bf16[4,128,512]{2,1,0:T(8,128)(2,1)S(1)}, u32[]{:S(2)}, u32[]{:S(2)}) collective-permute-start(bf16[4,128,512]{2,1,0:T(8,128)(2,1)S(1)} %collective-permute-done.13.refs_1_.refs_3_), channel_id=1, source_target_pairs={{0,1},{1,0},{2,3},{3,2},{4,5},{5,4},{6,7},{7,6},{8,9},{9,8},{10,11... | collective-permute-start | bytes 1572872 | tf_op jit(solution)/shard_map/ppermute | solution.py:26
  86.7 27.4 %collective-permute-start.5 = (bf16[4,128,512]{2,1,0:T(8,128)(2,1)S(1)}, bf16[4,128,512]{2,1,0:T(8,128)(2,1)S(1)}, u32[]{:S(2)}, u32[]{:S(2)}) collective-permute-start(bf16[4,128,512]{2,1,0:T(8,128)(2,1)S(1)} %collective-permute-done.3.refs_1_), channel_id=1, source_target_pairs={{0,1},{1,0},{2,3},{3,2},{4,5},{5,4},{6,7},{7,6},{8,9},{9,8},{10,11... | collective-permute-start | bytes 1572872 | tf_op jit(solution)/shard_map/ppermute | solution.py:26
  98.0 17.7 %collective-permute-start.10 = (bf16[4,128,512]{2,1,0:T(8,128)(2,1)S(1)}, bf16[4,128,512]{2,1,0:T(8,128)(2,1)S(1)}, u32[]{:S(2)}, u32[]{:S(2)}) collective-permute-start(bf16[4,128,512]{2,1,0:T(8,128)(2,1)S(1)} %collective-permute-done.8.refs_2_), channel_id=1, source_target_pairs={{0,1},{1,0},{2,3},{3,2},{4,5},{5,4},{6,7},{7,6},{8,9},{9,8},{10,11... | collective-permute-start | bytes 1572872 | tf_op jit(solution)/shard_map/ppermute | solution.py:26
  105.5 15.1 %collective-permute-start.16 = (bf16[4,128,512]{2,1,0:T(8,128)(2,1)S(1)}, bf16[4,128,512]{2,1,0:T(8,128)(2,1)S(1)}, u32[]{:S(2)}, u32[]{:S(2)}) collective-permute-start(bf16[4,128,512]{2,1,0:T(8,128)(2,1)S(1)} %collective-permute-done.14.refs_2_.refs_4_), channel_id=1, source_target_pairs={{0,1},{1,0},{2,3},{3,2},{4,5},{5,4},{6,7},{7,6},{8,9},{9,8},{10,11... | collective-permute-start | bytes 1572872 | tf_op jit(solution)/shard_map/ppermute | solution.py:26
  114.2 25.5 %collective-permute-start.2 = (bf16[4,128,512]{2,1,0:T(8,128)(2,1)S(1)}, bf16[4,128,512]{2,1,0:T(8,128)(2,1)S(1)}, u32[]{:S(2)}, u32[]{:S(2)}) collective-permute-start(bf16[4,128,512]{2,1,0:T(8,128)(2,1)S(1)} %get-tuple-element.71), channel_id=1, source_target_pairs={{0,4},{4,0},{8,12},{12,8},{16,20},{20,16},{24,28},{28,24},{1,5},{5... | collective-permute-start | bytes 1572872 | tf_op jit(solution)/shard_map/ppermute | solution.py:21
  115.7 46.5 %collective-permute-start.24 = (bf16[4,128,512]{2,1,0:T(8,128)(2,1)S(1)}, bf16[4,128,512]{2,1,0:T(8,128)(2,1)S(1)}, u32[]{:S(2)}, u32[]{:S(2)}) collective-permute-start(bf16[4,128,512]{2,1,0:T(8,128)(2,1)S(1)} %get-tuple-element.79), channel_id=1, source_target_pairs={{0,4},{4,0},{8,12},{12,8},{16,20},{20,16},{24,28},{28,24},{1,5},{5... | collective-permute-start | bytes 1572872 | tf_op jit(solution)/shard_map/ppermute | solution.py:21
  117.6 55.7 %collective-permute-start.12 = (bf16[4,128,512]{2,1,0:T(8,128)(2,1)S(1)}, bf16[4,128,512]{2,1,0:T(8,128)(2,1)S(1)}, u32[]{:S(2)}, u32[]{:S(2)}) collective-permute-start(bf16[4,128,512]{2,1,0:T(8,128)(2,1)S(1)} %gather_held.11), channel_id=1, source_target_pairs={{0,4},{4,0},{8,12},{12,8},{16,20},{20,16},{24,28},{28,24},{1,5},{5... | collective-permute-start | bytes 1572872 | tf_op jit(solution)/shard_map/ppermute | solution.py:21
  120.7 63.9 %collective-permute-start.11 = (bf16[4,128,512]{2,1,0:T(8,128)(2,1)S(1)}, bf16[4,128,512]{2,1,0:T(8,128)(2,1)S(1)}, u32[]{:S(2)}, u32[]{:S(2)}) collective-permute-start(bf16[4,128,512]{2,1,0:T(8,128)(2,1)S(1)} %gather_held.10), channel_id=1, source_target_pairs={{0,4},{4,0},{8,12},{12,8},{16,20},{20,16},{24,28},{28,24},{1,5},{5... | collective-permute-start | bytes 1572872 | tf_op jit(solution)/shard_map/ppermute | solution.py:21
  128.4 74.4 %collective-permute-start.26 = (bf16[4,128,512]{2,1,0:T(8,128)(2,1)S(1)}, bf16[4,128,512]{2,1,0:T(8,128)(2,1)S(1)}, u32[]{:S(2)}, u32[]{:S(2)}) collective-permute-start(bf16[4,128,512]{2,1,0:T(8,128)(2,1)S(1)} %get-tuple-element.81), channel_id=1, source_target_pairs={{0,8},{4,12},{8,0},{12,4},{16,24},{20,28},{24,16},{28,20},{1,9},{5... | collective-permute-start | bytes 1572872 | tf_op jit(solution)/shard_map/ppermute | solution.py:21
  139.7 63.2 %collective-permute-start.28 = (bf16[4,128,512]{2,1,0:T(8,128)(2,1)S(1)}, bf16[4,128,512]{2,1,0:T(8,128)(2,1)S(1)}, u32[]{:S(2)}, u32[]{:S(2)}) collective-permute-start(bf16[4,128,512]{2,1,0:T(8,128)(2,1)S(1)} %get-tuple-element.83), channel_id=1, source_target_pairs={{0,12},{4,8},{8,4},{12,0},{16,28},{20,24},{24,20},{28,16},{1,13},{... | collective-permute-start | bytes 1572872 | tf_op jit(solution)/shard_map/ppermute | solution.py:21
  162.1 44.0 %collective-permute-start.23 = (bf16[4,128,512]{2,1,0:T(8,128)(2,1)S(1)}, bf16[4,128,512]{2,1,0:T(8,128)(2,1)S(1)}, u32[]{:S(2)}, u32[]{:S(2)}) collective-permute-start(bf16[4,128,512]{2,1,0:T(8,128)(2,1)S(1)} %get-tuple-element.78), channel_id=1, source_target_pairs={{0,4},{4,0},{8,12},{12,8},{16,20},{20,16},{24,28},{28,24},{1,5},{5... | collective-permute-start | bytes 1572872 | tf_op jit(solution)/shard_map/ppermute | solution.py:21
  173.4 32.8 %collective-permute-start.25 = (bf16[4,128,512]{2,1,0:T(8,128)(2,1)S(1)}, bf16[4,128,512]{2,1,0:T(8,128)(2,1)S(1)}, u32[]{:S(2)}, u32[]{:S(2)}) collective-permute-start(bf16[4,128,512]{2,1,0:T(8,128)(2,1)S(1)} %get-tuple-element.80), channel_id=1, source_target_pairs={{0,8},{4,12},{8,0},{12,4},{16,24},{20,28},{24,16},{28,20},{1,9},{5... | collective-permute-start | bytes 1572872 | tf_op jit(solution)/shard_map/ppermute | solution.py:21
  184.6 21.5 %collective-permute-start.27 = (bf16[4,128,512]{2,1,0:T(8,128)(2,1)S(1)}, bf16[4,128,512]{2,1,0:T(8,128)(2,1)S(1)}, u32[]{:S(2)}, u32[]{:S(2)}) collective-permute-start(bf16[4,128,512]{2,1,0:T(8,128)(2,1)S(1)} %get-tuple-element.82), channel_id=1, source_target_pairs={{0,12},{4,8},{8,4},{12,0},{16,28},{20,24},{24,20},{28,16},{1,13},{... | collective-permute-start | bytes 1572872 | tf_op jit(solution)/shard_map/ppermute | solution.py:21
  218.8 40.8 %collective-permute-start.32 = (bf16[512,384]{1,0:T(8,128)(2,1)}, bf16[512,384]{1,0:T(8,128)(2,1)}, u32[]{:S(2)}, u32[]{:S(2)}) collective-permute-start(bf16[512,384]{1,0:T(8,128)(2,1)} %get-tuple-element.104), channel_id=1, source_target_pairs={{0,4},{4,0},{8,12},{12,8},{16,20},{20,16},{24,28},{28,24},{1,5},{5... | collective-permute-start | bytes 1179656 | tf_op jit(solution)/shard_map/ppermute | solution.py:21
  233.8 26.4 %collective-permute-start.33 = (bf16[512,384]{1,0:T(8,128)(2,1)}, bf16[512,384]{1,0:T(8,128)(2,1)}, u32[]{:S(2)}, u32[]{:S(2)}) collective-permute-start(bf16[512,384]{1,0:T(8,128)(2,1)} %get-tuple-element.105), channel_id=1, source_target_pairs={{0,8},{4,12},{8,0},{12,4},{16,24},{20,28},{24,16},{28,20},{1,9},{5... | collective-permute-start | bytes 1179656 | tf_op jit(solution)/shard_map/ppermute | solution.py:21
  235.1 21.6 %collective-permute-start.53 = (bf16[512,256]{1,0:T(8,128)(2,1)}, bf16[512,256]{1,0:T(8,128)(2,1)}, u32[]{:S(2)}, u32[]{:S(2)}) collective-permute-start(bf16[512,256]{1,0:T(8,128)(2,1)} %get-tuple-element.126), channel_id=1, source_target_pairs={{0,12},{4,8},{8,4},{12,0},{16,28},{20,24},{24,20},{28,16},{1,13},{... | collective-permute-start | bytes 786440 | tf_op jit(solution)/shard_map/ppermute | solution.py:21
  239.0 29.8 %collective-permute-start.34 = (bf16[512,384]{1,0:T(8,128)(2,1)}, bf16[512,384]{1,0:T(8,128)(2,1)S(1)}, u32[]{:S(2)}, u32[]{:S(2)}) collective-permute-start(bf16[512,384]{1,0:T(8,128)(2,1)} %get-tuple-element.106), channel_id=1, source_target_pairs={{0,12},{4,8},{8,4},{12,0},{16,28},{20,24},{24,20},{28,16},{1,13},{... | collective-permute-start | bytes 1179656 | tf_op jit(solution)/shard_map/ppermute | solution.py:21
  242.5 26.9 %collective-permute-start.38 = (bf16[512,384]{1,0:T(8,128)(2,1)}, bf16[512,384]{1,0:T(8,128)(2,1)S(1)}, u32[]{:S(2)}, u32[]{:S(2)}) collective-permute-start(bf16[512,384]{1,0:T(8,128)(2,1)} %copy-done.72), channel_id=1, source_target_pairs={{0,4},{4,0},{8,12},{12,8},{16,20},{20,16},{24,28},{28,24},{1,5},{5... | collective-permute-start | bytes 1179656 | tf_op jit(solution)/shard_map/ppermute | solution.py:21
  259.5 23.1 %collective-permute-start.54 = (bf16[8,128,256]{2,1,0:T(8,128)(2,1)S(1)}, bf16[8,128,256]{2,1,0:T(8,128)(2,1)S(1)}, u32[]{:S(2)}, u32[]{:S(2)}) collective-permute-start(bf16[8,128,256]{2,1,0:T(8,128)(2,1)S(1)} %get-tuple-element.128), channel_id=1, source_target_pairs={{0,1},{1,0},{2,3},{3,2},{4,5},{5,4},{6,7},{7,6},{8,9},{9,8},{10,11... | collective-permute-start | bytes 1572872 | tf_op jit(solution)/shard_map/ppermute | solution.py:26
  260.2 20.5 %collective-permute-start.40 = (bf16[512,384]{1,0:T(8,128)(2,1)}, bf16[512,384]{1,0:T(8,128)(2,1)S(1)}, u32[]{:S(2)}, u32[]{:S(2)}) collective-permute-start(bf16[512,384]{1,0:T(8,128)(2,1)} %copy-done.70), channel_id=1, source_target_pairs={{0,12},{4,8},{8,4},{12,0},{16,28},{20,24},{24,20},{28,16},{1,13},{... | collective-permute-start | bytes 1179656 | tf_op jit(solution)/shard_map/ppermute | solution.py:21
  268.7 22.9 %collective-permute-start.57 = (bf16[512,512]{1,0:T(8,128)(2,1)S(1)}, bf16[512,512]{1,0:T(8,128)(2,1)S(1)}, u32[]{:S(2)}, u32[]{:S(2)}) collective-permute-start(bf16[512,512]{1,0:T(8,128)(2,1)S(1)} %get-tuple-element.130), channel_id=1, source_target_pairs={{0,4},{4,0},{8,12},{12,8},{16,20},{20,16},{24,28},{28,24},{1,5},{5... | collective-permute-start | bytes 1572872 | tf_op jit(solution)/shard_map/ppermute | solution.py:21
  269.4 33.5 %collective-permute-start.29 = (bf16[512,512]{1,0:T(8,128)(2,1)S(1)}, bf16[512,512]{1,0:T(8,128)(2,1)S(1)}, u32[]{:S(2)}, u32[]{:S(2)}) collective-permute-start(bf16[512,512]{1,0:T(8,128)(2,1)S(1)} %get-tuple-element.100), channel_id=1, source_target_pairs={{0,4},{4,0},{8,12},{12,8},{16,20},{20,16},{24,28},{28,24},{1,5},{5... | collective-permute-start | bytes 1572872 | tf_op jit(solution)/shard_map/ppermute | solution.py:21
  271.8 42.3 %collective-permute-start.48 = (bf16[512,512]{1,0:T(8,128)(2,1)S(1)}, bf16[512,512]{1,0:T(8,128)(2,1)S(1)}, u32[]{:S(2)}, u32[]{:S(2)}) collective-permute-start(bf16[512,512]{1,0:T(8,128)(2,1)S(1)} %get-tuple-element.120), channel_id=1, source_target_pairs={{0,4},{4,0},{8,12},{12,8},{16,20},{20,16},{24,28},{28,24},{1,5},{5... | collective-permute-start | bytes 1572872 | tf_op jit(solution)/shard_map/ppermute | solution.py:21
  280.7 43.9 %collective-permute-start.44 = (bf16[512,512]{1,0:T(8,128)(2,1)S(1)}, bf16[512,512]{1,0:T(8,128)(2,1)S(1)}, u32[]{:S(2)}, u32[]{:S(2)}) collective-permute-start(bf16[512,512]{1,0:T(8,128)(2,1)S(1)} %get-tuple-element.116), channel_id=1, source_target_pairs={{0,4},{4,0},{8,12},{12,8},{16,20},{20,16},{24,28},{28,24},{1,5},{5... | collective-permute-start | bytes 1572872 | tf_op jit(solution)/shard_map/ppermute | solution.py:21
  282.6 44.2 %collective-permute-start.35 = (bf16[8,128,384]{2,1,0:T(8,128)(2,1)S(1)}, bf16[8,128,384]{2,1,0:T(8,128)(2,1)S(1)}, u32[]{:S(2)}, u32[]{:S(2)}) collective-permute-start(bf16[8,128,384]{2,1,0:T(8,128)(2,1)S(1)} %get-tuple-element.108), channel_id=1, source_target_pairs={{0,1},{1,0},{2,3},{3,2},{4,5},{5,4},{6,7},{7,6},{8,9},{9,8},{10,11... | collective-permute-start | bytes 2359304 | tf_op jit(solution)/shard_map/ppermute | solution.py:26
  291.7 35.5 %collective-permute-start.41 = (bf16[8,128,384]{2,1,0:T(8,128)(2,1)S(1)}, bf16[8,128,384]{2,1,0:T(8,128)(2,1)S(1)}, u32[]{:S(2)}, u32[]{:S(2)}) collective-permute-start(bf16[8,128,384]{2,1,0:T(8,128)(2,1)S(1)} %get-tuple-element.114), channel_id=1, source_target_pairs={{0,1},{1,0},{2,3},{3,2},{4,5},{5,4},{6,7},{7,6},{8,9},{9,8},{10,11... | collective-permute-start | bytes 2359304 | tf_op jit(solution)/shard_map/ppermute | solution.py:26
  302.9 23.3 %collective-permute-start.55 = (bf16[4,128,256]{2,1,0:T(8,128)(2,1)S(1)}, bf16[4,128,256]{2,1,0:T(8,128)(2,1)S(1)}, u32[]{:S(2)}, u32[]{:S(2)}) collective-permute-start(bf16[4,128,256]{2,1,0:T(8,128)(2,1)S(1)} %slice.164), channel_id=1, source_target_pairs={{0,2},{1,3},{2,0},{3,1},{4,6},{5,7},{6,4},{7,5},{8,10},{9,11},{10,... | collective-permute-start | bytes 786440 | tf_op jit(solution)/shard_map/ppermute | solution.py:26
  324.6 15.7 %collective-permute-start.49 = (bf16[8,128,512]{2,1,0:T(8,128)(2,1)S(1)}, bf16[8,128,512]{2,1,0:T(8,128)(2,1)S(1)}, u32[]{:S(2)}, u32[]{:S(2)}) collective-permute-start(bf16[8,128,512]{2,1,0:T(8,128)(2,1)S(1)} %get-tuple-element.122), channel_id=1, source_target_pairs={{0,1},{1,0},{2,3},{3,2},{4,5},{5,4},{6,7},{7,6},{8,9},{9,8},{10,11... | collective-permute-start | bytes 3145736 | tf_op jit(solution)/shard_map/ppermute | solution.py:26
  326.2 16.2 %collective-permute-start.30 = (bf16[8,128,512]{2,1,0:T(8,128)(2,1)S(1)}, bf16[8,128,512]{2,1,0:T(8,128)(2,1)S(1)}, u32[]{:S(2)}, u32[]{:S(2)}) collective-permute-start(bf16[8,128,512]{2,1,0:T(8,128)(2,1)S(1)} %get-tuple-element.102), channel_id=1, source_target_pairs={{0,1},{1,0},{2,3},{3,2},{4,5},{5,4},{6,7},{7,6},{8,9},{9,8},{10,11... | collective-permute-start | bytes 3145736 | tf_op jit(solution)/shard_map/ppermute | solution.py:26
  329.0 45.9 %collective-permute-start.56 = (bf16[4,128,256]{2,1,0:T(8,128)(2,1)S(1)}, bf16[4,128,256]{2,1,0:T(8,128)(2,1)S(1)}, u32[]{:S(2)}, u32[]{:S(2)}) collective-permute-start(bf16[4,128,256]{2,1,0:T(8,128)(2,1)S(1)} %fusion.8), channel_id=1, source_target_pairs={{0,16},{4,20},{8,24},{12,28},{16,0},{20,4},{24,8},{28,12},{1,17},{... | collective-permute-start | bytes 786440 | tf_op jit(solution)/shard_map/ppermute | solution.py:21
  338.8 37.0 %collective-permute-start.42 = (bf16[4,128,384]{2,1,0:T(8,128)(2,1)S(1)}, bf16[4,128,384]{2,1,0:T(8,128)(2,1)S(1)}, u32[]{:S(2)}, u32[]{:S(2)}) collective-permute-start(bf16[4,128,384]{2,1,0:T(8,128)(2,1)S(1)} %slice.162), channel_id=1, source_target_pairs={{0,2},{1,3},{2,0},{3,1},{4,6},{5,7},{6,4},{7,5},{8,10},{9,11},{10,... | collective-permute-start | bytes 1179656 | tf_op jit(solution)/shard_map/ppermute | solution.py:26
  340.4 36.7 %collective-permute-start.37 = (bf16[4,128,384]{2,1,0:T(8,128)(2,1)S(1)}, bf16[4,128,384]{2,1,0:T(8,128)(2,1)S(1)}, u32[]{:S(2)}, u32[]{:S(2)}) collective-permute-start(bf16[4,128,384]{2,1,0:T(8,128)(2,1)S(1)} %fusion.7), channel_id=1, source_target_pairs={{0,16},{4,20},{8,24},{12,28},{16,0},{20,4},{24,8},{28,12},{1,17},{... | collective-permute-start | bytes 1179656 | tf_op jit(solution)/shard_map/ppermute | solution.py:21
  341.3 20.7 %collective-permute-start.59 = (bf16[4,128,512]{2,1,0:T(8,128)(2,1)S(1)}, bf16[4,128,512]{2,1,0:T(8,128)(2,1)S(1)}, u32[]{:S(2)}, u32[]{:S(2)}) collective-permute-start(bf16[4,128,512]{2,1,0:T(8,128)(2,1)S(1)} %slice.158), channel_id=1, source_target_pairs={{0,2},{1,3},{2,0},{3,1},{4,6},{5,7},{6,4},{7,5},{8,10},{9,11},{10,... | collective-permute-start | bytes 1572872 | tf_op jit(solution)/shard_map/ppermute | solution.py:26
  342.4 30.8 %collective-permute-start.46 = (bf16[4,128,512]{2,1,0:T(8,128)(2,1)S(1)}, bf16[4,128,512]{2,1,0:T(8,128)(2,1)S(1)}, u32[]{:S(2)}, u32[]{:S(2)}) collective-permute-start(bf16[4,128,512]{2,1,0:T(8,128)(2,1)S(1)} %slice.160), channel_id=1, source_target_pairs={{0,2},{1,3},{2,0},{3,1},{4,6},{5,7},{6,4},{7,5},{8,10},{9,11},{10,... | collective-permute-start | bytes 1572872 | tf_op jit(solution)/shard_map/ppermute | solution.py:26
  362.0 41.9 %collective-permute-start.50 = (bf16[4,128,512]{2,1,0:T(8,128)(2,1)S(1)}, bf16[4,128,512]{2,1,0:T(8,128)(2,1)S(1)}, u32[]{:S(2)}, u32[]{:S(2)}) collective-permute-start(bf16[4,128,512]{2,1,0:T(8,128)(2,1)S(1)} %slice.159), channel_id=1, source_target_pairs={{0,2},{1,3},{2,0},{3,1},{4,6},{5,7},{6,4},{7,5},{8,10},{9,11},{10,... | collective-permute-start | bytes 1572872 | tf_op jit(solution)/shard_map/ppermute | solution.py:26
  373.2 30.7 %collective-permute-start.31 = (bf16[4,128,512]{2,1,0:T(8,128)(2,1)S(1)}, bf16[4,128,512]{2,1,0:T(8,128)(2,1)S(1)}, u32[]{:S(2)}, u32[]{:S(2)}) collective-permute-start(bf16[4,128,512]{2,1,0:T(8,128)(2,1)S(1)} %slice.161), channel_id=1, source_target_pairs={{0,2},{1,3},{2,0},{3,1},{4,6},{5,7},{6,4},{7,5},{8,10},{9,11},{10,... | collective-permute-start | bytes 1572872 | tf_op jit(solution)/shard_map/ppermute | solution.py:26
  374.9 29.0 %collective-permute-start.60 = (bf16[4,128,512]{2,1,0:T(8,128)(2,1)S(1)}, bf16[4,128,512]{2,1,0:T(8,128)(2,1)S(1)}, u32[]{:S(2)}, u32[]{:S(2)}) collective-permute-start(bf16[4,128,512]{2,1,0:T(8,128)(2,1)S(1)} %fusion), channel_id=1, source_target_pairs={{0,8},{4,12},{8,0},{12,4},{16,24},{20,28},{24,16},{28,20},{1,9},{5... | collective-permute-start | bytes 1572872 | tf_op jit(solution)/shard_map/ppermute | solution.py:21
  375.8 29.9 %collective-permute-start.47 = (bf16[4,128,512]{2,1,0:T(8,128)(2,1)S(1)}, bf16[4,128,512]{2,1,0:T(8,128)(2,1)S(1)}, u32[]{:S(2)}, u32[]{:S(2)}) collective-permute-start(bf16[4,128,512]{2,1,0:T(8,128)(2,1)S(1)} %fusion.3), channel_id=1, source_target_pairs={{0,8},{4,12},{8,0},{12,4},{16,24},{20,28},{24,16},{28,20},{1,9},{5... | collective-permute-start | bytes 1572872 | tf_op jit(solution)/shard_map/ppermute | solution.py:21
  377.1 26.8 %collective-permute-start.43 = (bf16[4,128,384]{2,1,0:T(8,128)(2,1)S(1)}, bf16[4,128,384]{2,1,0:T(8,128)(2,1)S(1)}, u32[]{:S(2)}, u32[]{:S(2)}) collective-permute-start(bf16[4,128,384]{2,1,0:T(8,128)(2,1)S(1)} %fusion.6), channel_id=1, source_target_pairs={{0,16},{4,20},{8,24},{12,28},{16,0},{20,4},{24,8},{28,12},{1,17},{... | collective-permute-start | bytes 1179656 | tf_op jit(solution)/shard_map/ppermute | solution.py:21
  (87 other events, 2281.5 us)
